TPU v7x, 256 devices: a whole 4x4x8 slice. The times are simulated.
256 devices in a mesh: frag: 32 (over x, z), basis: 8 (over y, core).
Axes of the slice: x: 4, y: 4, z: 8, core: 2. Of those that a mesh axis runs over, the one named last changes fastest.
Arguments:
- density: bfloat16 [1024, 256, 256], P('frag', 'basis'), as said below
- aux_factor: bfloat16 [1024, 256, 1024], P('frag', None, 'basis')
- pairs: int32 [1024, 2], P(('frag', 'basis')), may hold values from 0 to 1023, as said below
- slot_of: int32 [1024], replicated, may hold values from 0 to 1023, as said below
- costs: int32 [1024], P(('frag', 'basis')), may hold values from 1 to 5
Outputs:
- density_shift: float32 [1024, 256, 256], P('frag', 'basis')
- embedding: float32 [1024, 1024], P('frag', 'basis')
Inputs may be any that keep to these rules, and one draw needn't show every extreme that they name: Each density[s] is symmetric. A permutation: slot_of[f] is the storage slot of fragment f, and a slot s lies on index s // 32 of frag. The two fragments of a dimer differ. The rows of pairs on one index of frag hold 64 fragment references; at most 3 of them name fragments stored on any one index of frag, and in every draw some index of frag stores exactly 3 of them.
All inputs are finite; a program needn't handle non-finite values.
Results may differ from a plain program's by a relative error of at most 0.015.
Values may be sent and summed in bfloat16 or wider, within the bound.
No kernel may reach another device: no remote copies, remote signals or barrier semaphores. Data moves between devices by JAX's collectives and lax.ppermute only.
A program may use at most 64 MiB of HBM per device.

v0:
```python
import jax
import jax.numpy as jnp
from jax import lax
from jax.sharding import PartitionSpec as P

COUPLE = 0.015625


def purify_step(index, current):
    square = jnp.dot(current, current, preferred_element_type=jnp.float32)
    cube_term = jnp.dot(square.astype(jnp.bfloat16), current, preferred_element_type=jnp.float32)
    return (3.0 * square - 2.0 * cube_term).astype(jnp.bfloat16)


def fit_pair(rows_pair, aux_pair):
    projected = jnp.einsum(
        "smn,sbnq->sbmq", rows_pair, aux_pair, preferred_element_type=jnp.float32
    )
    return jnp.sum(aux_pair.astype(jnp.float32) * projected, axis=2).astype(jnp.bfloat16)


def dimer_pass(rows_pair, aux_pair, fitted_pair, steps):
    basis_width = rows_pair.shape[1]
    stacked = jnp.concatenate([aux_pair[0], aux_pair[1]], axis=1)
    coeff = fitted_pair[0].astype(jnp.float32) + fitted_pair[1].astype(jnp.float32)
    weighted = (stacked.astype(jnp.float32) * coeff[:, None, :]).astype(jnp.bfloat16)
    coulomb = jnp.einsum("bmq,bnq->mn", weighted, stacked, preferred_element_type=jnp.float32)
    rows_first = rows_pair[0].astype(jnp.float32)
    rows_second = rows_pair[1].astype(jnp.float32)
    zero_block = jnp.zeros_like(rows_first)
    blocks = jnp.block([[rows_first, zero_block], [zero_block, rows_second]])
    whole_eye = jnp.eye(2 * basis_width, dtype=jnp.float32)
    start = (0.5 * whole_eye + blocks + COUPLE * coulomb).astype(jnp.bfloat16)
    final = lax.fori_loop(0, steps, purify_step, start).astype(jnp.float32)
    half_eye = 0.5 * jnp.eye(basis_width, dtype=jnp.float32)
    change_first = final[:basis_width, :basis_width] - rows_first - half_eye
    change_second = final[basis_width:, basis_width:] - rows_second - half_eye
    changes = jnp.stack([change_first, change_second])
    partner = jnp.stack([fitted_pair[1], fitted_pair[0]]).astype(jnp.float32)
    return (changes, partner)


def shards(density, aux_factor, pairs, slot_of, costs):
    n_frag = lax.axis_size("frag")
    n_basis = lax.axis_size("basis")
    frag_index = lax.axis_index("frag")
    basis_index = lax.axis_index("basis")
    frag_dev, rows_dev, basis_width = density.shape
    aux_dev = aux_factor.shape[2]
    dimers_dev = pairs.shape[0]
    dimers_col = dimers_dev * n_basis
    refs_col = 2 * dimers_col
    refs_dev = 2 * dimers_dev
    capacity = 3 * dimers_col // n_frag
    all_pairs, all_costs = (
        lax.all_gather(pairs, ("frag", "basis"), axis=0, tiled=True),
        lax.all_gather(costs, ("frag", "basis"), axis=0, tiled=True),
    )
    lookup = all_pairs[:, :, None] == jnp.arange(slot_of.shape[0], dtype=jnp.int32)
    all_slots = jnp.sum(jnp.where(lookup, slot_of, 0), axis=2)
    col_slots = all_slots.reshape(n_frag, refs_col)
    col_owner = col_slots // frag_dev
    col_local = col_slots % frag_dev
    positions = jnp.arange(refs_col, dtype=jnp.int32)
    same_owner = col_owner[:, :, None] == col_owner[:, None, :]
    col_rank = jnp.sum(
        (same_owner & (positions[:, None] > positions[None, :])).astype(jnp.int32), axis=2
    )
    owned_here = col_owner == frag_index
    matches = owned_here[:, :, None] & (
        col_rank[:, :, None] == jnp.arange(capacity, dtype=jnp.int32)
    )
    send_local = jnp.sum(jnp.where(matches, col_local[:, :, None], 0), axis=1)
    is_live = jnp.any(matches, axis=1)
    flat_local = send_local.reshape(-1)
    out_rows = jnp.take(density, flat_local, axis=0).reshape(
        n_frag, capacity, rows_dev, basis_width
    )
    out_aux = jnp.take(aux_factor, flat_local, axis=0).reshape(
        n_frag, capacity, basis_width, aux_dev
    )
    my_owner = lax.dynamic_index_in_dim(col_owner, frag_index, 0, keepdims=False)
    my_rank = lax.dynamic_index_in_dim(col_rank, frag_index, 0, keepdims=False)
    my_position = my_owner * capacity + my_rank
    col_costs = lax.dynamic_index_in_dim(
        all_costs.reshape(n_frag, dimers_col), frag_index, 0, keepdims=False
    )
    assign = jnp.arange(dimers_col, dtype=jnp.int32).reshape(n_basis, dimers_dev)
    ref_of = (2 * assign[:, :, None] + jnp.arange(2, dtype=jnp.int32)).reshape(n_basis, refs_dev)
    pick = my_position[ref_of.T]
    my_assign = lax.dynamic_index_in_dim(assign, basis_index, 0, keepdims=False)
    my_steps = jnp.take(col_costs, my_assign, axis=0)
    in_rows, in_aux = (
        lax.all_to_all(out_rows, "frag", split_axis=0, concat_axis=0, tiled=True),
        lax.all_to_all(out_aux, "frag", split_axis=0, concat_axis=0, tiled=True),
    )
    send_rows = jnp.take(in_rows.reshape(n_frag * capacity, rows_dev, basis_width), pick, axis=0)
    send_aux = jnp.take(in_aux.reshape(n_frag * capacity, basis_width, aux_dev), pick, axis=0)
    got_rows, got_aux = (
        lax.all_to_all(
            send_rows.reshape(refs_dev, n_basis * rows_dev, basis_width),
            "basis",
            split_axis=1,
            concat_axis=1,
            tiled=True,
        ),
        lax.all_to_all(send_aux, "basis", split_axis=1, concat_axis=1, tiled=True),
    )
    rows_pairs = got_rows.reshape(dimers_dev, 2, basis_width, basis_width)
    aux_pairs = got_aux.reshape(dimers_dev, 2, n_basis, basis_width, aux_dev)

    def visit(carry, item):
        rows_pair, aux_pair, fit_given, steps = item
        fitted_pair = fit_pair(rows_pair, aux_pair)
        return (carry, dimer_pass(rows_pair, aux_pair, fitted_pair, steps))

    unused, outcome = lax.scan(visit, 0, (rows_pairs, aux_pairs, None, my_steps))
    changes, partners = outcome
    back_rows, back_fit = (
        lax.all_to_all(
            changes.reshape(refs_dev, basis_width, basis_width).astype(jnp.bfloat16),
            "basis",
            split_axis=1,
            concat_axis=0,
            tiled=True,
        ).astype(jnp.float32),
        lax.all_to_all(
            partners.reshape(refs_dev, n_basis, aux_dev).astype(jnp.bfloat16),
            "basis",
            split_axis=1,
            concat_axis=0,
            tiled=True,
        ).astype(jnp.float32),
    )
    slot_target = my_position[ref_of.reshape(-1)]
    placing = slot_target[None, :] == jnp.arange(n_frag * capacity, dtype=jnp.int32)[:, None]
    source_of = jnp.sum(jnp.where(placing, positions[None, :], 0), axis=1)
    ret_rows = jnp.take(back_rows, source_of, axis=0).reshape(
        n_frag, capacity, rows_dev, basis_width
    )
    ret_fit = jnp.take(back_fit.reshape(refs_col, aux_dev), source_of, axis=0).reshape(
        n_frag, capacity, aux_dev
    )
    home_rows, home_fit = (
        lax.all_to_all(
            ret_rows.astype(jnp.bfloat16), "frag", split_axis=0, concat_axis=0, tiled=True
        ).astype(ret_rows.dtype),
        lax.all_to_all(
            ret_fit.astype(jnp.bfloat16), "frag", split_axis=0, concat_axis=0, tiled=True
        ).astype(ret_fit.dtype),
    )
    weights = (
        flat_local[None, :] == jnp.arange(frag_dev, dtype=jnp.int32)[:, None]
    ) & is_live.reshape(-1)[None, :]
    weights = weights.astype(jnp.float32)
    density_shift = jnp.dot(
        weights,
        home_rows.reshape(n_frag * capacity, rows_dev * basis_width),
        precision=lax.Precision.HIGHEST,
        preferred_element_type=jnp.float32,
    )
    embedding = jnp.dot(
        weights,
        home_fit.reshape(n_frag * capacity, aux_dev),
        precision=lax.Precision.HIGHEST,
        preferred_element_type=jnp.float32,
    )
    return (density_shift.reshape(frag_dev, rows_dev, basis_width), embedding)


def solution(mesh):
    return jax.shard_map(
        shards,
        mesh=mesh,
        in_specs=(
            P("frag", "basis", None),
            P("frag", None, "basis"),
            P(("frag", "basis"), None),
            P(),
            P(("frag", "basis")),
        ),
        out_specs=(P("frag", "basis", None), P("frag", "basis")),
        check_vma=False,
    )
```

profile of v0, /device:TPU:32, one launch (start us, length us, event | category | flops | bytes accessed | tf_op | source)
XLA Modules:
  0.0 558.6 jit_solution(213320778677752210)
XLA Ops:
  0.7 65.1 %all-gather = s32[256,4,2]{1,2,0:T(2,128)S(1)} all-gather(s32[1,4,2]{1,2,0:T(2,128)} %bitcast.170), channel_id=1, replica_groups=mesh['frag'=32,'basis'=8] {'frag','basis'}, dimensions={0}, use_global_device_ids=true | all-gather | bytes 8224 | tf_op jit(solution)/shard_map/all_gather | solution.py:56
  65.9 2.2 select_reduce_fusion
  68.7 0.9 convert_reduce_fusion
  70.1 1.9 gather_fusion.2
  72.0 2.8 broadcast_select_fusion.2
  74.8 6.9 %all-to-all-start = ((bf16[32,3,32,256]{3,2,1,0:T(8,128)(2,1)}), bf16[32,3,32,256]{3,2,1,0:T(8,128)(2,1)}, u32[]{:S(2)}, u32[]{:S(2)}) async-start(bf16[32,3,32,256]{3,2,1,0:T(8,128)(2,1)} %broadcast_select_fusion.2), calls=%async_computation | async-start | bytes 3145728 | tf_op jit(solution)/shard_map/all_to_all | solution.py:94
  81.7 6.0 %gather_fusion.4 = bf16[96,256,128]{2,1,0:T(8,128)(2,1)} fusion(bf16[32,256,128]{2,1,0:T(8,128)(2,1)S(1)} %copy-done, s32[1024]{0:T(1024)S(1)} %pad_clamp_fusion.3), kind=kCustom, calls=%fused_computation.4 | custom fusion | bytes 12583296 | tf_op jit(solution)/shard_map/jit(_take)/gather | solution.py:79
  87.7 6.1 %broadcast_select_fusion = bf16[32,3,256,128]{3,2,1,0:T(8,128)(2,1)} fusion(bf16[32,3,256,128]{3,2,1,0:T(8,128)(2,1)} %bitcast.159, pred[32,3]{1,0:T(8,128)(4,1)S(1)} %copy.70), kind=kLoop, calls=%fused_computation.57 | loop fusion | flops 3145728 | bytes 12583008 | tf_op jit(solution)/shard_map/jit(_take)/select_n | solution.py:79
  93.8 27.1 %all-to-all-done = bf16[32,3,32,256]{3,2,1,0:T(8,128)(2,1)} async-done(((bf16[32,3,32,256]{3,2,1,0:T(8,128)(2,1)}), bf16[32,3,32,256]{3,2,1,0:T(8,128)(2,1)}, u32[]{:S(2)}, u32[]{:S(2)}) %all-to-all-start) | async-done | bytes 1572896 | tf_op jit(solution)/shard_map/all_to_all | solution.py:94
  120.8 6.4 %all-to-all-start.2 = ((bf16[32,3,256,128]{3,2,1,0:T(8,128)(2,1)}), bf16[32,3,256,128]{3,2,1,0:T(8,128)(2,1)}, u32[]{:S(2)}, u32[]{:S(2)}) async-start(bf16[32,3,256,128]{3,2,1,0:T(8,128)(2,1)} %broadcast_select_fusion), calls=%async_computation.2 | async-start | bytes 12582912 | tf_op jit(solution)/shard_map/all_to_all | solution.py:95
  127.6 0.8 gather_fusion.1
  128.9 2.0 gather_fusion.3
  131.4 1.6 copy.72
  132.9 135.0 %all-to-all-done.2 = bf16[32,3,256,128]{3,2,1,0:T(8,128)(2,1)} async-done(((bf16[32,3,256,128]{3,2,1,0:T(8,128)(2,1)}), bf16[32,3,256,128]{3,2,1,0:T(8,128)(2,1)}, u32[]{:S(2)}, u32[]{:S(2)}) %all-to-all-start.2) | async-done | bytes 6291488 | tf_op jit(solution)/shard_map/all_to_all | solution.py:95
  267.9 3.6 all-to-all-start.1
  271.4 5.8 %gather_fusion.5 = bf16[64,256,128]{2,1,0:T(8,128)(2,1)} fusion(bf16[96,256,128]{2,1,0:T(8,128)(2,1)} %bitcast.30, s32[1024]{0:T(1024)S(1)} %pad_clamp_fusion.2), kind=kCustom, calls=%fused_computation.5 | custom fusion | bytes 8388864 | tf_op jit(solution)/shard_map/jit(_take)/gather | solution.py:98
  277.3 2.6 broadcast_select_fusion.1
  279.9 2.5 copy.74
  282.4 4.9 all-to-all-done.1
  287.3 4.5 all-to-all-start.3
  292.5 0.8 gather_fusion
  293.3 114.6 %all-reduce.3 = s32[32,32]{1,0:T(8,128)S(1)} all-reduce(s32[32,32]{1,0:T(8,128)S(1)} %reshape.386), channel_id=1, replica_groups=mesh['frag'=32,'basis'=8] {'frag','basis'}, use_global_device_ids=true, to_apply=%add.2 | all-reduce | flops 1024 | bytes 8192
  408.8 53.5 %while.23 = (s32[]{:T(128)}, bf16[4,2,256,256]{3,2,1,0:T(8,128)(2,1)}, bf16[4,2,8,128]{3,2,1,0:T(8,128)(2,1)S(1)}, bf16[4,2,256,256]{3,2,1,0:T(8,128)(2,1)S(1)},...) while((s32[]{:T(128)}, ...), condition=%wide.region_9.10_spmd, body=%wide.region_5.9_spmd.sunk | while | flops 1354769408 | bytes 19436284 | solution.py:117
  408.8 1.3 constant_dynamic-slice_fusion.6
  411.3 1.3 dynamic-slice_bitcast_fusion.5
  414.0 6.8 %while.24 = (s32[]{:T(128)}, bf16[512,512]{1,0:T(8,128)(2,1)S(1)}, s32[]{:T(128)}, s32[]{:T(128)}) while((s32[]{:T(128)}, bf16[512,512]{1,0:T(8,128)(2,1)S(1)}, s32[]{:T(128)}, s32[]{:T(128)}) %tuple.60), condition=%wide.region_8.8_spmd, body=%wide.region_7.7_spmd.sunk | while | flops 538181632 | bytes 4718645 | solution.py:34
  421.8 1.3 constant_dynamic-slice_fusion.6
  424.3 1.3 dynamic-slice_bitcast_fusion.5
  427.0 8.4 %while.24 = (s32[]{:T(128)}, bf16[512,512]{1,0:T(8,128)(2,1)S(1)}, s32[]{:T(128)}, s32[]{:T(128)}) while((s32[]{:T(128)}, bf16[512,512]{1,0:T(8,128)(2,1)S(1)}, s32[]{:T(128)}, s32[]{:T(128)}) %tuple.60), condition=%wide.region_8.8_spmd, body=%wide.region_7.7_spmd.sunk | while | flops 538181632 | bytes 4718645 | solution.py:34
  436.3 1.3 constant_dynamic-slice_fusion.6
  438.8 1.3 dynamic-slice_bitcast_fusion.5
  441.5 6.8 %while.24 = (s32[]{:T(128)}, bf16[512,512]{1,0:T(8,128)(2,1)S(1)}, s32[]{:T(128)}, s32[]{:T(128)}) while((s32[]{:T(128)}, bf16[512,512]{1,0:T(8,128)(2,1)S(1)}, s32[]{:T(128)}, s32[]{:T(128)}) %tuple.60), condition=%wide.region_8.8_spmd, body=%wide.region_7.7_spmd.sunk | while | flops 538181632 | bytes 4718645 | solution.py:34
  449.3 1.3 constant_dynamic-slice_fusion.6
  451.8 1.3 dynamic-slice_bitcast_fusion.5
  454.5 6.8 %while.24 = (s32[]{:T(128)}, bf16[512,512]{1,0:T(8,128)(2,1)S(1)}, s32[]{:T(128)}, s32[]{:T(128)}) while((s32[]{:T(128)}, bf16[512,512]{1,0:T(8,128)(2,1)S(1)}, s32[]{:T(128)}, s32[]{:T(128)}) %tuple.60), condition=%wide.region_8.8_spmd, body=%wide.region_7.7_spmd.sunk | while | flops 538181632 | bytes 4718645 | solution.py:34
  462.9 5.8 %all-to-all-start.6 = ((bf16[8,8,128]{2,0,1:T(8,128)(2,1)}), bf16[8,8,128]{2,0,1:T(8,128)(2,1)S(1)}, u32[]{:S(2)}, u32[]{:S(2)}) async-start(bf16[8,8,128]{2,0,1:T(8,128)(2,1)} %copy.82), calls=%async_computation.6 | async-start | bytes 32768 | tf_op jit(solution)/shard_map/all_to_all | solution.py:127
  468.9 2.8 copy.86
  471.7 2.3 all-to-all-done.6
  474.0 3.6 all-to-all-start.4
  479.1 14.3 %all-to-all-done.4 = bf16[8,256,256]{2,0,1:T(8,128)(2,1)S(1)} async-done(((bf16[8,256,256]{2,0,1:T(8,128)(2,1)}), bf16[8,256,256]{2,0,1:T(8,128)(2,1)S(1)}, u32[]{:S(2)}, u32[]{:S(2)}) %all-to-all-start.4) | async-done | bytes 1048608 | tf_op jit(solution)/shard_map/all_to_all | solution.py:120
  493.4 7.5 %all-to-all-start.7 = ((bf16[32,3,128]{2,1,0:T(4,128)(2,1)}), bf16[32,3,128]{2,1,0:T(4,128)(2,1)S(1)}, u32[]{:S(2)}, u32[]{:S(2)}) async-start(bf16[32,3,128]{2,1,0:T(4,128)(2,1)} %select_convert_fusion.1), calls=%async_computation.7 | async-start | bytes 65536 | tf_op jit(solution)/shard_map/all_to_all | solution.py:148
  501.2 1.9 gather_fusion.7
  503.2 2.9 select_convert_fusion
  506.1 3.7 all-to-all-done.7
  509.8 6.1 %all-to-all-start.5 = ((bf16[32,3,32,256]{3,2,1,0:T(8,128)(2,1)}), bf16[32,3,32,256]{3,2,1,0:T(8,128)(2,1)}, u32[]{:S(2)}, u32[]{:S(2)}) async-start(bf16[32,3,32,256]{3,2,1,0:T(8,128)(2,1)} %select_convert_fusion), calls=%async_computation.5 | async-start | bytes 3145728 | tf_op jit(solution)/shard_map/all_to_all | solution.py:145
  517.1 37.2 %all-to-all-done.5 = bf16[32,3,32,256]{3,2,1,0:T(8,128)(2,1)} async-done(((bf16[32,3,32,256]{3,2,1,0:T(8,128)(2,1)}), bf16[32,3,32,256]{3,2,1,0:T(8,128)(2,1)}, u32[]{:S(2)}, u32[]{:S(2)}) %all-to-all-start.5) | async-done | bytes 1572896 | tf_op jit(solution)/shard_map/all_to_all | solution.py:145
  554.4 2.6 fusion.24
  557.0 1.6 copy.83
  (173 shorter events, 37.1 us)
Async XLA Ops:
  0.6 81.1 %copy-start = (bf16[32,256,128]{2,1,0:T(8,128)(2,1)S(1)}, bf16[32,256,128]{2,1,0:T(8,128)(2,1)}, u32[]{:S(2)}) copy-start(bf16[32,256,128]{2,1,0:T(8,128)(2,1)} %param.10) | copy-start | bytes 6291460
  0.6 69.5 %copy-start.2 = (bf16[32,32,256]{2,1,0:T(8,128)(2,1)S(1)}, bf16[32,32,256]{2,1,0:T(8,128)(2,1)}, u32[]{:S(2)}) copy-start(bf16[32,32,256]{2,1,0:T(8,128)(2,1)} %param.9) | copy-start | bytes 1572868
  74.8 46.1 %all-to-all-start = ((bf16[32,3,32,256]{3,2,1,0:T(8,128)(2,1)}), bf16[32,3,32,256]{3,2,1,0:T(8,128)(2,1)}, u32[]{:S(2)}, u32[]{:S(2)}) async-start(bf16[32,3,32,256]{3,2,1,0:T(8,128)(2,1)} %broadcast_select_fusion.2), calls=%async_computation | async-start | bytes 3145728 | tf_op jit(solution)/shard_map/all_to_all | solution.py:94
  120.8 147.0 %all-to-all-start.2 = ((bf16[32,3,256,128]{3,2,1,0:T(8,128)(2,1)}), bf16[32,3,256,128]{3,2,1,0:T(8,128)(2,1)}, u32[]{:S(2)}, u32[]{:S(2)}) async-start(bf16[32,3,256,128]{3,2,1,0:T(8,128)(2,1)} %broadcast_select_fusion), calls=%async_computation.2 | async-start | bytes 12582912 | tf_op jit(solution)/shard_map/all_to_all | solution.py:95
  267.9 19.4 %all-to-all-start.1 = ((bf16[8,256,256]{2,0,1:T(8,128)(2,1)}), bf16[8,256,256]{2,0,1:T(8,128)(2,1)S(1)}, u32[]{:S(2)}, u32[]{:S(2)}) async-start(bf16[8,256,256]{2,0,1:T(8,128)(2,1)} %copy.72), calls=%async_computation.1 | async-start | bytes 2097152 | tf_op jit(solution)/shard_map/all_to_all | solution.py:100
  282.4 9.5 %copy-start.3 = (s32[4]{0:T(128)S(1)}, s32[4]{0:T(128)}, u32[]{:S(2)}) copy-start(s32[4]{0:T(128)} %param.13) | copy-start | bytes 52
  287.3 121.5 %all-to-all-start.3 = ((bf16[8,8,256,128]{3,2,0,1:T(8,128)(2,1)}), bf16[8,8,256,128]{3,2,0,1:T(8,128)(2,1)}, u32[]{:S(2)}, u32[]{:S(2)}) async-start(bf16[8,8,256,128]{3,2,0,1:T(8,128)(2,1)} %copy.74), calls=%async_computation.3 | async-start | bytes 8388608 | tf_op jit(solution)/shard_map/all_to_all | solution.py:107
  462.9 11.1 %all-to-all-start.6 = ((bf16[8,8,128]{2,0,1:T(8,128)(2,1)}), bf16[8,8,128]{2,0,1:T(8,128)(2,1)S(1)}, u32[]{:S(2)}, u32[]{:S(2)}) async-start(bf16[8,8,128]{2,0,1:T(8,128)(2,1)} %copy.82), calls=%async_computation.6 | async-start | bytes 32768 | tf_op jit(solution)/shard_map/all_to_all | solution.py:127
  474.0 19.4 %all-to-all-start.4 = ((bf16[8,256,256]{2,0,1:T(8,128)(2,1)}), bf16[8,256,256]{2,0,1:T(8,128)(2,1)S(1)}, u32[]{:S(2)}, u32[]{:S(2)}) async-start(bf16[8,256,256]{2,0,1:T(8,128)(2,1)} %copy.86), calls=%async_computation.4 | async-start | bytes 2097152 | tf_op jit(solution)/shard_map/all_to_all | solution.py:120
  493.4 16.3 %all-to-all-start.7 = ((bf16[32,3,128]{2,1,0:T(4,128)(2,1)}), bf16[32,3,128]{2,1,0:T(4,128)(2,1)S(1)}, u32[]{:S(2)}, u32[]{:S(2)}) async-start(bf16[32,3,128]{2,1,0:T(4,128)(2,1)} %select_convert_fusion.1), calls=%async_computation.7 | async-start | bytes 65536 | tf_op jit(solution)/shard_map/all_to_all | solution.py:148
  509.8 44.6 %all-to-all-start.5 = ((bf16[32,3,32,256]{3,2,1,0:T(8,128)(2,1)}), bf16[32,3,32,256]{3,2,1,0:T(8,128)(2,1)}, u32[]{:S(2)}, u32[]{:S(2)}) async-start(bf16[32,3,32,256]{3,2,1,0:T(8,128)(2,1)} %select_convert_fusion), calls=%async_computation.5 | async-start | bytes 3145728 | tf_op jit(solution)/shard_map/all_to_all | solution.py:145
  554.4 4.2 copy-start.1
where the time goes:
time: 559 us
  waiting for transfers between devices  225 us (40%)
  blocking collectives  180 us (32%)
  local copies, waits for them, and re-layouts  48.5 us (9%)
  starting transfers between devices  44.4 us (8%)
  matrix products  23.6 us (4%)
  other arithmetic  23.2 us (4%)
  loops' own time  13.7 us (2%)
    all_to_all x1, waiting for transfers between devices, shards(): lax.all_to_all(out_aux, 'frag', split_axis=0, concat_axis=0, tiled=True)  135 us
    unnamed x1, blocking collectives  115 us
    all_gather x1, blocking collectives, shards(): lax.all_gather(pairs, ('frag', 'basis'), axis=0, tiled=True)  65.1 us
    all_to_all x1, waiting for transfers between devices, shards(): lax.all_to_all(ret_rows.astype(jnp.bfloat16), 'frag', split_axis=0, conca...  37.2 us
    all_to_all x1, waiting for transfers between devices, shards(): lax.all_to_all(out_rows, 'frag', split_axis=0, concat_axis=0, tiled=True)  27.1 us
    all_to_all x1, waiting for transfers between devices, shards(): lax.all_to_all(changes.reshape(refs_dev, basis_width, basis_width).astype...  14.3 us
    another operation x4, loops' own time, dimer_pass(): final = lax.fori_loop(0, steps, purify_step, start).astype(jnp.float32)  13.5 us
  transfers between devices with their start and end apart: 8, of which 7 were waited for; matrix products, arithmetic and copies ran while one was open for 7% of the time, Pallas kernels for 0%

commit v1 on v0

v1 whole, which is shorter than its diff:
```python
import functools

import jax
import jax.numpy as jnp
from jax import lax
from jax.experimental import pallas as pl
from jax.experimental.pallas import tpu as pltpu
from jax.sharding import PartitionSpec as P

COUPLE = 0.015625
BIG = 1 << 30
BF16 = jnp.bfloat16
F32 = jnp.float32
LOAD2 = 16

VMEM = pl.BlockSpec(memory_space=pltpu.VMEM)
SMEM = pl.BlockSpec(memory_space=pltpu.SMEM)


def copy_home(out_ref, row, aux_ref, den_ref, slot):
    out_ref[row, 0:256, :] = aux_ref[slot]
    block = den_ref[slot]
    out_ref[row, 256:288, :] = block[:, 0:128]
    out_ref[row, 288:320, :] = block[:, 128:256]


def pack_home(aux, den, index, outs):
    rows = index.shape[0] // outs

    def kernel(index_ref, aux_ref, den_ref, *out_refs):
        for n, out_ref in enumerate(out_refs):
            def step(row, unused, n=n, out_ref=out_ref):
                copy_home(out_ref, row, aux_ref, den_ref, index_ref[n * rows + row])
                return unused
            lax.fori_loop(0, rows, step, 0)

    shape = jax.ShapeDtypeStruct((rows, 320, 128), BF16)
    return pl.pallas_call(
        kernel,
        out_shape=[shape] * outs,
        in_specs=[SMEM, VMEM, VMEM],
        out_specs=[VMEM] * outs,
        name="pack_home",
    )(index, aux, den)


def pack_items(items, index, outs):
    rows = index.shape[0] // outs

    def kernel(index_ref, items_ref, *out_refs):
        for n, out_ref in enumerate(out_refs):
            for row in range(rows):
                out_ref[row] = items_ref[index_ref[n * rows + row]]

    shape = jax.ShapeDtypeStruct((rows,) + items.shape[1:], BF16)
    return pl.pallas_call(
        kernel,
        out_shape=[shape] * outs,
        in_specs=[SMEM, VMEM],
        out_specs=[VMEM] * outs,
        name="pack_items",
    )(index, items)


def pack_mixed(aux, den, items, index, outs):
    rows = index.shape[0] // outs

    def kernel(index_ref, aux_ref, den_ref, items_ref, *out_refs):
        for n, out_ref in enumerate(out_refs):
            def step(row, unused, n=n, out_ref=out_ref):
                at = index_ref[n * rows + row]

                @pl.when(at < 32)
                def _():
                    copy_home(out_ref, row, aux_ref, den_ref, at)

                @pl.when(at >= 32)
                def _():
                    out_ref[row] = items_ref[at - 32]

                return unused
            lax.fori_loop(0, rows, step, 0)

    shape = jax.ShapeDtypeStruct((rows, 320, 128), BF16)
    return pl.pallas_call(
        kernel,
        out_shape=[shape] * outs,
        in_specs=[SMEM, VMEM, VMEM, VMEM],
        out_specs=[VMEM] * outs,
        name="pack_mixed",
    )(index, aux, den, items)


def place_items(parts, target, rows):
    def kernel(target_ref, *refs):
        out_ref = refs[-1]
        for n, part_ref in enumerate(refs[:-1]):
            def step(row, unused, n=n, part_ref=part_ref):
                at = target_ref[n * rows + row]

                @pl.when(at >= 0)
                def _():
                    out_ref[at] = part_ref[row]

                return unused
            lax.fori_loop(0, rows, step, 0)

    return pl.pallas_call(
        kernel,
        out_shape=jax.ShapeDtypeStruct((32, 72, 128), BF16),
        in_specs=[SMEM] + [VMEM] * len(parts),
        out_specs=VMEM,
        name="place_items",
    )(target, *parts)


def dimer_kernel(steps_ref, me_ref, *refs):
    first, second, outs = refs[0:8], refs[8:16], refs[16:24]
    stacked, weighted, dens, current, squares = refs[24:]
    steps = steps_ref[pl.program_id(0)]
    me = me_ref[0]

    @pl.when(steps > 0)
    def _():
        for n in range(8):
            lanes = slice(n * 128, n * 128 + 128)
            at = pl.multiple_of(lax.bitwise_xor(me, n) * 32, 32)
            for half, part in ((0, first[n]), (256, second[n])):
                stacked[half : half + 256, lanes] = part[0, 0:256, :]
                dens[pl.ds(half + at, 32), 0:128] = part[0, 256:288, :]
                dens[pl.ds(half + at, 32), 128:256] = part[0, 288:320, :]
        fits = []
        for half in (0, 256):
            block = dens[half : half + 256, :]
            sums = []
            for n in range(4):
                lanes = slice(n * 256, n * 256 + 256)
                factor = stacked[half : half + 256, lanes]
                projected = jnp.dot(block, factor, preferred_element_type=F32)
                sums.append(jnp.sum(factor.astype(F32) * projected, axis=0, keepdims=True))
            fits.append(jnp.concatenate(sums, axis=1).astype(BF16).astype(F32))
        coeff = fits[0] + fits[1]
        for n in range(8):
            rows = slice(n * 64, n * 64 + 64)
            weighted[rows, :] = (stacked[rows, :].astype(F32) * coeff).astype(BF16)
        for n in range(4):
            rows = slice(n * 128, n * 128 + 128)
            coulomb = lax.dot_general(
                weighted[rows, :], stacked[...], (((1,), (1,)), ((), ())), preferred_element_type=F32
            )
            row_at = lax.broadcasted_iota(jnp.int32, (128, 512), 0) + n * 128
            col_at = lax.broadcasted_iota(jnp.int32, (128, 512), 1)
            own = dens[rows, :].astype(F32)
            blank = jnp.zeros((128, 256), F32)
            wide = jnp.concatenate([own, blank] if n < 2 else [blank, own], axis=1)
            eye = jnp.where(row_at == col_at, 0.5, 0.0)
            current[rows, :] = (eye + wide + COUPLE * coulomb).astype(BF16)

        def purify(index, unused):
            for n in range(4):
                rows = slice(n * 128, n * 128 + 128)
                square = jnp.dot(current[rows, :], current[...], preferred_element_type=F32)
                cube = jnp.dot(square.astype(BF16), current[...], preferred_element_type=F32)
                squares[rows, :] = (3.0 * square - 2.0 * cube).astype(BF16)
            current[...] = squares[...]
            return unused

        lax.fori_loop(0, steps, purify, 0)
        row_at = lax.broadcasted_iota(jnp.int32, (256, 256), 0)
        col_at = lax.broadcasted_iota(jnp.int32, (256, 256), 1)
        eye = jnp.where(row_at == col_at, 0.5, 0.0)
        for half in (0, 256):
            own = slice(half, half + 256)
            change = current[own, own].astype(F32) - dens[own, :].astype(F32) - eye
            dens[own, :] = change.astype(BF16)
        for n in range(8):
            at = pl.multiple_of(lax.bitwise_xor(me, n) * 32, 32)
            lanes = slice(n * 128, n * 128 + 128)
            for r in range(2):
                change = dens[pl.ds(r * 256 + at, 32), :]
                outs[n][r, 0:32, :] = change[:, 0:128]
                outs[n][r, 32:64, :] = change[:, 128:256]
                partner = jnp.broadcast_to(fits[1 - r][:, lanes], (8, 128))
                outs[n][r, 64:72, :] = partner.astype(BF16)


def run_dimers(steps, me, first, second, first_map, second_map):
    count = steps.shape[0]
    shape = jax.ShapeDtypeStruct((2 * count, 72, 128), BF16)
    return pl.pallas_call(
        dimer_kernel,
        out_shape=[shape] * 8,
        grid_spec=pltpu.PrefetchScalarGridSpec(
            num_scalar_prefetch=2,
            grid=(count,),
            in_specs=[pl.BlockSpec((1, 320, 128), first_map)] * 8
            + [pl.BlockSpec((1, 320, 128), second_map)] * 8,
            out_specs=[pl.BlockSpec((2, 72, 128), lambda i, *_: (i, 0, 0))] * 8,
            scratch_shapes=[
                pltpu.VMEM((512, 1024), BF16),
                pltpu.VMEM((512, 1024), BF16),
                pltpu.VMEM((512, 256), BF16),
                pltpu.VMEM((512, 512), BF16),
                pltpu.VMEM((512, 512), BF16),
            ],
        ),
        name="dimers",
        cost_estimate=pl.CostEstimate(
            flops=count * 4_000_000_000, bytes_accessed=count * 1_500_000, transcendentals=0
        ),
    )(steps, me, *first, *second)


def plan_kernel(me_ref, a_ref, b_ref, cost_ref, flag_ref, send_ref, pos_ref, steps_ref, left_ref, taken, load):
    me = me_ref[0]

    def clear(n, unused):
        taken[n] = 0
        load[n] = 0
        send_ref[n] = -1
        pos_ref[n] = 0
        return unused

    def clear_steps(n, unused):
        steps_ref[n] = 0
        return unused

    lax.fori_loop(0, 32, clear, 0)
    lax.fori_loop(0, LOAD2, clear_steps, 0)

    def visit(d, unused):
        left_ref[d] = 0

        @pl.when(flag_ref[d] > 0)
        def _():
            a, b = a_ref[d], b_ref[d]
            oa, ob = lax.shift_right_logical(a, 5), lax.shift_right_logical(b, 5)
            la, lb = a & 31, b & 31
            bit_a, bit_b = lax.shift_left(1, oa), lax.shift_left(1, ob)
            both = bit_a | bit_b
            free_a = ((taken[oa] & bit_b) == 0) & (load[oa] < LOAD2)
            free_b = ((taken[ob] & bit_a) == 0) & (load[ob] < LOAD2)
            inside = oa == ob
            use_a = free_a & (jnp.logical_not(free_b) | (load[oa] <= load[ob]))
            direct = jnp.where(use_a, oa, jnp.where(free_b, ob, -1))
            direct = jnp.where(inside, jnp.where(load[oa] < LOAD2, oa, -1), direct)

            def look(carry):
                n, found = carry
                c = (d + n) & 31
                good = ((taken[c] & both) == 0) & (load[c] < LOAD2) & (c != oa) & (c != ob)
                return n + 1, jnp.where(good, c, -1)

            start = jnp.where((direct >= 0) | inside, 32, 0)
            unused_n, c = lax.while_loop(
                lambda carry: (carry[0] < 32) & (carry[1] < 0), look, (start, direct)
            )

            @pl.when(c < 0)
            def _():
                left_ref[d] = 1

            @pl.when(c >= 0)
            def _():
                away = jnp.where(c == oa, 0, bit_a) | jnp.where(c == ob, 0, bit_b)
                taken[c] = taken[c] | away
                at = load[c]
                load[c] = at + 1

                @pl.when(c == me)
                def _():
                    pos_ref[2 * at] = jnp.where(c == oa, la, 32 + oa)
                    pos_ref[2 * at + 1] = jnp.where(c == ob, lb, 32 + ob)
                    steps_ref[at] = cost_ref[d]

                @pl.when((c != me) & (oa == me))
                def _():
                    send_ref[c] = la

                @pl.when((c != me) & (ob == me))
                def _():
                    send_ref[c] = lb

        return unused

    lax.fori_loop(0, a_ref.shape[0], visit, 0)


def plan_rest(me, a, b, cost, flag):
    s32 = jnp.int32
    return pl.pallas_call(
        plan_kernel,
        out_shape=[
            jax.ShapeDtypeStruct((32,), s32),
            jax.ShapeDtypeStruct((2 * LOAD2,), s32),
            jax.ShapeDtypeStruct((LOAD2,), s32),
            jax.ShapeDtypeStruct(a.shape, s32),
        ],
        in_specs=[SMEM] * 5,
        out_specs=[SMEM] * 4,
        scratch_shapes=[pltpu.SMEM((32,), s32), pltpu.SMEM((32,), s32)],
        name="plan",
        cost_estimate=pl.CostEstimate(flops=1000, bytes_accessed=30_000_000, transcendentals=0),
    )(me, a, b, cost, flag)


def add_up(dens, emb, lists, parts):
    counts = [part.shape[0] for part in parts]

    def kernel(*refs):
        n_parts = len(parts)
        slot_refs, part_refs = refs[:n_parts], refs[n_parts : 2 * n_parts]
        dens_in, emb_in, dens_ref, emb_ref = refs[2 * n_parts :]
        dens_ref[...] = dens_in[...]
        emb_ref[...] = emb_in[...]
        for slot_ref, part_ref, count in zip(slot_refs, part_refs, counts, strict=True):
            def step(row, unused, slot_ref=slot_ref, part_ref=part_ref):
                slot = slot_ref[row]

                @pl.when(slot >= 0)
                def _():
                    dens_ref[slot, :, 0:128] += part_ref[row, 0:32, :].astype(F32)
                    dens_ref[slot, :, 128:256] += part_ref[row, 32:64, :].astype(F32)
                    emb_ref[pl.ds(slot, 1), :] += part_ref[row, 64:72, :].astype(F32)[0:1, :]

                return unused
            lax.fori_loop(0, count, step, 0)

    n = len(parts)
    return pl.pallas_call(
        kernel,
        out_shape=[jax.ShapeDtypeStruct(dens.shape, F32), jax.ShapeDtypeStruct(emb.shape, F32)],
        in_specs=[SMEM] * n + [VMEM] * (n + 2),
        out_specs=[VMEM, VMEM],
        input_output_aliases={2 * n: 0, 2 * n + 1: 1},
        name="add_up",
    )(*lists, *parts, dens, emb)


def exchange(parts):
    got = [parts[0]]
    for k in range(1, 8):
        got.append(lax.ppermute(parts[k], "basis", [(i, i ^ k) for i in range(8)]))
    return got


def shards(density, aux_factor, pairs, slot_of, costs):
    n_frag = lax.axis_size("frag")
    n_basis = lax.axis_size("basis")
    me_frag = lax.axis_index("frag").astype(jnp.int32)
    me_basis = lax.axis_index("basis").astype(jnp.int32)
    dimers = pairs.shape[0] * n_frag * n_basis

    lookup = pairs[:, :, None] == jnp.arange(slot_of.shape[0], dtype=jnp.int32)
    slots = jnp.sum(jnp.where(lookup, slot_of, 0), axis=2)
    mine = jnp.concatenate([slots[:, 0], slots[:, 1], costs, jnp.zeros(116, jnp.int32)])
    column = lax.all_to_all(
        jnp.broadcast_to(mine, (n_basis, 1, 128)), "basis", split_axis=0, concat_axis=0, tiled=True
    )
    column = column[:, 0, 0:12].reshape(n_basis, 3, 4).transpose(1, 0, 2).reshape(96)
    column = jnp.concatenate([column, jnp.zeros(32, jnp.int32)])
    every = lax.all_to_all(
        jnp.broadcast_to(column, (n_frag, 1, 128)), "frag", split_axis=0, concat_axis=0, tiled=True
    )
    a = every[:, 0, 0:32].reshape(dimers)
    b = every[:, 0, 32:64].reshape(dimers)
    cost = every[:, 0, 64:96].reshape(dimers)

    order = jnp.arange(dimers, dtype=jnp.int32)
    columns = jnp.arange(n_frag, dtype=jnp.int32)
    own_a, own_b = a // 32, b // 32
    low, high = jnp.minimum(own_a, own_b), jnp.maximum(own_a, own_b)
    pair_id = low * 32 + high
    inside = own_a == own_b
    mine_a = (own_a == me_frag) & jnp.logical_not(inside)
    mine_b = (own_b == me_frag) & jnp.logical_not(inside)
    other = jnp.where(mine_a, own_b, jnp.where(mine_b, own_a, -1))
    local = jnp.where(mine_a, a, b) & 31
    key = order * 256 + local * 8 + cost
    xor_devices = lax.bitwise_xor(me_basis, jnp.arange(8, dtype=jnp.int32))
    served = (jnp.arange(4, dtype=jnp.int32)[None, :] * 8 + xor_devices[:, None]).reshape(32)
    served_hot = served[:, None] == columns[None, :]
    entries = (jnp.arange(2, dtype=jnp.int32)[None, :] * 8 + xor_devices[:, None]).reshape(16)
    entry_hot = entries[:, None] == jnp.arange(LOAD2, dtype=jnp.int32)[None, :]
    me_f, me_b = me_frag.reshape(1), me_basis.reshape(1)
    keep_first = (me_frag < columns) == ((me_frag + columns) % 2 == 0)

    def pick(hot, table):
        return jnp.sum(jnp.where(hot, table[None, :], 0), axis=1)

    def one_round(carry):
        unused_n, rest, dens, emb = carry
        open_dimer = rest > 0
        match = (other[None, :] == columns[:, None]) & open_dimer[None, :]
        keyed = jnp.where(match, key[None, :], BIG)
        key_0 = jnp.min(keyed, axis=1)
        key_1 = jnp.min(jnp.where(keyed > key_0[:, None], keyed, BIG), axis=1)
        here = jnp.where(keep_first, key_0, key_1)
        there = jnp.where(keep_first, key_1, key_0)
        send_1 = jnp.where(there < BIG, (there >> 3) & 31, -1)
        base_1 = jnp.where(here < BIG, (here >> 3) & 31, -1)
        steps_1 = jnp.where(here < BIG, here & 7, 0)

        (out_1,) = pack_home(aux_factor, density, jnp.maximum(send_1, 0), 1)
        in_1 = lax.all_to_all(out_1, "frag", split_axis=0, concat_axis=0, tiled=True)

        earlier = (pair_id[:, None] == pair_id[None, :]) & (order[None, :] < order[:, None])
        earlier = jnp.sum(jnp.where(earlier & open_dimer[None, :], 1, 0), axis=1)
        flag = jnp.where(open_dimer & ((earlier >= 2) | inside), 1, 0)
        send_2, pos_2, cost_2, left = plan_rest(me_f, a, b, cost, flag)

        base_at = pick(served_hot, base_1)
        home_1 = exchange(pack_home(aux_factor, density, jnp.maximum(base_at, 0), 8))

        (out_2,) = pack_home(aux_factor, density, jnp.maximum(send_2, 0), 1)
        out_2, in_1, home_1 = lax.optimization_barrier((out_2, in_1, home_1))
        in_2 = lax.all_to_all(out_2, "frag", split_axis=0, concat_axis=0, tiled=True)

        away_1 = exchange(pack_items(in_1, served, 8))
        my_steps_1 = jnp.sum(
            jnp.where(me_basis == jnp.arange(8, dtype=jnp.int32), steps_1.reshape(4, 8), 0), axis=1
        )
        same = lambda i, *_: (i, 0, 0)
        done_1 = exchange(run_dimers(my_steps_1, me_b, home_1, away_1, same, same))

        pos_at = jnp.stack([pick(entry_hot, pos_2[0::2]), pick(entry_hot, pos_2[1::2])], axis=1).reshape(32)
        both_2 = exchange(pack_mixed(aux_factor, density, in_2, pos_at, 8))
        my_steps_2 = jnp.sum(
            jnp.where(me_basis == jnp.arange(8, dtype=jnp.int32), cost_2.reshape(2, 8), 0), axis=1
        )
        done_2 = exchange(
            run_dimers(
                my_steps_2, me_b, both_2, both_2, lambda i, *_: (2 * i, 0, 0), lambda i, *_: (2 * i + 1, 0, 0)
            )
        )

        spread = jnp.stack([jnp.full(32, -1, jnp.int32), served], axis=1).reshape(64)
        back_1 = lax.all_to_all(place_items(done_1, spread, 8), "frag", split_axis=0, concat_axis=0, tiled=True)
        live_at = pick(entry_hot, cost_2) > 0
        live_at = jnp.stack([live_at, live_at], axis=1).reshape(32)
        target_2 = jnp.where(live_at & (pos_at >= 32), pos_at - 32, -1)
        back_2 = lax.all_to_all(place_items(done_2, target_2, 4), "frag", split_axis=0, concat_axis=0, tiled=True)

        stay_1 = jnp.stack([base_at, jnp.full(32, -1, jnp.int32)], axis=1).reshape(8, 8)
        stay_2 = jnp.where(live_at & (pos_at < 32), pos_at, -1).reshape(8, 4)
        lists = [stay_1[k] for k in range(8)] + [stay_2[k] for k in range(8)] + [send_1, send_2]
        dens, emb = add_up(dens, emb, lists, list(done_1) + list(done_2) + [back_1, back_2])
        return jnp.sum(left), left, dens, emb

    start = (
        jnp.int32(dimers),
        jnp.ones(dimers, jnp.int32),
        jnp.zeros(density.shape, F32),
        jnp.zeros((density.shape[0], aux_factor.shape[2]), F32),
    )
    unused_n, unused_rest, dens, emb = lax.while_loop(lambda carry: carry[0] > 0, one_round, start)
    return dens, emb


def solution(mesh):
    return jax.shard_map(
        shards,
        mesh=mesh,
        in_specs=(
            P("frag", "basis", None),
            P("frag", None, "basis"),
            P(("frag", "basis"), None),
            P(),
            P(("frag", "basis")),
        ),
        out_specs=(P("frag", "basis", None), P("frag", "basis")),
        check_vma=False,
    )
```

time: 559 us -> 308 us (0.55)
  blocking collectives: 180 us -> 0 us
  waiting for transfers between devices: 225 us -> 110 us
  Pallas kernels: 0 us -> 80.2 us
  starting transfers between devices: 44.4 us -> 90.6 us
  local copies, waits for them, and re-layouts: 48.5 us -> 15.5 us
  matrix products: 23.6 us -> 0 us
  other arithmetic: 23.2 us -> 8.79 us
  loops' own time: 13.7 us -> 1.01 us
    all_to_all x8 -> x6, waiting for transfers between devices: 225 us -> 49.5 us  [the longest x1 14.6 us: one_round(): lax.all_to_all(out_1, 'frag', split_axis=0, concat_axis=0, tiled=True)]
    unnamed x1 -> x0, blocking collectives: 115 us -> none
    pallas_call x0 -> x11, Pallas kernels: none -> 80.2 us  [the longest x2 27.5 us: run_dimers(): pl.pallas_call(dimer_kernel, out_shape=[shape] * 8, grid_spec=pltpu.Prefe...]
    all_gather x1 -> x0, blocking collectives: 65.1 us -> none  [shards(): lax.all_gather(pairs, ('frag', 'basis'), axis=0, tiled=True)]
    ppermute x0 -> x35, waiting for transfers between devices: none -> 60.1 us  [exchange(): got.append(lax.ppermute(parts[k], 'basis', [(i, i ^ k) for i in range(8)]))]
    ppermute x0 -> x35, starting transfers between devices: none -> 37.3 us  [exchange(): got.append(lax.ppermute(parts[k], 'basis', [(i, i ^ k) for i in range(8)]))]
    dot_general x44 -> x0, matrix products: 23.6 us -> none  [the longest x17 7.5 us: purify_step(): jnp.dot(square.astype(jnp.bfloat16), current, preferred_element_type=jnp....]
    gather x12 -> x0, local copies, waits for them, and re-layouts: 20.7 us -> none  [the longest x1 5.97 us: shards(): jnp.take(aux_factor, flat_local, axis=0)]
  transfers between devices with their start and end apart: 8 -> 41, of which waited for: 7 -> 22; matrix products, arithmetic and copies ran while one was open for 7% -> 5% of each run, Pallas kernels for 0% -> 24%
where the time goes in v1:
time: 308 us; the launch traced here: 306 us
  waiting for transfers between devices  110 us (36%)
  starting transfers between devices  90.6 us (29%)
  Pallas kernels  80.2 us (26%)
  local copies, waits for them, and re-layouts  15.5 us (5%)
  other arithmetic  8.79 us (3%)
    ppermute x35, waiting for transfers between devices, exchange(): got.append(lax.ppermute(parts[k], 'basis', [(i, i ^ k) for i in range(8)]))  60.1 us
    ppermute x35, starting transfers between devices, exchange(): got.append(lax.ppermute(parts[k], 'basis', [(i, i ^ k) for i in range(8)]))  37.3 us
    pallas_call x2, Pallas kernels, run_dimers(): pl.pallas_call(dimer_kernel, out_shape=[shape] * 8, grid_spec=pltpu.Prefe...  27.5 us
    pallas_call x1, Pallas kernels, plan_rest(): pl.pallas_call(plan_kernel, out_shape=[jax.ShapeDtypeStruct((32,), s32),...  26.5 us
    all_to_all x1, waiting for transfers between devices, one_round(): lax.all_to_all(out_1, 'frag', split_axis=0, concat_axis=0, tiled=True)  14.6 us
    all_to_all x1, starting transfers between devices, one_round(): lax.all_to_all(place_items(done_1, spread, 8), 'frag', split_axis=0, conc...  12.7 us
    all_to_all x1, waiting for transfers between devices, one_round(): lax.all_to_all(place_items(done_2, target_2, 4), 'frag', split_axis=0, co...  12.2 us
    all_to_all x1, starting transfers between devices, one_round(): lax.all_to_all(place_items(done_2, target_2, 4), 'frag', split_axis=0, co...  11.5 us
  transfers between devices with their start and end apart: 41, of which 22 were waited for; matrix products, arithmetic and copies ran while one was open for 5% of the time, Pallas kernels for 24%

profile of v1, /device:TPU:32, one launch (start us, length us, event | category | flops | bytes accessed | tf_op | source)
XLA Modules:
  0.0 306.4 jit_solution(17845791070073215654)
XLA Ops:
  3.0 4.5 %all-to-all-start.4 = ((s32[8,1,128]{2,1,0:T(1,128)}), s32[8,1,128]{2,1,0:T(1,128)S(1)}, u32[]{:S(2)}, u32[]{:S(2)}) async-start(s32[8,1,128]{2,1,0:T(1,128)} %broadcast_in_dim.196), calls=%async_computation.4 | async-start | bytes 8192 | tf_op jit(solution)/shard_map/all_to_all | solution.py:357
  7.5 5.2 %all-to-all-done.4 = s32[8,1,128]{2,1,0:T(1,128)S(1)} async-done(((s32[8,1,128]{2,1,0:T(1,128)}), s32[8,1,128]{2,1,0:T(1,128)S(1)}, u32[]{:S(2)}, u32[]{:S(2)}) %all-to-all-start.4) | async-done | bytes 4128 | tf_op jit(solution)/shard_map/all_to_all | solution.py:357
  13.6 11.2 %all-to-all-start.5 = ((s32[32,1,128]{2,1,0:T(1,128)}), s32[32,1,128]{2,1,0:T(1,128)S(1)}, u32[]{:S(2)}, u32[]{:S(2)}) async-start(s32[32,1,128]{2,1,0:T(1,128)} %broadcast_in_dim.197), calls=%async_computation.5 | async-start | bytes 32768 | tf_op jit(solution)/shard_map/all_to_all | solution.py:362
  25.0 8.3 %all-to-all-done.5 = s32[32,1,128]{2,1,0:T(1,128)S(1)} async-done(((s32[32,1,128]{2,1,0:T(1,128)}), s32[32,1,128]{2,1,0:T(1,128)S(1)}, u32[]{:S(2)}, u32[]{:S(2)}) %all-to-all-start.5) | async-done | bytes 16416 | tf_op jit(solution)/shard_map/all_to_all | solution.py:362
  34.9 270.9 %while.18 = (s32[]{:T(128)}, s32[1024]{0:T(1024)S(1)}, f32[32,32,256]{2,1,0:T(8,128)}, f32[32,128]{1,0:T(8,128)S(1)}, s32[1024]{0:T(1024)S(1)}, /*index=5*/pred[...) while((s32[]{:T(128)}, s32[1024]{0:T(1024)S(1)}, ...), condition=%wide.region_12.13_spmd.clone.clone, body=%wide.region_1.12_spmd.clone.clone.sunk | while | flops 24006631424 | bytes 134089368 | solution.py:456
  35.8 3.5 %pack_home.13 = bf16[32,320,128]{2,1,0:T(8,128)(2,1)} custom-call(s32[32]{0:T(128)} %get-tuple-element.865.index_ref, bf16[32,256,128]{2,1,0:T(8,128)(2,1)} %get-tuple-element.978.aux_ref, bf16[32,32,256]{2,1,0:T(8,128)(2,1)} %get-tuple-element.979.den_ref), custom_call_target="tpu_custom_call" | custom-call | tf_op jit(solution)/shard_map/while/body/pack_home/pallas_call | solution.py:38
  39.3 6.1 %all-to-all-start = ((bf16[32,320,128]{2,1,0:T(8,128)(2,1)}), bf16[32,320,128]{2,1,0:T(8,128)(2,1)}, u32[]{:S(2)}, u32[]{:S(2)}) async-start(bf16[32,320,128]{2,1,0:T(8,128)(2,1)} %pack_home.13), calls=%async_computation | async-start | bytes 5242880 | tf_op jit(solution)/shard_map/while/body/all_to_all | solution.py:405
  46.1 2.5 pack_home.14
  49.2 1.3 collective-permute-start.2
  51.7 2.0 collective-permute-start.4
  55.7 3.8 %collective-permute-done.1.refs_2_ = bf16[4,320,128]{2,1,0:T(8,128)(2,1)S(1)} collective-permute-done((bf16[4,320,128]{2,1,0:T(8,128)(2,1)}, bf16[4,320,128]{2,1,0:T(8,128)(2,1)S(1)}, u32[]{:S(2)}, u32[]{:S(2)}) %collective-permute-start.1) | collective-permute-done | bytes 327712 | tf_op jit(solution)/shard_map/while/body/ppermute | solution.py:343
  60.2 26.5 %plan.4 = (s32[32]{0:T(128)}, s32[32]{0:T(128)}, s32[16]{0:T(128)}, s32[1024]{0:T(1024)S(1)}) custom-call(s32[1]{0:T(128)} %get-tuple-element.971.me_ref, s32[1024]{0:T(1024)S(1)} %get-tuple-element.972.a_ref, s32[1024]{0:T(1024)S(1)} %get-tuple-element.973.b_ref, s32[1024]{0:T(1024)S(1)} %get-tuple-element.974.cost_ref, s32[1024]{0:T(1024)} %and_select_fusion.6.flag_ref), custom_call_target="tpu_custom_call" | custom-call | flops 1000 | bytes 30000000 | tf_op jit(solution)/shard_map/while/body/plan/pallas_call | solution.py:291
  87.9 2.5 pack_home.12
  90.5 14.6 %all-to-all-done.items_ref = bf16[32,320,128]{2,1,0:T(8,128)(2,1)} async-done(((bf16[32,320,128]{2,1,0:T(8,128)(2,1)}), bf16[32,320,128]{2,1,0:T(8,128)(2,1)}, u32[]{:S(2)}, u32[]{:S(2)}) %all-to-all-start) | async-done | bytes 2621472 | tf_op jit(solution)/shard_map/while/body/all_to_all | solution.py:405
  105.1 7.4 %all-to-all-start.1 = ((bf16[32,320,128]{2,1,0:T(8,128)(2,1)}), bf16[32,320,128]{2,1,0:T(8,128)(2,1)}, u32[]{:S(2)}, u32[]{:S(2)}) async-start(bf16[32,320,128]{2,1,0:T(8,128)(2,1)} %pack_home.12), calls=%async_computation.1 | async-start | bytes 5242880 | tf_op jit(solution)/shard_map/while/body/all_to_all | solution.py:417
  113.2 3.6 %pack_items.4 = (bf16[4,320,128]{2,1,0:T(8,128)(2,1)}, bf16[4,320,128]{2,1,0:T(8,128)(2,1)}, bf16[4,320,128]{2,1,0:T(8,128)(2,1)}, bf16[4,320,128]{2,1,0:T(8,128...) custom-call(s32[32]{0:T(128)} %add.289.index_ref, ...), custom_call_target="tpu_custom_call" | custom-call | tf_op jit(solution)/shard_map/while/body/pack_items/pallas_call | solution.py:56
  117.9 2.1 collective-permute-start.12
  120.0 3.0 collective-permute-start.13
  122.9 6.2 %collective-permute-done.10.refs_12_ = bf16[4,320,128]{2,1,0:T(8,128)(2,1)S(1)} collective-permute-done((bf16[4,320,128]{2,1,0:T(8,128)(2,1)}, bf16[4,320,128]{2,1,0:T(8,128)(2,1)S(1)}, u32[]{:S(2)}, u32[]{:S(2)}) %collective-permute-start.10) | collective-permute-done | bytes 327712 | tf_op jit(solution)/shard_map/while/body/ppermute | solution.py:343
  129.6 2.8 collective-permute-done.11.refs_13_
  132.4 4.0 %collective-permute-start.9 = (bf16[4,320,128]{2,1,0:T(8,128)(2,1)}, bf16[4,320,128]{2,1,0:T(8,128)(2,1)}, u32[]{:S(2)}, u32[]{:S(2)}) collective-permute-start(bf16[4,320,128]{2,1,0:T(8,128)(2,1)} %get-tuple-element.886), channel_id=1, source_target_pairs={{0,3},{1,2},{2,1},{3,0},{4,7},{5,6},{6,5},{7,4},{8,11},{9,10},{10,... | collective-permute-start | bytes 983048 | tf_op jit(solution)/shard_map/while/body/ppermute | solution.py:343
  137.4 2.6 collective-permute-done.12.refs_14_
  140.0 7.1 %collective-permute-done.13.refs_15_ = bf16[4,320,128]{2,1,0:T(8,128)(2,1)} collective-permute-done((bf16[4,320,128]{2,1,0:T(8,128)(2,1)}, bf16[4,320,128]{2,1,0:T(8,128)(2,1)}, u32[]{:S(2)}, u32[]{:S(2)}) %collective-permute-start.13) | collective-permute-done | bytes 327712 | tf_op jit(solution)/shard_map/while/body/ppermute | solution.py:343
  147.1 14.6 %dimers.8 = (bf16[8,72,128]{2,1,0:T(8,128)(2,1)}, bf16[8,72,128]{2,1,0:T(8,128)(2,1)}, bf16[8,72,128]{2,1,0:T(8,128)(2,1)}, bf16[8,72,128]{2,1,0:T(8,128)(2,1)},...) custom-call(s32[4]{0:T(128)} %select_reduce_fusion.14.steps_ref, ...), custom_call_target="tpu_custom_call" | custom-call | flops 16000000000 | bytes 6000000 | tf_op jit(solution)/shard_map/while/body/dimers/pallas_call | solution.py:190
  162.8 9.2 %all-to-all-done.1.items_ref = bf16[32,320,128]{2,1,0:T(8,128)(2,1)} async-done(((bf16[32,320,128]{2,1,0:T(8,128)(2,1)}), bf16[32,320,128]{2,1,0:T(8,128)(2,1)}, u32[]{:S(2)}, u32[]{:S(2)}) %all-to-all-start.1) | async-done | bytes 2621472 | tf_op jit(solution)/shard_map/while/body/all_to_all | solution.py:417
  172.0 4.1 %pack_mixed.4 = (bf16[4,320,128]{2,1,0:T(8,128)(2,1)}, bf16[4,320,128]{2,1,0:T(8,128)(2,1)}, bf16[4,320,128]{2,1,0:T(8,128)(2,1)}, bf16[4,320,128]{2,1,0:T(8,128...) custom-call(s32[32]{0:T(128)} %reshape.202.index_ref, ...), custom_call_target="tpu_custom_call" | custom-call | tf_op jit(solution)/shard_map/while/body/pack_mixed/pallas_call | solution.py:85
  176.6 1.5 collective-permute-start.15
  178.2 2.1 collective-permute-start.17
  180.3 9.6 %collective-permute-done.15.refs_2_.refs_20_ = bf16[8,72,128]{2,1,0:T(8,128)(2,1)S(1)} collective-permute-done((bf16[8,72,128]{2,1,0:T(8,128)(2,1)S(1)}, bf16[8,72,128]{2,1,0:T(8,128)(2,1)S(1)}, u32[]{:S(2)}, u32[]{:S(2)}) %collective-permute-start.15) | collective-permute-done | bytes 147488 | tf_op jit(solution)/shard_map/while/body/ppermute | solution.py:343
  190.0 2.2 collective-permute-done.16.refs_3_.refs_21_
  193.4 3.5 %collective-permute-done.17.refs_4_.refs_22_ = bf16[8,72,128]{2,1,0:T(8,128)(2,1)S(1)} collective-permute-done((bf16[8,72,128]{2,1,0:T(8,128)(2,1)S(1)}, bf16[8,72,128]{2,1,0:T(8,128)(2,1)S(1)}, u32[]{:S(2)}, u32[]{:S(2)}) %collective-permute-start.17) | collective-permute-done | bytes 147488 | tf_op jit(solution)/shard_map/while/body/ppermute | solution.py:343
  199.2 3.5 %collective-permute-done.19.refs_6_.refs_24_ = bf16[8,72,128]{2,1,0:T(8,128)(2,1)S(1)} collective-permute-done((bf16[8,72,128]{2,1,0:T(8,128)(2,1)}, bf16[8,72,128]{2,1,0:T(8,128)(2,1)S(1)}, u32[]{:S(2)}, u32[]{:S(2)}) %collective-permute-start.19) | collective-permute-done | bytes 147488 | tf_op jit(solution)/shard_map/while/body/ppermute | solution.py:343
  202.8 1.5 collective-permute-start.24
  204.2 1.7 collective-permute-done.20.refs_7_.refs_25_
  208.3 1.8 collective-permute-start.27
  210.1 3.1 %place_items.8 = bf16[32,72,128]{2,1,0:T(8,128)(2,1)} custom-call(s32[64]{0:T(128)} %reshape.204.target_ref, bf16[8,72,128]{2,1,0:T(8,128)(2,1)} %get-tuple-element.891.refs_0_.refs_18_, bf16[8,72,128]{2,1,0:T(8,128)(2,1)} %copy-done.6, bf16[8,72,128]{2,1,0:T(8,128)(2,1)} %copy-done.7, bf16[8,72,128]{2,1,0:T(8,128)(2,1)} %copy-done.8, ...), custom_call_target="tpu_custom_call" | custom-call | tf_op jit(solution)/shard_map/while/body/place_items/pallas_call | solution.py:108
  213.2 12.7 %all-to-all-start.2 = ((bf16[32,72,128]{2,1,0:T(8,128)(2,1)}), bf16[32,72,128]{2,1,0:T(8,128)(2,1)S(1)}, u32[]{:S(2)}, u32[]{:S(2)}) async-start(bf16[32,72,128]{2,1,0:T(8,128)(2,1)} %place_items.8), calls=%async_computation.2 | async-start | bytes 1179648 | tf_op jit(solution)/shard_map/while/body/all_to_all | solution.py:438
  226.7 5.5 %collective-permute-done.26.refs_6_.refs_14_ = bf16[4,320,128]{2,1,0:T(8,128)(2,1)} collective-permute-done((bf16[4,320,128]{2,1,0:T(8,128)(2,1)}, bf16[4,320,128]{2,1,0:T(8,128)(2,1)}, u32[]{:S(2)}, u32[]{:S(2)}) %collective-permute-start.26) | collective-permute-done | bytes 327712 | tf_op jit(solution)/shard_map/while/body/ppermute | solution.py:343
  232.2 6.9 %collective-permute-done.27.refs_7_.refs_15_ = bf16[4,320,128]{2,1,0:T(8,128)(2,1)} collective-permute-done((bf16[4,320,128]{2,1,0:T(8,128)(2,1)}, bf16[4,320,128]{2,1,0:T(8,128)(2,1)}, u32[]{:S(2)}, u32[]{:S(2)}) %collective-permute-start.27) | collective-permute-done | bytes 327712 | tf_op jit(solution)/shard_map/while/body/ppermute | solution.py:343
  239.1 12.9 %dimers.9 = (bf16[4,72,128]{2,1,0:T(8,128)(2,1)}, bf16[4,72,128]{2,1,0:T(8,128)(2,1)}, bf16[4,72,128]{2,1,0:T(8,128)(2,1)}, bf16[4,72,128]{2,1,0:T(8,128)(2,1)},...) custom-call(s32[2]{0:T(128)} %select_reduce_fusion.15.steps_ref, ...), custom_call_target="tpu_custom_call" | custom-call | flops 8000000000 | bytes 3000000 | tf_op jit(solution)/shard_map/while/body/dimers/pallas_call | solution.py:190
  252.5 1.8 collective-permute-start.30
  254.3 3.2 %collective-permute-start.32 = (bf16[4,72,128]{2,1,0:T(8,128)(2,1)}, bf16[4,72,128]{2,1,0:T(8,128)(2,1)S(1)}, u32[]{:S(2)}, u32[]{:S(2)}) collective-permute-start(bf16[4,72,128]{2,1,0:T(8,128)(2,1)} %get-tuple-element.913), channel_id=1, source_target_pairs={{0,5},{1,4},{2,7},{3,6},{4,1},{5,0},{6,3},{7,2},{8,13},{9,12},{10,... | collective-permute-start | bytes 221192 | tf_op jit(solution)/shard_map/while/body/ppermute | solution.py:343
  257.6 2.9 collective-permute-start.34
  261.6 2.5 collective-permute-done.33.refs_6_.refs_32_
  265.6 2.4 place_items.9
  268.0 11.5 %all-to-all-start.3 = ((bf16[32,72,128]{2,1,0:T(8,128)(2,1)}), bf16[32,72,128]{2,1,0:T(8,128)(2,1)S(1)}, u32[]{:S(2)}, u32[]{:S(2)}) async-start(bf16[32,72,128]{2,1,0:T(8,128)(2,1)} %place_items.9), calls=%async_computation.3 | async-start | bytes 1179648 | tf_op jit(solution)/shard_map/while/body/all_to_all | solution.py:442
  286.8 12.2 %all-to-all-done.3.refs_35_ = bf16[32,72,128]{2,1,0:T(8,128)(2,1)S(1)} async-done(((bf16[32,72,128]{2,1,0:T(8,128)(2,1)}), bf16[32,72,128]{2,1,0:T(8,128)(2,1)S(1)}, u32[]{:S(2)}, u32[]{:S(2)}) %all-to-all-start.3) | async-done | bytes 589856 | tf_op jit(solution)/shard_map/while/body/all_to_all | solution.py:442
  299.7 4.4 %add_up.4 = (f32[32,32,256]{2,1,0:T(8,128)S(1)}, f32[32,128]{1,0:T(8,128)S(1)}) custom-call(s32[8]{0:T(128)} %squeeze.64.refs_0_, s32[8]{0:T(128)} %squeeze.65.refs_1_, s32[8]{0:T(128)} %squeeze.66.refs_2_, s32[8]{0:T(128)} %squeeze.67.refs_3_, s32[8]{0:T(128)} %squeeze.68.refs_4_, ...), custom_call_target="tpu_custom_call", output_to_operand_aliasing={{0}: (36, {}), {1}: (37, {})} | custom-call | tf_op jit(solution)/shard_map/while/body/add_up/pallas_call | solution.py:330
  (192 shorter events, 36.4 us)
Async XLA Ops:
  3.0 9.7 %all-to-all-start.4 = ((s32[8,1,128]{2,1,0:T(1,128)}), s32[8,1,128]{2,1,0:T(1,128)S(1)}, u32[]{:S(2)}, u32[]{:S(2)}) async-start(s32[8,1,128]{2,1,0:T(1,128)} %broadcast_in_dim.196), calls=%async_computation.4 | async-start | bytes 8192 | tf_op jit(solution)/shard_map/all_to_all | solution.py:357
  13.6 19.8 %all-to-all-start.5 = ((s32[32,1,128]{2,1,0:T(1,128)}), s32[32,1,128]{2,1,0:T(1,128)S(1)}, u32[]{:S(2)}, u32[]{:S(2)}) async-start(s32[32,1,128]{2,1,0:T(1,128)} %broadcast_in_dim.197), calls=%async_computation.5 | async-start | bytes 32768 | tf_op jit(solution)/shard_map/all_to_all | solution.py:362
  39.3 65.7 %all-to-all-start = ((bf16[32,320,128]{2,1,0:T(8,128)(2,1)}), bf16[32,320,128]{2,1,0:T(8,128)(2,1)}, u32[]{:S(2)}, u32[]{:S(2)}) async-start(bf16[32,320,128]{2,1,0:T(8,128)(2,1)} %pack_home.13), calls=%async_computation | async-start | bytes 5242880 | tf_op jit(solution)/shard_map/while/body/all_to_all | solution.py:405
  48.7 5.7 %collective-permute-start = (bf16[4,320,128]{2,1,0:T(8,128)(2,1)}, bf16[4,320,128]{2,1,0:T(8,128)(2,1)S(1)}, u32[]{:S(2)}, u32[]{:S(2)}) collective-permute-start(bf16[4,320,128]{2,1,0:T(8,128)(2,1)} %get-tuple-element.867), channel_id=1, source_target_pairs={{0,1},{1,0},{2,3},{3,2},{4,5},{5,4},{6,7},{7,6},{8,9},{9,8},{10,11... | collective-permute-start | bytes 983048 | tf_op jit(solution)/shard_map/while/body/ppermute | solution.py:343
  48.7 10.8 %collective-permute-start.1 = (bf16[4,320,128]{2,1,0:T(8,128)(2,1)}, bf16[4,320,128]{2,1,0:T(8,128)(2,1)S(1)}, u32[]{:S(2)}, u32[]{:S(2)}) collective-permute-start(bf16[4,320,128]{2,1,0:T(8,128)(2,1)} %get-tuple-element.868), channel_id=1, source_target_pairs={{0,2},{1,3},{2,0},{3,1},{4,6},{5,7},{6,4},{7,5},{8,10},{9,11},{10,... | collective-permute-start | bytes 983048 | tf_op jit(solution)/shard_map/while/body/ppermute | solution.py:343
  49.2 41.2 %collective-permute-start.2 = (bf16[4,320,128]{2,1,0:T(8,128)(2,1)}, bf16[4,320,128]{2,1,0:T(8,128)(2,1)}, u32[]{:S(2)}, u32[]{:S(2)}) collective-permute-start(bf16[4,320,128]{2,1,0:T(8,128)(2,1)} %get-tuple-element.869), channel_id=1, source_target_pairs={{0,3},{1,2},{2,1},{3,0},{4,7},{5,6},{6,5},{7,4},{8,11},{9,10},{10,... | collective-permute-start | bytes 983048 | tf_op jit(solution)/shard_map/while/body/ppermute | solution.py:343
  50.5 39.9 %collective-permute-start.3 = (bf16[4,320,128]{2,1,0:T(8,128)(2,1)}, bf16[4,320,128]{2,1,0:T(8,128)(2,1)}, u32[]{:S(2)}, u32[]{:S(2)}) collective-permute-start(bf16[4,320,128]{2,1,0:T(8,128)(2,1)} %get-tuple-element.870), channel_id=1, source_target_pairs={{0,4},{1,5},{2,6},{3,7},{4,0},{5,1},{6,2},{7,3},{8,12},{9,13},{10,... | collective-permute-start | bytes 983048 | tf_op jit(solution)/shard_map/while/body/ppermute | solution.py:343
  51.7 38.8 %collective-permute-start.4 = (bf16[4,320,128]{2,1,0:T(8,128)(2,1)}, bf16[4,320,128]{2,1,0:T(8,128)(2,1)}, u32[]{:S(2)}, u32[]{:S(2)}) collective-permute-start(bf16[4,320,128]{2,1,0:T(8,128)(2,1)} %get-tuple-element.871), channel_id=1, source_target_pairs={{0,5},{1,4},{2,7},{3,6},{4,1},{5,0},{6,3},{7,2},{8,13},{9,12},{10,... | collective-permute-start | bytes 983048 | tf_op jit(solution)/shard_map/while/body/ppermute | solution.py:343
  54.4 36.0 %copy-start.23 = (bf16[4,320,128]{2,1,0:T(8,128)(2,1)}, bf16[4,320,128]{2,1,0:T(8,128)(2,1)S(1)}, u32[]{:S(2)}) copy-start(bf16[4,320,128]{2,1,0:T(8,128)(2,1)S(1)} %collective-permute-done.refs_1_) | copy-start | bytes 983044 | tf_op jit(solution)/shard_map/while
  54.4 36.0 %collective-permute-start.5 = (bf16[4,320,128]{2,1,0:T(8,128)(2,1)}, bf16[4,320,128]{2,1,0:T(8,128)(2,1)}, u32[]{:S(2)}, u32[]{:S(2)}) collective-permute-start(bf16[4,320,128]{2,1,0:T(8,128)(2,1)} %get-tuple-element.872), channel_id=1, source_target_pairs={{0,6},{1,7},{2,4},{3,5},{4,2},{5,3},{6,0},{7,1},{8,14},{9,15},{10,... | collective-permute-start | bytes 983048 | tf_op jit(solution)/shard_map/while/body/ppermute | solution.py:343
  59.5 31.0 %collective-permute-start.6 = (bf16[4,320,128]{2,1,0:T(8,128)(2,1)}, bf16[4,320,128]{2,1,0:T(8,128)(2,1)}, u32[]{:S(2)}, u32[]{:S(2)}) collective-permute-start(bf16[4,320,128]{2,1,0:T(8,128)(2,1)} %get-tuple-element.873), channel_id=1, source_target_pairs={{0,7},{1,6},{2,5},{3,4},{4,3},{5,2},{6,1},{7,0},{8,15},{9,14},{10,... | collective-permute-start | bytes 983048 | tf_op jit(solution)/shard_map/while/body/ppermute | solution.py:343
  105.1 66.9 %all-to-all-start.1 = ((bf16[32,320,128]{2,1,0:T(8,128)(2,1)}), bf16[32,320,128]{2,1,0:T(8,128)(2,1)}, u32[]{:S(2)}, u32[]{:S(2)}) async-start(bf16[32,320,128]{2,1,0:T(8,128)(2,1)} %pack_home.12), calls=%async_computation.1 | async-start | bytes 5242880 | tf_op jit(solution)/shard_map/while/body/all_to_all | solution.py:417
  112.5 24.0 %copy-start.34 = (s32[32]{0:T(128)S(1)}, s32[32]{0:T(128)}, u32[]{:S(2)}) copy-start(s32[32]{0:T(128)} %get-tuple-element.849) | copy-start | bytes 388 | tf_op jit(solution)/shard_map/while
  116.7 12.4 %collective-permute-start.10 = (bf16[4,320,128]{2,1,0:T(8,128)(2,1)}, bf16[4,320,128]{2,1,0:T(8,128)(2,1)S(1)}, u32[]{:S(2)}, u32[]{:S(2)}) collective-permute-start(bf16[4,320,128]{2,1,0:T(8,128)(2,1)} %get-tuple-element.887), channel_id=1, source_target_pairs={{0,4},{1,5},{2,6},{3,7},{4,0},{5,1},{6,2},{7,3},{8,12},{9,13},{10,... | collective-permute-start | bytes 983048 | tf_op jit(solution)/shard_map/while/body/ppermute | solution.py:343
  117.9 14.5 %collective-permute-start.11 = (bf16[4,320,128]{2,1,0:T(8,128)(2,1)}, bf16[4,320,128]{2,1,0:T(8,128)(2,1)S(1)}, u32[]{:S(2)}, u32[]{:S(2)}) collective-permute-start(bf16[4,320,128]{2,1,0:T(8,128)(2,1)} %get-tuple-element.888), channel_id=1, source_target_pairs={{0,5},{1,4},{2,7},{3,6},{4,1},{5,0},{6,3},{7,2},{8,13},{9,12},{10,... | collective-permute-start | bytes 983048 | tf_op jit(solution)/shard_map/while/body/ppermute | solution.py:343
  117.9 22.1 %collective-permute-start.12 = (bf16[4,320,128]{2,1,0:T(8,128)(2,1)}, bf16[4,320,128]{2,1,0:T(8,128)(2,1)}, u32[]{:S(2)}, u32[]{:S(2)}) collective-permute-start(bf16[4,320,128]{2,1,0:T(8,128)(2,1)} %get-tuple-element.889), channel_id=1, source_target_pairs={{0,6},{1,7},{2,4},{3,5},{4,2},{5,3},{6,0},{7,1},{8,14},{9,15},{10,... | collective-permute-start | bytes 983048 | tf_op jit(solution)/shard_map/while/body/ppermute | solution.py:343
  120.0 27.1 %collective-permute-start.13 = (bf16[4,320,128]{2,1,0:T(8,128)(2,1)}, bf16[4,320,128]{2,1,0:T(8,128)(2,1)}, u32[]{:S(2)}, u32[]{:S(2)}) collective-permute-start(bf16[4,320,128]{2,1,0:T(8,128)(2,1)} %get-tuple-element.890), channel_id=1, source_target_pairs={{0,7},{1,6},{2,5},{3,4},{4,3},{5,2},{6,1},{7,0},{8,15},{9,14},{10,... | collective-permute-start | bytes 983048 | tf_op jit(solution)/shard_map/while/body/ppermute | solution.py:343
  122.9 24.2 %collective-permute-start.7 = (bf16[4,320,128]{2,1,0:T(8,128)(2,1)}, bf16[4,320,128]{2,1,0:T(8,128)(2,1)}, u32[]{:S(2)}, u32[]{:S(2)}) collective-permute-start(bf16[4,320,128]{2,1,0:T(8,128)(2,1)} %get-tuple-element.884), channel_id=1, source_target_pairs={{0,1},{1,0},{2,3},{3,2},{4,5},{5,4},{6,7},{7,6},{8,9},{9,8},{10,11... | collective-permute-start | bytes 983048 | tf_op jit(solution)/shard_map/while/body/ppermute | solution.py:343
  129.1 18.0 %collective-permute-start.8 = (bf16[4,320,128]{2,1,0:T(8,128)(2,1)}, bf16[4,320,128]{2,1,0:T(8,128)(2,1)}, u32[]{:S(2)}, u32[]{:S(2)}) collective-permute-start(bf16[4,320,128]{2,1,0:T(8,128)(2,1)} %get-tuple-element.885), channel_id=1, source_target_pairs={{0,2},{1,3},{2,0},{3,1},{4,6},{5,7},{6,4},{7,5},{8,10},{9,11},{10,... | collective-permute-start | bytes 983048 | tf_op jit(solution)/shard_map/while/body/ppermute | solution.py:343
  132.4 14.7 %collective-permute-start.9 = (bf16[4,320,128]{2,1,0:T(8,128)(2,1)}, bf16[4,320,128]{2,1,0:T(8,128)(2,1)}, u32[]{:S(2)}, u32[]{:S(2)}) collective-permute-start(bf16[4,320,128]{2,1,0:T(8,128)(2,1)} %get-tuple-element.886), channel_id=1, source_target_pairs={{0,3},{1,2},{2,1},{3,0},{4,7},{5,6},{6,5},{7,4},{8,11},{9,10},{10,... | collective-permute-start | bytes 983048 | tf_op jit(solution)/shard_map/while/body/ppermute | solution.py:343
  161.7 16.4 %collective-permute-start.14 = (bf16[8,72,128]{2,1,0:T(8,128)(2,1)}, bf16[8,72,128]{2,1,0:T(8,128)(2,1)S(1)}, u32[]{:S(2)}, u32[]{:S(2)}) collective-permute-start(bf16[8,72,128]{2,1,0:T(8,128)(2,1)} %get-tuple-element.892), channel_id=1, source_target_pairs={{0,1},{1,0},{2,3},{3,2},{4,5},{5,4},{6,7},{7,6},{8,9},{9,8},{10,11... | collective-permute-start | bytes 442376 | tf_op jit(solution)/shard_map/while/body/ppermute | solution.py:343
  176.0 31.1 %collective-permute-start.21 = (bf16[4,320,128]{2,1,0:T(8,128)(2,1)}, bf16[4,320,128]{2,1,0:T(8,128)(2,1)S(1)}, u32[]{:S(2)}, u32[]{:S(2)}) collective-permute-start(bf16[4,320,128]{2,1,0:T(8,128)(2,1)} %get-tuple-element.901), channel_id=1, source_target_pairs={{0,1},{1,0},{2,3},{3,2},{4,5},{5,4},{6,7},{7,6},{8,9},{9,8},{10,11... | collective-permute-start | bytes 983048 | tf_op jit(solution)/shard_map/while/body/ppermute | solution.py:343
  176.0 32.2 %collective-permute-start.22 = (bf16[4,320,128]{2,1,0:T(8,128)(2,1)}, bf16[4,320,128]{2,1,0:T(8,128)(2,1)S(1)}, u32[]{:S(2)}, u32[]{:S(2)}) collective-permute-start(bf16[4,320,128]{2,1,0:T(8,128)(2,1)} %get-tuple-element.902), channel_id=1, source_target_pairs={{0,2},{1,3},{2,0},{3,1},{4,6},{5,7},{6,4},{7,5},{8,10},{9,11},{10,... | collective-permute-start | bytes 983048 | tf_op jit(solution)/shard_map/while/body/ppermute | solution.py:343
  176.6 13.4 %collective-permute-start.15 = (bf16[8,72,128]{2,1,0:T(8,128)(2,1)S(1)}, bf16[8,72,128]{2,1,0:T(8,128)(2,1)S(1)}, u32[]{:S(2)}, u32[]{:S(2)}) collective-permute-start(bf16[8,72,128]{2,1,0:T(8,128)(2,1)S(1)} %copy-done.33), channel_id=1, source_target_pairs={{0,2},{1,3},{2,0},{3,1},{4,6},{5,7},{6,4},{7,5},{8,10},{9,11},{10,... | collective-permute-start | bytes 442376 | tf_op jit(solution)/shard_map/while/body/ppermute | solution.py:343
  178.1 14.2 %collective-permute-start.16 = (bf16[8,72,128]{2,1,0:T(8,128)(2,1)S(1)}, bf16[8,72,128]{2,1,0:T(8,128)(2,1)S(1)}, u32[]{:S(2)}, u32[]{:S(2)}) collective-permute-start(bf16[8,72,128]{2,1,0:T(8,128)(2,1)S(1)} %copy-done.32), channel_id=1, source_target_pairs={{0,3},{1,2},{2,1},{3,0},{4,7},{5,6},{6,5},{7,4},{8,11},{9,10},{10,... | collective-permute-start | bytes 442376 | tf_op jit(solution)/shard_map/while/body/ppermute | solution.py:343
  178.2 31.9 %copy-start.6 = (bf16[8,72,128]{2,1,0:T(8,128)(2,1)}, bf16[8,72,128]{2,1,0:T(8,128)(2,1)S(1)}, u32[]{:S(2)}) copy-start(bf16[8,72,128]{2,1,0:T(8,128)(2,1)S(1)} %collective-permute-done.14.refs_1_.refs_19_) | copy-start | bytes 442372 | tf_op jit(solution)/shard_map/while
  178.2 18.7 %collective-permute-start.17 = (bf16[8,72,128]{2,1,0:T(8,128)(2,1)S(1)}, bf16[8,72,128]{2,1,0:T(8,128)(2,1)S(1)}, u32[]{:S(2)}, u32[]{:S(2)}) collective-permute-start(bf16[8,72,128]{2,1,0:T(8,128)(2,1)S(1)} %copy-done.31), channel_id=1, source_target_pairs={{0,4},{1,5},{2,6},{3,7},{4,0},{5,1},{6,2},{7,3},{8,12},{9,13},{10,... | collective-permute-start | bytes 442376 | tf_op jit(solution)/shard_map/while/body/ppermute | solution.py:343
  190.0 9.3 %collective-permute-start.18 = (bf16[8,72,128]{2,1,0:T(8,128)(2,1)}, bf16[8,72,128]{2,1,0:T(8,128)(2,1)S(1)}, u32[]{:S(2)}, u32[]{:S(2)}) collective-permute-start(bf16[8,72,128]{2,1,0:T(8,128)(2,1)} %get-tuple-element.896), channel_id=1, source_target_pairs={{0,5},{1,4},{2,7},{3,6},{4,1},{5,0},{6,3},{7,2},{8,13},{9,12},{10,... | collective-permute-start | bytes 442376 | tf_op jit(solution)/shard_map/while/body/ppermute | solution.py:343
  192.2 10.6 %collective-permute-start.19 = (bf16[8,72,128]{2,1,0:T(8,128)(2,1)}, bf16[8,72,128]{2,1,0:T(8,128)(2,1)S(1)}, u32[]{:S(2)}, u32[]{:S(2)}) collective-permute-start(bf16[8,72,128]{2,1,0:T(8,128)(2,1)} %get-tuple-element.897), channel_id=1, source_target_pairs={{0,6},{1,7},{2,4},{3,5},{4,2},{5,3},{6,0},{7,1},{8,14},{9,15},{10,... | collective-permute-start | bytes 442376 | tf_op jit(solution)/shard_map/while/body/ppermute | solution.py:343
  196.9 9.0 %collective-permute-start.20 = (bf16[8,72,128]{2,1,0:T(8,128)(2,1)}, bf16[8,72,128]{2,1,0:T(8,128)(2,1)S(1)}, u32[]{:S(2)}, u32[]{:S(2)}) collective-permute-start(bf16[8,72,128]{2,1,0:T(8,128)(2,1)} %get-tuple-element.898), channel_id=1, source_target_pairs={{0,7},{1,6},{2,5},{3,4},{4,3},{5,2},{6,1},{7,0},{8,15},{9,14},{10,... | collective-permute-start | bytes 442376 | tf_op jit(solution)/shard_map/while/body/ppermute | solution.py:343
  199.2 27.4 %collective-permute-start.23 = (bf16[4,320,128]{2,1,0:T(8,128)(2,1)}, bf16[4,320,128]{2,1,0:T(8,128)(2,1)S(1)}, u32[]{:S(2)}, u32[]{:S(2)}) collective-permute-start(bf16[4,320,128]{2,1,0:T(8,128)(2,1)} %get-tuple-element.903), channel_id=1, source_target_pairs={{0,3},{1,2},{2,1},{3,0},{4,7},{5,6},{6,5},{7,4},{8,11},{9,10},{10,... | collective-permute-start | bytes 983048 | tf_op jit(solution)/shard_map/while/body/ppermute | solution.py:343
  202.8 23.9 %collective-permute-start.24 = (bf16[4,320,128]{2,1,0:T(8,128)(2,1)}, bf16[4,320,128]{2,1,0:T(8,128)(2,1)S(1)}, u32[]{:S(2)}, u32[]{:S(2)}) collective-permute-start(bf16[4,320,128]{2,1,0:T(8,128)(2,1)} %get-tuple-element.904), channel_id=1, source_target_pairs={{0,4},{1,5},{2,6},{3,7},{4,0},{5,1},{6,2},{7,3},{8,12},{9,13},{10,... | collective-permute-start | bytes 983048 | tf_op jit(solution)/shard_map/while/body/ppermute | solution.py:343
  205.9 20.7 %collective-permute-start.25 = (bf16[4,320,128]{2,1,0:T(8,128)(2,1)}, bf16[4,320,128]{2,1,0:T(8,128)(2,1)}, u32[]{:S(2)}, u32[]{:S(2)}) collective-permute-start(bf16[4,320,128]{2,1,0:T(8,128)(2,1)} %get-tuple-element.905), channel_id=1, source_target_pairs={{0,5},{1,4},{2,7},{3,6},{4,1},{5,0},{6,3},{7,2},{8,13},{9,12},{10,... | collective-permute-start | bytes 983048 | tf_op jit(solution)/shard_map/while/body/ppermute | solution.py:343
  207.1 32.0 %copy-start.25 = (bf16[4,320,128]{2,1,0:T(8,128)(2,1)}, bf16[4,320,128]{2,1,0:T(8,128)(2,1)S(1)}, u32[]{:S(2)}) copy-start(bf16[4,320,128]{2,1,0:T(8,128)(2,1)S(1)} %collective-permute-done.21.refs_1_.refs_9_) | copy-start | bytes 983044 | tf_op jit(solution)/shard_map/while
  207.1 25.1 %collective-permute-start.26 = (bf16[4,320,128]{2,1,0:T(8,128)(2,1)}, bf16[4,320,128]{2,1,0:T(8,128)(2,1)}, u32[]{:S(2)}, u32[]{:S(2)}) collective-permute-start(bf16[4,320,128]{2,1,0:T(8,128)(2,1)} %get-tuple-element.906), channel_id=1, source_target_pairs={{0,6},{1,7},{2,4},{3,5},{4,2},{5,3},{6,0},{7,1},{8,14},{9,15},{10,... | collective-permute-start | bytes 983048 | tf_op jit(solution)/shard_map/while/body/ppermute | solution.py:343
  208.3 30.8 %copy-start.26 = (bf16[4,320,128]{2,1,0:T(8,128)(2,1)}, bf16[4,320,128]{2,1,0:T(8,128)(2,1)S(1)}, u32[]{:S(2)}) copy-start(bf16[4,320,128]{2,1,0:T(8,128)(2,1)S(1)} %collective-permute-done.22.refs_2_.refs_10_) | copy-start | bytes 983044 | tf_op jit(solution)/shard_map/while
  208.3 30.8 %collective-permute-start.27 = (bf16[4,320,128]{2,1,0:T(8,128)(2,1)}, bf16[4,320,128]{2,1,0:T(8,128)(2,1)}, u32[]{:S(2)}, u32[]{:S(2)}) collective-permute-start(bf16[4,320,128]{2,1,0:T(8,128)(2,1)} %get-tuple-element.907), channel_id=1, source_target_pairs={{0,7},{1,6},{2,5},{3,4},{4,3},{5,2},{6,1},{7,0},{8,15},{9,14},{10,... | collective-permute-start | bytes 983048 | tf_op jit(solution)/shard_map/while/body/ppermute | solution.py:343
  213.2 54.8 %all-to-all-start.2 = ((bf16[32,72,128]{2,1,0:T(8,128)(2,1)}), bf16[32,72,128]{2,1,0:T(8,128)(2,1)S(1)}, u32[]{:S(2)}, u32[]{:S(2)}) async-start(bf16[32,72,128]{2,1,0:T(8,128)(2,1)} %place_items.8), calls=%async_computation.2 | async-start | bytes 1179648 | tf_op jit(solution)/shard_map/while/body/all_to_all | solution.py:438
  252.1 47.7 %copy-start.4 = (f32[32,32,256]{2,1,0:T(8,128)S(1)}, f32[32,32,256]{2,1,0:T(8,128)}, u32[]{:S(2)}) copy-start(f32[32,32,256]{2,1,0:T(8,128)} %get-tuple-element.944.refs_36_) | copy-start | bytes 3145732 | tf_op jit(solution)/shard_map/while
  252.1 5.5 %collective-permute-start.28 = (bf16[4,72,128]{2,1,0:T(8,128)(2,1)}, bf16[4,72,128]{2,1,0:T(8,128)(2,1)S(1)}, u32[]{:S(2)}, u32[]{:S(2)}) collective-permute-start(bf16[4,72,128]{2,1,0:T(8,128)(2,1)} %get-tuple-element.909), channel_id=1, source_target_pairs={{0,1},{1,0},{2,3},{3,2},{4,5},{5,4},{6,7},{7,6},{8,9},{9,8},{10,11... | collective-permute-start | bytes 221192 | tf_op jit(solution)/shard_map/while/body/ppermute | solution.py:343
  252.2 5.4 %collective-permute-start.29 = (bf16[4,72,128]{2,1,0:T(8,128)(2,1)}, bf16[4,72,128]{2,1,0:T(8,128)(2,1)S(1)}, u32[]{:S(2)}, u32[]{:S(2)}) collective-permute-start(bf16[4,72,128]{2,1,0:T(8,128)(2,1)} %get-tuple-element.910), channel_id=1, source_target_pairs={{0,2},{1,3},{2,0},{3,1},{4,6},{5,7},{6,4},{7,5},{8,10},{9,11},{10,... | collective-permute-start | bytes 221192 | tf_op jit(solution)/shard_map/while/body/ppermute | solution.py:343
  252.5 8.6 %collective-permute-start.30 = (bf16[4,72,128]{2,1,0:T(8,128)(2,1)}, bf16[4,72,128]{2,1,0:T(8,128)(2,1)S(1)}, u32[]{:S(2)}, u32[]{:S(2)}) collective-permute-start(bf16[4,72,128]{2,1,0:T(8,128)(2,1)} %get-tuple-element.911), channel_id=1, source_target_pairs={{0,3},{1,2},{2,1},{3,0},{4,7},{5,6},{6,5},{7,4},{8,11},{9,10},{10,... | collective-permute-start | bytes 221192 | tf_op jit(solution)/shard_map/while/body/ppermute | solution.py:343
  254.3 6.9 %collective-permute-start.31 = (bf16[4,72,128]{2,1,0:T(8,128)(2,1)}, bf16[4,72,128]{2,1,0:T(8,128)(2,1)S(1)}, u32[]{:S(2)}, u32[]{:S(2)}) collective-permute-start(bf16[4,72,128]{2,1,0:T(8,128)(2,1)} %get-tuple-element.912), channel_id=1, source_target_pairs={{0,4},{1,5},{2,6},{3,7},{4,0},{5,1},{6,2},{7,3},{8,12},{9,13},{10,... | collective-permute-start | bytes 221192 | tf_op jit(solution)/shard_map/while/body/ppermute | solution.py:343
  254.3 7.3 %collective-permute-start.32 = (bf16[4,72,128]{2,1,0:T(8,128)(2,1)}, bf16[4,72,128]{2,1,0:T(8,128)(2,1)S(1)}, u32[]{:S(2)}, u32[]{:S(2)}) collective-permute-start(bf16[4,72,128]{2,1,0:T(8,128)(2,1)} %get-tuple-element.913), channel_id=1, source_target_pairs={{0,5},{1,4},{2,7},{3,6},{4,1},{5,0},{6,3},{7,2},{8,13},{9,12},{10,... | collective-permute-start | bytes 221192 | tf_op jit(solution)/shard_map/while/body/ppermute | solution.py:343
  257.6 6.6 %collective-permute-start.33 = (bf16[4,72,128]{2,1,0:T(8,128)(2,1)}, bf16[4,72,128]{2,1,0:T(8,128)(2,1)S(1)}, u32[]{:S(2)}, u32[]{:S(2)}) collective-permute-start(bf16[4,72,128]{2,1,0:T(8,128)(2,1)} %get-tuple-element.914), channel_id=1, source_target_pairs={{0,6},{1,7},{2,4},{3,5},{4,2},{5,3},{6,0},{7,1},{8,14},{9,15},{10,... | collective-permute-start | bytes 221192 | tf_op jit(solution)/shard_map/while/body/ppermute | solution.py:343
  257.6 7.3 %collective-permute-start.34 = (bf16[4,72,128]{2,1,0:T(8,128)(2,1)}, bf16[4,72,128]{2,1,0:T(8,128)(2,1)S(1)}, u32[]{:S(2)}, u32[]{:S(2)}) collective-permute-start(bf16[4,72,128]{2,1,0:T(8,128)(2,1)} %get-tuple-element.915), channel_id=1, source_target_pairs={{0,7},{1,6},{2,5},{3,4},{4,3},{5,2},{6,1},{7,0},{8,15},{9,14},{10,... | collective-permute-start | bytes 221192 | tf_op jit(solution)/shard_map/while/body/ppermute | solution.py:343
  268.0 30.9 %copy-start.2 = (bf16[32,72,128]{2,1,0:T(8,128)(2,1)}, bf16[32,72,128]{2,1,0:T(8,128)(2,1)S(1)}, u32[]{:S(2)}) copy-start(bf16[32,72,128]{2,1,0:T(8,128)(2,1)S(1)} %all-to-all-done.2.refs_34_) | copy-start | bytes 1769476 | tf_op jit(solution)/shard_map/while
  268.0 30.9 %all-to-all-start.3 = ((bf16[32,72,128]{2,1,0:T(8,128)(2,1)}), bf16[32,72,128]{2,1,0:T(8,128)(2,1)S(1)}, u32[]{:S(2)}, u32[]{:S(2)}) async-start(bf16[32,72,128]{2,1,0:T(8,128)(2,1)} %place_items.9), calls=%async_computation.3 | async-start | bytes 1179648 | tf_op jit(solution)/shard_map/while/body/all_to_all | solution.py:442
  (28 other events, 245.2 us)

commit v2 on v1

--- a/solution.py
+++ b/solution.py
@@ -423,6 +423,7 @@
         same = lambda i, *_: (i, 0, 0)
         done_1 = exchange(run_dimers(my_steps_1, me_b, home_1, away_1, same, same))
 
+        in_2, done_1 = lax.optimization_barrier((in_2, done_1))
         pos_at = jnp.stack([pick(entry_hot, pos_2[0::2]), pick(entry_hot, pos_2[1::2])], axis=1).reshape(32)
         both_2 = exchange(pack_mixed(aux_factor, density, in_2, pos_at, 8))
         my_steps_2 = jnp.sum(

time: 308 us -> 307 us (level)
  starting transfers between devices: 90.6 us -> 114 us
  waiting for transfers between devices: 110 us -> 89.4 us
  Pallas kernels: 80.2 us -> 70.4 us
  local copies, waits for them, and re-layouts: 15.5 us -> 19 us
    ppermute x35, starting transfers between devices: 37.3 us -> 51.9 us  [exchange(): got.append(lax.ppermute(parts[k], 'basis', [(i, i ^ k) for i in range(8)]))]
    pallas_call x2, Pallas kernels: 27.5 us -> 17.4 us  [run_dimers(): pl.pallas_call(dimer_kernel, out_shape=[shape] * 8, grid_spec=pltpu.Prefe...]
    ppermute x35, waiting for transfers between devices: 60.1 us -> 50 us  [exchange(): got.append(lax.ppermute(parts[k], 'basis', [(i, i ^ k) for i in range(8)]))]
    all_to_all x1, waiting for transfers between devices: 9.19 us -> 0.01 us  [one_round(): lax.all_to_all(out_2, 'frag', split_axis=0, concat_axis=0, tiled=True)]
    all_to_all x1, starting transfers between devices: 11.5 us -> 18.5 us  [one_round(): lax.all_to_all(place_items(done_2, target_2, 4), 'frag', split_axis=0, co...]
  transfers between devices with their start and end apart: 41 -> 41, of which waited for: 22 -> 19; matrix products, arithmetic and copies ran while one was open for 5% -> 7% of each run, Pallas kernels for 24% -> 19%
where the time goes in v2:
time: 307 us; the launch traced here: 306 us
  starting transfers between devices  114 us (37%)
  waiting for transfers between devices  89.4 us (29%)
  Pallas kernels  70.4 us (23%)
  local copies, waits for them, and re-layouts  19 us (6%)
  other arithmetic  11.1 us (4%)
    ppermute x35, starting transfers between devices, exchange(): got.append(lax.ppermute(parts[k], 'basis', [(i, i ^ k) for i in range(8)]))  51.9 us
    ppermute x35, waiting for transfers between devices, exchange(): got.append(lax.ppermute(parts[k], 'basis', [(i, i ^ k) for i in range(8)]))  50 us
    pallas_call x1, Pallas kernels, plan_rest(): pl.pallas_call(plan_kernel, out_shape=[jax.ShapeDtypeStruct((32,), s32),...  27 us
    all_to_all x1, starting transfers between devices, one_round(): lax.all_to_all(place_items(done_2, target_2, 4), 'frag', split_axis=0, co...  18.5 us
    pallas_call x2, Pallas kernels, run_dimers(): pl.pallas_call(dimer_kernel, out_shape=[shape] * 8, grid_spec=pltpu.Prefe...  17.4 us
    all_to_all x1, starting transfers between devices, one_round(): lax.all_to_all(place_items(done_1, spread, 8), 'frag', split_axis=0, conc...  14.4 us
    all_to_all x1, waiting for transfers between devices, one_round(): lax.all_to_all(out_1, 'frag', split_axis=0, concat_axis=0, tiled=True)  14.1 us
    all_to_all x1, waiting for transfers between devices, one_round(): lax.all_to_all(place_items(done_2, target_2, 4), 'frag', split_axis=0, co...  12.3 us
  transfers between devices with their start and end apart: 41, of which 19 were waited for; matrix products, arithmetic and copies ran while one was open for 7% of the time, Pallas kernels for 19%

profile of v2, /device:TPU:32, one launch (start us, length us, event | category | flops | bytes accessed | tf_op | source)
XLA Modules:
  0.0 305.8 jit_solution(2886275137577283603)
XLA Ops:
  3.0 4.5 %all-to-all-start.4 = ((s32[8,1,128]{2,1,0:T(1,128)}), s32[8,1,128]{2,1,0:T(1,128)S(1)}, u32[]{:S(2)}, u32[]{:S(2)}) async-start(s32[8,1,128]{2,1,0:T(1,128)} %broadcast_in_dim.189), calls=%async_computation.4 | async-start | bytes 8192 | tf_op jit(solution)/shard_map/all_to_all | solution.py:357
  7.5 5.2 %all-to-all-done.4 = s32[8,1,128]{2,1,0:T(1,128)S(1)} async-done(((s32[8,1,128]{2,1,0:T(1,128)}), s32[8,1,128]{2,1,0:T(1,128)S(1)}, u32[]{:S(2)}, u32[]{:S(2)}) %all-to-all-start.4) | async-done | bytes 4128 | tf_op jit(solution)/shard_map/all_to_all | solution.py:357
  13.6 11.2 %all-to-all-start.5 = ((s32[32,1,128]{2,1,0:T(1,128)}), s32[32,1,128]{2,1,0:T(1,128)S(1)}, u32[]{:S(2)}, u32[]{:S(2)}) async-start(s32[32,1,128]{2,1,0:T(1,128)} %broadcast_in_dim.190), calls=%async_computation.5 | async-start | bytes 32768 | tf_op jit(solution)/shard_map/all_to_all | solution.py:362
  25.5 7.8 %all-to-all-done.5 = s32[32,1,128]{2,1,0:T(1,128)S(1)} async-done(((s32[32,1,128]{2,1,0:T(1,128)}), s32[32,1,128]{2,1,0:T(1,128)S(1)}, u32[]{:S(2)}, u32[]{:S(2)}) %all-to-all-start.5) | async-done | bytes 16416 | tf_op jit(solution)/shard_map/all_to_all | solution.py:362
  34.9 270.2 %while.18 = (s32[]{:T(128)}, s32[1024]{0:T(1024)S(1)}, f32[32,32,256]{2,1,0:T(8,128)}, f32[32,128]{1,0:T(8,128)S(1)}, s32[1024]{0:T(1024)S(1)}, /*index=5*/pred[...) while((s32[]{:T(128)}, s32[1024]{0:T(1024)S(1)}, ...), condition=%wide.region_12.13_spmd.clone.clone, body=%wide.region_1.12_spmd.clone.clone.sunk | while | flops 24006631424 | bytes 135738640 | solution.py:457
  35.9 3.5 %pack_home.13 = bf16[32,320,128]{2,1,0:T(8,128)(2,1)} custom-call(s32[32]{0:T(128)} %get-tuple-element.900.index_ref, bf16[32,256,128]{2,1,0:T(8,128)(2,1)} %get-tuple-element.1022.aux_ref, bf16[32,32,256]{2,1,0:T(8,128)(2,1)} %get-tuple-element.1023.den_ref), custom_call_target="tpu_custom_call" | custom-call | tf_op jit(solution)/shard_map/while/body/pack_home/pallas_call | solution.py:38
  39.4 6.1 %all-to-all-start = ((bf16[32,320,128]{2,1,0:T(8,128)(2,1)}), bf16[32,320,128]{2,1,0:T(8,128)(2,1)}, u32[]{:S(2)}, u32[]{:S(2)}) async-start(bf16[32,320,128]{2,1,0:T(8,128)(2,1)} %pack_home.13), calls=%async_computation | async-start | bytes 5242880 | tf_op jit(solution)/shard_map/while/body/all_to_all | solution.py:405
  46.2 2.5 pack_home.14
  51.8 2.0 collective-permute-start.4
  55.8 3.8 %collective-permute-done.1.refs_2_ = bf16[4,320,128]{2,1,0:T(8,128)(2,1)S(1)} collective-permute-done((bf16[4,320,128]{2,1,0:T(8,128)(2,1)}, bf16[4,320,128]{2,1,0:T(8,128)(2,1)S(1)}, u32[]{:S(2)}, u32[]{:S(2)}) %collective-permute-start.1) | collective-permute-done | bytes 327712 | tf_op jit(solution)/shard_map/while/body/ppermute | solution.py:343
  60.3 27.0 %plan.4 = (s32[32]{0:T(128)}, s32[32]{0:T(128)}, s32[16]{0:T(128)}, s32[1024]{0:T(1024)S(1)}) custom-call(s32[1]{0:T(128)} %get-tuple-element.1016.me_ref, s32[1024]{0:T(1024)S(1)} %get-tuple-element.1017.a_ref, s32[1024]{0:T(1024)S(1)} %get-tuple-element.1018.b_ref, s32[1024]{0:T(1024)S(1)} %get-tuple-element.1019.cost_ref, s32[1024]{0:T(1024)} %and_select_fusion.6.flag_ref), custom_call_target="tpu_custom_call" | custom-call | flops 1000 | bytes 30000000 | tf_op jit(solution)/shard_map/while/body/plan/pallas_call | solution.py:291
  88.5 2.5 pack_home.12
  91.1 14.1 %all-to-all-done.items_ref = bf16[32,320,128]{2,1,0:T(8,128)(2,1)} async-done(((bf16[32,320,128]{2,1,0:T(8,128)(2,1)}), bf16[32,320,128]{2,1,0:T(8,128)(2,1)}, u32[]{:S(2)}, u32[]{:S(2)}) %all-to-all-start) | async-done | bytes 2621472 | tf_op jit(solution)/shard_map/while/body/all_to_all | solution.py:405
  105.1 7.4 %all-to-all-start.1 = ((bf16[32,320,128]{2,1,0:T(8,128)(2,1)}), bf16[32,320,128]{2,1,0:T(8,128)(2,1)}, u32[]{:S(2)}, u32[]{:S(2)}) async-start(bf16[32,320,128]{2,1,0:T(8,128)(2,1)} %pack_home.12), calls=%async_computation.1 | async-start | bytes 5242880 | tf_op jit(solution)/shard_map/while/body/all_to_all | solution.py:417
  113.2 3.5 %pack_items.4 = (bf16[4,320,128]{2,1,0:T(8,128)(2,1)}, bf16[4,320,128]{2,1,0:T(8,128)(2,1)}, bf16[4,320,128]{2,1,0:T(8,128)(2,1)}, bf16[4,320,128]{2,1,0:T(8,128...) custom-call(s32[32]{0:T(128)} %add.289.index_ref, ...), custom_call_target="tpu_custom_call" | custom-call | tf_op jit(solution)/shard_map/while/body/pack_items/pallas_call | solution.py:56
  117.9 2.1 collective-permute-start.12
  120.0 3.0 collective-permute-start.13
  123.0 6.2 %collective-permute-done.10.refs_12_ = bf16[4,320,128]{2,1,0:T(8,128)(2,1)S(1)} collective-permute-done((bf16[4,320,128]{2,1,0:T(8,128)(2,1)}, bf16[4,320,128]{2,1,0:T(8,128)(2,1)S(1)}, u32[]{:S(2)}, u32[]{:S(2)}) %collective-permute-start.10) | collective-permute-done | bytes 327712 | tf_op jit(solution)/shard_map/while/body/ppermute | solution.py:343
  129.7 2.8 collective-permute-done.11.refs_13_
  132.5 4.0 %collective-permute-start.9 = (bf16[4,320,128]{2,1,0:T(8,128)(2,1)}, bf16[4,320,128]{2,1,0:T(8,128)(2,1)}, u32[]{:S(2)}, u32[]{:S(2)}) collective-permute-start(bf16[4,320,128]{2,1,0:T(8,128)(2,1)} %get-tuple-element.923), channel_id=1, source_target_pairs={{0,3},{1,2},{2,1},{3,0},{4,7},{5,6},{6,5},{7,4},{8,11},{9,10},{10,... | collective-permute-start | bytes 983048 | tf_op jit(solution)/shard_map/while/body/ppermute | solution.py:343
  137.2 2.8 collective-permute-done.12.refs_14_
  140.0 7.1 %collective-permute-done.13.refs_15_ = bf16[4,320,128]{2,1,0:T(8,128)(2,1)} collective-permute-done((bf16[4,320,128]{2,1,0:T(8,128)(2,1)}, bf16[4,320,128]{2,1,0:T(8,128)(2,1)}, u32[]{:S(2)}, u32[]{:S(2)}) %collective-permute-start.13) | collective-permute-done | bytes 327712 | tf_op jit(solution)/shard_map/while/body/ppermute | solution.py:343
  147.2 11.1 %dimers.8 = (bf16[8,72,128]{2,1,0:T(8,128)(2,1)}, bf16[8,72,128]{2,1,0:T(8,128)(2,1)}, bf16[8,72,128]{2,1,0:T(8,128)(2,1)}, bf16[8,72,128]{2,1,0:T(8,128)(2,1)},...) custom-call(s32[4]{0:T(128)} %select_reduce_fusion.14.steps_ref, ...), custom_call_target="tpu_custom_call" | custom-call | flops 16000000000 | bytes 6000000 | tf_op jit(solution)/shard_map/while/body/dimers/pallas_call | solution.py:190
  158.3 1.7 collective-permute-start.14
  160.0 8.7 %collective-permute-start.15 = (bf16[8,72,128]{2,1,0:T(8,128)(2,1)}, bf16[8,72,128]{2,1,0:T(8,128)(2,1)S(1)}, u32[]{:S(2)}, u32[]{:S(2)}) collective-permute-start(bf16[8,72,128]{2,1,0:T(8,128)(2,1)} %get-tuple-element.930), channel_id=1, source_target_pairs={{0,2},{1,3},{2,0},{3,1},{4,6},{5,7},{6,4},{7,5},{8,10},{9,11},{10,... | collective-permute-start | bytes 442376 | tf_op jit(solution)/shard_map/while/body/ppermute | solution.py:343
  170.0 4.5 %collective-permute-start.17 = (bf16[8,72,128]{2,1,0:T(8,128)(2,1)}, bf16[8,72,128]{2,1,0:T(8,128)(2,1)S(1)}, u32[]{:S(2)}, u32[]{:S(2)}) collective-permute-start(bf16[8,72,128]{2,1,0:T(8,128)(2,1)} %get-tuple-element.932), channel_id=1, source_target_pairs={{0,4},{1,5},{2,6},{3,7},{4,0},{5,1},{6,2},{7,3},{8,12},{9,13},{10,... | collective-permute-start | bytes 442376 | tf_op jit(solution)/shard_map/while/body/ppermute | solution.py:343
  174.5 3.5 %collective-permute-start.19 = (bf16[8,72,128]{2,1,0:T(8,128)(2,1)}, bf16[8,72,128]{2,1,0:T(8,128)(2,1)S(1)}, u32[]{:S(2)}, u32[]{:S(2)}) collective-permute-start(bf16[8,72,128]{2,1,0:T(8,128)(2,1)} %get-tuple-element.934), channel_id=1, source_target_pairs={{0,6},{1,7},{2,4},{3,5},{4,2},{5,3},{6,0},{7,1},{8,14},{9,15},{10,... | collective-permute-start | bytes 442376 | tf_op jit(solution)/shard_map/while/body/ppermute | solution.py:343
  181.4 3.0 collective-permute-done.17.refs_4_.refs_22_
  184.5 2.0 collective-permute-done.18.refs_5_.refs_23_
  186.5 2.7 collective-permute-done.19.refs_6_.refs_24_
  189.2 2.7 collective-permute-done.20.refs_7_.refs_25_
  191.9 4.0 %pack_mixed.4 = (bf16[4,320,128]{2,1,0:T(8,128)(2,1)}, bf16[4,320,128]{2,1,0:T(8,128)(2,1)}, bf16[4,320,128]{2,1,0:T(8,128)(2,1)}, bf16[4,320,128]{2,1,0:T(8,128...) custom-call(s32[32]{0:T(128)} %reshape.202.index_ref, ...), custom_call_target="tpu_custom_call" | custom-call | tf_op jit(solution)/shard_map/while/body/pack_mixed/pallas_call | solution.py:85
  197.8 1.7 collective-permute-start.23
  199.7 3.0 collective-permute-start.25
  203.0 4.0 %collective-permute-done.22.refs_2_.refs_10_ = bf16[4,320,128]{2,1,0:T(8,128)(2,1)S(1)} collective-permute-done((bf16[4,320,128]{2,1,0:T(8,128)(2,1)}, bf16[4,320,128]{2,1,0:T(8,128)(2,1)S(1)}, u32[]{:S(2)}, u32[]{:S(2)}) %collective-permute-start.22) | collective-permute-done | bytes 327712 | tf_op jit(solution)/shard_map/while/body/ppermute | solution.py:343
  207.6 3.1 %place_items.8 = bf16[32,72,128]{2,1,0:T(8,128)(2,1)} custom-call(s32[64]{0:T(128)} %reshape.204.target_ref, bf16[8,72,128]{2,1,0:T(8,128)(2,1)} %get-tuple-element.936.refs_0_.refs_18_, bf16[8,72,128]{2,1,0:T(8,128)(2,1)} %copy-done.6, bf16[8,72,128]{2,1,0:T(8,128)(2,1)} %copy-done.7, bf16[8,72,128]{2,1,0:T(8,128)(2,1)} %copy-done.8, ...), custom_call_target="tpu_custom_call" | custom-call | tf_op jit(solution)/shard_map/while/body/place_items/pallas_call | solution.py:108
  210.7 14.4 %all-to-all-start.2 = ((bf16[32,72,128]{2,1,0:T(8,128)(2,1)}), bf16[32,72,128]{2,1,0:T(8,128)(2,1)S(1)}, u32[]{:S(2)}, u32[]{:S(2)}) async-start(bf16[32,72,128]{2,1,0:T(8,128)(2,1)} %place_items.8), calls=%async_computation.2 | async-start | bytes 1179648 | tf_op jit(solution)/shard_map/while/body/all_to_all | solution.py:439
  226.6 2.2 collective-permute-done.26.refs_6_.refs_14_
  228.8 5.9 %collective-permute-done.27.refs_7_.refs_15_ = bf16[4,320,128]{2,1,0:T(8,128)(2,1)S(1)} collective-permute-done((bf16[4,320,128]{2,1,0:T(8,128)(2,1)}, bf16[4,320,128]{2,1,0:T(8,128)(2,1)S(1)}, u32[]{:S(2)}, u32[]{:S(2)}) %collective-permute-start.27) | collective-permute-done | bytes 327712 | tf_op jit(solution)/shard_map/while/body/ppermute | solution.py:343
  235.4 6.3 %dimers.9 = (bf16[4,72,128]{2,1,0:T(8,128)(2,1)}, bf16[4,72,128]{2,1,0:T(8,128)(2,1)}, bf16[4,72,128]{2,1,0:T(8,128)(2,1)}, bf16[4,72,128]{2,1,0:T(8,128)(2,1)},...) custom-call(s32[2]{0:T(128)} %select_reduce_fusion.15.steps_ref, ...), custom_call_target="tpu_custom_call" | custom-call | flops 8000000000 | bytes 3000000 | tf_op jit(solution)/shard_map/while/body/dimers/pallas_call | solution.py:190
  242.5 3.7 %collective-permute-start.29 = (bf16[4,72,128]{2,1,0:T(8,128)(2,1)}, bf16[4,72,128]{2,1,0:T(8,128)(2,1)S(1)}, u32[]{:S(2)}, u32[]{:S(2)}) collective-permute-start(bf16[4,72,128]{2,1,0:T(8,128)(2,1)} %get-tuple-element.955), channel_id=1, source_target_pairs={{0,2},{1,3},{2,0},{3,1},{4,6},{5,7},{6,4},{7,5},{8,10},{9,11},{10,... | collective-permute-start | bytes 221192 | tf_op jit(solution)/shard_map/while/body/ppermute | solution.py:343
  247.1 2.4 collective-permute-start.32
  251.0 1.9 collective-permute-start.34
  253.4 2.6 collective-permute-done.33.refs_6_.refs_32_
  257.9 2.4 place_items.9
  260.3 18.5 %all-to-all-start.3 = ((bf16[32,72,128]{2,1,0:T(8,128)(2,1)}), bf16[32,72,128]{2,1,0:T(8,128)(2,1)S(1)}, u32[]{:S(2)}, u32[]{:S(2)}) async-start(bf16[32,72,128]{2,1,0:T(8,128)(2,1)} %place_items.9), calls=%async_computation.3 | async-start | bytes 1179648 | tf_op jit(solution)/shard_map/while/body/all_to_all | solution.py:443
  286.0 12.3 %all-to-all-done.3.refs_35_ = bf16[32,72,128]{2,1,0:T(8,128)(2,1)S(1)} async-done(((bf16[32,72,128]{2,1,0:T(8,128)(2,1)}), bf16[32,72,128]{2,1,0:T(8,128)(2,1)S(1)}, u32[]{:S(2)}, u32[]{:S(2)}) %all-to-all-start.3) | async-done | bytes 589856 | tf_op jit(solution)/shard_map/while/body/all_to_all | solution.py:443
  299.1 4.4 %add_up.4 = (f32[32,32,256]{2,1,0:T(8,128)S(1)}, f32[32,128]{1,0:T(8,128)S(1)}) custom-call(s32[8]{0:T(128)} %squeeze.64.refs_0_, s32[8]{0:T(128)} %squeeze.65.refs_1_, s32[8]{0:T(128)} %squeeze.66.refs_2_, s32[8]{0:T(128)} %squeeze.67.refs_3_, s32[8]{0:T(128)} %squeeze.68.refs_4_, ...), custom_call_target="tpu_custom_call", output_to_operand_aliasing={{0}: (36, {}), {1}: (37, {})} | custom-call | tf_op jit(solution)/shard_map/while/body/add_up/pallas_call | solution.py:330
  (220 shorter events, 41.9 us)
Async XLA Ops:
  3.0 9.7 %all-to-all-start.4 = ((s32[8,1,128]{2,1,0:T(1,128)}), s32[8,1,128]{2,1,0:T(1,128)S(1)}, u32[]{:S(2)}, u32[]{:S(2)}) async-start(s32[8,1,128]{2,1,0:T(1,128)} %broadcast_in_dim.189), calls=%async_computation.4 | async-start | bytes 8192 | tf_op jit(solution)/shard_map/all_to_all | solution.py:357
  13.6 19.8 %all-to-all-start.5 = ((s32[32,1,128]{2,1,0:T(1,128)}), s32[32,1,128]{2,1,0:T(1,128)S(1)}, u32[]{:S(2)}, u32[]{:S(2)}) async-start(s32[32,1,128]{2,1,0:T(1,128)} %broadcast_in_dim.190), calls=%async_computation.5 | async-start | bytes 32768 | tf_op jit(solution)/shard_map/all_to_all | solution.py:362
  34.9 77.6 %copy-start.27 = (s32[8]{0:T(128)}, s32[8]{0:T(128)S(1)}, u32[]{:S(2)}) copy-start(s32[8]{0:T(128)S(1)} %get-tuple-element.1029) | copy-start | bytes 100 | tf_op jit(solution)/shard_map/while
  35.0 77.6 %copy-start.29 = (s32[4]{0:T(128)}, s32[4]{0:T(128)S(1)}, u32[]{:S(2)}) copy-start(s32[4]{0:T(128)S(1)} %get-tuple-element.1030) | copy-start | bytes 52 | tf_op jit(solution)/shard_map/while
  39.4 65.7 %all-to-all-start = ((bf16[32,320,128]{2,1,0:T(8,128)(2,1)}), bf16[32,320,128]{2,1,0:T(8,128)(2,1)}, u32[]{:S(2)}, u32[]{:S(2)}) async-start(bf16[32,320,128]{2,1,0:T(8,128)(2,1)} %pack_home.13), calls=%async_computation | async-start | bytes 5242880 | tf_op jit(solution)/shard_map/while/body/all_to_all | solution.py:405
  45.7 45.3 %copy-start.31 = (s32[32]{0:T(128)}, s32[32]{0:T(128)S(1)}, u32[]{:S(2)}) copy-start(s32[32]{0:T(128)S(1)} %select_reduce_fusion.13) | copy-start | bytes 388 | tf_op jit(solution)/shard_map/while
  48.8 5.7 %collective-permute-start = (bf16[4,320,128]{2,1,0:T(8,128)(2,1)}, bf16[4,320,128]{2,1,0:T(8,128)(2,1)S(1)}, u32[]{:S(2)}, u32[]{:S(2)}) collective-permute-start(bf16[4,320,128]{2,1,0:T(8,128)(2,1)} %get-tuple-element.902), channel_id=1, source_target_pairs={{0,1},{1,0},{2,3},{3,2},{4,5},{5,4},{6,7},{7,6},{8,9},{9,8},{10,11... | collective-permute-start | bytes 983048 | tf_op jit(solution)/shard_map/while/body/ppermute | solution.py:343
  48.8 10.8 %collective-permute-start.1 = (bf16[4,320,128]{2,1,0:T(8,128)(2,1)}, bf16[4,320,128]{2,1,0:T(8,128)(2,1)S(1)}, u32[]{:S(2)}, u32[]{:S(2)}) collective-permute-start(bf16[4,320,128]{2,1,0:T(8,128)(2,1)} %get-tuple-element.903), channel_id=1, source_target_pairs={{0,2},{1,3},{2,0},{3,1},{4,6},{5,7},{6,4},{7,5},{8,10},{9,11},{10,... | collective-permute-start | bytes 983048 | tf_op jit(solution)/shard_map/while/body/ppermute | solution.py:343
  49.3 41.7 %collective-permute-start.2 = (bf16[4,320,128]{2,1,0:T(8,128)(2,1)}, bf16[4,320,128]{2,1,0:T(8,128)(2,1)}, u32[]{:S(2)}, u32[]{:S(2)}) collective-permute-start(bf16[4,320,128]{2,1,0:T(8,128)(2,1)} %get-tuple-element.904), channel_id=1, source_target_pairs={{0,3},{1,2},{2,1},{3,0},{4,7},{5,6},{6,5},{7,4},{8,11},{9,10},{10,... | collective-permute-start | bytes 983048 | tf_op jit(solution)/shard_map/while/body/ppermute | solution.py:343
  50.6 40.4 %collective-permute-start.3 = (bf16[4,320,128]{2,1,0:T(8,128)(2,1)}, bf16[4,320,128]{2,1,0:T(8,128)(2,1)}, u32[]{:S(2)}, u32[]{:S(2)}) collective-permute-start(bf16[4,320,128]{2,1,0:T(8,128)(2,1)} %get-tuple-element.905), channel_id=1, source_target_pairs={{0,4},{1,5},{2,6},{3,7},{4,0},{5,1},{6,2},{7,3},{8,12},{9,13},{10,... | collective-permute-start | bytes 983048 | tf_op jit(solution)/shard_map/while/body/ppermute | solution.py:343
  51.8 39.2 %collective-permute-start.4 = (bf16[4,320,128]{2,1,0:T(8,128)(2,1)}, bf16[4,320,128]{2,1,0:T(8,128)(2,1)}, u32[]{:S(2)}, u32[]{:S(2)}) collective-permute-start(bf16[4,320,128]{2,1,0:T(8,128)(2,1)} %get-tuple-element.906), channel_id=1, source_target_pairs={{0,5},{1,4},{2,7},{3,6},{4,1},{5,0},{6,3},{7,2},{8,13},{9,12},{10,... | collective-permute-start | bytes 983048 | tf_op jit(solution)/shard_map/while/body/ppermute | solution.py:343
  54.5 36.5 %collective-permute-start.5 = (bf16[4,320,128]{2,1,0:T(8,128)(2,1)}, bf16[4,320,128]{2,1,0:T(8,128)(2,1)}, u32[]{:S(2)}, u32[]{:S(2)}) collective-permute-start(bf16[4,320,128]{2,1,0:T(8,128)(2,1)} %get-tuple-element.907), channel_id=1, source_target_pairs={{0,6},{1,7},{2,4},{3,5},{4,2},{5,3},{6,0},{7,1},{8,14},{9,15},{10,... | collective-permute-start | bytes 983048 | tf_op jit(solution)/shard_map/while/body/ppermute | solution.py:343
  59.6 31.5 %collective-permute-start.6 = (bf16[4,320,128]{2,1,0:T(8,128)(2,1)}, bf16[4,320,128]{2,1,0:T(8,128)(2,1)}, u32[]{:S(2)}, u32[]{:S(2)}) collective-permute-start(bf16[4,320,128]{2,1,0:T(8,128)(2,1)} %get-tuple-element.908), channel_id=1, source_target_pairs={{0,7},{1,6},{2,5},{3,4},{4,3},{5,2},{6,1},{7,0},{8,15},{9,14},{10,... | collective-permute-start | bytes 983048 | tf_op jit(solution)/shard_map/while/body/ppermute | solution.py:343
  105.1 86.8 %all-to-all-start.1 = ((bf16[32,320,128]{2,1,0:T(8,128)(2,1)}), bf16[32,320,128]{2,1,0:T(8,128)(2,1)}, u32[]{:S(2)}, u32[]{:S(2)}) async-start(bf16[32,320,128]{2,1,0:T(8,128)(2,1)} %pack_home.12), calls=%async_computation.1 | async-start | bytes 5242880 | tf_op jit(solution)/shard_map/while/body/all_to_all | solution.py:417
  116.8 12.4 %collective-permute-start.10 = (bf16[4,320,128]{2,1,0:T(8,128)(2,1)}, bf16[4,320,128]{2,1,0:T(8,128)(2,1)S(1)}, u32[]{:S(2)}, u32[]{:S(2)}) collective-permute-start(bf16[4,320,128]{2,1,0:T(8,128)(2,1)} %get-tuple-element.924), channel_id=1, source_target_pairs={{0,4},{1,5},{2,6},{3,7},{4,0},{5,1},{6,2},{7,3},{8,12},{9,13},{10,... | collective-permute-start | bytes 983048 | tf_op jit(solution)/shard_map/while/body/ppermute | solution.py:343
  117.9 14.5 %collective-permute-start.11 = (bf16[4,320,128]{2,1,0:T(8,128)(2,1)}, bf16[4,320,128]{2,1,0:T(8,128)(2,1)S(1)}, u32[]{:S(2)}, u32[]{:S(2)}) collective-permute-start(bf16[4,320,128]{2,1,0:T(8,128)(2,1)} %get-tuple-element.925), channel_id=1, source_target_pairs={{0,5},{1,4},{2,7},{3,6},{4,1},{5,0},{6,3},{7,2},{8,13},{9,12},{10,... | collective-permute-start | bytes 983048 | tf_op jit(solution)/shard_map/while/body/ppermute | solution.py:343
  117.9 22.1 %collective-permute-start.12 = (bf16[4,320,128]{2,1,0:T(8,128)(2,1)}, bf16[4,320,128]{2,1,0:T(8,128)(2,1)}, u32[]{:S(2)}, u32[]{:S(2)}) collective-permute-start(bf16[4,320,128]{2,1,0:T(8,128)(2,1)} %get-tuple-element.926), channel_id=1, source_target_pairs={{0,6},{1,7},{2,4},{3,5},{4,2},{5,3},{6,0},{7,1},{8,14},{9,15},{10,... | collective-permute-start | bytes 983048 | tf_op jit(solution)/shard_map/while/body/ppermute | solution.py:343
  120.0 27.1 %collective-permute-start.13 = (bf16[4,320,128]{2,1,0:T(8,128)(2,1)}, bf16[4,320,128]{2,1,0:T(8,128)(2,1)}, u32[]{:S(2)}, u32[]{:S(2)}) collective-permute-start(bf16[4,320,128]{2,1,0:T(8,128)(2,1)} %get-tuple-element.927), channel_id=1, source_target_pairs={{0,7},{1,6},{2,5},{3,4},{4,3},{5,2},{6,1},{7,0},{8,15},{9,14},{10,... | collective-permute-start | bytes 983048 | tf_op jit(solution)/shard_map/while/body/ppermute | solution.py:343
  123.0 24.2 %collective-permute-start.7 = (bf16[4,320,128]{2,1,0:T(8,128)(2,1)}, bf16[4,320,128]{2,1,0:T(8,128)(2,1)}, u32[]{:S(2)}, u32[]{:S(2)}) collective-permute-start(bf16[4,320,128]{2,1,0:T(8,128)(2,1)} %get-tuple-element.921), channel_id=1, source_target_pairs={{0,1},{1,0},{2,3},{3,2},{4,5},{5,4},{6,7},{7,6},{8,9},{9,8},{10,11... | collective-permute-start | bytes 983048 | tf_op jit(solution)/shard_map/while/body/ppermute | solution.py:343
  129.1 18.0 %collective-permute-start.8 = (bf16[4,320,128]{2,1,0:T(8,128)(2,1)}, bf16[4,320,128]{2,1,0:T(8,128)(2,1)}, u32[]{:S(2)}, u32[]{:S(2)}) collective-permute-start(bf16[4,320,128]{2,1,0:T(8,128)(2,1)} %get-tuple-element.922), channel_id=1, source_target_pairs={{0,2},{1,3},{2,0},{3,1},{4,6},{5,7},{6,4},{7,5},{8,10},{9,11},{10,... | collective-permute-start | bytes 983048 | tf_op jit(solution)/shard_map/while/body/ppermute | solution.py:343
  132.5 14.7 %collective-permute-start.9 = (bf16[4,320,128]{2,1,0:T(8,128)(2,1)}, bf16[4,320,128]{2,1,0:T(8,128)(2,1)}, u32[]{:S(2)}, u32[]{:S(2)}) collective-permute-start(bf16[4,320,128]{2,1,0:T(8,128)(2,1)} %get-tuple-element.923), channel_id=1, source_target_pairs={{0,3},{1,2},{2,1},{3,0},{4,7},{5,6},{6,5},{7,4},{8,11},{9,10},{10,... | collective-permute-start | bytes 983048 | tf_op jit(solution)/shard_map/while/body/ppermute | solution.py:343
  158.3 16.2 %collective-permute-start.14 = (bf16[8,72,128]{2,1,0:T(8,128)(2,1)}, bf16[8,72,128]{2,1,0:T(8,128)(2,1)S(1)}, u32[]{:S(2)}, u32[]{:S(2)}) collective-permute-start(bf16[8,72,128]{2,1,0:T(8,128)(2,1)} %get-tuple-element.929), channel_id=1, source_target_pairs={{0,1},{1,0},{2,3},{3,2},{4,5},{5,4},{6,7},{7,6},{8,9},{9,8},{10,11... | collective-permute-start | bytes 442376 | tf_op jit(solution)/shard_map/while/body/ppermute | solution.py:343
  160.0 18.0 %collective-permute-start.15 = (bf16[8,72,128]{2,1,0:T(8,128)(2,1)}, bf16[8,72,128]{2,1,0:T(8,128)(2,1)S(1)}, u32[]{:S(2)}, u32[]{:S(2)}) collective-permute-start(bf16[8,72,128]{2,1,0:T(8,128)(2,1)} %get-tuple-element.930), channel_id=1, source_target_pairs={{0,2},{1,3},{2,0},{3,1},{4,6},{5,7},{6,4},{7,5},{8,10},{9,11},{10,... | collective-permute-start | bytes 442376 | tf_op jit(solution)/shard_map/while/body/ppermute | solution.py:343
  170.0 11.5 %collective-permute-start.16 = (bf16[8,72,128]{2,1,0:T(8,128)(2,1)}, bf16[8,72,128]{2,1,0:T(8,128)(2,1)S(1)}, u32[]{:S(2)}, u32[]{:S(2)}) collective-permute-start(bf16[8,72,128]{2,1,0:T(8,128)(2,1)} %get-tuple-element.931), channel_id=1, source_target_pairs={{0,3},{1,2},{2,1},{3,0},{4,7},{5,6},{6,5},{7,4},{8,11},{9,10},{10,... | collective-permute-start | bytes 442376 | tf_op jit(solution)/shard_map/while/body/ppermute | solution.py:343
  170.0 14.5 %collective-permute-start.17 = (bf16[8,72,128]{2,1,0:T(8,128)(2,1)}, bf16[8,72,128]{2,1,0:T(8,128)(2,1)S(1)}, u32[]{:S(2)}, u32[]{:S(2)}) collective-permute-start(bf16[8,72,128]{2,1,0:T(8,128)(2,1)} %get-tuple-element.932), channel_id=1, source_target_pairs={{0,4},{1,5},{2,6},{3,7},{4,0},{5,1},{6,2},{7,3},{8,12},{9,13},{10,... | collective-permute-start | bytes 442376 | tf_op jit(solution)/shard_map/while/body/ppermute | solution.py:343
  174.5 12.1 %collective-permute-start.18 = (bf16[8,72,128]{2,1,0:T(8,128)(2,1)}, bf16[8,72,128]{2,1,0:T(8,128)(2,1)S(1)}, u32[]{:S(2)}, u32[]{:S(2)}) collective-permute-start(bf16[8,72,128]{2,1,0:T(8,128)(2,1)} %get-tuple-element.933), channel_id=1, source_target_pairs={{0,5},{1,4},{2,7},{3,6},{4,1},{5,0},{6,3},{7,2},{8,13},{9,12},{10,... | collective-permute-start | bytes 442376 | tf_op jit(solution)/shard_map/while/body/ppermute | solution.py:343
  174.5 14.7 %collective-permute-start.19 = (bf16[8,72,128]{2,1,0:T(8,128)(2,1)}, bf16[8,72,128]{2,1,0:T(8,128)(2,1)S(1)}, u32[]{:S(2)}, u32[]{:S(2)}) collective-permute-start(bf16[8,72,128]{2,1,0:T(8,128)(2,1)} %get-tuple-element.934), channel_id=1, source_target_pairs={{0,6},{1,7},{2,4},{3,5},{4,2},{5,3},{6,0},{7,1},{8,14},{9,15},{10,... | collective-permute-start | bytes 442376 | tf_op jit(solution)/shard_map/while/body/ppermute | solution.py:343
  178.0 13.9 %collective-permute-start.20 = (bf16[8,72,128]{2,1,0:T(8,128)(2,1)}, bf16[8,72,128]{2,1,0:T(8,128)(2,1)}, u32[]{:S(2)}, u32[]{:S(2)}) collective-permute-start(bf16[8,72,128]{2,1,0:T(8,128)(2,1)} %get-tuple-element.935), channel_id=1, source_target_pairs={{0,7},{1,6},{2,5},{3,4},{4,3},{5,2},{6,1},{7,0},{8,15},{9,14},{10,... | collective-permute-start | bytes 442376 | tf_op jit(solution)/shard_map/while/body/ppermute | solution.py:343
  196.0 6.8 %collective-permute-start.21 = (bf16[4,320,128]{2,1,0:T(8,128)(2,1)}, bf16[4,320,128]{2,1,0:T(8,128)(2,1)S(1)}, u32[]{:S(2)}, u32[]{:S(2)}) collective-permute-start(bf16[4,320,128]{2,1,0:T(8,128)(2,1)} %get-tuple-element.946), channel_id=1, source_target_pairs={{0,1},{1,0},{2,3},{3,2},{4,5},{5,4},{6,7},{7,6},{8,9},{9,8},{10,11... | collective-permute-start | bytes 983048 | tf_op jit(solution)/shard_map/while/body/ppermute | solution.py:343
  196.2 10.8 %collective-permute-start.22 = (bf16[4,320,128]{2,1,0:T(8,128)(2,1)}, bf16[4,320,128]{2,1,0:T(8,128)(2,1)S(1)}, u32[]{:S(2)}, u32[]{:S(2)}) collective-permute-start(bf16[4,320,128]{2,1,0:T(8,128)(2,1)} %get-tuple-element.947), channel_id=1, source_target_pairs={{0,2},{1,3},{2,0},{3,1},{4,6},{5,7},{6,4},{7,5},{8,10},{9,11},{10,... | collective-permute-start | bytes 983048 | tf_op jit(solution)/shard_map/while/body/ppermute | solution.py:343
  197.8 28.0 %collective-permute-start.23 = (bf16[4,320,128]{2,1,0:T(8,128)(2,1)}, bf16[4,320,128]{2,1,0:T(8,128)(2,1)S(1)}, u32[]{:S(2)}, u32[]{:S(2)}) collective-permute-start(bf16[4,320,128]{2,1,0:T(8,128)(2,1)} %get-tuple-element.948), channel_id=1, source_target_pairs={{0,3},{1,2},{2,1},{3,0},{4,7},{5,6},{6,5},{7,4},{8,11},{9,10},{10,... | collective-permute-start | bytes 983048 | tf_op jit(solution)/shard_map/while/body/ppermute | solution.py:343
  199.5 26.3 %collective-permute-start.24 = (bf16[4,320,128]{2,1,0:T(8,128)(2,1)}, bf16[4,320,128]{2,1,0:T(8,128)(2,1)S(1)}, u32[]{:S(2)}, u32[]{:S(2)}) collective-permute-start(bf16[4,320,128]{2,1,0:T(8,128)(2,1)} %get-tuple-element.949), channel_id=1, source_target_pairs={{0,4},{1,5},{2,6},{3,7},{4,0},{5,1},{6,2},{7,3},{8,12},{9,13},{10,... | collective-permute-start | bytes 983048 | tf_op jit(solution)/shard_map/while/body/ppermute | solution.py:343
  199.7 26.9 %collective-permute-start.25 = (bf16[4,320,128]{2,1,0:T(8,128)(2,1)}, bf16[4,320,128]{2,1,0:T(8,128)(2,1)S(1)}, u32[]{:S(2)}, u32[]{:S(2)}) collective-permute-start(bf16[4,320,128]{2,1,0:T(8,128)(2,1)} %get-tuple-element.950), channel_id=1, source_target_pairs={{0,5},{1,4},{2,7},{3,6},{4,1},{5,0},{6,3},{7,2},{8,13},{9,12},{10,... | collective-permute-start | bytes 983048 | tf_op jit(solution)/shard_map/while/body/ppermute | solution.py:343
  202.8 26.0 %collective-permute-start.26 = (bf16[4,320,128]{2,1,0:T(8,128)(2,1)}, bf16[4,320,128]{2,1,0:T(8,128)(2,1)S(1)}, u32[]{:S(2)}, u32[]{:S(2)}) collective-permute-start(bf16[4,320,128]{2,1,0:T(8,128)(2,1)} %get-tuple-element.951), channel_id=1, source_target_pairs={{0,6},{1,7},{2,4},{3,5},{4,2},{5,3},{6,0},{7,1},{8,14},{9,15},{10,... | collective-permute-start | bytes 983048 | tf_op jit(solution)/shard_map/while/body/ppermute | solution.py:343
  207.0 27.7 %collective-permute-start.27 = (bf16[4,320,128]{2,1,0:T(8,128)(2,1)}, bf16[4,320,128]{2,1,0:T(8,128)(2,1)S(1)}, u32[]{:S(2)}, u32[]{:S(2)}) collective-permute-start(bf16[4,320,128]{2,1,0:T(8,128)(2,1)} %get-tuple-element.952), channel_id=1, source_target_pairs={{0,7},{1,6},{2,5},{3,4},{4,3},{5,2},{6,1},{7,0},{8,15},{9,14},{10,... | collective-permute-start | bytes 983048 | tf_op jit(solution)/shard_map/while/body/ppermute | solution.py:343
  210.7 49.6 %all-to-all-start.2 = ((bf16[32,72,128]{2,1,0:T(8,128)(2,1)}), bf16[32,72,128]{2,1,0:T(8,128)(2,1)S(1)}, u32[]{:S(2)}, u32[]{:S(2)}) async-start(bf16[32,72,128]{2,1,0:T(8,128)(2,1)} %place_items.8), calls=%async_computation.2 | async-start | bytes 1179648 | tf_op jit(solution)/shard_map/while/body/all_to_all | solution.py:439
  241.7 57.3 %copy-start.4 = (f32[32,32,256]{2,1,0:T(8,128)S(1)}, f32[32,32,256]{2,1,0:T(8,128)}, u32[]{:S(2)}) copy-start(f32[32,32,256]{2,1,0:T(8,128)} %get-tuple-element.989.refs_36_) | copy-start | bytes 3145732 | tf_op jit(solution)/shard_map/while
  241.7 7.8 %collective-permute-start.28 = (bf16[4,72,128]{2,1,0:T(8,128)(2,1)}, bf16[4,72,128]{2,1,0:T(8,128)(2,1)S(1)}, u32[]{:S(2)}, u32[]{:S(2)}) collective-permute-start(bf16[4,72,128]{2,1,0:T(8,128)(2,1)} %get-tuple-element.954), channel_id=1, source_target_pairs={{0,1},{1,0},{2,3},{3,2},{4,5},{5,4},{6,7},{7,6},{8,9},{9,8},{10,11... | collective-permute-start | bytes 221192 | tf_op jit(solution)/shard_map/while/body/ppermute | solution.py:343
  242.5 8.4 %collective-permute-start.29 = (bf16[4,72,128]{2,1,0:T(8,128)(2,1)}, bf16[4,72,128]{2,1,0:T(8,128)(2,1)S(1)}, u32[]{:S(2)}, u32[]{:S(2)}) collective-permute-start(bf16[4,72,128]{2,1,0:T(8,128)(2,1)} %get-tuple-element.955), channel_id=1, source_target_pairs={{0,2},{1,3},{2,0},{3,1},{4,6},{5,7},{6,4},{7,5},{8,10},{9,11},{10,... | collective-permute-start | bytes 221192 | tf_op jit(solution)/shard_map/while/body/ppermute | solution.py:343
  246.4 6.9 %collective-permute-start.30 = (bf16[4,72,128]{2,1,0:T(8,128)(2,1)}, bf16[4,72,128]{2,1,0:T(8,128)(2,1)S(1)}, u32[]{:S(2)}, u32[]{:S(2)}) collective-permute-start(bf16[4,72,128]{2,1,0:T(8,128)(2,1)} %get-tuple-element.956), channel_id=1, source_target_pairs={{0,3},{1,2},{2,1},{3,0},{4,7},{5,6},{6,5},{7,4},{8,11},{9,10},{10,... | collective-permute-start | bytes 221192 | tf_op jit(solution)/shard_map/while/body/ppermute | solution.py:343
  246.5 6.9 %collective-permute-start.31 = (bf16[4,72,128]{2,1,0:T(8,128)(2,1)}, bf16[4,72,128]{2,1,0:T(8,128)(2,1)S(1)}, u32[]{:S(2)}, u32[]{:S(2)}) collective-permute-start(bf16[4,72,128]{2,1,0:T(8,128)(2,1)} %get-tuple-element.957), channel_id=1, source_target_pairs={{0,4},{1,5},{2,6},{3,7},{4,0},{5,1},{6,2},{7,3},{8,12},{9,13},{10,... | collective-permute-start | bytes 221192 | tf_op jit(solution)/shard_map/while/body/ppermute | solution.py:343
  247.1 6.3 %collective-permute-start.32 = (bf16[4,72,128]{2,1,0:T(8,128)(2,1)}, bf16[4,72,128]{2,1,0:T(8,128)(2,1)S(1)}, u32[]{:S(2)}, u32[]{:S(2)}) collective-permute-start(bf16[4,72,128]{2,1,0:T(8,128)(2,1)} %get-tuple-element.958), channel_id=1, source_target_pairs={{0,5},{1,4},{2,7},{3,6},{4,1},{5,0},{6,3},{7,2},{8,13},{9,12},{10,... | collective-permute-start | bytes 221192 | tf_op jit(solution)/shard_map/while/body/ppermute | solution.py:343
  249.5 6.6 %collective-permute-start.33 = (bf16[4,72,128]{2,1,0:T(8,128)(2,1)}, bf16[4,72,128]{2,1,0:T(8,128)(2,1)S(1)}, u32[]{:S(2)}, u32[]{:S(2)}) collective-permute-start(bf16[4,72,128]{2,1,0:T(8,128)(2,1)} %get-tuple-element.959), channel_id=1, source_target_pairs={{0,6},{1,7},{2,4},{3,5},{4,2},{5,3},{6,0},{7,1},{8,14},{9,15},{10,... | collective-permute-start | bytes 221192 | tf_op jit(solution)/shard_map/while/body/ppermute | solution.py:343
  251.0 6.3 %collective-permute-start.34 = (bf16[4,72,128]{2,1,0:T(8,128)(2,1)}, bf16[4,72,128]{2,1,0:T(8,128)(2,1)S(1)}, u32[]{:S(2)}, u32[]{:S(2)}) collective-permute-start(bf16[4,72,128]{2,1,0:T(8,128)(2,1)} %get-tuple-element.960), channel_id=1, source_target_pairs={{0,7},{1,6},{2,5},{3,4},{4,3},{5,2},{6,1},{7,0},{8,15},{9,14},{10,... | collective-permute-start | bytes 221192 | tf_op jit(solution)/shard_map/while/body/ppermute | solution.py:343
  260.3 44.2 %copy-start.21 = (s32[1024]{0:T(1024)S(1)}, s32[1024]{0:T(1024)}, u32[]{:S(2)}) copy-start(s32[1024]{0:T(1024)} %copy-done.20) | copy-start | bytes 12292 | tf_op jit(solution)/shard_map/while
  260.3 44.2 %copy-start.26 = (pred[1024]{0:T(1024)(128)(4,1)S(1)}, pred[1024]{0:T(1024)(128)(4,1)}, u32[]{:S(2)}) copy-start(pred[1024]{0:T(1024)(128)(4,1)} %copy-done.25) | copy-start | bytes 3076 | tf_op jit(solution)/shard_map/while
  260.3 44.2 %copy-start.28 = (s32[8]{0:T(128)S(1)}, s32[8]{0:T(128)}, u32[]{:S(2)}) copy-start(s32[8]{0:T(128)} %copy-done.27) | copy-start | bytes 100 | tf_op jit(solution)/shard_map/while
  260.3 37.9 %all-to-all-start.3 = ((bf16[32,72,128]{2,1,0:T(8,128)(2,1)}), bf16[32,72,128]{2,1,0:T(8,128)(2,1)S(1)}, u32[]{:S(2)}, u32[]{:S(2)}) async-start(bf16[32,72,128]{2,1,0:T(8,128)(2,1)} %place_items.9), calls=%async_computation.3 | async-start | bytes 1179648 | tf_op jit(solution)/shard_map/while/body/all_to_all | solution.py:443
  (42 other events, 701.1 us)

commit v3 on v1

v3 whole, which is shorter than its diff:
```python
import jax
import jax.numpy as jnp
from jax import lax
from jax.experimental import pallas as pl
from jax.experimental.pallas import tpu as pltpu
from jax.sharding import PartitionSpec as P

COUPLE = 0.015625
BIG = 1 << 30
BF16 = jnp.bfloat16
F32 = jnp.float32
KX, KZ = 6, 2
NX, NZ = 3 * KX, 8 * KZ
SENT, RELAY, POS, HOME, LATE, STEPS, MODE, TABLE = 0, 32, 64, 128, 160, 192, 224, 256
OUT, BASE, STEP1, RANKED = 0, 32, 64, 96

VMEM = pl.BlockSpec(memory_space=pltpu.VMEM)
SMEM = pl.BlockSpec(memory_space=pltpu.SMEM)


def loop(count, body):
    def step(n, unused):
        body(n)
        return unused

    lax.fori_loop(0, count, step, 0)


def ranked_at(device, place):
    return place * 8 + jnp.where(place % 2 == 0, device, 7 - device)


def pack(tables, me, find, outs, rows, home, items):
    sizes = ([32] if home else []) + [item.shape[0] for item in items]

    def kernel(*refs):
        table_refs, me_ref, refs = refs[: len(tables)], refs[len(tables)], refs[len(tables) + 1 :]
        sources, out_refs = refs[: len(refs) - outs], refs[len(refs) - outs :]
        for n, out_ref in enumerate(out_refs):

            def body(row, n=n, out_ref=out_ref):
                at = jnp.maximum(find(table_refs, me_ref[0], n, row), 0)
                base, left = 0, list(sources)
                for which, size in enumerate(sizes):
                    here = (at >= base) & (at < base + size)
                    if home and which == 0:
                        aux_ref, den_ref = left.pop(0), left.pop(0)

                        @pl.when(here)
                        def _(aux_ref=aux_ref, den_ref=den_ref):
                            out_ref[row, 0:256, :] = aux_ref[at]
                            block = den_ref[at]
                            out_ref[row, 256:288, :] = block[:, 0:128]
                            out_ref[row, 288:320, :] = block[:, 128:256]
                    else:
                        item_ref = left.pop(0)

                        @pl.when(here)
                        def _(item_ref=item_ref, base=base):
                            out_ref[row] = item_ref[at - base]

                    base += size

            loop(rows, body)

    sources = list(home) + list(items)
    return pl.pallas_call(
        kernel,
        out_shape=[jax.ShapeDtypeStruct((rows, 320, 128), BF16)] * outs,
        in_specs=[SMEM] * (len(tables) + 1) + [VMEM] * len(sources),
        out_specs=[VMEM] * outs,
        name="pack",
    )(*tables, me, *sources)


def place(tables, me, parts, finds, out_rows):
    def kernel(*refs):
        table_refs, me_ref, refs = refs[: len(tables)], refs[len(tables)], refs[len(tables) + 1 :]
        for part_ref, find in zip(refs[: len(parts)], finds, strict=True):

            def body(row, part_ref=part_ref, find=find):
                at = find(table_refs, me_ref[0], row)
                base = 0
                for out_ref, size in zip(refs[len(parts) :], out_rows, strict=True):

                    @pl.when((at >= base) & (at < base + size))
                    def _(out_ref=out_ref, base=base):
                        out_ref[at - base] = part_ref[row]

                    base += size

            loop(part_ref.shape[0], body)

    return pl.pallas_call(
        kernel,
        out_shape=[jax.ShapeDtypeStruct((size, 72, 128), BF16) for size in out_rows],
        in_specs=[SMEM] * (len(tables) + 1) + [VMEM] * len(parts),
        out_specs=[VMEM] * len(out_rows),
        name="place",
    )(*tables, me, *parts)


def add_up(tables, me, parts, finds, dens, emb):
    def kernel(*refs):
        table_refs, me_ref, refs = refs[: len(tables)], refs[len(tables)], refs[len(tables) + 1 :]
        dens_in, emb_in, dens_ref, emb_ref = refs[len(parts) :]
        dens_ref[...] = dens_in[...]
        emb_ref[...] = emb_in[...]
        for part_ref, find in zip(refs[: len(parts)], finds, strict=True):

            def body(row, part_ref=part_ref, find=find):
                slot = find(table_refs, me_ref[0], row)

                @pl.when((slot >= 0) & (slot < 32))
                def _():
                    dens_ref[slot, :, 0:128] += part_ref[row, 0:32, :].astype(F32)
                    dens_ref[slot, :, 128:256] += part_ref[row, 32:64, :].astype(F32)
                    emb_ref[pl.ds(slot, 1), :] += part_ref[row, 64:72, :].astype(F32)[0:1, :]

            loop(part_ref.shape[0], body)

    first = len(tables) + 1 + len(parts)
    return pl.pallas_call(
        kernel,
        out_shape=[jax.ShapeDtypeStruct(dens.shape, F32), jax.ShapeDtypeStruct(emb.shape, F32)],
        in_specs=[SMEM] * (len(tables) + 1) + [VMEM] * (len(parts) + 2),
        out_specs=[VMEM, VMEM],
        input_output_aliases={first: 0, first + 1: 1},
        name="add_up",
    )(*tables, me, *parts, dens, emb)


def take(half, me, parts, row, stacked, dens):
    for n in range(8):
        lanes = slice(n * 128, n * 128 + 128)
        at = pl.multiple_of(lax.bitwise_xor(me, n) * 32, 32)
        stacked[half : half + 256, lanes] = parts[n][row, 0:256, :]
        dens[pl.ds(half + at, 32), 0:128] = parts[n][row, 256:288, :]
        dens[pl.ds(half + at, 32), 128:256] = parts[n][row, 288:320, :]


def one_dimer(steps, me, load, outs, scratch):
    stacked, weighted, dens, current, squares = scratch

    @pl.when(steps > 0)
    def _():
        load()
        fits = []
        for half in (0, 256):
            block = dens[half : half + 256, :]
            sums = []
            for n in range(4):
                lanes = slice(n * 256, n * 256 + 256)
                factor = stacked[half : half + 256, lanes]
                projected = jnp.dot(block, factor, preferred_element_type=F32)
                sums.append(jnp.sum(factor.astype(F32) * projected, axis=0, keepdims=True))
            fits.append(jnp.concatenate(sums, axis=1).astype(BF16).astype(F32))
        coeff = fits[0] + fits[1]
        for n in range(8):
            rows = slice(n * 64, n * 64 + 64)
            weighted[rows, :] = (stacked[rows, :].astype(F32) * coeff).astype(BF16)
        for n in range(4):
            rows = slice(n * 128, n * 128 + 128)
            coulomb = lax.dot_general(
                weighted[rows, :], stacked[...], (((1,), (1,)), ((), ())), preferred_element_type=F32
            )
            row_at = lax.broadcasted_iota(jnp.int32, (128, 512), 0) + n * 128
            col_at = lax.broadcasted_iota(jnp.int32, (128, 512), 1)
            own = dens[rows, :].astype(F32)
            blank = jnp.zeros((128, 256), F32)
            wide = jnp.concatenate([own, blank] if n < 2 else [blank, own], axis=1)
            eye = jnp.where(row_at == col_at, 0.5, 0.0)
            current[rows, :] = (eye + wide + COUPLE * coulomb).astype(BF16)

        def purify(index, unused):
            for n in range(4):
                rows = slice(n * 128, n * 128 + 128)
                square = jnp.dot(current[rows, :], current[...], preferred_element_type=F32)
                cube = jnp.dot(square.astype(BF16), current[...], preferred_element_type=F32)
                squares[rows, :] = (3.0 * square - 2.0 * cube).astype(BF16)
            current[...] = squares[...]
            return unused

        lax.fori_loop(0, steps, purify, 0)
        row_at = lax.broadcasted_iota(jnp.int32, (256, 256), 0)
        col_at = lax.broadcasted_iota(jnp.int32, (256, 256), 1)
        eye = jnp.where(row_at == col_at, 0.5, 0.0)
        for half in (0, 256):
            own = slice(half, half + 256)
            change = current[own, own].astype(F32) - dens[own, :].astype(F32) - eye
            dens[own, :] = change.astype(BF16)
        for n in range(8):
            at = pl.multiple_of(lax.bitwise_xor(me, n) * 32, 32)
            lanes = slice(n * 128, n * 128 + 128)
            for r in range(2):
                change = dens[pl.ds(r * 256 + at, 32), :]
                outs[n][r, 0:32, :] = change[:, 0:128]
                outs[n][r, 32:64, :] = change[:, 128:256]
                partner = jnp.broadcast_to(fits[1 - r][:, lanes], (8, 128))
                outs[n][r, 64:72, :] = partner.astype(BF16)


SCRATCH = [
    pltpu.VMEM((512, 1024), BF16),
    pltpu.VMEM((512, 1024), BF16),
    pltpu.VMEM((512, 256), BF16),
    pltpu.VMEM((512, 512), BF16),
    pltpu.VMEM((512, 512), BF16),
]


def run_dimers(kernel, count, tables, blocks, maps, parts):
    shape = jax.ShapeDtypeStruct((2 * count, 72, 128), BF16)
    specs = []
    for block, index_map in zip(blocks, maps, strict=True):
        specs += [pl.BlockSpec((block, 320, 128), index_map)] * 8
    return pl.pallas_call(
        kernel,
        out_shape=[shape] * 8,
        grid_spec=pltpu.PrefetchScalarGridSpec(
            num_scalar_prefetch=2,
            grid=(count,),
            in_specs=specs,
            out_specs=[pl.BlockSpec((2, 72, 128), lambda i, *_: (i, 0, 0))] * 8,
            scratch_shapes=SCRATCH,
        ),
        name="dimers",
        cost_estimate=pl.CostEstimate(
            flops=count * 4_000_000_000, bytes_accessed=count * 1_500_000, transcendentals=0
        ),
    )(*tables, *parts)


def kernel_1(table_ref, me_ref, *refs):
    me, i = me_ref[0], pl.program_id(0)
    first, second, outs, scratch = refs[0:8], refs[8:16], refs[16:24], refs[24:]
    stacked, dens = scratch[0], scratch[2]

    def load():
        take(0, me, first, 0, stacked, dens)
        take(256, me, second, 0, stacked, dens)

    other = table_ref[RANKED + ranked_at(me, i)]
    one_dimer(table_ref[STEP1 + other], me, load, outs, scratch)


def kernel_2(table_ref, me_ref, *refs):
    me, i = me_ref[0], pl.program_id(0)
    home, late, outs, scratch = refs[0:8], refs[8:16], refs[16:24], refs[24:]
    stacked, dens = scratch[0], scratch[2]
    split = table_ref[MODE + me] > 0

    def load():
        both_late = split & (i == 0)
        both_home = split & (i == 1)

        @pl.when(both_late)
        def _():
            take(0, me, late, 0, stacked, dens)

        @pl.when(jnp.logical_not(both_late))
        def _():
            take(0, me, home, jnp.where(split, 0, i), stacked, dens)

        @pl.when(both_home)
        def _():
            take(256, me, home, 1, stacked, dens)

        @pl.when(jnp.logical_not(both_home))
        def _():
            take(256, me, late, jnp.where(split, 1, i), stacked, dens)

    one_dimer(table_ref[STEPS + 2 * me + i], me, load, outs, scratch)


def plan_kernel(me_ref, inside_ref, a_ref, b_ref, cost_ref, flag_ref, table_ref, left_ref, to_x, to_z, n_direct, n_third, n_self):
    me = me_ref[0]

    def clear(n):
        to_z[n] = 0
        table_ref[n] = jnp.where(n < STEPS, -1, 0)

    def clear_x(n):
        to_x[n] = 0

    def clear_c(n):
        n_direct[n] = 0
        n_third[n] = 0
        n_self[n] = 0

    loop(TABLE, clear)
    loop(128, clear_x)
    loop(32, clear_c)

    def put(at, good, spare, value):
        table_ref[jnp.where(good, at, spare)] = value

    def can(o, c, extra=0):
        xo, zo, xc, zc = o >> 3, o & 7, c >> 3, c & 7
        return ((xo == xc) | (to_x[o * 4 + xc] < KX)) & ((zo == zc) | (to_z[xc * 64 + zo * 8 + zc] + extra < KZ))

    def send(o, slot, c):
        xo, zo, xc, zc = o >> 3, o & 7, c >> 3, c & 7
        at_x, at_z = o * 4 + xc, xc * 64 + zo * 8 + zc
        n_x, n_z = to_x[at_x], to_z[at_z]
        move_x, move_z = xo != xc, zo != zc
        to_x[at_x] = n_x + jnp.where(move_x, 1, 0)
        to_z[at_z] = n_z + jnp.where(move_z, 1, 0)
        in_x = (lax.bitwise_xor(xo, xc) - 1) * KX + n_x
        put(SENT + in_x, move_x & (o == me), SENT + 31, slot)
        put(RELAY + zc * KZ + n_z, move_z & (xc * 8 + zo == me), RELAY + 31, jnp.where(move_x, 32 + in_x, slot))
        return jnp.where(move_z, 32 + NX + zo * KZ + n_z, 32 + in_x)

    def visit(d):
        @pl.when(flag_ref[d] > 0)
        def _():
            a, b, cost = a_ref[d], b_ref[d], cost_ref[d]
            oa, ob, la, lb = a >> 5, b >> 5, a & 31, b & 31
            left_ref[d] = 0

            @pl.when(oa == ob)
            def _():
                q = n_self[oa]

                @pl.when(q < 8)
                def _():
                    n_self[oa] = q + 1

                    @pl.when(oa == me)
                    def _():
                        at = 2 * (7 - q)
                        table_ref[POS + 2 * at + 2] = la
                        table_ref[POS + 2 * at + 3] = lb
                        table_ref[HOME + at] = la
                        table_ref[HOME + at + 1] = lb
                        table_ref[STEPS + at + 1] = cost
                        table_ref[MODE + 7 - q] = 1

                @pl.when(q >= 8)
                def _():
                    left_ref[d] = 1

            @pl.when(oa != ob)
            def _():
                n_a, n_b = n_direct[oa], n_direct[ob]
                fit_a = ((n_a + 2) >> 1) + jnp.maximum(n_third[oa], inside_ref[oa]) <= 8
                fit_b = ((n_b + 2) >> 1) + jnp.maximum(n_third[ob], inside_ref[ob]) <= 8
                can_a, can_b = can(ob, oa) & fit_a, can(oa, ob) & fit_b
                full_a = to_z[(oa >> 3) * 64 + (ob & 7) * 8 + (oa & 7)] * 4 + n_a
                full_b = to_z[(ob >> 3) * 64 + (oa & 7) * 8 + (ob & 7)] * 4 + n_b
                use_a = can_a & (jnp.logical_not(can_b) | (full_a <= full_b))
                direct = can_a | can_b

                @pl.when(direct)
                def _():
                    c, o = jnp.where(use_a, oa, ob), jnp.where(use_a, ob, oa)
                    stay, move = jnp.where(use_a, la, lb), jnp.where(use_a, lb, la)
                    at = jnp.where(use_a, n_a, n_b)
                    n_direct[c] = at + 1
                    late = send(o, move, c)

                    @pl.when(c == me)
                    def _():
                        table_ref[POS + 2 * at] = stay
                        table_ref[POS + 2 * at + 1] = late
                        table_ref[HOME + at] = stay
                        table_ref[LATE + at] = late
                        table_ref[STEPS + at] = cost

                @pl.when(jnp.logical_not(direct))
                def _():
                    same_z = jnp.where((oa & 7) == (ob & 7), 1, 0)

                    def look(carry):
                        n, unused = carry
                        c = (d + n) & 31
                        fit = ((n_direct[c] + 1) >> 1) + jnp.maximum(n_third[c] + 1, inside_ref[c]) <= 8
                        good = fit & can(oa, c, same_z) & can(ob, c, same_z) & (c != oa) & (c != ob)
                        return n + 1, jnp.where(good, c, -1)

                    unused, c = lax.while_loop(
                        lambda carry: (carry[0] < 32) & (carry[1] < 0), look, (jnp.int32(0), jnp.int32(-1))
                    )

                    @pl.when(c < 0)
                    def _():
                        left_ref[d] = 1

                    @pl.when(c >= 0)
                    def _():
                        t = n_third[c]
                        n_third[c] = t + 1
                        late_a = send(oa, la, c)
                        late_b = send(ob, lb, c)

                        @pl.when(c == me)
                        def _():
                            at = 2 * (7 - t)
                            table_ref[POS + 2 * at] = late_a
                            table_ref[POS + 2 * at + 1] = late_b
                            table_ref[LATE + at] = late_a
                            table_ref[LATE + at + 1] = late_b
                            table_ref[STEPS + at] = cost
                            table_ref[MODE + 7 - t] = 1

    loop(a_ref.shape[0], visit)


def plan_rest(me, inside_count, a, b, cost, flag):
    s32 = jnp.int32
    return pl.pallas_call(
        plan_kernel,
        out_shape=[jax.ShapeDtypeStruct((TABLE,), s32), jax.ShapeDtypeStruct(a.shape, s32)],
        in_specs=[SMEM] * 6,
        out_specs=[SMEM] * 2,
        scratch_shapes=[pltpu.SMEM((128,), s32), pltpu.SMEM((256,), s32)] + [pltpu.SMEM((32,), s32)] * 3,
        name="plan",
        cost_estimate=pl.CostEstimate(flops=1000, bytes_accessed=30_000_000, transcendentals=0),
    )(me, inside_count, a, b, cost, flag)


def exchange(parts):
    got = [parts[0]]
    for k in range(1, 8):
        got.append(lax.ppermute(parts[k], "basis", [(i, i ^ k) for i in range(8)]))
    return got


def along_x(parts):
    return [lax.ppermute(parts[k - 1], "frag", [(i, i ^ (8 * k)) for i in range(32)]) for k in (1, 2, 3)]


def along_z(part):
    groups = [[8 * x + z for z in range(8)] for x in range(4)]
    return lax.all_to_all(part, "frag", 0, 0, tiled=True, axis_index_groups=groups)


def across(part):
    return lax.all_to_all(part, "frag", split_axis=0, concat_axis=0, tiled=True)


def after(value, *others):
    return lax.optimization_barrier((value, others))[0]


def shards(density, aux_factor, pairs, slot_of, costs):
    n_frag = lax.axis_size("frag")
    n_basis = lax.axis_size("basis")
    me_frag = lax.axis_index("frag").astype(jnp.int32)
    me_basis = lax.axis_index("basis").astype(jnp.int32)
    dimers = pairs.shape[0] * n_frag * n_basis

    lookup = pairs[:, :, None] == jnp.arange(slot_of.shape[0], dtype=jnp.int32)
    slots = jnp.sum(jnp.where(lookup, slot_of, 0), axis=2)
    mine = jnp.concatenate([slots[:, 0], slots[:, 1], costs, jnp.zeros(116, jnp.int32)])
    column = lax.all_to_all(
        jnp.broadcast_to(mine, (n_basis, 1, 128)), "basis", split_axis=0, concat_axis=0, tiled=True
    )
    column = column[:, 0, 0:12].reshape(n_basis, 3, 4).transpose(1, 0, 2).reshape(96)
    column = jnp.concatenate([column, jnp.zeros(32, jnp.int32)])
    every = across(jnp.broadcast_to(column, (n_frag, 1, 128)))
    a = every[:, 0, 0:32].reshape(dimers)
    b = every[:, 0, 32:64].reshape(dimers)
    cost = every[:, 0, 64:96].reshape(dimers)

    order = jnp.arange(dimers, dtype=jnp.int32)
    columns = jnp.arange(n_frag, dtype=jnp.int32)
    own_a, own_b = a // 32, b // 32
    low, high = jnp.minimum(own_a, own_b), jnp.maximum(own_a, own_b)
    pair_id = low * 32 + high
    inside = own_a == own_b
    mine_a = (own_a == me_frag) & jnp.logical_not(inside)
    mine_b = (own_b == me_frag) & jnp.logical_not(inside)
    other = jnp.where(mine_a, own_b, jnp.where(mine_b, own_a, -1))
    local = jnp.where(mine_a, a, b) & 31
    key = order * 256 + local * 8 + cost
    me_f, me_b = me_frag.reshape(1), me_basis.reshape(1)
    keep_first = (me_frag < columns) == ((me_frag + columns) % 2 == 0)
    home = (aux_factor, density)

    def one_round(carry):
        unused_n, rest, dens, emb = carry
        open_dimer = rest > 0
        match = (other[None, :] == columns[:, None]) & open_dimer[None, :]
        keyed = jnp.where(match, key[None, :], BIG)
        key_0 = jnp.min(keyed, axis=1)
        key_1 = jnp.min(jnp.where(keyed > key_0[:, None], keyed, BIG), axis=1)
        here = jnp.where(keep_first, key_0, key_1)
        there = jnp.where(keep_first, key_1, key_0)
        send_1 = jnp.where(there < BIG, (there >> 3) & 31, -1)
        base_1 = jnp.where(here < BIG, (here >> 3) & 31, -1)
        steps_1 = jnp.where(here < BIG, here & 7, 0)

        (out_1,) = pack((send_1,), me_b, lambda t, me, n, row: t[0][row], 1, 32, home, [])
        in_1 = across(out_1)

        weight = steps_1 * 64 - columns
        rank = jnp.sum((weight[None, :] > weight[:, None]).astype(jnp.int32), axis=1)
        ranked = jnp.sum(jnp.where(rank[None, :] == columns[:, None], columns[None, :], 0), axis=1)
        table_1 = jnp.concatenate([send_1, base_1, steps_1, ranked])

        earlier = (pair_id[:, None] == pair_id[None, :]) & (order[None, :] < order[:, None])
        earlier = jnp.sum(jnp.where(earlier & open_dimer[None, :], 1, 0), axis=1)
        flagged = open_dimer & ((earlier >= 2) | inside)
        flag = jnp.where(flagged, 1, 0)
        inside_here = (own_a[None, :] == columns[:, None]) & (inside & open_dimer)[None, :]
        inside_count = jnp.sum(jnp.where(inside_here, 1, 0), axis=1)
        table_2, left = plan_rest(me_f, inside_count, a, b, cost, flag)
        left = jnp.where(flagged, left, 0)
        tables = (table_1, table_2)

        def served(t, me, n, row):
            return t[0][RANKED + ranked_at(lax.bitwise_xor(me, n), row)]

        home_1 = exchange(
            pack(tables[:1], me_b, lambda t, me, n, row: t[0][BASE + served(t, me, n, row)], 8, 4, home, [])
        )
        in_x = along_x(pack(tables, me_b, lambda t, me, n, row: t[1][SENT + n * KX + row], 3, KX, home, []))
        (out_2,) = pack(tables, me_b, lambda t, me, n, row: t[1][RELAY + row], 1, NZ, home, in_x)
        in_z = along_z(after(out_2, in_1))
        home_2 = exchange(
            pack(
                tables, me_b, lambda t, me, n, row: t[1][HOME + 2 * lax.bitwise_xor(me, n) + row], 8, 2, home, []
            )
        )

        away_1 = exchange(pack(tables, me_b, served, 8, 4, (), [in_1]))
        one = lambda i, *_: (i, 0, 0)
        done_1 = exchange(
            run_dimers(kernel_1, 4, (table_1, me_b), (1, 1), (one, one), [*home_1, *away_1])
        )

        late_2 = exchange(
            pack(
                tables,
                me_b,
                lambda t, me, n, row: t[1][LATE + 2 * lax.bitwise_xor(me, n) + row] - 32,
                8,
                2,
                (),
                [*in_x, after(in_z, away_1)],
            )
        )
        whole = lambda i, *_: (0, 0, 0)
        done_2 = exchange(
            run_dimers(kernel_2, 2, (table_2, me_b), (2, 2), (whole, whole), [*home_2, *late_2])
        )

        def back_to(k):
            return lambda t, me, row: jnp.where(row % 2 == 1, served(t, me, k, row // 2), -1)

        (ret_1,) = place(tables, me_b, done_1, [back_to(k) for k in range(8)], [32])
        back_1 = across(ret_1)

        def place_2(t, me, k, row):
            at = 2 * lax.bitwise_xor(me, k) + row // 2
            return jnp.where(t[1][STEPS + at] > 0, t[1][POS + 2 * at + row % 2], -1)

        def back_z(k):
            return lambda t, me, row: place_2(t, me, k, row) - 32 - NX

        def back_x(k):
            return lambda t, me, row: place_2(t, me, k, row) - 32

        (ret_z,) = place(tables, me_b, done_2, [back_z(k) for k in range(8)], [NZ])
        rest_z = along_z(after(ret_z, back_1))
        ret_x = place(
            tables,
            me_b,
            [*done_2, rest_z],
            [back_x(k) for k in range(8)] + [lambda t, me, row: t[1][RELAY + row] - 32],
            [KX] * 3,
        )
        rest_x = along_x(ret_x)

        def stay_1(k):
            return lambda t, me, row: jnp.where(row % 2 == 0, t[0][BASE + served(t, me, k, row // 2)], -1)

        def stay_2(k):
            return lambda t, me, row: place_2(t, me, k, row)

        def from_x(k):
            return lambda t, me, row: t[1][SENT + k * KX + row]

        finds = (
            [stay_1(k) for k in range(8)]
            + [stay_2(k) for k in range(8)]
            + [lambda t, me, row: t[0][OUT + row], lambda t, me, row: t[1][RELAY + row]]
            + [from_x(k) for k in range(3)]
        )
        dens, emb = add_up(tables, me_b, [*done_1, *done_2, back_1, rest_z, *rest_x], finds, dens, emb)
        return jnp.sum(left), left, dens, emb

    start = (
        jnp.int32(dimers),
        jnp.ones(dimers, jnp.int32),
        jnp.zeros(density.shape, F32),
        jnp.zeros((density.shape[0], aux_factor.shape[2]), F32),
    )
    unused_n, unused_rest, dens, emb = lax.while_loop(lambda carry: carry[0] > 0, one_round, start)
    return dens, emb


def solution(mesh):
    return jax.shard_map(
        shards,
        mesh=mesh,
        in_specs=(
            P("frag", "basis", None),
            P("frag", None, "basis"),
            P(("frag", "basis"), None),
            P(),
            P(("frag", "basis")),
        ),
        out_specs=(P("frag", "basis", None), P("frag", "basis")),
        check_vma=False,
    )
```

time: 308 us -> 329 us (1.068)
  blocking collectives: 0 us -> 30.9 us
  waiting for transfers between devices: 110 us -> 79.2 us
  Pallas kernels: 80.2 us -> 107 us
  local copies, waits for them, and re-layouts: 15.5 us -> 6.36 us
    all_to_all x6 -> x4, waiting for transfers between devices: 49.5 us -> 15.4 us  [the longest x3 15.4 us: across(): return lax.all_to_all(part, 'frag', split_axis=0, concat_axis=0, tiled=True)]
    all_to_all x0 -> x2, blocking collectives: none -> 30.9 us  [the longest x1 21.4 us: along_z(): lax.all_to_all(part, 'frag', 0, 0, tiled=True, axis_index_groups=groups)]
    pallas_call x10 -> x13, Pallas kernels: 75.8 us -> 101 us  [the longest x1 37.2 us: plan_rest(): pl.pallas_call(plan_kernel, out_shape=[jax.ShapeDtypeStruct((TABLE,), s32...]
    all_to_all x6 -> x4, starting transfers between devices: 53.3 us -> 35.3 us  [the longest x3 29.3 us: across(): return lax.all_to_all(part, 'frag', split_axis=0, concat_axis=0, tiled=True)]
    ppermute x0 -> x6, starting transfers between devices: none -> 11.5 us  [along_x(): lax.ppermute(parts[k - 1], 'frag', [(i, i ^ 8 * k) for i in range(32)])]
    ppermute x0 -> x6, waiting for transfers between devices: none -> 9.8 us  [along_x(): lax.ppermute(parts[k - 1], 'frag', [(i, i ^ 8 * k) for i in range(32)])]
    ppermute x35 -> x42, starting transfers between devices: 37.3 us -> 45.9 us  [exchange(): got.append(lax.ppermute(parts[k], 'basis', [(i, i ^ k) for i in range(8)]))]
    ppermute x35 -> x42, waiting for transfers between devices: 60.1 us -> 54 us  [exchange(): got.append(lax.ppermute(parts[k], 'basis', [(i, i ^ k) for i in range(8)]))]
  transfers between devices with their start and end apart: 41 -> 52, of which waited for: 22 -> 23; matrix products, arithmetic and copies ran while one was open for 5% -> 1% of each run, Pallas kernels for 24% -> 29%
where the time goes in v3:
time: 329 us; the launch traced here: 326 us
  Pallas kernels  107 us (33%)
  starting transfers between devices  92.7 us (28%)
  waiting for transfers between devices  79.2 us (24%)
  blocking collectives  30.9 us (9%)
  local copies, waits for them, and re-layouts  6.36 us (2%)
  other arithmetic  6.07 us (2%)
    ppermute x42, waiting for transfers between devices, exchange(): got.append(lax.ppermute(parts[k], 'basis', [(i, i ^ k) for i in range(8)]))  54 us
    ppermute x42, starting transfers between devices, exchange(): got.append(lax.ppermute(parts[k], 'basis', [(i, i ^ k) for i in range(8)]))  45.9 us
    pallas_call x1, Pallas kernels, plan_rest(): pl.pallas_call(plan_kernel, out_shape=[jax.ShapeDtypeStruct((TABLE,), s32...  37.2 us
    pallas_call x2, Pallas kernels, run_dimers(): pl.pallas_call(kernel, out_shape=[shape] * 8, grid_spec=pltpu.PrefetchSca...  31.5 us
    all_to_all x3, starting transfers between devices, across(): return lax.all_to_all(part, 'frag', split_axis=0, concat_axis=0, tiled=True)  29.3 us
    pallas_call x7, Pallas kernels, pack(): pl.pallas_call(kernel, out_shape=[jax.ShapeDtypeStruct((rows, 320, 128),...  21.9 us
    all_to_all x1, blocking collectives, along_z(): lax.all_to_all(part, 'frag', 0, 0, tiled=True, axis_index_groups=groups)  21.4 us
    all_to_all x3, waiting for transfers between devices, across(): return lax.all_to_all(part, 'frag', split_axis=0, concat_axis=0, tiled=True)  15.4 us
  transfers between devices with their start and end apart: 52, of which 23 were waited for; matrix products, arithmetic and copies ran while one was open for 1% of the time, Pallas kernels for 29%

profile of v3, /device:TPU:32, one launch (start us, length us, event | category | flops | bytes accessed | tf_op | source)
XLA Modules:
  0.0 325.5 jit_solution(15267237695363517145)
XLA Ops:
  2.3 9.6 %all_to_all.34 = s32[8,1,128]{2,1,0:T(1,128)S(1)} all-to-all(s32[8,1,128]{2,1,0:T(1,128)S(1)} %broadcast_in_dim.112), channel_id=1, replica_groups=mesh['frag'=32,'basis'=8] {'basis'}, dimensions={0} | all-to-all | bytes 8192 | tf_op jit(solution)/shard_map/all_to_all | solution.py:456
  12.8 11.2 %all-to-all-start.5 = ((s32[32,1,128]{2,1,0:T(1,128)}), s32[32,1,128]{2,1,0:T(1,128)S(1)}, u32[]{:S(2)}, u32[]{:S(2)}) async-start(s32[32,1,128]{2,1,0:T(1,128)} %broadcast_in_dim.113), calls=%async_computation.5 | async-start | bytes 32768 | tf_op jit(solution)/shard_map/all_to_all | solution.py:439
  24.0 8.6 %all-to-all-done.5 = s32[32,1,128]{2,1,0:T(1,128)S(1)} async-done(((s32[32,1,128]{2,1,0:T(1,128)}), s32[32,1,128]{2,1,0:T(1,128)S(1)}, u32[]{:S(2)}, u32[]{:S(2)}) %all-to-all-start.5) | async-done | bytes 16416 | tf_op jit(solution)/shard_map/all_to_all | solution.py:439
  34.1 290.4 %while.15 = (s32[]{:T(128)}, s32[1024]{0:T(1024)S(1)}, f32[32,32,256]{2,1,0:T(8,128)}, f32[32,128]{1,0:T(8,128)S(1)}, s32[1024]{0:T(1024)S(1)}, /*index=5*/pred[...) while((s32[]{:T(128)}, s32[1024]{0:T(1024)S(1)}, ...), condition=%region_9.10_spmd.clone.clone, body=%region_1.9_spmd.clone.clone | while | flops 24006766592 | bytes 136043888 | solution.py:600
  35.3 3.8 %pack.8 = bf16[32,320,128]{2,1,0:T(8,128)(2,1)} custom-call(s32[32]{0:T(128)} %get-tuple-element.423.refs_0_, s32[1]{0:T(128)} %get-tuple-element.495.refs_1_.refs_2_.me_ref, bf16[32,256,128]{2,1,0:T(8,128)(2,1)} %get-tuple-element.496.refs_2_.refs_3_, bf16[32,32,256]{2,1,0:T(8,128)(2,1)} %get-tuple-element.497.refs_3_.refs_4_), custom_call_target="tpu_custom_call" | custom-call | tf_op jit(solution)/shard_map/while/body/pack/pallas_call | solution.py:67
  39.1 6.1 %all-to-all-start = ((bf16[32,320,128]{2,1,0:T(8,128)(2,1)}), bf16[32,320,128]{2,1,0:T(8,128)(2,1)}, u32[]{:S(2)}, u32[]{:S(2)}) async-start(bf16[32,320,128]{2,1,0:T(8,128)(2,1)} %pack.8), calls=%async_computation | async-start | bytes 5242880 | tf_op jit(solution)/shard_map/while/body/all_to_all | solution.py:439
  46.1 3.1 pack.7
  51.7 37.2 %plan.1 = (s32[256]{0:T(256)}, s32[1024]{0:T(1024)}) custom-call(s32[1]{0:T(128)} %get-tuple-element.489.me_ref, s32[32]{0:T(128)} %select_reduce_fusion.2.inside_ref, s32[1024]{0:T(1024)S(1)} %get-tuple-element.490.a_ref, s32[1024]{0:T(1024)S(1)} %get-tuple-element.491.b_ref, s32[1024]{0:T(1024)S(1)} %get-tuple-element.492.cost_ref, ...), custom_call_target="tpu_custom_call" | custom-call | flops 1000 | bytes 30000000 | tf_op jit(solution)/shard_map/while/body/plan/pallas_call | solution.py:411
  88.9 2.2 pack.11
  92.6 2.8 collective-permute-start.29
  98.0 6.8 %all-to-all-done.refs_3_ = bf16[32,320,128]{2,1,0:T(8,128)(2,1)} async-done(((bf16[32,320,128]{2,1,0:T(8,128)(2,1)}), bf16[32,320,128]{2,1,0:T(8,128)(2,1)}, u32[]{:S(2)}, u32[]{:S(2)}) %all-to-all-start) | async-done | bytes 2621472 | tf_op jit(solution)/shard_map/while/body/all_to_all | solution.py:439
  104.8 4.1 %pack.9 = (bf16[4,320,128]{2,1,0:T(8,128)(2,1)}, bf16[4,320,128]{2,1,0:T(8,128)(2,1)}, bf16[4,320,128]{2,1,0:T(8,128)(2,1)}, bf16[4,320,128]{2,1,0:T(8,128)(2,1)...) custom-call(s32[128]{0:T(128)} %pad_add_fusion.refs_0_.table_ref, ...), custom_call_target="tpu_custom_call" | custom-call | tf_op jit(solution)/shard_map/while/body/pack/pallas_call | solution.py:67
  108.9 4.9 %collective-permute-done.3.refs_4_ = bf16[4,320,128]{2,1,0:T(8,128)(2,1)} collective-permute-done((bf16[4,320,128]{2,1,0:T(8,128)(2,1)}, bf16[4,320,128]{2,1,0:T(8,128)(2,1)}, u32[]{:S(2)}, u32[]{:S(2)}) %collective-permute-start.3) | collective-permute-done | bytes 327712 | tf_op jit(solution)/shard_map/while/body/ppermute | solution.py:425
  113.8 2.1 collective-permute-start.5
  116.4 4.7 %collective-permute-done.29.refs_6_.refs_4_ = bf16[6,320,128]{2,1,0:T(8,128)(2,1)} collective-permute-done((bf16[6,320,128]{2,1,0:T(8,128)(2,1)}, bf16[6,320,128]{2,1,0:T(8,128)(2,1)}, u32[]{:S(2)}, u32[]{:S(2)}) %collective-permute-start.29) | collective-permute-done | bytes 491552 | tf_op jit(solution)/shard_map/while/body/ppermute | solution.py:430
  123.7 3.0 pack.12
  126.6 6.1 %all-to-all-start.1 = ((bf16[16,320,128]{2,1,0:T(8,128)(2,1)}), bf16[16,320,128]{2,1,0:T(8,128)(2,1)}, u32[]{:S(2)}, u32[]{:S(2)}) async-start(bf16[16,320,128]{2,1,0:T(8,128)(2,1)} %pack.12), calls=%async_computation.1 | async-start | bytes 2621440 | tf_op jit(solution)/shard_map/while/body/all_to_all | solution.py:435
  133.9 8.0 %collective-permute-done.5.refs_6_ = bf16[4,320,128]{2,1,0:T(8,128)(2,1)} collective-permute-done((bf16[4,320,128]{2,1,0:T(8,128)(2,1)}, bf16[4,320,128]{2,1,0:T(8,128)(2,1)}, u32[]{:S(2)}, u32[]{:S(2)}) %collective-permute-start.5) | collective-permute-done | bytes 327712 | tf_op jit(solution)/shard_map/while/body/ppermute | solution.py:425
  143.6 5.2 %collective-permute-done.6.refs_7_ = bf16[4,320,128]{2,1,0:T(8,128)(2,1)} collective-permute-done((bf16[4,320,128]{2,1,0:T(8,128)(2,1)}, bf16[4,320,128]{2,1,0:T(8,128)(2,1)}, u32[]{:S(2)}, u32[]{:S(2)}) %collective-permute-start.6) | collective-permute-done | bytes 327712 | tf_op jit(solution)/shard_map/while/body/ppermute | solution.py:425
  150.6 2.1 pack.10
  152.8 3.2 collective-permute-done.12.refs_14_
  156.5 6.3 %collective-permute-done.13.refs_15_ = bf16[4,320,128]{2,1,0:T(8,128)(2,1)} collective-permute-done((bf16[4,320,128]{2,1,0:T(8,128)(2,1)}, bf16[4,320,128]{2,1,0:T(8,128)(2,1)}, u32[]{:S(2)}, u32[]{:S(2)}) %collective-permute-start.13) | collective-permute-done | bytes 327712 | tf_op jit(solution)/shard_map/while/body/ppermute | solution.py:425
  164.4 2.1 collective-permute-start.24
  166.5 17.6 %dimers.2 = (bf16[8,72,128]{2,1,0:T(8,128)(2,1)}, bf16[8,72,128]{2,1,0:T(8,128)(2,1)}, bf16[8,72,128]{2,1,0:T(8,128)(2,1)}, bf16[8,72,128]{2,1,0:T(8,128)(2,1)},...) custom-call(s32[128]{0:T(128)} %pad_add_fusion.refs_0_.table_ref, ...), custom_call_target="tpu_custom_call" | custom-call | flops 16000000000 | bytes 6000000 | tf_op jit(solution)/shard_map/while/body/dimers/pallas_call | solution.py:217
  186.5 2.8 collective-permute-start.18
  192.3 3.6 %pack.13 = (bf16[2,320,128]{2,1,0:T(8,128)(2,1)}, bf16[2,320,128]{2,1,0:T(8,128)(2,1)}, bf16[2,320,128]{2,1,0:T(8,128)(2,1)}, bf16[2,320,128]{2,1,0:T(8,128)(2,1...) custom-call(s32[128]{0:T(128)} %pad_add_fusion.refs_0_.table_ref, ...), custom_call_target="tpu_custom_call" | custom-call | tf_op jit(solution)/shard_map/while/body/pack/pallas_call | solution.py:67
  196.7 3.6 %collective-permute-start.26 = (bf16[2,320,128]{2,1,0:T(8,128)(2,1)S(1)}, bf16[2,320,128]{2,1,0:T(8,128)(2,1)S(1)}, u32[]{:S(2)}, u32[]{:S(2)}) collective-permute-start(bf16[2,320,128]{2,1,0:T(8,128)(2,1)S(1)} %copy-done.32), channel_id=1, source_target_pairs={{0,6},{1,7},{2,4},{3,5},{4,2},{5,3},{6,0},{7,1},{8,14},{9,15},{10,... | collective-permute-start | bytes 491528 | tf_op jit(solution)/shard_map/while/body/ppermute | solution.py:425
  200.3 2.8 collective-permute-start.27
  203.2 2.4 collective-permute-done.19.refs_9_
  205.6 3.0 collective-permute-done.20.refs_10_
  209.3 3.9 %place.3 = bf16[32,72,128]{2,1,0:T(8,128)(2,1)} custom-call(s32[128]{0:T(128)} %pad_add_fusion.refs_0_.table_ref, s32[256]{0:T(256)} %get-tuple-element.292.refs_1_.table_ref, s32[1]{0:T(128)} %get-tuple-element.495.refs_1_.refs_2_.me_ref, bf16[8,72,128]{2,1,0:T(8,128)(2,1)} %get-tuple-element.312.refs_3_, bf16[8,72,128]{2,1,0:T(8,128)(2,1)} %copy-done.13, ...), custom_call_target="tpu_custom_call" | custom-call | tf_op jit(solution)/shard_map/while/body/place/pallas_call | solution.py:94
  213.3 12.0 %all-to-all-start.2 = ((bf16[32,72,128]{2,1,0:T(8,128)(2,1)}), bf16[32,72,128]{2,1,0:T(8,128)(2,1)S(1)}, u32[]{:S(2)}, u32[]{:S(2)}) async-start(bf16[32,72,128]{2,1,0:T(8,128)(2,1)} %place.3), calls=%async_computation.2 | async-start | bytes 1179648 | tf_op jit(solution)/shard_map/while/body/all_to_all | solution.py:439
  233.0 3.9 %collective-permute-done.34.refs_12_ = bf16[2,320,128]{2,1,0:T(8,128)(2,1)S(1)} collective-permute-done((bf16[2,320,128]{2,1,0:T(8,128)(2,1)}, bf16[2,320,128]{2,1,0:T(8,128)(2,1)S(1)}, u32[]{:S(2)}, u32[]{:S(2)}) %collective-permute-start.34) | collective-permute-done | bytes 163872 | tf_op jit(solution)/shard_map/while/body/ppermute | solution.py:425
  236.9 3.5 %collective-permute-done.35.refs_13_ = bf16[2,320,128]{2,1,0:T(8,128)(2,1)S(1)} collective-permute-done((bf16[2,320,128]{2,1,0:T(8,128)(2,1)}, bf16[2,320,128]{2,1,0:T(8,128)(2,1)S(1)}, u32[]{:S(2)}, u32[]{:S(2)}) %collective-permute-start.35) | collective-permute-done | bytes 163872 | tf_op jit(solution)/shard_map/while/body/ppermute | solution.py:425
  240.4 3.5 %collective-permute-done.36.refs_14_ = bf16[2,320,128]{2,1,0:T(8,128)(2,1)S(1)} collective-permute-done((bf16[2,320,128]{2,1,0:T(8,128)(2,1)}, bf16[2,320,128]{2,1,0:T(8,128)(2,1)S(1)}, u32[]{:S(2)}, u32[]{:S(2)}) %collective-permute-start.36) | collective-permute-done | bytes 163872 | tf_op jit(solution)/shard_map/while/body/ppermute | solution.py:425
  243.9 3.4 %collective-permute-done.37.refs_15_ = bf16[2,320,128]{2,1,0:T(8,128)(2,1)S(1)} collective-permute-done((bf16[2,320,128]{2,1,0:T(8,128)(2,1)S(1)}, bf16[2,320,128]{2,1,0:T(8,128)(2,1)S(1)}, u32[]{:S(2)}, u32[]{:S(2)}) %collective-permute-start.37) | collective-permute-done | bytes 163872 | tf_op jit(solution)/shard_map/while/body/ppermute | solution.py:425
  247.9 13.9 %dimers.3 = (bf16[4,72,128]{2,1,0:T(8,128)(2,1)}, bf16[4,72,128]{2,1,0:T(8,128)(2,1)}, bf16[4,72,128]{2,1,0:T(8,128)(2,1)}, bf16[4,72,128]{2,1,0:T(8,128)(2,1)},...) custom-call(s32[256]{0:T(256)} %get-tuple-element.292.refs_1_.table_, ...), custom_call_target="tpu_custom_call" | custom-call | flops 8000000000 | bytes 3000000 | tf_op jit(solution)/shard_map/while/body/dimers/pallas_call | solution.py:217
  263.9 3.2 collective-permute-start.42
  267.4 2.6 collective-permute-start.44
  271.1 2.5 collective-permute-done.43.refs_9_.refs_17_
  275.1 2.6 place.4
  277.7 21.4 %all_to_all.35.refs_11_.refs_20_ = bf16[16,72,128]{2,1,0:T(8,128)(2,1)} all-to-all(bf16[16,72,128]{2,1,0:T(8,128)(2,1)} %place.4), channel_id=1, replica_groups={{0,8,16,24,32,40,48,56},{64,72,80,88,96,104,112,120},{128,136,144,152,1..., dimensions={0} | all-to-all | bytes 589824 | tf_op jit(solution)/shard_map/while/body/all_to_all | solution.py:435
  299.1 3.5 %place.5 = (bf16[6,72,128]{2,1,0:T(8,128)(2,1)}, bf16[6,72,128]{2,1,0:T(8,128)(2,1)}, bf16[6,72,128]{2,1,0:T(8,128)(2,1)}) custom-call(s32[128]{0:T(128)} %pad_add_fusion.refs_0_.table_ref, s32[256]{0:T(256)} %get-tuple-element.292.refs_1_.table_ref, s32[1]{0:T(128)} %get-tuple-element.495.refs_1_.refs_2_.me_ref, ...), custom_call_target="tpu_custom_call" | custom-call | tf_op jit(solution)/shard_map/while/body/place/pallas_call | solution.py:94
  302.6 2.3 collective-permute-start.45
  304.9 4.0 %collective-permute-start.46 = (bf16[6,72,128]{2,1,0:T(8,128)(2,1)}, bf16[6,72,128]{2,1,0:T(8,128)(2,1)S(1)}, u32[]{:S(2)}, u32[]{:S(2)}) collective-permute-start(bf16[6,72,128]{2,1,0:T(8,128)(2,1)} %get-tuple-element.351), channel_id=1, source_target_pairs={{0,128},{8,136},{16,144},{24,152},{32,160},{40,168},{48,176},{56,1... | collective-permute-start | bytes 331784 | tf_op jit(solution)/shard_map/while/body/ppermute | solution.py:430
  310.1 2.9 collective-permute-done.46.refs_22_
  313.0 2.1 collective-permute-done.47.refs_23_
  315.8 5.9 %add_up.1 = (f32[32,32,256]{2,1,0:T(8,128)S(1)}, f32[32,128]{1,0:T(8,128)S(1)}) custom-call(s32[128]{0:T(128)} %pad_add_fusion.refs_0_.table_ref, s32[256]{0:T(256)} %get-tuple-element.292.refs_1_.table_ref, s32[1]{0:T(128)} %get-tuple-element.495.refs_1_.refs_2_.me_ref, ...), custom_call_target="tpu_custom_call", output_to_operand_aliasing={{0}: (24, {}), {1}: (25, {})} | custom-call | tf_op jit(solution)/shard_map/while/body/add_up/pallas_call | solution.py:123
  (188 shorter events, 45.8 us)
Async XLA Ops:
  12.8 19.8 %all-to-all-start.5 = ((s32[32,1,128]{2,1,0:T(1,128)}), s32[32,1,128]{2,1,0:T(1,128)S(1)}, u32[]{:S(2)}, u32[]{:S(2)}) async-start(s32[32,1,128]{2,1,0:T(1,128)} %broadcast_in_dim.113), calls=%async_computation.5 | async-start | bytes 32768 | tf_op jit(solution)/shard_map/all_to_all | solution.py:439
  39.1 65.7 %all-to-all-start = ((bf16[32,320,128]{2,1,0:T(8,128)(2,1)}), bf16[32,320,128]{2,1,0:T(8,128)(2,1)}, u32[]{:S(2)}, u32[]{:S(2)}) async-start(bf16[32,320,128]{2,1,0:T(8,128)(2,1)} %pack.8), calls=%async_computation | async-start | bytes 5242880 | tf_op jit(solution)/shard_map/while/body/all_to_all | solution.py:439
  49.2 46.7 %collective-permute-start = (bf16[4,320,128]{2,1,0:T(8,128)(2,1)}, bf16[4,320,128]{2,1,0:T(8,128)(2,1)}, u32[]{:S(2)}, u32[]{:S(2)}) collective-permute-start(bf16[4,320,128]{2,1,0:T(8,128)(2,1)} %get-tuple-element.297), channel_id=1, source_target_pairs={{0,1},{1,0},{2,3},{3,2},{4,5},{5,4},{6,7},{7,6},{8,9},{9,8},{10,11... | collective-permute-start | bytes 983048 | tf_op jit(solution)/shard_map/while/body/ppermute | solution.py:425
  49.2 47.1 %collective-permute-start.1 = (bf16[4,320,128]{2,1,0:T(8,128)(2,1)}, bf16[4,320,128]{2,1,0:T(8,128)(2,1)}, u32[]{:S(2)}, u32[]{:S(2)}) collective-permute-start(bf16[4,320,128]{2,1,0:T(8,128)(2,1)} %get-tuple-element.298), channel_id=1, source_target_pairs={{0,2},{1,3},{2,0},{3,1},{4,6},{5,7},{6,4},{7,5},{8,10},{9,11},{10,... | collective-permute-start | bytes 983048 | tf_op jit(solution)/shard_map/while/body/ppermute | solution.py:425
  91.1 24.7 %collective-permute-start.28 = (bf16[6,320,128]{2,1,0:T(8,128)(2,1)}, bf16[6,320,128]{2,1,0:T(8,128)(2,1)S(1)}, u32[]{:S(2)}, u32[]{:S(2)}) collective-permute-start(bf16[6,320,128]{2,1,0:T(8,128)(2,1)} %get-tuple-element.328), channel_id=1, source_target_pairs={{0,64},{8,72},{16,80},{24,88},{32,96},{40,104},{48,112},{56,120},{... | collective-permute-start | bytes 1474568 | tf_op jit(solution)/shard_map/while/body/ppermute | solution.py:430
  92.6 28.5 %collective-permute-start.29 = (bf16[6,320,128]{2,1,0:T(8,128)(2,1)}, bf16[6,320,128]{2,1,0:T(8,128)(2,1)}, u32[]{:S(2)}, u32[]{:S(2)}) collective-permute-start(bf16[6,320,128]{2,1,0:T(8,128)(2,1)} %get-tuple-element.329), channel_id=1, source_target_pairs={{0,128},{8,136},{16,144},{24,152},{32,160},{40,168},{48,176},{56,1... | collective-permute-start | bytes 1474568 | tf_op jit(solution)/shard_map/while/body/ppermute | solution.py:430
  95.4 27.6 %collective-permute-start.30 = (bf16[6,320,128]{2,1,0:T(8,128)(2,1)}, bf16[6,320,128]{2,1,0:T(8,128)(2,1)}, u32[]{:S(2)}, u32[]{:S(2)}) collective-permute-start(bf16[6,320,128]{2,1,0:T(8,128)(2,1)} %get-tuple-element.330), channel_id=1, source_target_pairs={{0,192},{8,200},{16,208},{24,216},{32,224},{40,232},{48,240},{56,2... | collective-permute-start | bytes 1474568 | tf_op jit(solution)/shard_map/while/body/ppermute | solution.py:430
  95.8 13.1 %collective-permute-start.2 = (bf16[4,320,128]{2,1,0:T(8,128)(2,1)}, bf16[4,320,128]{2,1,0:T(8,128)(2,1)}, u32[]{:S(2)}, u32[]{:S(2)}) collective-permute-start(bf16[4,320,128]{2,1,0:T(8,128)(2,1)} %get-tuple-element.299), channel_id=1, source_target_pairs={{0,3},{1,2},{2,1},{3,0},{4,7},{5,6},{6,5},{7,4},{8,11},{9,10},{10,... | collective-permute-start | bytes 983048 | tf_op jit(solution)/shard_map/while/body/ppermute | solution.py:425
  96.3 17.5 %collective-permute-start.3 = (bf16[4,320,128]{2,1,0:T(8,128)(2,1)}, bf16[4,320,128]{2,1,0:T(8,128)(2,1)}, u32[]{:S(2)}, u32[]{:S(2)}) collective-permute-start(bf16[4,320,128]{2,1,0:T(8,128)(2,1)} %get-tuple-element.300), channel_id=1, source_target_pairs={{0,4},{1,5},{2,6},{3,7},{4,0},{5,1},{6,2},{7,3},{8,12},{9,13},{10,... | collective-permute-start | bytes 983048 | tf_op jit(solution)/shard_map/while/body/ppermute | solution.py:425
  108.9 23.8 %collective-permute-start.4 = (bf16[4,320,128]{2,1,0:T(8,128)(2,1)}, bf16[4,320,128]{2,1,0:T(8,128)(2,1)}, u32[]{:S(2)}, u32[]{:S(2)}) collective-permute-start(bf16[4,320,128]{2,1,0:T(8,128)(2,1)} %get-tuple-element.301), channel_id=1, source_target_pairs={{0,5},{1,4},{2,7},{3,6},{4,1},{5,0},{6,3},{7,2},{8,13},{9,12},{10,... | collective-permute-start | bytes 983048 | tf_op jit(solution)/shard_map/while/body/ppermute | solution.py:425
  113.8 28.1 %collective-permute-start.5 = (bf16[4,320,128]{2,1,0:T(8,128)(2,1)}, bf16[4,320,128]{2,1,0:T(8,128)(2,1)}, u32[]{:S(2)}, u32[]{:S(2)}) collective-permute-start(bf16[4,320,128]{2,1,0:T(8,128)(2,1)} %get-tuple-element.302), channel_id=1, source_target_pairs={{0,6},{1,7},{2,4},{3,5},{4,2},{5,3},{6,0},{7,1},{8,14},{9,15},{10,... | collective-permute-start | bytes 983048 | tf_op jit(solution)/shard_map/while/body/ppermute | solution.py:425
  115.8 32.9 %collective-permute-start.6 = (bf16[4,320,128]{2,1,0:T(8,128)(2,1)}, bf16[4,320,128]{2,1,0:T(8,128)(2,1)}, u32[]{:S(2)}, u32[]{:S(2)}) collective-permute-start(bf16[4,320,128]{2,1,0:T(8,128)(2,1)} %get-tuple-element.303), channel_id=1, source_target_pairs={{0,7},{1,6},{2,5},{3,4},{4,3},{5,2},{6,1},{7,0},{8,15},{9,14},{10,... | collective-permute-start | bytes 983048 | tf_op jit(solution)/shard_map/while/body/ppermute | solution.py:425
  121.1 28.0 %collective-permute-start.10 = (bf16[4,320,128]{2,1,0:T(8,128)(2,1)}, bf16[4,320,128]{2,1,0:T(8,128)(2,1)}, u32[]{:S(2)}, u32[]{:S(2)}) collective-permute-start(bf16[4,320,128]{2,1,0:T(8,128)(2,1)} %get-tuple-element.308), channel_id=1, source_target_pairs={{0,4},{1,5},{2,6},{3,7},{4,0},{5,1},{6,2},{7,3},{8,12},{9,13},{10,... | collective-permute-start | bytes 983048 | tf_op jit(solution)/shard_map/while/body/ppermute | solution.py:425
  123.0 26.4 %collective-permute-start.11 = (bf16[4,320,128]{2,1,0:T(8,128)(2,1)}, bf16[4,320,128]{2,1,0:T(8,128)(2,1)}, u32[]{:S(2)}, u32[]{:S(2)}) collective-permute-start(bf16[4,320,128]{2,1,0:T(8,128)(2,1)} %get-tuple-element.309), channel_id=1, source_target_pairs={{0,5},{1,4},{2,7},{3,6},{4,1},{5,0},{6,3},{7,2},{8,13},{9,12},{10,... | collective-permute-start | bytes 983048 | tf_op jit(solution)/shard_map/while/body/ppermute | solution.py:425
  126.6 65.7 %all-to-all-start.1 = ((bf16[16,320,128]{2,1,0:T(8,128)(2,1)}), bf16[16,320,128]{2,1,0:T(8,128)(2,1)}, u32[]{:S(2)}, u32[]{:S(2)}) async-start(bf16[16,320,128]{2,1,0:T(8,128)(2,1)} %pack.12), calls=%async_computation.1 | async-start | bytes 2621440 | tf_op jit(solution)/shard_map/while/body/all_to_all | solution.py:435
  132.7 23.3 %collective-permute-start.12 = (bf16[4,320,128]{2,1,0:T(8,128)(2,1)}, bf16[4,320,128]{2,1,0:T(8,128)(2,1)}, u32[]{:S(2)}, u32[]{:S(2)}) collective-permute-start(bf16[4,320,128]{2,1,0:T(8,128)(2,1)} %get-tuple-element.310), channel_id=1, source_target_pairs={{0,6},{1,7},{2,4},{3,5},{4,2},{5,3},{6,0},{7,1},{8,14},{9,15},{10,... | collective-permute-start | bytes 983048 | tf_op jit(solution)/shard_map/while/body/ppermute | solution.py:425
  141.9 20.9 %collective-permute-start.13 = (bf16[4,320,128]{2,1,0:T(8,128)(2,1)}, bf16[4,320,128]{2,1,0:T(8,128)(2,1)}, u32[]{:S(2)}, u32[]{:S(2)}) collective-permute-start(bf16[4,320,128]{2,1,0:T(8,128)(2,1)} %get-tuple-element.311), channel_id=1, source_target_pairs={{0,7},{1,6},{2,5},{3,4},{4,3},{5,2},{6,1},{7,0},{8,15},{9,14},{10,... | collective-permute-start | bytes 983048 | tf_op jit(solution)/shard_map/while/body/ppermute | solution.py:425
  148.8 14.6 %collective-permute-start.7 = (bf16[4,320,128]{2,1,0:T(8,128)(2,1)}, bf16[4,320,128]{2,1,0:T(8,128)(2,1)}, u32[]{:S(2)}, u32[]{:S(2)}) collective-permute-start(bf16[4,320,128]{2,1,0:T(8,128)(2,1)} %get-tuple-element.305), channel_id=1, source_target_pairs={{0,1},{1,0},{2,3},{3,2},{4,5},{5,4},{6,7},{7,6},{8,9},{9,8},{10,11... | collective-permute-start | bytes 983048 | tf_op jit(solution)/shard_map/while/body/ppermute | solution.py:425
  149.1 15.3 %collective-permute-start.8 = (bf16[4,320,128]{2,1,0:T(8,128)(2,1)}, bf16[4,320,128]{2,1,0:T(8,128)(2,1)}, u32[]{:S(2)}, u32[]{:S(2)}) collective-permute-start(bf16[4,320,128]{2,1,0:T(8,128)(2,1)} %get-tuple-element.306), channel_id=1, source_target_pairs={{0,2},{1,3},{2,0},{3,1},{4,6},{5,7},{6,4},{7,5},{8,10},{9,11},{10,... | collective-permute-start | bytes 983048 | tf_op jit(solution)/shard_map/while/body/ppermute | solution.py:425
  149.4 17.1 %collective-permute-start.9 = (bf16[4,320,128]{2,1,0:T(8,128)(2,1)S(1)}, bf16[4,320,128]{2,1,0:T(8,128)(2,1)}, u32[]{:S(2)}, u32[]{:S(2)}) collective-permute-start(bf16[4,320,128]{2,1,0:T(8,128)(2,1)S(1)} %copy-done.26), channel_id=1, source_target_pairs={{0,3},{1,2},{2,1},{3,0},{4,7},{5,6},{6,5},{7,4},{8,11},{9,10},{10,... | collective-permute-start | bytes 983048 | tf_op jit(solution)/shard_map/while/body/ppermute | solution.py:425
  156.0 28.2 %collective-permute-start.21 = (bf16[2,320,128]{2,1,0:T(8,128)(2,1)}, bf16[2,320,128]{2,1,0:T(8,128)(2,1)S(1)}, u32[]{:S(2)}, u32[]{:S(2)}) collective-permute-start(bf16[2,320,128]{2,1,0:T(8,128)(2,1)} %get-tuple-element.321), channel_id=1, source_target_pairs={{0,1},{1,0},{2,3},{3,2},{4,5},{5,4},{6,7},{7,6},{8,9},{9,8},{10,11... | collective-permute-start | bytes 491528 | tf_op jit(solution)/shard_map/while/body/ppermute | solution.py:425
  162.8 21.5 %collective-permute-start.22 = (bf16[2,320,128]{2,1,0:T(8,128)(2,1)}, bf16[2,320,128]{2,1,0:T(8,128)(2,1)S(1)}, u32[]{:S(2)}, u32[]{:S(2)}) collective-permute-start(bf16[2,320,128]{2,1,0:T(8,128)(2,1)} %get-tuple-element.322), channel_id=1, source_target_pairs={{0,2},{1,3},{2,0},{3,1},{4,6},{5,7},{6,4},{7,5},{8,10},{9,11},{10,... | collective-permute-start | bytes 491528 | tf_op jit(solution)/shard_map/while/body/ppermute | solution.py:425
  163.3 22.7 %collective-permute-start.23 = (bf16[2,320,128]{2,1,0:T(8,128)(2,1)}, bf16[2,320,128]{2,1,0:T(8,128)(2,1)S(1)}, u32[]{:S(2)}, u32[]{:S(2)}) collective-permute-start(bf16[2,320,128]{2,1,0:T(8,128)(2,1)} %get-tuple-element.323), channel_id=1, source_target_pairs={{0,3},{1,2},{2,1},{3,0},{4,7},{5,6},{6,5},{7,4},{8,11},{9,10},{10,... | collective-permute-start | bytes 491528 | tf_op jit(solution)/shard_map/while/body/ppermute | solution.py:425
  164.4 22.1 %collective-permute-start.24 = (bf16[2,320,128]{2,1,0:T(8,128)(2,1)}, bf16[2,320,128]{2,1,0:T(8,128)(2,1)S(1)}, u32[]{:S(2)}, u32[]{:S(2)}) collective-permute-start(bf16[2,320,128]{2,1,0:T(8,128)(2,1)} %get-tuple-element.324), channel_id=1, source_target_pairs={{0,4},{1,5},{2,6},{3,7},{4,0},{5,1},{6,2},{7,3},{8,12},{9,13},{10,... | collective-permute-start | bytes 491528 | tf_op jit(solution)/shard_map/while/body/ppermute | solution.py:425
  184.2 7.0 %collective-permute-start.15 = (bf16[8,72,128]{2,1,0:T(8,128)(2,1)}, bf16[8,72,128]{2,1,0:T(8,128)(2,1)S(1)}, u32[]{:S(2)}, u32[]{:S(2)}) collective-permute-start(bf16[8,72,128]{2,1,0:T(8,128)(2,1)} %get-tuple-element.314), channel_id=1, source_target_pairs={{0,2},{1,3},{2,0},{3,1},{4,6},{5,7},{6,4},{7,5},{8,10},{9,11},{10,... | collective-permute-start | bytes 442376 | tf_op jit(solution)/shard_map/while/body/ppermute | solution.py:425
  184.3 11.5 %collective-permute-start.16 = (bf16[8,72,128]{2,1,0:T(8,128)(2,1)}, bf16[8,72,128]{2,1,0:T(8,128)(2,1)S(1)}, u32[]{:S(2)}, u32[]{:S(2)}) collective-permute-start(bf16[8,72,128]{2,1,0:T(8,128)(2,1)} %get-tuple-element.315), channel_id=1, source_target_pairs={{0,3},{1,2},{2,1},{3,0},{4,7},{5,6},{6,5},{7,4},{8,11},{9,10},{10,... | collective-permute-start | bytes 442376 | tf_op jit(solution)/shard_map/while/body/ppermute | solution.py:425
  186.1 10.7 %collective-permute-start.17 = (bf16[8,72,128]{2,1,0:T(8,128)(2,1)}, bf16[8,72,128]{2,1,0:T(8,128)(2,1)S(1)}, u32[]{:S(2)}, u32[]{:S(2)}) collective-permute-start(bf16[8,72,128]{2,1,0:T(8,128)(2,1)} %get-tuple-element.316), channel_id=1, source_target_pairs={{0,4},{1,5},{2,6},{3,7},{4,0},{5,1},{6,2},{7,3},{8,12},{9,13},{10,... | collective-permute-start | bytes 442376 | tf_op jit(solution)/shard_map/while/body/ppermute | solution.py:425
  186.5 13.8 %collective-permute-start.18 = (bf16[8,72,128]{2,1,0:T(8,128)(2,1)}, bf16[8,72,128]{2,1,0:T(8,128)(2,1)S(1)}, u32[]{:S(2)}, u32[]{:S(2)}) collective-permute-start(bf16[8,72,128]{2,1,0:T(8,128)(2,1)} %get-tuple-element.317), channel_id=1, source_target_pairs={{0,5},{1,4},{2,7},{3,6},{4,1},{5,0},{6,3},{7,2},{8,13},{9,12},{10,... | collective-permute-start | bytes 442376 | tf_op jit(solution)/shard_map/while/body/ppermute | solution.py:425
  189.3 16.3 %collective-permute-start.19 = (bf16[8,72,128]{2,1,0:T(8,128)(2,1)}, bf16[8,72,128]{2,1,0:T(8,128)(2,1)S(1)}, u32[]{:S(2)}, u32[]{:S(2)}) collective-permute-start(bf16[8,72,128]{2,1,0:T(8,128)(2,1)} %get-tuple-element.318), channel_id=1, source_target_pairs={{0,6},{1,7},{2,4},{3,5},{4,2},{5,3},{6,0},{7,1},{8,14},{9,15},{10,... | collective-permute-start | bytes 442376 | tf_op jit(solution)/shard_map/while/body/ppermute | solution.py:425
  191.2 17.4 %collective-permute-start.20 = (bf16[8,72,128]{2,1,0:T(8,128)(2,1)}, bf16[8,72,128]{2,1,0:T(8,128)(2,1)S(1)}, u32[]{:S(2)}, u32[]{:S(2)}) collective-permute-start(bf16[8,72,128]{2,1,0:T(8,128)(2,1)} %get-tuple-element.319), channel_id=1, source_target_pairs={{0,7},{1,6},{2,5},{3,4},{4,3},{5,2},{6,1},{7,0},{8,15},{9,14},{10,... | collective-permute-start | bytes 442376 | tf_op jit(solution)/shard_map/while/body/ppermute | solution.py:425
  195.9 29.4 %collective-permute-start.25 = (bf16[2,320,128]{2,1,0:T(8,128)(2,1)S(1)}, bf16[2,320,128]{2,1,0:T(8,128)(2,1)S(1)}, u32[]{:S(2)}, u32[]{:S(2)}) collective-permute-start(bf16[2,320,128]{2,1,0:T(8,128)(2,1)S(1)} %copy-done.33), channel_id=1, source_target_pairs={{0,5},{1,4},{2,7},{3,6},{4,1},{5,0},{6,3},{7,2},{8,13},{9,12},{10,... | collective-permute-start | bytes 491528 | tf_op jit(solution)/shard_map/while/body/ppermute | solution.py:425
  196.7 30.0 %collective-permute-start.26 = (bf16[2,320,128]{2,1,0:T(8,128)(2,1)S(1)}, bf16[2,320,128]{2,1,0:T(8,128)(2,1)S(1)}, u32[]{:S(2)}, u32[]{:S(2)}) collective-permute-start(bf16[2,320,128]{2,1,0:T(8,128)(2,1)S(1)} %copy-done.32), channel_id=1, source_target_pairs={{0,6},{1,7},{2,4},{3,5},{4,2},{5,3},{6,0},{7,1},{8,14},{9,15},{10,... | collective-permute-start | bytes 491528 | tf_op jit(solution)/shard_map/while/body/ppermute | solution.py:425
  200.3 27.8 %collective-permute-start.27 = (bf16[2,320,128]{2,1,0:T(8,128)(2,1)S(1)}, bf16[2,320,128]{2,1,0:T(8,128)(2,1)}, u32[]{:S(2)}, u32[]{:S(2)}) collective-permute-start(bf16[2,320,128]{2,1,0:T(8,128)(2,1)S(1)} %copy-done.31), channel_id=1, source_target_pairs={{0,7},{1,6},{2,5},{3,4},{4,3},{5,2},{6,1},{7,0},{8,15},{9,14},{10,... | collective-permute-start | bytes 491528 | tf_op jit(solution)/shard_map/while/body/ppermute | solution.py:425
  205.6 24.4 %collective-permute-start.31 = (bf16[2,320,128]{2,1,0:T(8,128)(2,1)}, bf16[2,320,128]{2,1,0:T(8,128)(2,1)}, u32[]{:S(2)}, u32[]{:S(2)}) collective-permute-start(bf16[2,320,128]{2,1,0:T(8,128)(2,1)} %get-tuple-element.334), channel_id=1, source_target_pairs={{0,1},{1,0},{2,3},{3,2},{4,5},{5,4},{6,7},{7,6},{8,9},{9,8},{10,11... | collective-permute-start | bytes 491528 | tf_op jit(solution)/shard_map/while/body/ppermute | solution.py:425
  208.6 22.9 %collective-permute-start.32 = (bf16[2,320,128]{2,1,0:T(8,128)(2,1)}, bf16[2,320,128]{2,1,0:T(8,128)(2,1)}, u32[]{:S(2)}, u32[]{:S(2)}) collective-permute-start(bf16[2,320,128]{2,1,0:T(8,128)(2,1)} %get-tuple-element.335), channel_id=1, source_target_pairs={{0,2},{1,3},{2,0},{3,1},{4,6},{5,7},{6,4},{7,5},{8,10},{9,11},{10,... | collective-permute-start | bytes 491528 | tf_op jit(solution)/shard_map/while/body/ppermute | solution.py:425
  213.3 64.5 %all-to-all-start.2 = ((bf16[32,72,128]{2,1,0:T(8,128)(2,1)}), bf16[32,72,128]{2,1,0:T(8,128)(2,1)S(1)}, u32[]{:S(2)}, u32[]{:S(2)}) async-start(bf16[32,72,128]{2,1,0:T(8,128)(2,1)} %place.3), calls=%async_computation.2 | async-start | bytes 1179648 | tf_op jit(solution)/shard_map/while/body/all_to_all | solution.py:439
  225.3 7.7 %collective-permute-start.33 = (bf16[2,320,128]{2,1,0:T(8,128)(2,1)}, bf16[2,320,128]{2,1,0:T(8,128)(2,1)S(1)}, u32[]{:S(2)}, u32[]{:S(2)}) collective-permute-start(bf16[2,320,128]{2,1,0:T(8,128)(2,1)} %get-tuple-element.336), channel_id=1, source_target_pairs={{0,3},{1,2},{2,1},{3,0},{4,7},{5,6},{6,5},{7,4},{8,11},{9,10},{10,... | collective-permute-start | bytes 491528 | tf_op jit(solution)/shard_map/while/body/ppermute | solution.py:425
  226.7 10.1 %collective-permute-start.34 = (bf16[2,320,128]{2,1,0:T(8,128)(2,1)}, bf16[2,320,128]{2,1,0:T(8,128)(2,1)S(1)}, u32[]{:S(2)}, u32[]{:S(2)}) collective-permute-start(bf16[2,320,128]{2,1,0:T(8,128)(2,1)} %get-tuple-element.337), channel_id=1, source_target_pairs={{0,4},{1,5},{2,6},{3,7},{4,0},{5,1},{6,2},{7,3},{8,12},{9,13},{10,... | collective-permute-start | bytes 491528 | tf_op jit(solution)/shard_map/while/body/ppermute | solution.py:425
  228.1 12.3 %collective-permute-start.35 = (bf16[2,320,128]{2,1,0:T(8,128)(2,1)}, bf16[2,320,128]{2,1,0:T(8,128)(2,1)S(1)}, u32[]{:S(2)}, u32[]{:S(2)}) collective-permute-start(bf16[2,320,128]{2,1,0:T(8,128)(2,1)} %get-tuple-element.338), channel_id=1, source_target_pairs={{0,5},{1,4},{2,7},{3,6},{4,1},{5,0},{6,3},{7,2},{8,13},{9,12},{10,... | collective-permute-start | bytes 491528 | tf_op jit(solution)/shard_map/while/body/ppermute | solution.py:425
  230.0 13.9 %collective-permute-start.36 = (bf16[2,320,128]{2,1,0:T(8,128)(2,1)}, bf16[2,320,128]{2,1,0:T(8,128)(2,1)S(1)}, u32[]{:S(2)}, u32[]{:S(2)}) collective-permute-start(bf16[2,320,128]{2,1,0:T(8,128)(2,1)} %get-tuple-element.339), channel_id=1, source_target_pairs={{0,6},{1,7},{2,4},{3,5},{4,2},{5,3},{6,0},{7,1},{8,14},{9,15},{10,... | collective-permute-start | bytes 491528 | tf_op jit(solution)/shard_map/while/body/ppermute | solution.py:425
  231.6 15.7 %collective-permute-start.37 = (bf16[2,320,128]{2,1,0:T(8,128)(2,1)S(1)}, bf16[2,320,128]{2,1,0:T(8,128)(2,1)S(1)}, u32[]{:S(2)}, u32[]{:S(2)}) collective-permute-start(bf16[2,320,128]{2,1,0:T(8,128)(2,1)S(1)} %copy-done.35), channel_id=1, source_target_pairs={{0,7},{1,6},{2,5},{3,4},{4,3},{5,2},{6,1},{7,0},{8,15},{9,14},{10,... | collective-permute-start | bytes 491528 | tf_op jit(solution)/shard_map/while/body/ppermute | solution.py:425
  262.3 7.8 %collective-permute-start.40 = (bf16[4,72,128]{2,1,0:T(8,128)(2,1)}, bf16[4,72,128]{2,1,0:T(8,128)(2,1)S(1)}, u32[]{:S(2)}, u32[]{:S(2)}) collective-permute-start(bf16[4,72,128]{2,1,0:T(8,128)(2,1)} %get-tuple-element.344), channel_id=1, source_target_pairs={{0,3},{1,2},{2,1},{3,0},{4,7},{5,6},{6,5},{7,4},{8,11},{9,10},{10,... | collective-permute-start | bytes 221192 | tf_op jit(solution)/shard_map/while/body/ppermute | solution.py:425
  263.8 6.9 %collective-permute-start.41 = (bf16[4,72,128]{2,1,0:T(8,128)(2,1)}, bf16[4,72,128]{2,1,0:T(8,128)(2,1)S(1)}, u32[]{:S(2)}, u32[]{:S(2)}) collective-permute-start(bf16[4,72,128]{2,1,0:T(8,128)(2,1)} %get-tuple-element.345), channel_id=1, source_target_pairs={{0,4},{1,5},{2,6},{3,7},{4,0},{5,1},{6,2},{7,3},{8,12},{9,13},{10,... | collective-permute-start | bytes 221192 | tf_op jit(solution)/shard_map/while/body/ppermute | solution.py:425
  263.9 7.3 %collective-permute-start.42 = (bf16[4,72,128]{2,1,0:T(8,128)(2,1)}, bf16[4,72,128]{2,1,0:T(8,128)(2,1)S(1)}, u32[]{:S(2)}, u32[]{:S(2)}) collective-permute-start(bf16[4,72,128]{2,1,0:T(8,128)(2,1)} %get-tuple-element.346), channel_id=1, source_target_pairs={{0,5},{1,4},{2,7},{3,6},{4,1},{5,0},{6,3},{7,2},{8,13},{9,12},{10,... | collective-permute-start | bytes 221192 | tf_op jit(solution)/shard_map/while/body/ppermute | solution.py:425
  267.1 6.6 %collective-permute-start.43 = (bf16[4,72,128]{2,1,0:T(8,128)(2,1)}, bf16[4,72,128]{2,1,0:T(8,128)(2,1)S(1)}, u32[]{:S(2)}, u32[]{:S(2)}) collective-permute-start(bf16[4,72,128]{2,1,0:T(8,128)(2,1)} %get-tuple-element.347), channel_id=1, source_target_pairs={{0,6},{1,7},{2,4},{3,5},{4,2},{5,3},{6,0},{7,1},{8,14},{9,15},{10,... | collective-permute-start | bytes 221192 | tf_op jit(solution)/shard_map/while/body/ppermute | solution.py:425
  267.4 7.0 %collective-permute-start.44 = (bf16[4,72,128]{2,1,0:T(8,128)(2,1)}, bf16[4,72,128]{2,1,0:T(8,128)(2,1)S(1)}, u32[]{:S(2)}, u32[]{:S(2)}) collective-permute-start(bf16[4,72,128]{2,1,0:T(8,128)(2,1)} %get-tuple-element.348), channel_id=1, source_target_pairs={{0,7},{1,6},{2,5},{3,4},{4,3},{5,2},{6,1},{7,0},{8,15},{9,14},{10,... | collective-permute-start | bytes 221192 | tf_op jit(solution)/shard_map/while/body/ppermute | solution.py:425
  302.6 7.4 %collective-permute-start.45 = (bf16[6,72,128]{2,1,0:T(8,128)(2,1)}, bf16[6,72,128]{2,1,0:T(8,128)(2,1)S(1)}, u32[]{:S(2)}, u32[]{:S(2)}) collective-permute-start(bf16[6,72,128]{2,1,0:T(8,128)(2,1)} %get-tuple-element.350), channel_id=1, source_target_pairs={{0,64},{8,72},{16,80},{24,88},{32,96},{40,104},{48,112},{56,120},{... | collective-permute-start | bytes 331784 | tf_op jit(solution)/shard_map/while/body/ppermute | solution.py:430
  304.9 8.1 %collective-permute-start.46 = (bf16[6,72,128]{2,1,0:T(8,128)(2,1)}, bf16[6,72,128]{2,1,0:T(8,128)(2,1)S(1)}, u32[]{:S(2)}, u32[]{:S(2)}) collective-permute-start(bf16[6,72,128]{2,1,0:T(8,128)(2,1)} %get-tuple-element.351), channel_id=1, source_target_pairs={{0,128},{8,136},{16,144},{24,152},{32,160},{40,168},{48,176},{56,1... | collective-permute-start | bytes 331784 | tf_op jit(solution)/shard_map/while/body/ppermute | solution.py:430
  (46 other events, 604.0 us)

commit v4 on v3

--- a/solution.py
+++ b/solution.py
@@ -4,6 +4,7 @@
 from jax.experimental import pallas as pl
 from jax.experimental.pallas import tpu as pltpu
 from jax.sharding import PartitionSpec as P
+
 
 COUPLE = 0.015625
 BIG = 1 << 30
@@ -156,9 +157,12 @@
                 sums.append(jnp.sum(factor.astype(F32) * projected, axis=0, keepdims=True))
             fits.append(jnp.concatenate(sums, axis=1).astype(BF16).astype(F32))
         coeff = fits[0] + fits[1]
-        for n in range(8):
-            rows = slice(n * 64, n * 64 + 64)
+
+        def weigh(n):
+            rows = pl.ds(pl.multiple_of(n * 64, 64), 64)
             weighted[rows, :] = (stacked[rows, :].astype(F32) * coeff).astype(BF16)
+
+        loop(8, weigh)
         for n in range(4):
             rows = slice(n * 128, n * 128 + 128)
             coulomb = lax.dot_general(
@@ -173,11 +177,15 @@
             current[rows, :] = (eye + wide + COUPLE * coulomb).astype(BF16)
 
         def purify(index, unused):
-            for n in range(4):
-                rows = slice(n * 128, n * 128 + 128)
+
+            def block(n):
+                rows = pl.ds(pl.multiple_of(n * 128, 128), 128)
                 square = jnp.dot(current[rows, :], current[...], preferred_element_type=F32)
                 cube = jnp.dot(square.astype(BF16), current[...], preferred_element_type=F32)
                 squares[rows, :] = (3.0 * square - 2.0 * cube).astype(BF16)
+
+            for n in range(4):
+                block(n)
             current[...] = squares[...]
             return unused
 
@@ -273,7 +281,7 @@
     one_dimer(table_ref[STEPS + 2 * me + i], me, load, outs, scratch)
 
 
-def plan_kernel(me_ref, inside_ref, a_ref, b_ref, cost_ref, flag_ref, table_ref, left_ref, to_x, to_z, n_direct, n_third, n_self):
+def plan_kernel(me_ref, inside_ref, count_ref, list_ref, table_ref, left_ref, to_x, to_z, n_direct, n_third, n_self):
     me = me_ref[0]
 
     def clear(n):
@@ -312,111 +320,110 @@
         return jnp.where(move_z, 32 + NX + zo * KZ + n_z, 32 + in_x)
 
     def visit(d):
-        @pl.when(flag_ref[d] > 0)
+        word = list_ref[d]
+        a, b, cost = word & 1023, (word >> 10) & 1023, word >> 20
+        oa, ob, la, lb = a >> 5, b >> 5, a & 31, b & 31
+        left_ref[d] = 0
+
+        @pl.when(oa == ob)
         def _():
-            a, b, cost = a_ref[d], b_ref[d], cost_ref[d]
-            oa, ob, la, lb = a >> 5, b >> 5, a & 31, b & 31
-            left_ref[d] = 0
-
-            @pl.when(oa == ob)
+            q = n_self[oa]
+
+            @pl.when(q < 8)
             def _():
-                q = n_self[oa]
-
-                @pl.when(q < 8)
+                n_self[oa] = q + 1
+
+                @pl.when(oa == me)
                 def _():
-                    n_self[oa] = q + 1
-
-                    @pl.when(oa == me)
-                    def _():
-                        at = 2 * (7 - q)
-                        table_ref[POS + 2 * at + 2] = la
-                        table_ref[POS + 2 * at + 3] = lb
-                        table_ref[HOME + at] = la
-                        table_ref[HOME + at + 1] = lb
-                        table_ref[STEPS + at + 1] = cost
-                        table_ref[MODE + 7 - q] = 1
-
-                @pl.when(q >= 8)
+                    at = 2 * (7 - q)
+                    table_ref[POS + 2 * at + 2] = la
+                    table_ref[POS + 2 * at + 3] = lb
+                    table_ref[HOME + at] = la
+                    table_ref[HOME + at + 1] = lb
+                    table_ref[STEPS + at + 1] = cost
+                    table_ref[MODE + 7 - q] = 1
+
+            @pl.when(q >= 8)
+            def _():
+                left_ref[d] = 1
+
+        @pl.when(oa != ob)
+        def _():
+            n_a, n_b = n_direct[oa], n_direct[ob]
+            fit_a = ((n_a + 2) >> 1) + jnp.maximum(n_third[oa], inside_ref[oa]) <= 8
+            fit_b = ((n_b + 2) >> 1) + jnp.maximum(n_third[ob], inside_ref[ob]) <= 8
+            can_a, can_b = can(ob, oa) & fit_a, can(oa, ob) & fit_b
+            full_a = to_z[(oa >> 3) * 64 + (ob & 7) * 8 + (oa & 7)] * 4 + n_a
+            full_b = to_z[(ob >> 3) * 64 + (oa & 7) * 8 + (ob & 7)] * 4 + n_b
+            use_a = can_a & (jnp.logical_not(can_b) | (full_a <= full_b))
+            direct = can_a | can_b
+
+            @pl.when(direct)
+            def _():
+                c, o = jnp.where(use_a, oa, ob), jnp.where(use_a, ob, oa)
+                stay, move = jnp.where(use_a, la, lb), jnp.where(use_a, lb, la)
+                at = jnp.where(use_a, n_a, n_b)
+                n_direct[c] = at + 1
+                late = send(o, move, c)
+
+                @pl.when(c == me)
+                def _():
+                    table_ref[POS + 2 * at] = stay
+                    table_ref[POS + 2 * at + 1] = late
+                    table_ref[HOME + at] = stay
+                    table_ref[LATE + at] = late
+                    table_ref[STEPS + at] = cost
+
+            @pl.when(jnp.logical_not(direct))
+            def _():
+                same_z = jnp.where((oa & 7) == (ob & 7), 1, 0)
+
+                def look(carry):
+                    n, _ = carry
+                    c = (d + n) & 31
+                    fit = ((n_direct[c] + 1) >> 1) + jnp.maximum(n_third[c] + 1, inside_ref[c]) <= 8
+                    good = fit & can(oa, c, same_z) & can(ob, c, same_z) & (c != oa) & (c != ob)
+                    return n + 1, jnp.where(good, c, -1)
+
+                _, c = lax.while_loop(
+                    lambda carry: (carry[0] < 32) & (carry[1] < 0), look, (jnp.int32(0), jnp.int32(-1))
+                )
+
+                @pl.when(c < 0)
                 def _():
                     left_ref[d] = 1
 
-            @pl.when(oa != ob)
-            def _():
-                n_a, n_b = n_direct[oa], n_direct[ob]
-                fit_a = ((n_a + 2) >> 1) + jnp.maximum(n_third[oa], inside_ref[oa]) <= 8
-                fit_b = ((n_b + 2) >> 1) + jnp.maximum(n_third[ob], inside_ref[ob]) <= 8
-                can_a, can_b = can(ob, oa) & fit_a, can(oa, ob) & fit_b
-                full_a = to_z[(oa >> 3) * 64 + (ob & 7) * 8 + (oa & 7)] * 4 + n_a
-                full_b = to_z[(ob >> 3) * 64 + (oa & 7) * 8 + (ob & 7)] * 4 + n_b
-                use_a = can_a & (jnp.logical_not(can_b) | (full_a <= full_b))
-                direct = can_a | can_b
-
-                @pl.when(direct)
+                @pl.when(c >= 0)
                 def _():
-                    c, o = jnp.where(use_a, oa, ob), jnp.where(use_a, ob, oa)
-                    stay, move = jnp.where(use_a, la, lb), jnp.where(use_a, lb, la)
-                    at = jnp.where(use_a, n_a, n_b)
-                    n_direct[c] = at + 1
-                    late = send(o, move, c)
+                    t = n_third[c]
+                    n_third[c] = t + 1
+                    late_a = send(oa, la, c)
+                    late_b = send(ob, lb, c)
 
                     @pl.when(c == me)
                     def _():
-                        table_ref[POS + 2 * at] = stay
-                        table_ref[POS + 2 * at + 1] = late
-                        table_ref[HOME + at] = stay
-                        table_ref[LATE + at] = late
+                        at = 2 * (7 - t)
+                        table_ref[POS + 2 * at] = late_a
+                        table_ref[POS + 2 * at + 1] = late_b
+                        table_ref[LATE + at] = late_a
+                        table_ref[LATE + at + 1] = late_b
                         table_ref[STEPS + at] = cost
-
-                @pl.when(jnp.logical_not(direct))
-                def _():
-                    same_z = jnp.where((oa & 7) == (ob & 7), 1, 0)
-
-                    def look(carry):
-                        n, unused = carry
-                        c = (d + n) & 31
-                        fit = ((n_direct[c] + 1) >> 1) + jnp.maximum(n_third[c] + 1, inside_ref[c]) <= 8
-                        good = fit & can(oa, c, same_z) & can(ob, c, same_z) & (c != oa) & (c != ob)
-                        return n + 1, jnp.where(good, c, -1)
-
-                    unused, c = lax.while_loop(
-                        lambda carry: (carry[0] < 32) & (carry[1] < 0), look, (jnp.int32(0), jnp.int32(-1))
-                    )
-
-                    @pl.when(c < 0)
-                    def _():
-                        left_ref[d] = 1
-
-                    @pl.when(c >= 0)
-                    def _():
-                        t = n_third[c]
-                        n_third[c] = t + 1
-                        late_a = send(oa, la, c)
-                        late_b = send(ob, lb, c)
-
-                        @pl.when(c == me)
-                        def _():
-                            at = 2 * (7 - t)
-                            table_ref[POS + 2 * at] = late_a
-                            table_ref[POS + 2 * at + 1] = late_b
-                            table_ref[LATE + at] = late_a
-                            table_ref[LATE + at + 1] = late_b
-                            table_ref[STEPS + at] = cost
-                            table_ref[MODE + 7 - t] = 1
-
-    loop(a_ref.shape[0], visit)
-
-
-def plan_rest(me, inside_count, a, b, cost, flag):
+                        table_ref[MODE + 7 - t] = 1
+
+    loop(count_ref[0], visit)
+
+
+def plan_rest(me, inside_count, count, words):
     s32 = jnp.int32
     return pl.pallas_call(
         plan_kernel,
-        out_shape=[jax.ShapeDtypeStruct((TABLE,), s32), jax.ShapeDtypeStruct(a.shape, s32)],
-        in_specs=[SMEM] * 6,
+        out_shape=[jax.ShapeDtypeStruct((TABLE,), s32), jax.ShapeDtypeStruct(words.shape, s32)],
+        in_specs=[SMEM] * 4,
         out_specs=[SMEM] * 2,
         scratch_shapes=[pltpu.SMEM((128,), s32), pltpu.SMEM((256,), s32)] + [pltpu.SMEM((32,), s32)] * 3,
         name="plan",
         cost_estimate=pl.CostEstimate(flops=1000, bytes_accessed=30_000_000, transcendentals=0),
-    )(me, inside_count, a, b, cost, flag)
+    )(me, inside_count, count, words)
 
 
 def exchange(parts):
@@ -474,12 +481,16 @@
     other = jnp.where(mine_a, own_b, jnp.where(mine_b, own_a, -1))
     local = jnp.where(mine_a, a, b) & 31
     key = order * 256 + local * 8 + cost
+    word = a + b * 1024 + cost * 1048576
     me_f, me_b = me_frag.reshape(1), me_basis.reshape(1)
     keep_first = (me_frag < columns) == ((me_frag + columns) % 2 == 0)
     home = (aux_factor, density)
 
     def one_round(carry):
-        unused_n, rest, dens, emb = carry
+        return body_round(carry)
+
+    def body_round(carry):
+        _, rest, dens, emb = carry
         open_dimer = rest > 0
         match = (other[None, :] == columns[:, None]) & open_dimer[None, :]
         keyed = jnp.where(match, key[None, :], BIG)
@@ -502,11 +513,15 @@
         earlier = (pair_id[:, None] == pair_id[None, :]) & (order[None, :] < order[:, None])
         earlier = jnp.sum(jnp.where(earlier & open_dimer[None, :], 1, 0), axis=1)
         flagged = open_dimer & ((earlier >= 2) | inside)
-        flag = jnp.where(flagged, 1, 0)
+        ahead = jnp.sum(jnp.where((order[None, :] < order[:, None]) & flagged[None, :], 1, 0), axis=1)
+        ahead = jnp.where(flagged, ahead, -1)
+        words = jnp.sum(jnp.where(ahead[None, :] == order[:, None], word[None, :], 0), axis=1)
+        count = jnp.sum(jnp.where(flagged, 1, 0)).reshape(1)
         inside_here = (own_a[None, :] == columns[:, None]) & (inside & open_dimer)[None, :]
         inside_count = jnp.sum(jnp.where(inside_here, 1, 0), axis=1)
-        table_2, left = plan_rest(me_f, inside_count, a, b, cost, flag)
-        left = jnp.where(flagged, left, 0)
+        table_2, listed = plan_rest(me_f, inside_count, count, words)
+        listed = jnp.where(order < count, listed, 0)
+        left = jnp.sum(jnp.where(ahead[:, None] == order[None, :], listed[None, :], 0), axis=1)
         tables = (table_1, table_2)
 
         def served(t, me, n, row):
@@ -517,30 +532,30 @@
         )
         in_x = along_x(pack(tables, me_b, lambda t, me, n, row: t[1][SENT + n * KX + row], 3, KX, home, []))
         (out_2,) = pack(tables, me_b, lambda t, me, n, row: t[1][RELAY + row], 1, NZ, home, in_x)
-        in_z = along_z(after(out_2, in_1))
+        in_z = along_z(after(out_2, in_1, home_1))
         home_2 = exchange(
             pack(
                 tables, me_b, lambda t, me, n, row: t[1][HOME + 2 * lax.bitwise_xor(me, n) + row], 8, 2, home, []
             )
         )
 
-        away_1 = exchange(pack(tables, me_b, served, 8, 4, (), [in_1]))
+        away_1 = exchange(pack(tables, me_b, served, 8, 4, (), [after(in_1, home_2)]))
         one = lambda i, *_: (i, 0, 0)
         done_1 = exchange(
             run_dimers(kernel_1, 4, (table_1, me_b), (1, 1), (one, one), [*home_1, *away_1])
         )
 
-        late_2 = exchange(
-            pack(
-                tables,
-                me_b,
-                lambda t, me, n, row: t[1][LATE + 2 * lax.bitwise_xor(me, n) + row] - 32,
-                8,
-                2,
-                (),
-                [*in_x, after(in_z, away_1)],
-            )
+        late_parts = pack(
+            tables,
+            me_b,
+            lambda t, me, n, row: t[1][LATE + 2 * lax.bitwise_xor(me, n) + row] - 32,
+            8,
+            2,
+            (),
+            [*in_x, after(in_z, away_1)],
         )
+        late_2 = exchange(late_parts)
+        done_1 = after(done_1, late_parts)
         whole = lambda i, *_: (0, 0, 0)
         done_2 = exchange(
             run_dimers(kernel_2, 2, (table_2, me_b), (2, 2), (whole, whole), [*home_2, *late_2])
@@ -585,10 +600,11 @@
         finds = (
             [stay_1(k) for k in range(8)]
             + [stay_2(k) for k in range(8)]
-            + [lambda t, me, row: t[0][OUT + row], lambda t, me, row: t[1][RELAY + row]]
-            + [from_x(k) for k in range(3)]
+            + [lambda t, me, row: t[0][OUT + row]]
         )
-        dens, emb = add_up(tables, me_b, [*done_1, *done_2, back_1, rest_z, *rest_x], finds, dens, emb)
+        dens, emb = add_up(tables, me_b, [*done_1, *done_2, back_1], finds, dens, emb)
+        finds = [lambda t, me, row: t[1][RELAY + row]] + [from_x(k) for k in range(3)]
+        dens, emb = add_up(tables, me_b, [rest_z, *rest_x], finds, dens, emb)
         return jnp.sum(left), left, dens, emb
 
     start = (
@@ -597,7 +613,7 @@
         jnp.zeros(density.shape, F32),
         jnp.zeros((density.shape[0], aux_factor.shape[2]), F32),
     )
-    unused_n, unused_rest, dens, emb = lax.while_loop(lambda carry: carry[0] > 0, one_round, start)
+    _, _, dens, emb = lax.while_loop(lambda carry: carry[0] > 0, one_round, start)
     return dens, emb
 
 

time: 329 us -> 338 us (1.027)
  waiting for transfers between devices: 79.2 us -> 104 us
  blocking collectives: 30.9 us -> 9.55 us
  Pallas kernels: 107 us -> 93.3 us
  starting transfers between devices: 92.7 us -> 104 us
  other arithmetic: 6.07 us -> 9.48 us
    ppermute x42, waiting for transfers between devices: 54 us -> 78.7 us  [exchange(): got.append(lax.ppermute(parts[k], 'basis', [(i, i ^ k) for i in range(8)]))]
    all_to_all x1 -> x0, blocking collectives: 21.4 us -> none  [along_z(): lax.all_to_all(part, 'frag', 0, 0, tiled=True, axis_index_groups=groups)]
    pallas_call x1, Pallas kernels: 37.2 us -> 25 us  [plan_rest(): pl.pallas_call(plan_kernel, out_shape=[jax.ShapeDtypeStruct((TABLE,), s32...]
    all_to_all x1 -> x2, waiting for transfers between devices: 0.01 us -> 10.9 us  [along_z(): lax.all_to_all(part, 'frag', 0, 0, tiled=True, axis_index_groups=groups)]
    all_to_all x1 -> x2, starting transfers between devices: 6.07 us -> 16.4 us  [along_z(): lax.all_to_all(part, 'frag', 0, 0, tiled=True, axis_index_groups=groups)]
    all_to_all x3, waiting for transfers between devices: 15.4 us -> 8.57 us  [across(): return lax.all_to_all(part, 'frag', split_axis=0, concat_axis=0, tiled=True)]
    ppermute x6, waiting for transfers between devices: 9.8 us -> 5.64 us  [along_x(): lax.ppermute(parts[k - 1], 'frag', [(i, i ^ 8 * k) for i in range(32)])]
    all_to_all x3, starting transfers between devices: 29.3 us -> 25.2 us  [across(): return lax.all_to_all(part, 'frag', split_axis=0, concat_axis=0, tiled=True)]
  transfers between devices with their start and end apart: 52 -> 53, of which waited for: 23 -> 28; matrix products, arithmetic and copies ran while one was open for 1% -> 2% of each run, Pallas kernels for 29% -> 25%
where the time goes in v4:
time: 338 us; the launch traced here: 333 us
  starting transfers between devices  104 us (31%)
  waiting for transfers between devices  104 us (31%)
  Pallas kernels  93.3 us (28%)
  blocking collectives  9.55 us (3%)
  other arithmetic  9.48 us (3%)
  local copies, waits for them, and re-layouts  9.24 us (3%)
    ppermute x42, waiting for transfers between devices, exchange(): got.append(lax.ppermute(parts[k], 'basis', [(i, i ^ k) for i in range(8)]))  78.7 us
    ppermute x42, starting transfers between devices, exchange(): got.append(lax.ppermute(parts[k], 'basis', [(i, i ^ k) for i in range(8)]))  48.7 us
    pallas_call x2, Pallas kernels, run_dimers(): pl.pallas_call(kernel, out_shape=[shape] * 8, grid_spec=pltpu.PrefetchSca...  29.5 us
    all_to_all x3, starting transfers between devices, across(): return lax.all_to_all(part, 'frag', split_axis=0, concat_axis=0, tiled=True)  25.2 us
    pallas_call x1, Pallas kernels, plan_rest(): pl.pallas_call(plan_kernel, out_shape=[jax.ShapeDtypeStruct((TABLE,), s32...  25 us
    pallas_call x7, Pallas kernels, pack(): pl.pallas_call(kernel, out_shape=[jax.ShapeDtypeStruct((rows, 320, 128),...  21.8 us
    all_to_all x2, starting transfers between devices, along_z(): lax.all_to_all(part, 'frag', 0, 0, tiled=True, axis_index_groups=groups)  16.4 us
    ppermute x6, starting transfers between devices, along_x(): lax.ppermute(parts[k - 1], 'frag', [(i, i ^ 8 * k) for i in range(32)])  13.6 us
  transfers between devices with their start and end apart: 53, of which 28 were waited for; matrix products, arithmetic and copies ran while one was open for 2% of the time, Pallas kernels for 25%

profile of v4, /device:TPU:32, one launch (start us, length us, event | category | flops | bytes accessed | tf_op | source)
XLA Modules:
  0.0 333.1 jit_solution(3647309167272270044)
XLA Ops:
  2.3 9.6 %all_to_all.34 = s32[8,1,128]{2,1,0:T(1,128)S(1)} all-to-all(s32[8,1,128]{2,1,0:T(1,128)S(1)} %broadcast_in_dim.142), channel_id=1, replica_groups=mesh['frag'=32,'basis'=8] {'basis'}, dimensions={0} | all-to-all | bytes 8192 | tf_op jit(solution)/shard_map/all_to_all | solution.py:463
  12.8 11.2 %all-to-all-start.5 = ((s32[32,1,128]{2,1,0:T(1,128)}), s32[32,1,128]{2,1,0:T(1,128)S(1)}, u32[]{:S(2)}, u32[]{:S(2)}) async-start(s32[32,1,128]{2,1,0:T(1,128)} %broadcast_in_dim.143), calls=%async_computation.5 | async-start | bytes 32768 | tf_op jit(solution)/shard_map/all_to_all | solution.py:446
  24.0 8.6 %all-to-all-done.5 = s32[32,1,128]{2,1,0:T(1,128)S(1)} async-done(((s32[32,1,128]{2,1,0:T(1,128)}), s32[32,1,128]{2,1,0:T(1,128)S(1)}, u32[]{:S(2)}, u32[]{:S(2)}) %all-to-all-start.5) | async-done | bytes 16416 | tf_op jit(solution)/shard_map/all_to_all | solution.py:446
  34.1 298.0 %while.15 = (s32[]{:T(128)}, s32[1024]{0:T(1024)S(1)}, f32[32,32,256]{2,1,0:T(8,128)}, f32[32,128]{1,0:T(8,128)S(1)}, s32[1024]{0:T(1024)S(1)}, /*index=5*/pred[...) while((s32[]{:T(128)}, s32[1024]{0:T(1024)S(1)}, ...), condition=%region_13.14_spmd.clone.clone, body=%region_1.13_spmd.clone.clone | while | flops 24018298880 | bytes 158524208 | solution.py:616
  35.3 3.8 %pack.10 = bf16[32,320,128]{2,1,0:T(8,128)(2,1)} custom-call(s32[32]{0:T(128)} %get-tuple-element.452.refs_0_, s32[1]{0:T(128)} %get-tuple-element.517.refs_2_.refs_1_.me_ref, bf16[32,256,128]{2,1,0:T(8,128)(2,1)} %get-tuple-element.518.refs_3_.refs_2_, bf16[32,32,256]{2,1,0:T(8,128)(2,1)} %get-tuple-element.519.refs_4_.refs_3_), custom_call_target="tpu_custom_call" | custom-call | tf_op jit(solution)/shard_map/while/body/pack/pallas_call | solution.py:68
  39.1 6.1 %all-to-all-start = ((bf16[32,320,128]{2,1,0:T(8,128)(2,1)}), bf16[32,320,128]{2,1,0:T(8,128)(2,1)}, u32[]{:S(2)}, u32[]{:S(2)}) async-start(bf16[32,320,128]{2,1,0:T(8,128)(2,1)} %pack.10), calls=%async_computation | async-start | bytes 5242880 | tf_op jit(solution)/shard_map/while/body/all_to_all | solution.py:446
  48.5 25.0 %plan.1 = (s32[256]{0:T(256)}, s32[1024]{0:T(1024)}) custom-call(s32[1]{0:T(128)} %get-tuple-element.514.me_ref, s32[32]{0:T(128)} %select_reduce_fusion.6.inside_ref, s32[1]{0:T(128)} %bitcast.5.count_ref, s32[1024]{0:T(1024)} %select_reduce_fusion.2.list_ref), custom_call_target="tpu_custom_call" | custom-call | flops 1000 | bytes 30000000 | tf_op jit(solution)/shard_map/while/body/plan/pallas_call | solution.py:418
  74.4 2.1 pack.7
  81.6 3.1 pack.11
  87.6 4.0 %collective-permute-done.3.refs_4_ = bf16[2,320,128]{2,1,0:T(8,128)(2,1)} collective-permute-done((bf16[2,320,128]{2,1,0:T(8,128)(2,1)}, bf16[2,320,128]{2,1,0:T(8,128)(2,1)}, u32[]{:S(2)}, u32[]{:S(2)}) %collective-permute-start.3) | collective-permute-done | bytes 163872 | tf_op jit(solution)/shard_map/while/body/ppermute | solution.py:432
  92.4 2.2 pack.8
  98.1 3.5 %collective-permute-done.6.refs_7_ = bf16[2,320,128]{2,1,0:T(8,128)(2,1)} collective-permute-done((bf16[2,320,128]{2,1,0:T(8,128)(2,1)}, bf16[2,320,128]{2,1,0:T(8,128)(2,1)}, u32[]{:S(2)}, u32[]{:S(2)}) %collective-permute-start.6) | collective-permute-done | bytes 163872 | tf_op jit(solution)/shard_map/while/body/ppermute | solution.py:432
  103.1 3.0 collective-permute-start.8
  108.0 2.1 collective-permute-start.14
  110.1 7.1 %collective-permute-done.13.refs_4_ = bf16[4,320,128]{2,1,0:T(8,128)(2,1)S(1)} collective-permute-done((bf16[4,320,128]{2,1,0:T(8,128)(2,1)}, bf16[4,320,128]{2,1,0:T(8,128)(2,1)S(1)}, u32[]{:S(2)}, u32[]{:S(2)}) %collective-permute-start.13) | collective-permute-done | bytes 327712 | tf_op jit(solution)/shard_map/while/body/ppermute | solution.py:432
  120.0 4.0 %pack.12 = (bf16[4,320,128]{2,1,0:T(8,128)(2,1)}, bf16[4,320,128]{2,1,0:T(8,128)(2,1)}, bf16[4,320,128]{2,1,0:T(8,128)(2,1)}, bf16[4,320,128]{2,1,0:T(8,128)(2,1...) custom-call(s32[128]{0:T(128)} %pad_add_fusion.refs_0_.table_ref, ...), custom_call_target="tpu_custom_call" | custom-call | tf_op jit(solution)/shard_map/while/body/pack/pallas_call | solution.py:68
  125.3 5.6 %collective-permute-done.9.refs_7_.refs_5_ = bf16[6,320,128]{2,1,0:T(8,128)(2,1)} collective-permute-done((bf16[6,320,128]{2,1,0:T(8,128)(2,1)}, bf16[6,320,128]{2,1,0:T(8,128)(2,1)}, u32[]{:S(2)}, u32[]{:S(2)}) %collective-permute-start.9) | collective-permute-done | bytes 491552 | tf_op jit(solution)/shard_map/while/body/ppermute | solution.py:437
  132.4 3.0 pack.9
  135.4 2.5 collective-permute-done.16.refs_7_
  137.9 7.2 %all-to-all-start.1 = ((bf16[16,320,128]{2,1,0:T(8,128)(2,1)}), bf16[16,320,128]{2,1,0:T(8,128)(2,1)S(1)}, u32[]{:S(2)}, u32[]{:S(2)}) async-start(bf16[16,320,128]{2,1,0:T(8,128)(2,1)} %pack.9), calls=%async_computation.1 | async-start | bytes 2621440 | tf_op jit(solution)/shard_map/while/body/all_to_all | solution.py:442
  151.5 3.7 %collective-permute-done.19.refs_11_ = bf16[4,320,128]{2,1,0:T(8,128)(2,1)S(1)} collective-permute-done((bf16[4,320,128]{2,1,0:T(8,128)(2,1)S(1)}, bf16[4,320,128]{2,1,0:T(8,128)(2,1)S(1)}, u32[]{:S(2)}, u32[]{:S(2)}) %collective-permute-start.19) | collective-permute-done | bytes 327712 | tf_op jit(solution)/shard_map/while/body/ppermute | solution.py:432
  155.2 7.2 %collective-permute-done.20.refs_12_ = bf16[4,320,128]{2,1,0:T(8,128)(2,1)S(1)} collective-permute-done((bf16[4,320,128]{2,1,0:T(8,128)(2,1)S(1)}, bf16[4,320,128]{2,1,0:T(8,128)(2,1)S(1)}, u32[]{:S(2)}, u32[]{:S(2)}) %collective-permute-start.20) | collective-permute-done | bytes 327712 | tf_op jit(solution)/shard_map/while/body/ppermute | solution.py:432
  162.4 7.3 %collective-permute-done.21.refs_13_ = bf16[4,320,128]{2,1,0:T(8,128)(2,1)S(1)} collective-permute-done((bf16[4,320,128]{2,1,0:T(8,128)(2,1)S(1)}, bf16[4,320,128]{2,1,0:T(8,128)(2,1)S(1)}, u32[]{:S(2)}, u32[]{:S(2)}) %collective-permute-start.21) | collective-permute-done | bytes 327712 | tf_op jit(solution)/shard_map/while/body/ppermute | solution.py:432
  169.7 3.6 %collective-permute-done.22.refs_14_ = bf16[4,320,128]{2,1,0:T(8,128)(2,1)S(1)} collective-permute-done((bf16[4,320,128]{2,1,0:T(8,128)(2,1)S(1)}, bf16[4,320,128]{2,1,0:T(8,128)(2,1)S(1)}, u32[]{:S(2)}, u32[]{:S(2)}) %collective-permute-start.22) | collective-permute-done | bytes 327712 | tf_op jit(solution)/shard_map/while/body/ppermute | solution.py:432
  173.3 7.3 %collective-permute-done.23.refs_15_ = bf16[4,320,128]{2,1,0:T(8,128)(2,1)S(1)} collective-permute-done((bf16[4,320,128]{2,1,0:T(8,128)(2,1)S(1)}, bf16[4,320,128]{2,1,0:T(8,128)(2,1)S(1)}, u32[]{:S(2)}, u32[]{:S(2)}) %collective-permute-start.23) | collective-permute-done | bytes 327712 | tf_op jit(solution)/shard_map/while/body/ppermute | solution.py:432
  181.3 18.5 %dimers.3 = (bf16[8,72,128]{2,1,0:T(8,128)(2,1)}, bf16[8,72,128]{2,1,0:T(8,128)(2,1)}, bf16[8,72,128]{2,1,0:T(8,128)(2,1)}, bf16[8,72,128]{2,1,0:T(8,128)(2,1)},...) custom-call(s32[128]{0:T(128)} %pad_add_fusion.refs_0_.table_ref, ...), custom_call_target="tpu_custom_call" | custom-call | flops 16000000000 | bytes 6000000 | tf_op jit(solution)/shard_map/while/body/dimers/pallas_call | solution.py:225
  201.8 3.2 collective-permute-start.42
  209.1 3.5 %pack.13 = (bf16[2,320,128]{2,1,0:T(8,128)(2,1)}, bf16[2,320,128]{2,1,0:T(8,128)(2,1)}, bf16[2,320,128]{2,1,0:T(8,128)(2,1)}, bf16[2,320,128]{2,1,0:T(8,128)(2,1...) custom-call(s32[128]{0:T(128)} %pad_add_fusion.refs_0_.table_ref, ...), custom_call_target="tpu_custom_call" | custom-call | tf_op jit(solution)/shard_map/while/body/pack/pallas_call | solution.py:68
  214.3 4.0 %collective-permute-done.43.refs_9_ = bf16[8,72,128]{2,1,0:T(8,128)(2,1)S(1)} collective-permute-done((bf16[8,72,128]{2,1,0:T(8,128)(2,1)}, bf16[8,72,128]{2,1,0:T(8,128)(2,1)S(1)}, u32[]{:S(2)}, u32[]{:S(2)}) %collective-permute-start.43) | collective-permute-done | bytes 147488 | tf_op jit(solution)/shard_map/while/body/ppermute | solution.py:432
  218.4 2.8 collective-permute-done.44.refs_10_
  221.8 3.9 %place.4 = bf16[32,72,128]{2,1,0:T(8,128)(2,1)} custom-call(s32[128]{0:T(128)} %pad_add_fusion.refs_0_.table_ref, s32[256]{0:T(256)} %get-tuple-element.316.refs_1_.table_ref, s32[1]{0:T(128)} %get-tuple-element.517.refs_2_.refs_1_.me_ref, bf16[8,72,128]{2,1,0:T(8,128)(2,1)} %get-tuple-element.374.refs_3_, bf16[8,72,128]{2,1,0:T(8,128)(2,1)} %copy-done.15, ...), custom_call_target="tpu_custom_call" | custom-call | tf_op jit(solution)/shard_map/while/body/place/pallas_call | solution.py:95
  225.8 8.0 %all-to-all-start.2 = ((bf16[32,72,128]{2,1,0:T(8,128)(2,1)}), bf16[32,72,128]{2,1,0:T(8,128)(2,1)S(1)}, u32[]{:S(2)}, u32[]{:S(2)}) async-start(bf16[32,72,128]{2,1,0:T(8,128)(2,1)} %place.4), calls=%async_computation.2 | async-start | bytes 1179648 | tf_op jit(solution)/shard_map/while/body/all_to_all | solution.py:446
  233.9 3.4 %collective-permute-start.27 = (bf16[2,320,128]{2,1,0:T(8,128)(2,1)S(1)}, bf16[2,320,128]{2,1,0:T(8,128)(2,1)S(1)}, u32[]{:S(2)}, u32[]{:S(2)}) collective-permute-start(bf16[2,320,128]{2,1,0:T(8,128)(2,1)S(1)} %copy-done.49), channel_id=1, source_target_pairs={{0,4},{1,5},{2,6},{3,7},{4,0},{5,1},{6,2},{7,3},{8,12},{9,13},{10,... | collective-permute-start | bytes 491528 | tf_op jit(solution)/shard_map/while/body/ppermute | solution.py:432
  240.8 4.9 %collective-permute-done.27.refs_12_ = bf16[2,320,128]{2,1,0:T(8,128)(2,1)S(1)} collective-permute-done((bf16[2,320,128]{2,1,0:T(8,128)(2,1)S(1)}, bf16[2,320,128]{2,1,0:T(8,128)(2,1)S(1)}, u32[]{:S(2)}, u32[]{:S(2)}) %collective-permute-start.27) | collective-permute-done | bytes 163872 | tf_op jit(solution)/shard_map/while/body/ppermute | solution.py:432
  245.7 3.8 %collective-permute-done.28.refs_13_ = bf16[2,320,128]{2,1,0:T(8,128)(2,1)S(1)} collective-permute-done((bf16[2,320,128]{2,1,0:T(8,128)(2,1)S(1)}, bf16[2,320,128]{2,1,0:T(8,128)(2,1)S(1)}, u32[]{:S(2)}, u32[]{:S(2)}) %collective-permute-start.28) | collective-permute-done | bytes 163872 | tf_op jit(solution)/shard_map/while/body/ppermute | solution.py:432
  249.5 3.5 %collective-permute-done.29.refs_14_ = bf16[2,320,128]{2,1,0:T(8,128)(2,1)S(1)} collective-permute-done((bf16[2,320,128]{2,1,0:T(8,128)(2,1)S(1)}, bf16[2,320,128]{2,1,0:T(8,128)(2,1)S(1)}, u32[]{:S(2)}, u32[]{:S(2)}) %collective-permute-start.29) | collective-permute-done | bytes 163872 | tf_op jit(solution)/shard_map/while/body/ppermute | solution.py:432
  253.0 2.4 collective-permute-done.30.refs_15_
  256.1 11.0 %dimers.2 = (bf16[4,72,128]{2,1,0:T(8,128)(2,1)}, bf16[4,72,128]{2,1,0:T(8,128)(2,1)}, bf16[4,72,128]{2,1,0:T(8,128)(2,1)}, bf16[4,72,128]{2,1,0:T(8,128)(2,1)},...) custom-call(s32[256]{0:T(256)} %get-tuple-element.316.refs_1_.table_, ...), custom_call_target="tpu_custom_call" | custom-call | flops 8000000000 | bytes 3000000 | tf_op jit(solution)/shard_map/while/body/dimers/pallas_call | solution.py:225
  267.1 3.9 %collective-permute-start.31 = (bf16[4,72,128]{2,1,0:T(8,128)(2,1)}, bf16[4,72,128]{2,1,0:T(8,128)(2,1)S(1)}, u32[]{:S(2)}, u32[]{:S(2)}) collective-permute-start(bf16[4,72,128]{2,1,0:T(8,128)(2,1)} %get-tuple-element.359), channel_id=1, source_target_pairs={{0,1},{1,0},{2,3},{3,2},{4,5},{5,4},{6,7},{7,6},{8,9},{9,8},{10,11... | collective-permute-start | bytes 221192 | tf_op jit(solution)/shard_map/while/body/ppermute | solution.py:432
  272.5 3.5 %collective-permute-start.35 = (bf16[4,72,128]{2,1,0:T(8,128)(2,1)}, bf16[4,72,128]{2,1,0:T(8,128)(2,1)S(1)}, u32[]{:S(2)}, u32[]{:S(2)}) collective-permute-start(bf16[4,72,128]{2,1,0:T(8,128)(2,1)} %get-tuple-element.363), channel_id=1, source_target_pairs={{0,5},{1,4},{2,7},{3,6},{4,1},{5,0},{6,3},{7,2},{8,13},{9,12},{10,... | collective-permute-start | bytes 221192 | tf_op jit(solution)/shard_map/while/body/ppermute | solution.py:432
  276.4 2.3 collective-permute-start.37
  280.4 2.2 collective-permute-done.36.refs_9_.refs_17_
  284.1 2.6 place.3
  286.7 9.1 %all-to-all-start.3 = ((bf16[16,72,128]{2,1,0:T(8,128)(2,1)}), bf16[16,72,128]{2,1,0:T(8,128)(2,1)S(1)}, u32[]{:S(2)}, u32[]{:S(2)}) async-start(bf16[16,72,128]{2,1,0:T(8,128)(2,1)} %place.3), calls=%async_computation.3 | async-start | bytes 589824 | tf_op jit(solution)/shard_map/while/body/all_to_all | solution.py:442
  296.4 10.9 %all-to-all-done.3.refs_11_.refs_3_ = bf16[16,72,128]{2,1,0:T(8,128)(2,1)S(1)} async-done(((bf16[16,72,128]{2,1,0:T(8,128)(2,1)}), bf16[16,72,128]{2,1,0:T(8,128)(2,1)S(1)}, u32[]{:S(2)}, u32[]{:S(2)}) %all-to-all-start.3) | async-done | bytes 294944 | tf_op jit(solution)/shard_map/while/body/all_to_all | solution.py:442
  308.1 3.6 %place.5 = (bf16[6,72,128]{2,1,0:T(8,128)(2,1)}, bf16[6,72,128]{2,1,0:T(8,128)(2,1)}, bf16[6,72,128]{2,1,0:T(8,128)(2,1)}) custom-call(s32[128]{0:T(128)} %pad_add_fusion.refs_0_.table_ref, s32[256]{0:T(256)} %get-tuple-element.316.refs_1_.table_ref, s32[1]{0:T(128)} %get-tuple-element.517.refs_2_.refs_1_.me_ref, ...), custom_call_target="tpu_custom_call" | custom-call | tf_op jit(solution)/shard_map/while/body/place/pallas_call | solution.py:95
  312.4 7.0 %collective-permute-start.46 = (bf16[6,72,128]{2,1,0:T(8,128)(2,1)}, bf16[6,72,128]{2,1,0:T(8,128)(2,1)S(1)}, u32[]{:S(2)}, u32[]{:S(2)}) collective-permute-start(bf16[6,72,128]{2,1,0:T(8,128)(2,1)} %get-tuple-element.384), channel_id=1, source_target_pairs={{0,128},{8,136},{16,144},{24,152},{32,160},{40,168},{48,176},{56,1... | collective-permute-start | bytes 331784 | tf_op jit(solution)/shard_map/while/body/ppermute | solution.py:437
  321.5 5.2 %add_up.2 = (f32[32,32,256]{2,1,0:T(8,128)S(1)}, f32[32,128]{1,0:T(8,128)S(1)}) custom-call(s32[128]{0:T(128)} %pad_add_fusion.refs_0_.table_ref, s32[256]{0:T(256)} %get-tuple-element.316.refs_1_.table_ref, s32[1]{0:T(128)} %get-tuple-element.517.refs_2_.refs_1_.me_ref, ...), custom_call_target="tpu_custom_call", output_to_operand_aliasing={{0}: (20, {}), {1}: (21, {})} | custom-call | tf_op jit(solution)/shard_map/while/body/add_up/pallas_call | solution.py:124
  (222 shorter events, 63.0 us)
Async XLA Ops:
  12.8 19.8 %all-to-all-start.5 = ((s32[32,1,128]{2,1,0:T(1,128)}), s32[32,1,128]{2,1,0:T(1,128)S(1)}, u32[]{:S(2)}, u32[]{:S(2)}) async-start(s32[32,1,128]{2,1,0:T(1,128)} %broadcast_in_dim.143), calls=%async_computation.5 | async-start | bytes 32768 | tf_op jit(solution)/shard_map/all_to_all | solution.py:446
  39.1 80.9 %all-to-all-start = ((bf16[32,320,128]{2,1,0:T(8,128)(2,1)}), bf16[32,320,128]{2,1,0:T(8,128)(2,1)}, u32[]{:S(2)}, u32[]{:S(2)}) async-start(bf16[32,320,128]{2,1,0:T(8,128)(2,1)} %pack.10), calls=%async_computation | async-start | bytes 5242880 | tf_op jit(solution)/shard_map/while/body/all_to_all | solution.py:446
  76.5 8.1 %collective-permute-start = (bf16[2,320,128]{2,1,0:T(8,128)(2,1)}, bf16[2,320,128]{2,1,0:T(8,128)(2,1)S(1)}, u32[]{:S(2)}, u32[]{:S(2)}) collective-permute-start(bf16[2,320,128]{2,1,0:T(8,128)(2,1)} %get-tuple-element.321), channel_id=1, source_target_pairs={{0,1},{1,0},{2,3},{3,2},{4,5},{5,4},{6,7},{7,6},{8,9},{9,8},{10,11... | collective-permute-start | bytes 491528 | tf_op jit(solution)/shard_map/while/body/ppermute | solution.py:432
  76.5 8.7 %collective-permute-start.1 = (bf16[2,320,128]{2,1,0:T(8,128)(2,1)}, bf16[2,320,128]{2,1,0:T(8,128)(2,1)S(1)}, u32[]{:S(2)}, u32[]{:S(2)}) collective-permute-start(bf16[2,320,128]{2,1,0:T(8,128)(2,1)} %get-tuple-element.322), channel_id=1, source_target_pairs={{0,2},{1,3},{2,0},{3,1},{4,6},{5,7},{6,4},{7,5},{8,10},{9,11},{10,... | collective-permute-start | bytes 491528 | tf_op jit(solution)/shard_map/while/body/ppermute | solution.py:432
  77.1 9.2 %collective-permute-start.2 = (bf16[2,320,128]{2,1,0:T(8,128)(2,1)}, bf16[2,320,128]{2,1,0:T(8,128)(2,1)S(1)}, u32[]{:S(2)}, u32[]{:S(2)}) collective-permute-start(bf16[2,320,128]{2,1,0:T(8,128)(2,1)} %get-tuple-element.323), channel_id=1, source_target_pairs={{0,3},{1,2},{2,1},{3,0},{4,7},{5,6},{6,5},{7,4},{8,11},{9,10},{10,... | collective-permute-start | bytes 491528 | tf_op jit(solution)/shard_map/while/body/ppermute | solution.py:432
  78.4 13.2 %collective-permute-start.3 = (bf16[2,320,128]{2,1,0:T(8,128)(2,1)}, bf16[2,320,128]{2,1,0:T(8,128)(2,1)}, u32[]{:S(2)}, u32[]{:S(2)}) collective-permute-start(bf16[2,320,128]{2,1,0:T(8,128)(2,1)} %get-tuple-element.324), channel_id=1, source_target_pairs={{0,4},{1,5},{2,6},{3,7},{4,0},{5,1},{6,2},{7,3},{8,12},{9,13},{10,... | collective-permute-start | bytes 491528 | tf_op jit(solution)/shard_map/while/body/ppermute | solution.py:432
  79.6 15.1 %collective-permute-start.4 = (bf16[2,320,128]{2,1,0:T(8,128)(2,1)}, bf16[2,320,128]{2,1,0:T(8,128)(2,1)}, u32[]{:S(2)}, u32[]{:S(2)}) collective-permute-start(bf16[2,320,128]{2,1,0:T(8,128)(2,1)} %get-tuple-element.325), channel_id=1, source_target_pairs={{0,5},{1,4},{2,7},{3,6},{4,1},{5,0},{6,3},{7,2},{8,13},{9,12},{10,... | collective-permute-start | bytes 491528 | tf_op jit(solution)/shard_map/while/body/ppermute | solution.py:432
  84.7 18.4 %collective-permute-start.10 = (bf16[4,320,128]{2,1,0:T(8,128)(2,1)}, bf16[4,320,128]{2,1,0:T(8,128)(2,1)S(1)}, u32[]{:S(2)}, u32[]{:S(2)}) collective-permute-start(bf16[4,320,128]{2,1,0:T(8,128)(2,1)} %get-tuple-element.332), channel_id=1, source_target_pairs={{0,1},{1,0},{2,3},{3,2},{4,5},{5,4},{6,7},{7,6},{8,9},{9,8},{10,11... | collective-permute-start | bytes 983048 | tf_op jit(solution)/shard_map/while/body/ppermute | solution.py:432
  85.2 20.9 %collective-permute-start.11 = (bf16[4,320,128]{2,1,0:T(8,128)(2,1)}, bf16[4,320,128]{2,1,0:T(8,128)(2,1)}, u32[]{:S(2)}, u32[]{:S(2)}) collective-permute-start(bf16[4,320,128]{2,1,0:T(8,128)(2,1)} %get-tuple-element.333), channel_id=1, source_target_pairs={{0,2},{1,3},{2,0},{3,1},{4,6},{5,7},{6,4},{7,5},{8,10},{9,11},{10,... | collective-permute-start | bytes 983048 | tf_op jit(solution)/shard_map/while/body/ppermute | solution.py:432
  86.4 11.7 %collective-permute-start.5 = (bf16[2,320,128]{2,1,0:T(8,128)(2,1)}, bf16[2,320,128]{2,1,0:T(8,128)(2,1)}, u32[]{:S(2)}, u32[]{:S(2)}) collective-permute-start(bf16[2,320,128]{2,1,0:T(8,128)(2,1)} %get-tuple-element.326), channel_id=1, source_target_pairs={{0,6},{1,7},{2,4},{3,5},{4,2},{5,3},{6,0},{7,1},{8,14},{9,15},{10,... | collective-permute-start | bytes 491528 | tf_op jit(solution)/shard_map/while/body/ppermute | solution.py:432
  91.6 10.0 %collective-permute-start.6 = (bf16[2,320,128]{2,1,0:T(8,128)(2,1)}, bf16[2,320,128]{2,1,0:T(8,128)(2,1)}, u32[]{:S(2)}, u32[]{:S(2)}) collective-permute-start(bf16[2,320,128]{2,1,0:T(8,128)(2,1)} %get-tuple-element.327), channel_id=1, source_target_pairs={{0,7},{1,6},{2,5},{3,4},{4,3},{5,2},{6,1},{7,0},{8,15},{9,14},{10,... | collective-permute-start | bytes 491528 | tf_op jit(solution)/shard_map/while/body/ppermute | solution.py:432
  94.7 23.7 %collective-permute-start.7 = (bf16[6,320,128]{2,1,0:T(8,128)(2,1)}, bf16[6,320,128]{2,1,0:T(8,128)(2,1)S(1)}, u32[]{:S(2)}, u32[]{:S(2)}) collective-permute-start(bf16[6,320,128]{2,1,0:T(8,128)(2,1)} %get-tuple-element.328), channel_id=1, source_target_pairs={{0,64},{8,72},{16,80},{24,88},{32,96},{40,104},{48,112},{56,120},{... | collective-permute-start | bytes 1474568 | tf_op jit(solution)/shard_map/while/body/ppermute | solution.py:437
  98.1 9.9 %collective-permute-start.12 = (bf16[4,320,128]{2,1,0:T(8,128)(2,1)}, bf16[4,320,128]{2,1,0:T(8,128)(2,1)S(1)}, u32[]{:S(2)}, u32[]{:S(2)}) collective-permute-start(bf16[4,320,128]{2,1,0:T(8,128)(2,1)} %get-tuple-element.334), channel_id=1, source_target_pairs={{0,3},{1,2},{2,1},{3,0},{4,7},{5,6},{6,5},{7,4},{8,11},{9,10},{10,... | collective-permute-start | bytes 983048 | tf_op jit(solution)/shard_map/while/body/ppermute | solution.py:432
  101.6 15.5 %collective-permute-start.13 = (bf16[4,320,128]{2,1,0:T(8,128)(2,1)}, bf16[4,320,128]{2,1,0:T(8,128)(2,1)S(1)}, u32[]{:S(2)}, u32[]{:S(2)}) collective-permute-start(bf16[4,320,128]{2,1,0:T(8,128)(2,1)} %get-tuple-element.335), channel_id=1, source_target_pairs={{0,4},{1,5},{2,6},{3,7},{4,0},{5,1},{6,2},{7,3},{8,12},{9,13},{10,... | collective-permute-start | bytes 983048 | tf_op jit(solution)/shard_map/while/body/ppermute | solution.py:432
  103.1 20.9 %collective-permute-start.8 = (bf16[6,320,128]{2,1,0:T(8,128)(2,1)}, bf16[6,320,128]{2,1,0:T(8,128)(2,1)}, u32[]{:S(2)}, u32[]{:S(2)}) collective-permute-start(bf16[6,320,128]{2,1,0:T(8,128)(2,1)} %get-tuple-element.329), channel_id=1, source_target_pairs={{0,128},{8,136},{16,144},{24,152},{32,160},{40,168},{48,176},{56,1... | collective-permute-start | bytes 1474568 | tf_op jit(solution)/shard_map/while/body/ppermute | solution.py:437
  106.2 24.8 %collective-permute-start.9 = (bf16[6,320,128]{2,1,0:T(8,128)(2,1)}, bf16[6,320,128]{2,1,0:T(8,128)(2,1)}, u32[]{:S(2)}, u32[]{:S(2)}) collective-permute-start(bf16[6,320,128]{2,1,0:T(8,128)(2,1)} %get-tuple-element.330), channel_id=1, source_target_pairs={{0,192},{8,200},{16,208},{24,216},{32,224},{40,232},{48,240},{56,2... | collective-permute-start | bytes 1474568 | tf_op jit(solution)/shard_map/while/body/ppermute | solution.py:437
  108.0 27.4 %collective-permute-start.14 = (bf16[4,320,128]{2,1,0:T(8,128)(2,1)}, bf16[4,320,128]{2,1,0:T(8,128)(2,1)}, u32[]{:S(2)}, u32[]{:S(2)}) collective-permute-start(bf16[4,320,128]{2,1,0:T(8,128)(2,1)} %get-tuple-element.336), channel_id=1, source_target_pairs={{0,5},{1,4},{2,7},{3,6},{4,1},{5,0},{6,3},{7,2},{8,13},{9,12},{10,... | collective-permute-start | bytes 983048 | tf_op jit(solution)/shard_map/while/body/ppermute | solution.py:432
  117.2 18.3 %collective-permute-start.15 = (bf16[4,320,128]{2,1,0:T(8,128)(2,1)}, bf16[4,320,128]{2,1,0:T(8,128)(2,1)}, u32[]{:S(2)}, u32[]{:S(2)}) collective-permute-start(bf16[4,320,128]{2,1,0:T(8,128)(2,1)} %get-tuple-element.337), channel_id=1, source_target_pairs={{0,6},{1,7},{2,4},{3,5},{4,2},{5,3},{6,0},{7,1},{8,14},{9,15},{10,... | collective-permute-start | bytes 983048 | tf_op jit(solution)/shard_map/while/body/ppermute | solution.py:432
  118.4 19.6 %collective-permute-start.16 = (bf16[4,320,128]{2,1,0:T(8,128)(2,1)}, bf16[4,320,128]{2,1,0:T(8,128)(2,1)}, u32[]{:S(2)}, u32[]{:S(2)}) collective-permute-start(bf16[4,320,128]{2,1,0:T(8,128)(2,1)} %get-tuple-element.338), channel_id=1, source_target_pairs={{0,7},{1,6},{2,5},{3,4},{4,3},{5,2},{6,1},{7,0},{8,15},{9,14},{10,... | collective-permute-start | bytes 983048 | tf_op jit(solution)/shard_map/while/body/ppermute | solution.py:432
  124.0 23.7 %collective-permute-start.17 = (bf16[4,320,128]{2,1,0:T(8,128)(2,1)}, bf16[4,320,128]{2,1,0:T(8,128)(2,1)}, u32[]{:S(2)}, u32[]{:S(2)}) collective-permute-start(bf16[4,320,128]{2,1,0:T(8,128)(2,1)} %get-tuple-element.342), channel_id=1, source_target_pairs={{0,1},{1,0},{2,3},{3,2},{4,5},{5,4},{6,7},{7,6},{8,9},{9,8},{10,11... | collective-permute-start | bytes 983048 | tf_op jit(solution)/shard_map/while/body/ppermute | solution.py:432
  130.9 18.8 %collective-permute-start.18 = (bf16[4,320,128]{2,1,0:T(8,128)(2,1)}, bf16[4,320,128]{2,1,0:T(8,128)(2,1)}, u32[]{:S(2)}, u32[]{:S(2)}) collective-permute-start(bf16[4,320,128]{2,1,0:T(8,128)(2,1)} %get-tuple-element.343), channel_id=1, source_target_pairs={{0,2},{1,3},{2,0},{3,1},{4,6},{5,7},{6,4},{7,5},{8,10},{9,11},{10,... | collective-permute-start | bytes 983048 | tf_op jit(solution)/shard_map/while/body/ppermute | solution.py:432
  137.9 70.1 %all-to-all-start.1 = ((bf16[16,320,128]{2,1,0:T(8,128)(2,1)}), bf16[16,320,128]{2,1,0:T(8,128)(2,1)S(1)}, u32[]{:S(2)}, u32[]{:S(2)}) async-start(bf16[16,320,128]{2,1,0:T(8,128)(2,1)} %pack.9), calls=%async_computation.1 | async-start | bytes 2621440 | tf_op jit(solution)/shard_map/while/body/all_to_all | solution.py:442
  145.2 10.0 %collective-permute-start.19 = (bf16[4,320,128]{2,1,0:T(8,128)(2,1)S(1)}, bf16[4,320,128]{2,1,0:T(8,128)(2,1)S(1)}, u32[]{:S(2)}, u32[]{:S(2)}) collective-permute-start(bf16[4,320,128]{2,1,0:T(8,128)(2,1)S(1)} %copy-done.35), channel_id=1, source_target_pairs={{0,3},{1,2},{2,1},{3,0},{4,7},{5,6},{6,5},{7,4},{8,11},{9,10},{10,... | collective-permute-start | bytes 983048 | tf_op jit(solution)/shard_map/while/body/ppermute | solution.py:432
  145.2 17.2 %collective-permute-start.20 = (bf16[4,320,128]{2,1,0:T(8,128)(2,1)S(1)}, bf16[4,320,128]{2,1,0:T(8,128)(2,1)S(1)}, u32[]{:S(2)}, u32[]{:S(2)}) collective-permute-start(bf16[4,320,128]{2,1,0:T(8,128)(2,1)S(1)} %copy-done.34), channel_id=1, source_target_pairs={{0,4},{1,5},{2,6},{3,7},{4,0},{5,1},{6,2},{7,3},{8,12},{9,13},{10,... | collective-permute-start | bytes 983048 | tf_op jit(solution)/shard_map/while/body/ppermute | solution.py:432
  147.0 22.7 %collective-permute-start.21 = (bf16[4,320,128]{2,1,0:T(8,128)(2,1)S(1)}, bf16[4,320,128]{2,1,0:T(8,128)(2,1)S(1)}, u32[]{:S(2)}, u32[]{:S(2)}) collective-permute-start(bf16[4,320,128]{2,1,0:T(8,128)(2,1)S(1)} %copy-done.33), channel_id=1, source_target_pairs={{0,5},{1,4},{2,7},{3,6},{4,1},{5,0},{6,3},{7,2},{8,13},{9,12},{10,... | collective-permute-start | bytes 983048 | tf_op jit(solution)/shard_map/while/body/ppermute | solution.py:432
  147.7 25.6 %collective-permute-start.22 = (bf16[4,320,128]{2,1,0:T(8,128)(2,1)S(1)}, bf16[4,320,128]{2,1,0:T(8,128)(2,1)S(1)}, u32[]{:S(2)}, u32[]{:S(2)}) collective-permute-start(bf16[4,320,128]{2,1,0:T(8,128)(2,1)S(1)} %copy-done.32), channel_id=1, source_target_pairs={{0,6},{1,7},{2,4},{3,5},{4,2},{5,3},{6,0},{7,1},{8,14},{9,15},{10,... | collective-permute-start | bytes 983048 | tf_op jit(solution)/shard_map/while/body/ppermute | solution.py:432
  149.7 30.9 %collective-permute-start.23 = (bf16[4,320,128]{2,1,0:T(8,128)(2,1)S(1)}, bf16[4,320,128]{2,1,0:T(8,128)(2,1)S(1)}, u32[]{:S(2)}, u32[]{:S(2)}) collective-permute-start(bf16[4,320,128]{2,1,0:T(8,128)(2,1)S(1)} %copy-done.31), channel_id=1, source_target_pairs={{0,7},{1,6},{2,5},{3,4},{4,3},{5,2},{6,1},{7,0},{8,15},{9,14},{10,... | collective-permute-start | bytes 983048 | tf_op jit(solution)/shard_map/while/body/ppermute | solution.py:432
  200.0 7.0 %collective-permute-start.39 = (bf16[8,72,128]{2,1,0:T(8,128)(2,1)}, bf16[8,72,128]{2,1,0:T(8,128)(2,1)S(1)}, u32[]{:S(2)}, u32[]{:S(2)}) collective-permute-start(bf16[8,72,128]{2,1,0:T(8,128)(2,1)} %get-tuple-element.368), channel_id=1, source_target_pairs={{0,2},{1,3},{2,0},{3,1},{4,6},{5,7},{6,4},{7,5},{8,10},{9,11},{10,... | collective-permute-start | bytes 442376 | tf_op jit(solution)/shard_map/while/body/ppermute | solution.py:432
  200.1 12.6 %collective-permute-start.40 = (bf16[8,72,128]{2,1,0:T(8,128)(2,1)}, bf16[8,72,128]{2,1,0:T(8,128)(2,1)S(1)}, u32[]{:S(2)}, u32[]{:S(2)}) collective-permute-start(bf16[8,72,128]{2,1,0:T(8,128)(2,1)} %get-tuple-element.369), channel_id=1, source_target_pairs={{0,3},{1,2},{2,1},{3,0},{4,7},{5,6},{6,5},{7,4},{8,11},{9,10},{10,... | collective-permute-start | bytes 442376 | tf_op jit(solution)/shard_map/while/body/ppermute | solution.py:432
  201.8 11.3 %collective-permute-start.41 = (bf16[8,72,128]{2,1,0:T(8,128)(2,1)}, bf16[8,72,128]{2,1,0:T(8,128)(2,1)S(1)}, u32[]{:S(2)}, u32[]{:S(2)}) collective-permute-start(bf16[8,72,128]{2,1,0:T(8,128)(2,1)} %get-tuple-element.370), channel_id=1, source_target_pairs={{0,4},{1,5},{2,6},{3,7},{4,0},{5,1},{6,2},{7,3},{8,12},{9,13},{10,... | collective-permute-start | bytes 442376 | tf_op jit(solution)/shard_map/while/body/ppermute | solution.py:432
  201.8 12.5 %collective-permute-start.42 = (bf16[8,72,128]{2,1,0:T(8,128)(2,1)}, bf16[8,72,128]{2,1,0:T(8,128)(2,1)S(1)}, u32[]{:S(2)}, u32[]{:S(2)}) collective-permute-start(bf16[8,72,128]{2,1,0:T(8,128)(2,1)} %get-tuple-element.371), channel_id=1, source_target_pairs={{0,5},{1,4},{2,7},{3,6},{4,1},{5,0},{6,3},{7,2},{8,13},{9,12},{10,... | collective-permute-start | bytes 442376 | tf_op jit(solution)/shard_map/while/body/ppermute | solution.py:432
  205.1 13.3 %collective-permute-start.43 = (bf16[8,72,128]{2,1,0:T(8,128)(2,1)}, bf16[8,72,128]{2,1,0:T(8,128)(2,1)S(1)}, u32[]{:S(2)}, u32[]{:S(2)}) collective-permute-start(bf16[8,72,128]{2,1,0:T(8,128)(2,1)} %get-tuple-element.372), channel_id=1, source_target_pairs={{0,6},{1,7},{2,4},{3,5},{4,2},{5,3},{6,0},{7,1},{8,14},{9,15},{10,... | collective-permute-start | bytes 442376 | tf_op jit(solution)/shard_map/while/body/ppermute | solution.py:432
  207.0 14.2 %collective-permute-start.44 = (bf16[8,72,128]{2,1,0:T(8,128)(2,1)}, bf16[8,72,128]{2,1,0:T(8,128)(2,1)S(1)}, u32[]{:S(2)}, u32[]{:S(2)}) collective-permute-start(bf16[8,72,128]{2,1,0:T(8,128)(2,1)} %get-tuple-element.373), channel_id=1, source_target_pairs={{0,7},{1,6},{2,5},{3,4},{4,3},{5,2},{6,1},{7,0},{8,15},{9,14},{10,... | collective-permute-start | bytes 442376 | tf_op jit(solution)/shard_map/while/body/ppermute | solution.py:432
  212.7 25.3 %collective-permute-start.24 = (bf16[2,320,128]{2,1,0:T(8,128)(2,1)}, bf16[2,320,128]{2,1,0:T(8,128)(2,1)S(1)}, u32[]{:S(2)}, u32[]{:S(2)}) collective-permute-start(bf16[2,320,128]{2,1,0:T(8,128)(2,1)} %get-tuple-element.351), channel_id=1, source_target_pairs={{0,1},{1,0},{2,3},{3,2},{4,5},{5,4},{6,7},{7,6},{8,9},{9,8},{10,11... | collective-permute-start | bytes 491528 | tf_op jit(solution)/shard_map/while/body/ppermute | solution.py:432
  213.1 26.2 %collective-permute-start.25 = (bf16[2,320,128]{2,1,0:T(8,128)(2,1)}, bf16[2,320,128]{2,1,0:T(8,128)(2,1)S(1)}, u32[]{:S(2)}, u32[]{:S(2)}) collective-permute-start(bf16[2,320,128]{2,1,0:T(8,128)(2,1)} %get-tuple-element.352), channel_id=1, source_target_pairs={{0,2},{1,3},{2,0},{3,1},{4,6},{5,7},{6,4},{7,5},{8,10},{9,11},{10,... | collective-permute-start | bytes 491528 | tf_op jit(solution)/shard_map/while/body/ppermute | solution.py:432
  225.8 60.9 %all-to-all-start.2 = ((bf16[32,72,128]{2,1,0:T(8,128)(2,1)}), bf16[32,72,128]{2,1,0:T(8,128)(2,1)S(1)}, u32[]{:S(2)}, u32[]{:S(2)}) async-start(bf16[32,72,128]{2,1,0:T(8,128)(2,1)} %place.4), calls=%async_computation.2 | async-start | bytes 1179648 | tf_op jit(solution)/shard_map/while/body/all_to_all | solution.py:446
  233.9 11.8 %collective-permute-start.27 = (bf16[2,320,128]{2,1,0:T(8,128)(2,1)S(1)}, bf16[2,320,128]{2,1,0:T(8,128)(2,1)S(1)}, u32[]{:S(2)}, u32[]{:S(2)}) collective-permute-start(bf16[2,320,128]{2,1,0:T(8,128)(2,1)S(1)} %copy-done.49), channel_id=1, source_target_pairs={{0,4},{1,5},{2,6},{3,7},{4,0},{5,1},{6,2},{7,3},{8,12},{9,13},{10,... | collective-permute-start | bytes 491528 | tf_op jit(solution)/shard_map/while/body/ppermute | solution.py:432
  237.3 12.2 %collective-permute-start.28 = (bf16[2,320,128]{2,1,0:T(8,128)(2,1)S(1)}, bf16[2,320,128]{2,1,0:T(8,128)(2,1)S(1)}, u32[]{:S(2)}, u32[]{:S(2)}) collective-permute-start(bf16[2,320,128]{2,1,0:T(8,128)(2,1)S(1)} %copy-done.48), channel_id=1, source_target_pairs={{0,5},{1,4},{2,7},{3,6},{4,1},{5,0},{6,3},{7,2},{8,13},{9,12},{10,... | collective-permute-start | bytes 491528 | tf_op jit(solution)/shard_map/while/body/ppermute | solution.py:432
  238.0 15.0 %collective-permute-start.29 = (bf16[2,320,128]{2,1,0:T(8,128)(2,1)S(1)}, bf16[2,320,128]{2,1,0:T(8,128)(2,1)S(1)}, u32[]{:S(2)}, u32[]{:S(2)}) collective-permute-start(bf16[2,320,128]{2,1,0:T(8,128)(2,1)S(1)} %copy-done.47), channel_id=1, source_target_pairs={{0,6},{1,7},{2,4},{3,5},{4,2},{5,3},{6,0},{7,1},{8,14},{9,15},{10,... | collective-permute-start | bytes 491528 | tf_op jit(solution)/shard_map/while/body/ppermute | solution.py:432
  239.4 16.0 %collective-permute-start.30 = (bf16[2,320,128]{2,1,0:T(8,128)(2,1)S(1)}, bf16[2,320,128]{2,1,0:T(8,128)(2,1)S(1)}, u32[]{:S(2)}, u32[]{:S(2)}) collective-permute-start(bf16[2,320,128]{2,1,0:T(8,128)(2,1)S(1)} %copy-done.46), channel_id=1, source_target_pairs={{0,7},{1,6},{2,5},{3,4},{4,3},{5,2},{6,1},{7,0},{8,15},{9,14},{10,... | collective-permute-start | bytes 491528 | tf_op jit(solution)/shard_map/while/body/ppermute | solution.py:432
  267.1 8.9 %collective-permute-start.31 = (bf16[4,72,128]{2,1,0:T(8,128)(2,1)}, bf16[4,72,128]{2,1,0:T(8,128)(2,1)S(1)}, u32[]{:S(2)}, u32[]{:S(2)}) collective-permute-start(bf16[4,72,128]{2,1,0:T(8,128)(2,1)} %get-tuple-element.359), channel_id=1, source_target_pairs={{0,1},{1,0},{2,3},{3,2},{4,5},{5,4},{6,7},{7,6},{8,9},{9,8},{10,11... | collective-permute-start | bytes 221192 | tf_op jit(solution)/shard_map/while/body/ppermute | solution.py:432
  271.0 7.7 %collective-permute-start.33 = (bf16[4,72,128]{2,1,0:T(8,128)(2,1)}, bf16[4,72,128]{2,1,0:T(8,128)(2,1)S(1)}, u32[]{:S(2)}, u32[]{:S(2)}) collective-permute-start(bf16[4,72,128]{2,1,0:T(8,128)(2,1)} %get-tuple-element.361), channel_id=1, source_target_pairs={{0,3},{1,2},{2,1},{3,0},{4,7},{5,6},{6,5},{7,4},{8,11},{9,10},{10,... | collective-permute-start | bytes 221192 | tf_op jit(solution)/shard_map/while/body/ppermute | solution.py:432
  272.5 7.9 %collective-permute-start.35 = (bf16[4,72,128]{2,1,0:T(8,128)(2,1)}, bf16[4,72,128]{2,1,0:T(8,128)(2,1)S(1)}, u32[]{:S(2)}, u32[]{:S(2)}) collective-permute-start(bf16[4,72,128]{2,1,0:T(8,128)(2,1)} %get-tuple-element.363), channel_id=1, source_target_pairs={{0,5},{1,4},{2,7},{3,6},{4,1},{5,0},{6,3},{7,2},{8,13},{9,12},{10,... | collective-permute-start | bytes 221192 | tf_op jit(solution)/shard_map/while/body/ppermute | solution.py:432
  276.4 7.0 %collective-permute-start.37 = (bf16[4,72,128]{2,1,0:T(8,128)(2,1)}, bf16[4,72,128]{2,1,0:T(8,128)(2,1)S(1)}, u32[]{:S(2)}, u32[]{:S(2)}) collective-permute-start(bf16[4,72,128]{2,1,0:T(8,128)(2,1)} %get-tuple-element.365), channel_id=1, source_target_pairs={{0,7},{1,6},{2,5},{3,4},{4,3},{5,2},{6,1},{7,0},{8,15},{9,14},{10,... | collective-permute-start | bytes 221192 | tf_op jit(solution)/shard_map/while/body/ppermute | solution.py:432
  286.7 20.6 %all-to-all-start.3 = ((bf16[16,72,128]{2,1,0:T(8,128)(2,1)}), bf16[16,72,128]{2,1,0:T(8,128)(2,1)S(1)}, u32[]{:S(2)}, u32[]{:S(2)}) async-start(bf16[16,72,128]{2,1,0:T(8,128)(2,1)} %place.3), calls=%async_computation.3 | async-start | bytes 589824 | tf_op jit(solution)/shard_map/while/body/all_to_all | solution.py:442
  311.6 15.1 %collective-permute-start.45 = (bf16[6,72,128]{2,1,0:T(8,128)(2,1)}, bf16[6,72,128]{2,1,0:T(8,128)(2,1)S(1)}, u32[]{:S(2)}, u32[]{:S(2)}) collective-permute-start(bf16[6,72,128]{2,1,0:T(8,128)(2,1)} %get-tuple-element.383), channel_id=1, source_target_pairs={{0,64},{8,72},{16,80},{24,88},{32,96},{40,104},{48,112},{56,120},{... | collective-permute-start | bytes 331784 | tf_op jit(solution)/shard_map/while/body/ppermute | solution.py:437
  312.4 14.4 %collective-permute-start.46 = (bf16[6,72,128]{2,1,0:T(8,128)(2,1)}, bf16[6,72,128]{2,1,0:T(8,128)(2,1)S(1)}, u32[]{:S(2)}, u32[]{:S(2)}) collective-permute-start(bf16[6,72,128]{2,1,0:T(8,128)(2,1)} %get-tuple-element.384), channel_id=1, source_target_pairs={{0,128},{8,136},{16,144},{24,152},{32,160},{40,168},{48,176},{56,1... | collective-permute-start | bytes 331784 | tf_op jit(solution)/shard_map/while/body/ppermute | solution.py:437
  319.4 7.4 %collective-permute-start.47 = (bf16[6,72,128]{2,1,0:T(8,128)(2,1)}, bf16[6,72,128]{2,1,0:T(8,128)(2,1)S(1)}, u32[]{:S(2)}, u32[]{:S(2)}) collective-permute-start(bf16[6,72,128]{2,1,0:T(8,128)(2,1)} %get-tuple-element.385), channel_id=1, source_target_pairs={{0,192},{8,200},{16,208},{24,216},{32,224},{40,232},{48,240},{56,2... | collective-permute-start | bytes 331784 | tf_op jit(solution)/shard_map/while/body/ppermute | solution.py:437
  (61 other events, 770.8 us)

commit v5 on v4

--- a/solution.py
+++ b/solution.py
@@ -281,102 +281,119 @@
     one_dimer(table_ref[STEPS + 2 * me + i], me, load, outs, scratch)
 
 
-def plan_kernel(me_ref, inside_ref, count_ref, list_ref, table_ref, left_ref, to_x, to_z, n_direct, n_third, n_self):
+def plan_kernel(me_ref, inside_ref, count_ref, list_ref, table_ref, left_ref, to_x, to_z, n_direct, n_third, n_self, n_split, room):
     me = me_ref[0]
+    me_x, me_z = me >> 3, me & 7
 
     def clear(n):
-        to_z[n] = 0
-        table_ref[n] = jnp.where(n < STEPS, -1, 0)
+        for i in range(8):
+            to_z[n * 8 + i] = 0
+            table_ref[n * 8 + i] = jnp.where(n < STEPS // 8, -1, 0)
 
     def clear_x(n):
-        to_x[n] = 0
+        for i in range(8):
+            to_x[n * 8 + i] = 0
 
     def clear_c(n):
         n_direct[n] = 0
         n_third[n] = 0
         n_self[n] = 0
-
-    loop(TABLE, clear)
-    loop(128, clear_x)
+        n_split[n] = inside_ref[n]
+        room[n] = 1 + inside_ref[n]
+
+    loop(TABLE // 8, clear)
+    loop(16, clear_x)
     loop(32, clear_c)
 
     def put(at, good, spare, value):
         table_ref[jnp.where(good, at, spare)] = value
 
-    def can(o, c, extra=0):
+    def can(o, c, extra):
+        zo, xc, zc = o & 7, c >> 3, c & 7
+        return (to_x[o * 4 + xc] < KX) & ((zo == zc) | (to_z[xc * 64 + zo * 8 + zc] + extra < KZ))
+
+    def send(o, slot, c, at_x, at_z, n_x, n_z):
         xo, zo, xc, zc = o >> 3, o & 7, c >> 3, c & 7
-        return ((xo == xc) | (to_x[o * 4 + xc] < KX)) & ((zo == zc) | (to_z[xc * 64 + zo * 8 + zc] + extra < KZ))
-
-    def send(o, slot, c):
-        xo, zo, xc, zc = o >> 3, o & 7, c >> 3, c & 7
-        at_x, at_z = o * 4 + xc, xc * 64 + zo * 8 + zc
-        n_x, n_z = to_x[at_x], to_z[at_z]
         move_x, move_z = xo != xc, zo != zc
         to_x[at_x] = n_x + jnp.where(move_x, 1, 0)
         to_z[at_z] = n_z + jnp.where(move_z, 1, 0)
         in_x = (lax.bitwise_xor(xo, xc) - 1) * KX + n_x
-        put(SENT + in_x, move_x & (o == me), SENT + 31, slot)
-        put(RELAY + zc * KZ + n_z, move_z & (xc * 8 + zo == me), RELAY + 31, jnp.where(move_x, 32 + in_x, slot))
+
+        @pl.when(zo == me_z)
+        def _():
+            put(SENT + in_x, move_x & (o == me), SENT + 31, slot)
+            put(RELAY + zc * KZ + n_z, move_z & (xc == me_x), RELAY + 31, jnp.where(move_x, 32 + in_x, slot))
+
         return jnp.where(move_z, 32 + NX + zo * KZ + n_z, 32 + in_x)
 
     def visit(d):
         word = list_ref[d]
-        a, b, cost = word & 1023, (word >> 10) & 1023, word >> 20
-        oa, ob, la, lb = a >> 5, b >> 5, a & 31, b & 31
+        cost = word >> 20
+        la, oa, lb, ob = word & 31, (word >> 5) & 31, (word >> 10) & 31, (word >> 15) & 31
         left_ref[d] = 0
-
-        @pl.when(oa == ob)
+        za, xa, zb, xb = oa & 7, oa >> 3, ob & 7, ob >> 3
+        x_at_a, z_at_a = ob * 4 + xa, xa * 64 + zb * 8 + za
+        x_at_b, z_at_b = oa * 4 + xb, xb * 64 + za * 8 + zb
+        x_a, z_a, x_b, z_b = to_x[x_at_a], to_z[z_at_a], to_x[x_at_b], to_z[z_at_b]
+        room_a, room_b = room[oa], room[ob]
+        can_a = (x_a < KX) & (z_a < KZ) & (room_a <= 8)
+        can_b = (x_b < KX) & (z_b < KZ) & (room_b <= 8)
+        use_a = can_a & (jnp.logical_not(can_b) | (z_a * 4 + room_a <= z_b * 4 + room_b))
+        apart = oa != ob
+        direct = apart & (can_a | can_b)
+
+        @pl.when(direct)
         def _():
-            q = n_self[oa]
-
-            @pl.when(q < 8)
+            c, o = jnp.where(use_a, oa, ob), jnp.where(use_a, ob, oa)
+            stay, move = jnp.where(use_a, la, lb), jnp.where(use_a, lb, la)
+            at = n_direct[c]
+            n_direct[c] = at + 1
+            room[c] = ((at + 3) >> 1) + n_split[c]
+            late = send(
+                o,
+                move,
+                c,
+                jnp.where(use_a, x_at_a, x_at_b),
+                jnp.where(use_a, z_at_a, z_at_b),
+                jnp.where(use_a, x_a, x_b),
+                jnp.where(use_a, z_a, z_b),
+            )
+
+            @pl.when(c == me)
             def _():
-                n_self[oa] = q + 1
-
-                @pl.when(oa == me)
+                table_ref[POS + 2 * at] = stay
+                table_ref[POS + 2 * at + 1] = late
+                table_ref[HOME + at] = stay
+                table_ref[LATE + at] = late
+                table_ref[STEPS + at] = cost
+
+        @pl.when(jnp.logical_not(direct))
+        def _():
+            @pl.when(jnp.logical_not(apart))
+            def _():
+                q = n_self[oa]
+
+                @pl.when(q < 8)
                 def _():
-                    at = 2 * (7 - q)
-                    table_ref[POS + 2 * at + 2] = la
-                    table_ref[POS + 2 * at + 3] = lb
-                    table_ref[HOME + at] = la
-                    table_ref[HOME + at + 1] = lb
-                    table_ref[STEPS + at + 1] = cost
-                    table_ref[MODE + 7 - q] = 1
-
-            @pl.when(q >= 8)
+                    n_self[oa] = q + 1
+
+                    @pl.when(oa == me)
+                    def _():
+                        at = 2 * (7 - q)
+                        table_ref[POS + 2 * at + 2] = la
+                        table_ref[POS + 2 * at + 3] = lb
+                        table_ref[HOME + at] = la
+                        table_ref[HOME + at + 1] = lb
+                        table_ref[STEPS + at + 1] = cost
+                        table_ref[MODE + 7 - q] = 1
+
+                @pl.when(q >= 8)
+                def _():
+                    left_ref[d] = 1
+
+            @pl.when(apart)
             def _():
-                left_ref[d] = 1
-
-        @pl.when(oa != ob)
-        def _():
-            n_a, n_b = n_direct[oa], n_direct[ob]
-            fit_a = ((n_a + 2) >> 1) + jnp.maximum(n_third[oa], inside_ref[oa]) <= 8
-            fit_b = ((n_b + 2) >> 1) + jnp.maximum(n_third[ob], inside_ref[ob]) <= 8
-            can_a, can_b = can(ob, oa) & fit_a, can(oa, ob) & fit_b
-            full_a = to_z[(oa >> 3) * 64 + (ob & 7) * 8 + (oa & 7)] * 4 + n_a
-            full_b = to_z[(ob >> 3) * 64 + (oa & 7) * 8 + (ob & 7)] * 4 + n_b
-            use_a = can_a & (jnp.logical_not(can_b) | (full_a <= full_b))
-            direct = can_a | can_b
-
-            @pl.when(direct)
-            def _():
-                c, o = jnp.where(use_a, oa, ob), jnp.where(use_a, ob, oa)
-                stay, move = jnp.where(use_a, la, lb), jnp.where(use_a, lb, la)
-                at = jnp.where(use_a, n_a, n_b)
-                n_direct[c] = at + 1
-                late = send(o, move, c)
-
-                @pl.when(c == me)
-                def _():
-                    table_ref[POS + 2 * at] = stay
-                    table_ref[POS + 2 * at + 1] = late
-                    table_ref[HOME + at] = stay
-                    table_ref[LATE + at] = late
-                    table_ref[STEPS + at] = cost
-
-            @pl.when(jnp.logical_not(direct))
-            def _():
-                same_z = jnp.where((oa & 7) == (ob & 7), 1, 0)
+                same_z = jnp.where(za == zb, 1, 0)
 
                 def look(carry):
                     n, _ = carry
@@ -397,8 +414,14 @@
                 def _():
                     t = n_third[c]
                     n_third[c] = t + 1
-                    late_a = send(oa, la, c)
-                    late_b = send(ob, lb, c)
+                    split = jnp.maximum(t + 1, inside_ref[c])
+                    n_split[c] = split
+                    room[c] = ((n_direct[c] + 2) >> 1) + split
+                    xc, zc = c >> 3, c & 7
+                    x_at, z_at = oa * 4 + xc, xc * 64 + za * 8 + zc
+                    late_a = send(oa, la, c, x_at, z_at, to_x[x_at], to_z[z_at])
+                    x_at, z_at = ob * 4 + xc, xc * 64 + zb * 8 + zc
+                    late_b = send(ob, lb, c, x_at, z_at, to_x[x_at], to_z[z_at])
 
                     @pl.when(c == me)
                     def _():
@@ -420,7 +443,7 @@
         out_shape=[jax.ShapeDtypeStruct((TABLE,), s32), jax.ShapeDtypeStruct(words.shape, s32)],
         in_specs=[SMEM] * 4,
         out_specs=[SMEM] * 2,
-        scratch_shapes=[pltpu.SMEM((128,), s32), pltpu.SMEM((256,), s32)] + [pltpu.SMEM((32,), s32)] * 3,
+        scratch_shapes=[pltpu.SMEM((128,), s32), pltpu.SMEM((256,), s32)] + [pltpu.SMEM((32,), s32)] * 5,
         name="plan",
         cost_estimate=pl.CostEstimate(flops=1000, bytes_accessed=30_000_000, transcendentals=0),
     )(me, inside_count, count, words)
@@ -531,19 +554,21 @@
             pack(tables[:1], me_b, lambda t, me, n, row: t[0][BASE + served(t, me, n, row)], 8, 4, home, [])
         )
         in_x = along_x(pack(tables, me_b, lambda t, me, n, row: t[1][SENT + n * KX + row], 3, KX, home, []))
-        (out_2,) = pack(tables, me_b, lambda t, me, n, row: t[1][RELAY + row], 1, NZ, home, in_x)
-        in_z = along_z(after(out_2, in_1, home_1))
-        home_2 = exchange(
-            pack(
-                tables, me_b, lambda t, me, n, row: t[1][HOME + 2 * lax.bitwise_xor(me, n) + row], 8, 2, home, []
-            )
+        parts_1 = pack(tables, me_b, served, 8, 4, (), [in_1])
+        away_1 = exchange(parts_1)
+        (out_2,) = pack(
+            tables, me_b, lambda t, me, n, row: t[1][RELAY + row], 1, NZ, home, after(in_x, parts_1)
         )
-
-        away_1 = exchange(pack(tables, me_b, served, 8, 4, (), [after(in_1, home_2)]))
+        in_z = along_z(out_2)
+
+        def home_at(t, me, n, row):
+            return t[1][HOME + 2 * lax.bitwise_xor(me, n) + row]
+
+        home_parts = pack(tuple(after(tables, away_1)), me_b, home_at, 8, 2, home, [])
+        home_2 = exchange(home_parts)
         one = lambda i, *_: (i, 0, 0)
-        done_1 = exchange(
-            run_dimers(kernel_1, 4, (table_1, me_b), (1, 1), (one, one), [*home_1, *away_1])
-        )
+        ready_1 = run_dimers(kernel_1, 4, (table_1, me_b), (1, 1), (one, one), [*home_1, *away_1])
+        done_1 = exchange(ready_1)
 
         late_parts = pack(
             tables,
@@ -600,8 +625,8 @@
         finds = (
             [stay_1(k) for k in range(8)]
             + [stay_2(k) for k in range(8)]
-            + [lambda t, me, row: t[0][OUT + row]]
         )
+        finds += [lambda t, me, row: t[0][OUT + row]]
         dens, emb = add_up(tables, me_b, [*done_1, *done_2, back_1], finds, dens, emb)
         finds = [lambda t, me, row: t[1][RELAY + row]] + [from_x(k) for k in range(3)]
         dens, emb = add_up(tables, me_b, [rest_z, *rest_x], finds, dens, emb)

time: 338 us -> 329 us (0.973)
  starting transfers between devices: 104 us -> 97.2 us
    all_to_all x3, waiting for transfers between devices: 8.57 us -> 31.1 us  [across(): return lax.all_to_all(part, 'frag', split_axis=0, concat_axis=0, tiled=True)]
    ppermute x42, waiting for transfers between devices: 78.7 us -> 63.2 us  [exchange(): got.append(lax.ppermute(parts[k], 'basis', [(i, i ^ k) for i in range(8)]))]
    ppermute x6, waiting for transfers between devices: 5.64 us -> 0.02 us  [along_x(): lax.ppermute(parts[k - 1], 'frag', [(i, i ^ 8 * k) for i in range(32)])]
    pallas_call x1, Pallas kernels: 25 us -> 20.1 us  [plan_rest(): pl.pallas_call(plan_kernel, out_shape=[jax.ShapeDtypeStruct((TABLE,), s32...]
    ppermute x42, starting transfers between devices: 48.7 us -> 43.9 us  [exchange(): got.append(lax.ppermute(parts[k], 'basis', [(i, i ^ k) for i in range(8)]))]
    ppermute x6, starting transfers between devices: 13.6 us -> 9.4 us  [along_x(): lax.ppermute(parts[k - 1], 'frag', [(i, i ^ 8 * k) for i in range(32)])]
    pallas_call x2, Pallas kernels: 29.5 us -> 33.1 us  [run_dimers(): pl.pallas_call(kernel, out_shape=[shape] * 8, grid_spec=pltpu.PrefetchSca...]
  transfers between devices with their start and end apart: 53 -> 53, of which waited for: 28 -> 24; matrix products, arithmetic and copies ran while one was open for 2% -> 2% of each run, Pallas kernels for 25% -> 26%
where the time goes in v5:
time: 329 us; the launch traced here: 325 us
  waiting for transfers between devices  105 us (32%)
  starting transfers between devices  97.2 us (30%)
  Pallas kernels  92.2 us (28%)
  blocking collectives  9.55 us (3%)
  other arithmetic  9.38 us (3%)
  local copies, waits for them, and re-layouts  7.42 us (2%)
    ppermute x42, waiting for transfers between devices, exchange(): got.append(lax.ppermute(parts[k], 'basis', [(i, i ^ k) for i in range(8)]))  63.2 us
    ppermute x42, starting transfers between devices, exchange(): got.append(lax.ppermute(parts[k], 'basis', [(i, i ^ k) for i in range(8)]))  43.9 us
    pallas_call x2, Pallas kernels, run_dimers(): pl.pallas_call(kernel, out_shape=[shape] * 8, grid_spec=pltpu.PrefetchSca...  33.1 us
    all_to_all x3, waiting for transfers between devices, across(): return lax.all_to_all(part, 'frag', split_axis=0, concat_axis=0, tiled=True)  31.1 us
    all_to_all x3, starting transfers between devices, across(): return lax.all_to_all(part, 'frag', split_axis=0, concat_axis=0, tiled=True)  26 us
    pallas_call x7, Pallas kernels, pack(): pl.pallas_call(kernel, out_shape=[jax.ShapeDtypeStruct((rows, 320, 128),...  21.9 us
    pallas_call x1, Pallas kernels, plan_rest(): pl.pallas_call(plan_kernel, out_shape=[jax.ShapeDtypeStruct((TABLE,), s32...  20.1 us
    all_to_all x2, starting transfers between devices, along_z(): lax.all_to_all(part, 'frag', 0, 0, tiled=True, axis_index_groups=groups)  17.9 us
  transfers between devices with their start and end apart: 53, of which 24 were waited for; matrix products, arithmetic and copies ran while one was open for 2% of the time, Pallas kernels for 26%

profile of v5, /device:TPU:32, one launch (start us, length us, event | category | flops | bytes accessed | tf_op | source)
XLA Modules:
  0.0 324.6 jit_solution(5414749357312306336)
XLA Ops:
  2.3 9.6 %all_to_all.34 = s32[8,1,128]{2,1,0:T(1,128)S(1)} all-to-all(s32[8,1,128]{2,1,0:T(1,128)S(1)} %broadcast_in_dim.142), channel_id=1, replica_groups=mesh['frag'=32,'basis'=8] {'basis'}, dimensions={0} | all-to-all | bytes 8192 | tf_op jit(solution)/shard_map/all_to_all | solution.py:486
  12.8 11.2 %all-to-all-start.5 = ((s32[32,1,128]{2,1,0:T(1,128)}), s32[32,1,128]{2,1,0:T(1,128)S(1)}, u32[]{:S(2)}, u32[]{:S(2)}) async-start(s32[32,1,128]{2,1,0:T(1,128)} %broadcast_in_dim.143), calls=%async_computation.5 | async-start | bytes 32768 | tf_op jit(solution)/shard_map/all_to_all | solution.py:469
  24.0 8.6 %all-to-all-done.5 = s32[32,1,128]{2,1,0:T(1,128)S(1)} async-done(((s32[32,1,128]{2,1,0:T(1,128)}), s32[32,1,128]{2,1,0:T(1,128)S(1)}, u32[]{:S(2)}, u32[]{:S(2)}) %all-to-all-start.5) | async-done | bytes 16416 | tf_op jit(solution)/shard_map/all_to_all | solution.py:469
  34.1 289.5 %while.15 = (s32[]{:T(128)}, s32[1024]{0:T(1024)S(1)}, f32[32,32,256]{2,1,0:T(8,128)}, f32[32,128]{1,0:T(8,128)S(1)}, s32[1024]{0:T(1024)S(1)}, /*index=5*/pred[...) while((s32[]{:T(128)}, s32[1024]{0:T(1024)S(1)}, ...), condition=%region_13.14_spmd.clone.clone, body=%region_1.13_spmd.clone.clone | while | flops 24018298880 | bytes 146727568 | solution.py:641
  35.3 3.8 %pack.7 = bf16[32,320,128]{2,1,0:T(8,128)(2,1)} custom-call(s32[32]{0:T(128)} %get-tuple-element.461.refs_0_, s32[1]{0:T(128)} %get-tuple-element.526.refs_1_.refs_2_.me_ref, bf16[32,256,128]{2,1,0:T(8,128)(2,1)} %get-tuple-element.527.refs_2_.refs_3_, bf16[32,32,256]{2,1,0:T(8,128)(2,1)} %get-tuple-element.528.refs_3_.refs_4_), custom_call_target="tpu_custom_call" | custom-call | tf_op jit(solution)/shard_map/while/body/pack/pallas_call | solution.py:68
  39.1 6.1 %all-to-all-start = ((bf16[32,320,128]{2,1,0:T(8,128)(2,1)}), bf16[32,320,128]{2,1,0:T(8,128)(2,1)}, u32[]{:S(2)}, u32[]{:S(2)}) async-start(bf16[32,320,128]{2,1,0:T(8,128)(2,1)} %pack.7), calls=%async_computation | async-start | bytes 5242880 | tf_op jit(solution)/shard_map/while/body/all_to_all | solution.py:469
  46.1 3.1 pack.13
  53.1 20.1 %plan.1 = (s32[256]{0:T(256)}, s32[1024]{0:T(1024)}) custom-call(s32[1]{0:T(128)} %get-tuple-element.523.me_ref, s32[32]{0:T(128)} %select_reduce_fusion.6.inside_ref, s32[1]{0:T(128)} %bitcast.5.count_ref, s32[1024]{0:T(1024)} %select_reduce_fusion.2.list_ref), custom_call_target="tpu_custom_call" | custom-call | flops 1000 | bytes 30000000 | tf_op jit(solution)/shard_map/while/body/plan/pallas_call | solution.py:441
  73.3 2.2 pack.10
  77.0 2.8 collective-permute-start.15
  82.4 22.5 %all-to-all-done.refs_3_ = bf16[32,320,128]{2,1,0:T(8,128)(2,1)} async-done(((bf16[32,320,128]{2,1,0:T(8,128)(2,1)}), bf16[32,320,128]{2,1,0:T(8,128)(2,1)}, u32[]{:S(2)}, u32[]{:S(2)}) %all-to-all-start) | async-done | bytes 2621472 | tf_op jit(solution)/shard_map/while/body/all_to_all | solution.py:469
  104.9 4.1 %pack.8 = (bf16[4,320,128]{2,1,0:T(8,128)(2,1)}, bf16[4,320,128]{2,1,0:T(8,128)(2,1)}, bf16[4,320,128]{2,1,0:T(8,128)(2,1)}, bf16[4,320,128]{2,1,0:T(8,128)(2,1)...) custom-call(s32[128]{0:T(128)} %pad_add_fusion.refs_0_.table_ref, ...), custom_call_target="tpu_custom_call" | custom-call | tf_op jit(solution)/shard_map/while/body/pack/pallas_call | solution.py:68
  110.3 2.5 collective-permute-start.37
  113.0 3.0 pack.11
  116.0 7.9 %all-to-all-start.1 = ((bf16[16,320,128]{2,1,0:T(8,128)(2,1)}), bf16[16,320,128]{2,1,0:T(8,128)(2,1)}, u32[]{:S(2)}, u32[]{:S(2)}) async-start(bf16[16,320,128]{2,1,0:T(8,128)(2,1)} %pack.11), calls=%async_computation.1 | async-start | bytes 2621440 | tf_op jit(solution)/shard_map/while/body/all_to_all | solution.py:465
  128.4 5.2 %collective-permute-done.37.refs_7_ = bf16[4,320,128]{2,1,0:T(8,128)(2,1)} collective-permute-done((bf16[4,320,128]{2,1,0:T(8,128)(2,1)}, bf16[4,320,128]{2,1,0:T(8,128)(2,1)}, u32[]{:S(2)}, u32[]{:S(2)}) %collective-permute-start.37) | collective-permute-done | bytes 327712 | tf_op jit(solution)/shard_map/while/body/ppermute | solution.py:455
  136.4 2.3 collective-permute-start.6
  138.7 4.0 %collective-permute-done.3.refs_12_ = bf16[4,320,128]{2,1,0:T(8,128)(2,1)S(1)} collective-permute-done((bf16[4,320,128]{2,1,0:T(8,128)(2,1)}, bf16[4,320,128]{2,1,0:T(8,128)(2,1)S(1)}, u32[]{:S(2)}, u32[]{:S(2)}) %collective-permute-start.3) | collective-permute-done | bytes 327712 | tf_op jit(solution)/shard_map/while/body/ppermute | solution.py:455
  142.7 5.9 %collective-permute-done.4.refs_13_ = bf16[4,320,128]{2,1,0:T(8,128)(2,1)S(1)} collective-permute-done((bf16[4,320,128]{2,1,0:T(8,128)(2,1)}, bf16[4,320,128]{2,1,0:T(8,128)(2,1)S(1)}, u32[]{:S(2)}, u32[]{:S(2)}) %collective-permute-start.4) | collective-permute-done | bytes 327712 | tf_op jit(solution)/shard_map/while/body/ppermute | solution.py:455
  148.7 7.5 %collective-permute-done.5.refs_14_ = bf16[4,320,128]{2,1,0:T(8,128)(2,1)S(1)} collective-permute-done((bf16[4,320,128]{2,1,0:T(8,128)(2,1)}, bf16[4,320,128]{2,1,0:T(8,128)(2,1)S(1)}, u32[]{:S(2)}, u32[]{:S(2)}) %collective-permute-start.5) | collective-permute-done | bytes 327712 | tf_op jit(solution)/shard_map/while/body/ppermute | solution.py:455
  156.2 6.9 %collective-permute-done.6.refs_15_ = bf16[4,320,128]{2,1,0:T(8,128)(2,1)S(1)} collective-permute-done((bf16[4,320,128]{2,1,0:T(8,128)(2,1)S(1)}, bf16[4,320,128]{2,1,0:T(8,128)(2,1)S(1)}, u32[]{:S(2)}, u32[]{:S(2)}) %collective-permute-start.6) | collective-permute-done | bytes 327712 | tf_op jit(solution)/shard_map/while/body/ppermute | solution.py:455
  163.9 18.5 %dimers.3 = (bf16[8,72,128]{2,1,0:T(8,128)(2,1)}, bf16[8,72,128]{2,1,0:T(8,128)(2,1)}, bf16[8,72,128]{2,1,0:T(8,128)(2,1)}, bf16[8,72,128]{2,1,0:T(8,128)(2,1)},...) custom-call(s32[128]{0:T(128)} %pad_add_fusion.refs_0_.table_ref, ...), custom_call_target="tpu_custom_call" | custom-call | flops 16000000000 | bytes 6000000 | tf_op jit(solution)/shard_map/while/body/dimers/pallas_call | solution.py:225
  185.1 2.4 collective-permute-start.42
  188.5 2.1 pack.9
  192.9 3.0 collective-permute-done.41.refs_7_
  195.9 2.1 collective-permute-done.42.refs_8_
  198.0 2.8 collective-permute-start.10
  201.2 3.5 %pack.12 = (bf16[2,320,128]{2,1,0:T(8,128)(2,1)}, bf16[2,320,128]{2,1,0:T(8,128)(2,1)}, bf16[2,320,128]{2,1,0:T(8,128)(2,1)}, bf16[2,320,128]{2,1,0:T(8,128)(2,1...) custom-call(s32[128]{0:T(128)} %pad_add_fusion.refs_0_.table_ref, ...), custom_call_target="tpu_custom_call" | custom-call | tf_op jit(solution)/shard_map/while/body/pack/pallas_call | solution.py:68
  204.8 6.7 %collective-permute-done.44.refs_10_ = bf16[8,72,128]{2,1,0:T(8,128)(2,1)S(1)} collective-permute-done((bf16[8,72,128]{2,1,0:T(8,128)(2,1)}, bf16[8,72,128]{2,1,0:T(8,128)(2,1)S(1)}, u32[]{:S(2)}, u32[]{:S(2)}) %collective-permute-start.44) | collective-permute-done | bytes 147488 | tf_op jit(solution)/shard_map/while/body/ppermute | solution.py:455
  211.5 2.0 collective-permute-start.12
  215.7 4.0 %place.4 = bf16[32,72,128]{2,1,0:T(8,128)(2,1)} custom-call(s32[128]{0:T(128)} %pad_add_fusion.refs_0_.table_ref, s32[256]{0:T(256)} %get-tuple-element.335.refs_1_.table_ref, s32[1]{0:T(128)} %get-tuple-element.526.refs_1_.refs_2_.me_ref, bf16[8,72,128]{2,1,0:T(8,128)(2,1)} %get-tuple-element.383.refs_3_, bf16[8,72,128]{2,1,0:T(8,128)(2,1)} %copy-done.14, ...), custom_call_target="tpu_custom_call" | custom-call | tf_op jit(solution)/shard_map/while/body/place/pallas_call | solution.py:95
  219.7 8.7 %all-to-all-start.2 = ((bf16[32,72,128]{2,1,0:T(8,128)(2,1)}), bf16[32,72,128]{2,1,0:T(8,128)(2,1)S(1)}, u32[]{:S(2)}, u32[]{:S(2)}) async-start(bf16[32,72,128]{2,1,0:T(8,128)(2,1)} %place.4), calls=%async_computation.2 | async-start | bytes 1179648 | tf_op jit(solution)/shard_map/while/body/all_to_all | solution.py:469
  228.9 2.1 collective-permute-start.20
  235.2 4.5 %collective-permute-done.20.refs_12_ = bf16[2,320,128]{2,1,0:T(8,128)(2,1)S(1)} collective-permute-done((bf16[2,320,128]{2,1,0:T(8,128)(2,1)}, bf16[2,320,128]{2,1,0:T(8,128)(2,1)S(1)}, u32[]{:S(2)}, u32[]{:S(2)}) %collective-permute-start.20) | collective-permute-done | bytes 163872 | tf_op jit(solution)/shard_map/while/body/ppermute | solution.py:455
  239.7 2.4 collective-permute-done.21.refs_13_
  242.2 4.0 %collective-permute-done.22.refs_14_ = bf16[2,320,128]{2,1,0:T(8,128)(2,1)S(1)} collective-permute-done((bf16[2,320,128]{2,1,0:T(8,128)(2,1)S(1)}, bf16[2,320,128]{2,1,0:T(8,128)(2,1)S(1)}, u32[]{:S(2)}, u32[]{:S(2)}) %collective-permute-start.22) | collective-permute-done | bytes 163872 | tf_op jit(solution)/shard_map/while/body/ppermute | solution.py:455
  246.2 3.3 %collective-permute-done.23.refs_15_ = bf16[2,320,128]{2,1,0:T(8,128)(2,1)S(1)} collective-permute-done((bf16[2,320,128]{2,1,0:T(8,128)(2,1)S(1)}, bf16[2,320,128]{2,1,0:T(8,128)(2,1)S(1)}, u32[]{:S(2)}, u32[]{:S(2)}) %collective-permute-start.23) | collective-permute-done | bytes 163872 | tf_op jit(solution)/shard_map/while/body/ppermute | solution.py:455
  250.2 14.6 %dimers.2 = (bf16[4,72,128]{2,1,0:T(8,128)(2,1)}, bf16[4,72,128]{2,1,0:T(8,128)(2,1)}, bf16[4,72,128]{2,1,0:T(8,128)(2,1)}, bf16[4,72,128]{2,1,0:T(8,128)(2,1)},...) custom-call(s32[256]{0:T(256)} %get-tuple-element.335.refs_1_.table_, ...), custom_call_target="tpu_custom_call" | custom-call | flops 8000000000 | bytes 3000000 | tf_op jit(solution)/shard_map/while/body/dimers/pallas_call | solution.py:225
  266.7 3.2 collective-permute-start.28
  270.3 2.6 collective-permute-start.30
  274.0 2.5 collective-permute-done.29.refs_9_.refs_17_
  278.0 2.6 place.3
  280.6 10.1 %all-to-all-start.3 = ((bf16[16,72,128]{2,1,0:T(8,128)(2,1)}), bf16[16,72,128]{2,1,0:T(8,128)(2,1)S(1)}, u32[]{:S(2)}, u32[]{:S(2)}) async-start(bf16[16,72,128]{2,1,0:T(8,128)(2,1)} %place.3), calls=%async_computation.3 | async-start | bytes 589824 | tf_op jit(solution)/shard_map/while/body/all_to_all | solution.py:465
  291.2 10.9 %all-to-all-done.3.refs_11_.refs_3_ = bf16[16,72,128]{2,1,0:T(8,128)(2,1)S(1)} async-done(((bf16[16,72,128]{2,1,0:T(8,128)(2,1)}), bf16[16,72,128]{2,1,0:T(8,128)(2,1)S(1)}, u32[]{:S(2)}, u32[]{:S(2)}) %all-to-all-start.3) | async-done | bytes 294944 | tf_op jit(solution)/shard_map/while/body/all_to_all | solution.py:465
  302.9 3.6 %place.5 = (bf16[6,72,128]{2,1,0:T(8,128)(2,1)}, bf16[6,72,128]{2,1,0:T(8,128)(2,1)}, bf16[6,72,128]{2,1,0:T(8,128)(2,1)}) custom-call(s32[128]{0:T(128)} %pad_add_fusion.refs_0_.table_ref, s32[256]{0:T(256)} %get-tuple-element.335.refs_1_.table_ref, s32[1]{0:T(128)} %get-tuple-element.526.refs_1_.refs_2_.me_ref, ...), custom_call_target="tpu_custom_call" | custom-call | tf_op jit(solution)/shard_map/while/body/place/pallas_call | solution.py:95
  306.5 3.0 collective-permute-start.46
  311.1 2.0 select_reduce_fusion
  313.2 5.2 %add_up.2 = (f32[32,32,256]{2,1,0:T(8,128)S(1)}, f32[32,128]{1,0:T(8,128)S(1)}) custom-call(s32[128]{0:T(128)} %pad_add_fusion.refs_0_.table_ref, s32[256]{0:T(256)} %get-tuple-element.335.refs_1_.table_ref, s32[1]{0:T(128)} %get-tuple-element.526.refs_1_.refs_2_.me_ref, ...), custom_call_target="tpu_custom_call", output_to_operand_aliasing={{0}: (20, {}), {1}: (21, {})} | custom-call | tf_op jit(solution)/shard_map/while/body/add_up/pallas_call | solution.py:124
  (212 shorter events, 49.1 us)
Async XLA Ops:
  12.8 19.8 %all-to-all-start.5 = ((s32[32,1,128]{2,1,0:T(1,128)}), s32[32,1,128]{2,1,0:T(1,128)S(1)}, u32[]{:S(2)}, u32[]{:S(2)}) async-start(s32[32,1,128]{2,1,0:T(1,128)} %broadcast_in_dim.143), calls=%async_computation.5 | async-start | bytes 32768 | tf_op jit(solution)/shard_map/all_to_all | solution.py:469
  39.1 65.8 %all-to-all-start = ((bf16[32,320,128]{2,1,0:T(8,128)(2,1)}), bf16[32,320,128]{2,1,0:T(8,128)(2,1)}, u32[]{:S(2)}, u32[]{:S(2)}) async-start(bf16[32,320,128]{2,1,0:T(8,128)(2,1)} %pack.7), calls=%async_computation | async-start | bytes 5242880 | tf_op jit(solution)/shard_map/while/body/all_to_all | solution.py:469
  49.3 31.0 %collective-permute-start.31 = (bf16[4,320,128]{2,1,0:T(8,128)(2,1)}, bf16[4,320,128]{2,1,0:T(8,128)(2,1)S(1)}, u32[]{:S(2)}, u32[]{:S(2)}) collective-permute-start(bf16[4,320,128]{2,1,0:T(8,128)(2,1)} %get-tuple-element.368), channel_id=1, source_target_pairs={{0,1},{1,0},{2,3},{3,2},{4,5},{5,4},{6,7},{7,6},{8,9},{9,8},{10,11... | collective-permute-start | bytes 983048 | tf_op jit(solution)/shard_map/while/body/ppermute | solution.py:455
  49.3 31.4 %collective-permute-start.32 = (bf16[4,320,128]{2,1,0:T(8,128)(2,1)}, bf16[4,320,128]{2,1,0:T(8,128)(2,1)}, u32[]{:S(2)}, u32[]{:S(2)}) collective-permute-start(bf16[4,320,128]{2,1,0:T(8,128)(2,1)} %get-tuple-element.369), channel_id=1, source_target_pairs={{0,2},{1,3},{2,0},{3,1},{4,6},{5,7},{6,4},{7,5},{8,10},{9,11},{10,... | collective-permute-start | bytes 983048 | tf_op jit(solution)/shard_map/while/body/ppermute | solution.py:455
  75.5 34.8 %collective-permute-start.14 = (bf16[6,320,128]{2,1,0:T(8,128)(2,1)}, bf16[6,320,128]{2,1,0:T(8,128)(2,1)S(1)}, u32[]{:S(2)}, u32[]{:S(2)}) collective-permute-start(bf16[6,320,128]{2,1,0:T(8,128)(2,1)} %get-tuple-element.344), channel_id=1, source_target_pairs={{0,64},{8,72},{16,80},{24,88},{32,96},{40,104},{48,112},{56,120},{... | collective-permute-start | bytes 1474568 | tf_op jit(solution)/shard_map/while/body/ppermute | solution.py:460
  77.0 35.8 %collective-permute-start.15 = (bf16[6,320,128]{2,1,0:T(8,128)(2,1)}, bf16[6,320,128]{2,1,0:T(8,128)(2,1)}, u32[]{:S(2)}, u32[]{:S(2)}) collective-permute-start(bf16[6,320,128]{2,1,0:T(8,128)(2,1)} %get-tuple-element.345), channel_id=1, source_target_pairs={{0,128},{8,136},{16,144},{24,152},{32,160},{40,168},{48,176},{56,1... | collective-permute-start | bytes 1474568 | tf_op jit(solution)/shard_map/while/body/ppermute | solution.py:460
  79.8 33.0 %collective-permute-start.16 = (bf16[6,320,128]{2,1,0:T(8,128)(2,1)}, bf16[6,320,128]{2,1,0:T(8,128)(2,1)}, u32[]{:S(2)}, u32[]{:S(2)}) collective-permute-start(bf16[6,320,128]{2,1,0:T(8,128)(2,1)} %get-tuple-element.346), channel_id=1, source_target_pairs={{0,192},{8,200},{16,208},{24,216},{32,224},{40,232},{48,240},{56,2... | collective-permute-start | bytes 1474568 | tf_op jit(solution)/shard_map/while/body/ppermute | solution.py:460
  80.2 28.7 %collective-permute-start.33 = (bf16[4,320,128]{2,1,0:T(8,128)(2,1)}, bf16[4,320,128]{2,1,0:T(8,128)(2,1)}, u32[]{:S(2)}, u32[]{:S(2)}) collective-permute-start(bf16[4,320,128]{2,1,0:T(8,128)(2,1)} %get-tuple-element.370), channel_id=1, source_target_pairs={{0,3},{1,2},{2,1},{3,0},{4,7},{5,6},{6,5},{7,4},{8,11},{9,10},{10,... | collective-permute-start | bytes 983048 | tf_op jit(solution)/shard_map/while/body/ppermute | solution.py:455
  80.7 28.3 %collective-permute-start.34 = (bf16[4,320,128]{2,1,0:T(8,128)(2,1)}, bf16[4,320,128]{2,1,0:T(8,128)(2,1)}, u32[]{:S(2)}, u32[]{:S(2)}) collective-permute-start(bf16[4,320,128]{2,1,0:T(8,128)(2,1)} %get-tuple-element.371), channel_id=1, source_target_pairs={{0,4},{1,5},{2,6},{3,7},{4,0},{5,1},{6,2},{7,3},{8,12},{9,13},{10,... | collective-permute-start | bytes 983048 | tf_op jit(solution)/shard_map/while/body/ppermute | solution.py:455
  109.0 14.9 %collective-permute-start.35 = (bf16[4,320,128]{2,1,0:T(8,128)(2,1)}, bf16[4,320,128]{2,1,0:T(8,128)(2,1)}, u32[]{:S(2)}, u32[]{:S(2)}) collective-permute-start(bf16[4,320,128]{2,1,0:T(8,128)(2,1)} %get-tuple-element.372), channel_id=1, source_target_pairs={{0,5},{1,4},{2,7},{3,6},{4,1},{5,0},{6,3},{7,2},{8,13},{9,12},{10,... | collective-permute-start | bytes 983048 | tf_op jit(solution)/shard_map/while/body/ppermute | solution.py:455
  109.1 17.4 %collective-permute-start.36 = (bf16[4,320,128]{2,1,0:T(8,128)(2,1)}, bf16[4,320,128]{2,1,0:T(8,128)(2,1)}, u32[]{:S(2)}, u32[]{:S(2)}) collective-permute-start(bf16[4,320,128]{2,1,0:T(8,128)(2,1)} %get-tuple-element.373), channel_id=1, source_target_pairs={{0,6},{1,7},{2,4},{3,5},{4,2},{5,3},{6,0},{7,1},{8,14},{9,15},{10,... | collective-permute-start | bytes 983048 | tf_op jit(solution)/shard_map/while/body/ppermute | solution.py:455
  110.3 23.2 %collective-permute-start.37 = (bf16[4,320,128]{2,1,0:T(8,128)(2,1)}, bf16[4,320,128]{2,1,0:T(8,128)(2,1)}, u32[]{:S(2)}, u32[]{:S(2)}) collective-permute-start(bf16[4,320,128]{2,1,0:T(8,128)(2,1)} %get-tuple-element.374), channel_id=1, source_target_pairs={{0,7},{1,6},{2,5},{3,4},{4,3},{5,2},{6,1},{7,0},{8,15},{9,14},{10,... | collective-permute-start | bytes 983048 | tf_op jit(solution)/shard_map/while/body/ppermute | solution.py:455
  112.9 22.2 %collective-permute-start = (bf16[4,320,128]{2,1,0:T(8,128)(2,1)}, bf16[4,320,128]{2,1,0:T(8,128)(2,1)}, u32[]{:S(2)}, u32[]{:S(2)}) collective-permute-start(bf16[4,320,128]{2,1,0:T(8,128)(2,1)} %get-tuple-element.327), channel_id=1, source_target_pairs={{0,1},{1,0},{2,3},{3,2},{4,5},{5,4},{6,7},{7,6},{8,9},{9,8},{10,11... | collective-permute-start | bytes 983048 | tf_op jit(solution)/shard_map/while/body/ppermute | solution.py:455
  112.9 23.6 %collective-permute-start.1 = (bf16[4,320,128]{2,1,0:T(8,128)(2,1)}, bf16[4,320,128]{2,1,0:T(8,128)(2,1)}, u32[]{:S(2)}, u32[]{:S(2)}) collective-permute-start(bf16[4,320,128]{2,1,0:T(8,128)(2,1)} %get-tuple-element.328), channel_id=1, source_target_pairs={{0,2},{1,3},{2,0},{3,1},{4,6},{5,7},{6,4},{7,5},{8,10},{9,11},{10,... | collective-permute-start | bytes 983048 | tf_op jit(solution)/shard_map/while/body/ppermute | solution.py:455
  116.0 85.2 %all-to-all-start.1 = ((bf16[16,320,128]{2,1,0:T(8,128)(2,1)}), bf16[16,320,128]{2,1,0:T(8,128)(2,1)}, u32[]{:S(2)}, u32[]{:S(2)}) async-start(bf16[16,320,128]{2,1,0:T(8,128)(2,1)} %pack.11), calls=%async_computation.1 | async-start | bytes 2621440 | tf_op jit(solution)/shard_map/while/body/all_to_all | solution.py:465
  123.9 14.9 %collective-permute-start.2 = (bf16[4,320,128]{2,1,0:T(8,128)(2,1)}, bf16[4,320,128]{2,1,0:T(8,128)(2,1)S(1)}, u32[]{:S(2)}, u32[]{:S(2)}) collective-permute-start(bf16[4,320,128]{2,1,0:T(8,128)(2,1)} %get-tuple-element.329), channel_id=1, source_target_pairs={{0,3},{1,2},{2,1},{3,0},{4,7},{5,6},{6,5},{7,4},{8,11},{9,10},{10,... | collective-permute-start | bytes 983048 | tf_op jit(solution)/shard_map/while/body/ppermute | solution.py:455
  126.5 16.3 %collective-permute-start.3 = (bf16[4,320,128]{2,1,0:T(8,128)(2,1)}, bf16[4,320,128]{2,1,0:T(8,128)(2,1)S(1)}, u32[]{:S(2)}, u32[]{:S(2)}) collective-permute-start(bf16[4,320,128]{2,1,0:T(8,128)(2,1)} %get-tuple-element.330), channel_id=1, source_target_pairs={{0,4},{1,5},{2,6},{3,7},{4,0},{5,1},{6,2},{7,3},{8,12},{9,13},{10,... | collective-permute-start | bytes 983048 | tf_op jit(solution)/shard_map/while/body/ppermute | solution.py:455
  133.5 15.1 %collective-permute-start.4 = (bf16[4,320,128]{2,1,0:T(8,128)(2,1)}, bf16[4,320,128]{2,1,0:T(8,128)(2,1)S(1)}, u32[]{:S(2)}, u32[]{:S(2)}) collective-permute-start(bf16[4,320,128]{2,1,0:T(8,128)(2,1)} %get-tuple-element.331), channel_id=1, source_target_pairs={{0,5},{1,4},{2,7},{3,6},{4,1},{5,0},{6,3},{7,2},{8,13},{9,12},{10,... | collective-permute-start | bytes 983048 | tf_op jit(solution)/shard_map/while/body/ppermute | solution.py:455
  135.1 21.1 %collective-permute-start.5 = (bf16[4,320,128]{2,1,0:T(8,128)(2,1)}, bf16[4,320,128]{2,1,0:T(8,128)(2,1)S(1)}, u32[]{:S(2)}, u32[]{:S(2)}) collective-permute-start(bf16[4,320,128]{2,1,0:T(8,128)(2,1)} %get-tuple-element.332), channel_id=1, source_target_pairs={{0,6},{1,7},{2,4},{3,5},{4,2},{5,3},{6,0},{7,1},{8,14},{9,15},{10,... | collective-permute-start | bytes 983048 | tf_op jit(solution)/shard_map/while/body/ppermute | solution.py:455
  136.4 26.7 %collective-permute-start.6 = (bf16[4,320,128]{2,1,0:T(8,128)(2,1)S(1)}, bf16[4,320,128]{2,1,0:T(8,128)(2,1)S(1)}, u32[]{:S(2)}, u32[]{:S(2)}) collective-permute-start(bf16[4,320,128]{2,1,0:T(8,128)(2,1)S(1)} %copy-done.28), channel_id=1, source_target_pairs={{0,7},{1,6},{2,5},{3,4},{4,3},{5,2},{6,1},{7,0},{8,15},{9,14},{10,... | collective-permute-start | bytes 983048 | tf_op jit(solution)/shard_map/while/body/ppermute | solution.py:455
  182.6 8.1 %collective-permute-start.39 = (bf16[8,72,128]{2,1,0:T(8,128)(2,1)}, bf16[8,72,128]{2,1,0:T(8,128)(2,1)S(1)}, u32[]{:S(2)}, u32[]{:S(2)}) collective-permute-start(bf16[8,72,128]{2,1,0:T(8,128)(2,1)} %get-tuple-element.377), channel_id=1, source_target_pairs={{0,2},{1,3},{2,0},{3,1},{4,6},{5,7},{6,4},{7,5},{8,10},{9,11},{10,... | collective-permute-start | bytes 442376 | tf_op jit(solution)/shard_map/while/body/ppermute | solution.py:455
  184.0 7.7 %collective-permute-start.40 = (bf16[8,72,128]{2,1,0:T(8,128)(2,1)}, bf16[8,72,128]{2,1,0:T(8,128)(2,1)S(1)}, u32[]{:S(2)}, u32[]{:S(2)}) collective-permute-start(bf16[8,72,128]{2,1,0:T(8,128)(2,1)} %get-tuple-element.378), channel_id=1, source_target_pairs={{0,3},{1,2},{2,1},{3,0},{4,7},{5,6},{6,5},{7,4},{8,11},{9,10},{10,... | collective-permute-start | bytes 442376 | tf_op jit(solution)/shard_map/while/body/ppermute | solution.py:455
  184.3 11.6 %collective-permute-start.41 = (bf16[8,72,128]{2,1,0:T(8,128)(2,1)}, bf16[8,72,128]{2,1,0:T(8,128)(2,1)S(1)}, u32[]{:S(2)}, u32[]{:S(2)}) collective-permute-start(bf16[8,72,128]{2,1,0:T(8,128)(2,1)} %get-tuple-element.379), channel_id=1, source_target_pairs={{0,4},{1,5},{2,6},{3,7},{4,0},{5,1},{6,2},{7,3},{8,12},{9,13},{10,... | collective-permute-start | bytes 442376 | tf_op jit(solution)/shard_map/while/body/ppermute | solution.py:455
  185.1 12.9 %collective-permute-start.42 = (bf16[8,72,128]{2,1,0:T(8,128)(2,1)}, bf16[8,72,128]{2,1,0:T(8,128)(2,1)S(1)}, u32[]{:S(2)}, u32[]{:S(2)}) collective-permute-start(bf16[8,72,128]{2,1,0:T(8,128)(2,1)} %get-tuple-element.380), channel_id=1, source_target_pairs={{0,5},{1,4},{2,7},{3,6},{4,1},{5,0},{6,3},{7,2},{8,13},{9,12},{10,... | collective-permute-start | bytes 442376 | tf_op jit(solution)/shard_map/while/body/ppermute | solution.py:455
  187.6 13.4 %collective-permute-start.43 = (bf16[8,72,128]{2,1,0:T(8,128)(2,1)}, bf16[8,72,128]{2,1,0:T(8,128)(2,1)S(1)}, u32[]{:S(2)}, u32[]{:S(2)}) collective-permute-start(bf16[8,72,128]{2,1,0:T(8,128)(2,1)} %get-tuple-element.381), channel_id=1, source_target_pairs={{0,6},{1,7},{2,4},{3,5},{4,2},{5,3},{6,0},{7,1},{8,14},{9,15},{10,... | collective-permute-start | bytes 442376 | tf_op jit(solution)/shard_map/while/body/ppermute | solution.py:455
  190.7 20.8 %collective-permute-start.7 = (bf16[2,320,128]{2,1,0:T(8,128)(2,1)}, bf16[2,320,128]{2,1,0:T(8,128)(2,1)S(1)}, u32[]{:S(2)}, u32[]{:S(2)}) collective-permute-start(bf16[2,320,128]{2,1,0:T(8,128)(2,1)} %get-tuple-element.337), channel_id=1, source_target_pairs={{0,1},{1,0},{2,3},{3,2},{4,5},{5,4},{6,7},{7,6},{8,9},{9,8},{10,11... | collective-permute-start | bytes 491528 | tf_op jit(solution)/shard_map/while/body/ppermute | solution.py:455
  191.7 21.9 %collective-permute-start.8 = (bf16[2,320,128]{2,1,0:T(8,128)(2,1)}, bf16[2,320,128]{2,1,0:T(8,128)(2,1)S(1)}, u32[]{:S(2)}, u32[]{:S(2)}) collective-permute-start(bf16[2,320,128]{2,1,0:T(8,128)(2,1)} %get-tuple-element.338), channel_id=1, source_target_pairs={{0,2},{1,3},{2,0},{3,1},{4,6},{5,7},{6,4},{7,5},{8,10},{9,11},{10,... | collective-permute-start | bytes 491528 | tf_op jit(solution)/shard_map/while/body/ppermute | solution.py:455
  195.9 18.4 %collective-permute-start.9 = (bf16[2,320,128]{2,1,0:T(8,128)(2,1)}, bf16[2,320,128]{2,1,0:T(8,128)(2,1)S(1)}, u32[]{:S(2)}, u32[]{:S(2)}) collective-permute-start(bf16[2,320,128]{2,1,0:T(8,128)(2,1)} %get-tuple-element.339), channel_id=1, source_target_pairs={{0,3},{1,2},{2,1},{3,0},{4,7},{5,6},{6,5},{7,4},{8,11},{9,10},{10,... | collective-permute-start | bytes 491528 | tf_op jit(solution)/shard_map/while/body/ppermute | solution.py:455
  198.0 17.0 %collective-permute-start.10 = (bf16[2,320,128]{2,1,0:T(8,128)(2,1)}, bf16[2,320,128]{2,1,0:T(8,128)(2,1)S(1)}, u32[]{:S(2)}, u32[]{:S(2)}) collective-permute-start(bf16[2,320,128]{2,1,0:T(8,128)(2,1)} %get-tuple-element.340), channel_id=1, source_target_pairs={{0,4},{1,5},{2,6},{3,7},{4,0},{5,1},{6,2},{7,3},{8,12},{9,13},{10,... | collective-permute-start | bytes 491528 | tf_op jit(solution)/shard_map/while/body/ppermute | solution.py:455
  200.9 10.5 %collective-permute-start.44 = (bf16[8,72,128]{2,1,0:T(8,128)(2,1)}, bf16[8,72,128]{2,1,0:T(8,128)(2,1)S(1)}, u32[]{:S(2)}, u32[]{:S(2)}) collective-permute-start(bf16[8,72,128]{2,1,0:T(8,128)(2,1)} %get-tuple-element.382), channel_id=1, source_target_pairs={{0,7},{1,6},{2,5},{3,4},{4,3},{5,2},{6,1},{7,0},{8,15},{9,14},{10,... | collective-permute-start | bytes 442376 | tf_op jit(solution)/shard_map/while/body/ppermute | solution.py:455
  211.5 16.9 %collective-permute-start.11 = (bf16[2,320,128]{2,1,0:T(8,128)(2,1)S(1)}, bf16[2,320,128]{2,1,0:T(8,128)(2,1)S(1)}, u32[]{:S(2)}, u32[]{:S(2)}) collective-permute-start(bf16[2,320,128]{2,1,0:T(8,128)(2,1)S(1)} %copy-done.41), channel_id=1, source_target_pairs={{0,5},{1,4},{2,7},{3,6},{4,1},{5,0},{6,3},{7,2},{8,13},{9,12},{10,... | collective-permute-start | bytes 491528 | tf_op jit(solution)/shard_map/while/body/ppermute | solution.py:455
  211.5 17.3 %collective-permute-start.12 = (bf16[2,320,128]{2,1,0:T(8,128)(2,1)S(1)}, bf16[2,320,128]{2,1,0:T(8,128)(2,1)S(1)}, u32[]{:S(2)}, u32[]{:S(2)}) collective-permute-start(bf16[2,320,128]{2,1,0:T(8,128)(2,1)S(1)} %copy-done.39), channel_id=1, source_target_pairs={{0,6},{1,7},{2,4},{3,5},{4,2},{5,3},{6,0},{7,1},{8,14},{9,15},{10,... | collective-permute-start | bytes 491528 | tf_op jit(solution)/shard_map/while/body/ppermute | solution.py:455
  213.5 17.5 %collective-permute-start.13 = (bf16[2,320,128]{2,1,0:T(8,128)(2,1)S(1)}, bf16[2,320,128]{2,1,0:T(8,128)(2,1)}, u32[]{:S(2)}, u32[]{:S(2)}) collective-permute-start(bf16[2,320,128]{2,1,0:T(8,128)(2,1)S(1)} %copy-done.38), channel_id=1, source_target_pairs={{0,7},{1,6},{2,5},{3,4},{4,3},{5,2},{6,1},{7,0},{8,15},{9,14},{10,... | collective-permute-start | bytes 491528 | tf_op jit(solution)/shard_map/while/body/ppermute | solution.py:455
  214.4 18.6 %collective-permute-start.17 = (bf16[2,320,128]{2,1,0:T(8,128)(2,1)}, bf16[2,320,128]{2,1,0:T(8,128)(2,1)}, u32[]{:S(2)}, u32[]{:S(2)}) collective-permute-start(bf16[2,320,128]{2,1,0:T(8,128)(2,1)} %get-tuple-element.352), channel_id=1, source_target_pairs={{0,1},{1,0},{2,3},{3,2},{4,5},{5,4},{6,7},{7,6},{8,9},{9,8},{10,11... | collective-permute-start | bytes 491528 | tf_op jit(solution)/shard_map/while/body/ppermute | solution.py:455
  215.1 19.4 %collective-permute-start.18 = (bf16[2,320,128]{2,1,0:T(8,128)(2,1)}, bf16[2,320,128]{2,1,0:T(8,128)(2,1)}, u32[]{:S(2)}, u32[]{:S(2)}) collective-permute-start(bf16[2,320,128]{2,1,0:T(8,128)(2,1)} %get-tuple-element.353), channel_id=1, source_target_pairs={{0,2},{1,3},{2,0},{3,1},{4,6},{5,7},{6,4},{7,5},{8,10},{9,11},{10,... | collective-permute-start | bytes 491528 | tf_op jit(solution)/shard_map/while/body/ppermute | solution.py:455
  219.7 60.9 %all-to-all-start.2 = ((bf16[32,72,128]{2,1,0:T(8,128)(2,1)}), bf16[32,72,128]{2,1,0:T(8,128)(2,1)S(1)}, u32[]{:S(2)}, u32[]{:S(2)}) async-start(bf16[32,72,128]{2,1,0:T(8,128)(2,1)} %place.4), calls=%async_computation.2 | async-start | bytes 1179648 | tf_op jit(solution)/shard_map/while/body/all_to_all | solution.py:469
  228.9 10.9 %collective-permute-start.20 = (bf16[2,320,128]{2,1,0:T(8,128)(2,1)}, bf16[2,320,128]{2,1,0:T(8,128)(2,1)S(1)}, u32[]{:S(2)}, u32[]{:S(2)}) collective-permute-start(bf16[2,320,128]{2,1,0:T(8,128)(2,1)} %get-tuple-element.355), channel_id=1, source_target_pairs={{0,4},{1,5},{2,6},{3,7},{4,0},{5,1},{6,2},{7,3},{8,12},{9,13},{10,... | collective-permute-start | bytes 491528 | tf_op jit(solution)/shard_map/while/body/ppermute | solution.py:455
  231.0 11.2 %collective-permute-start.21 = (bf16[2,320,128]{2,1,0:T(8,128)(2,1)S(1)}, bf16[2,320,128]{2,1,0:T(8,128)(2,1)S(1)}, u32[]{:S(2)}, u32[]{:S(2)}) collective-permute-start(bf16[2,320,128]{2,1,0:T(8,128)(2,1)S(1)} %copy-done.45), channel_id=1, source_target_pairs={{0,5},{1,4},{2,7},{3,6},{4,1},{5,0},{6,3},{7,2},{8,13},{9,12},{10,... | collective-permute-start | bytes 491528 | tf_op jit(solution)/shard_map/while/body/ppermute | solution.py:455
  232.9 13.3 %collective-permute-start.22 = (bf16[2,320,128]{2,1,0:T(8,128)(2,1)S(1)}, bf16[2,320,128]{2,1,0:T(8,128)(2,1)S(1)}, u32[]{:S(2)}, u32[]{:S(2)}) collective-permute-start(bf16[2,320,128]{2,1,0:T(8,128)(2,1)S(1)} %copy-done.44), channel_id=1, source_target_pairs={{0,6},{1,7},{2,4},{3,5},{4,2},{5,3},{6,0},{7,1},{8,14},{9,15},{10,... | collective-permute-start | bytes 491528 | tf_op jit(solution)/shard_map/while/body/ppermute | solution.py:455
  234.4 15.1 %collective-permute-start.23 = (bf16[2,320,128]{2,1,0:T(8,128)(2,1)S(1)}, bf16[2,320,128]{2,1,0:T(8,128)(2,1)S(1)}, u32[]{:S(2)}, u32[]{:S(2)}) collective-permute-start(bf16[2,320,128]{2,1,0:T(8,128)(2,1)S(1)} %copy-done.42), channel_id=1, source_target_pairs={{0,7},{1,6},{2,5},{3,4},{4,3},{5,2},{6,1},{7,0},{8,15},{9,14},{10,... | collective-permute-start | bytes 491528 | tf_op jit(solution)/shard_map/while/body/ppermute | solution.py:455
  265.0 8.0 %collective-permute-start.26 = (bf16[4,72,128]{2,1,0:T(8,128)(2,1)}, bf16[4,72,128]{2,1,0:T(8,128)(2,1)S(1)}, u32[]{:S(2)}, u32[]{:S(2)}) collective-permute-start(bf16[4,72,128]{2,1,0:T(8,128)(2,1)} %get-tuple-element.362), channel_id=1, source_target_pairs={{0,3},{1,2},{2,1},{3,0},{4,7},{5,6},{6,5},{7,4},{8,11},{9,10},{10,... | collective-permute-start | bytes 221192 | tf_op jit(solution)/shard_map/while/body/ppermute | solution.py:455
  266.7 6.9 %collective-permute-start.27 = (bf16[4,72,128]{2,1,0:T(8,128)(2,1)}, bf16[4,72,128]{2,1,0:T(8,128)(2,1)S(1)}, u32[]{:S(2)}, u32[]{:S(2)}) collective-permute-start(bf16[4,72,128]{2,1,0:T(8,128)(2,1)} %get-tuple-element.363), channel_id=1, source_target_pairs={{0,4},{1,5},{2,6},{3,7},{4,0},{5,1},{6,2},{7,3},{8,12},{9,13},{10,... | collective-permute-start | bytes 221192 | tf_op jit(solution)/shard_map/while/body/ppermute | solution.py:455
  266.7 7.3 %collective-permute-start.28 = (bf16[4,72,128]{2,1,0:T(8,128)(2,1)}, bf16[4,72,128]{2,1,0:T(8,128)(2,1)S(1)}, u32[]{:S(2)}, u32[]{:S(2)}) collective-permute-start(bf16[4,72,128]{2,1,0:T(8,128)(2,1)} %get-tuple-element.364), channel_id=1, source_target_pairs={{0,5},{1,4},{2,7},{3,6},{4,1},{5,0},{6,3},{7,2},{8,13},{9,12},{10,... | collective-permute-start | bytes 221192 | tf_op jit(solution)/shard_map/while/body/ppermute | solution.py:455
  270.3 7.0 %collective-permute-start.30 = (bf16[4,72,128]{2,1,0:T(8,128)(2,1)}, bf16[4,72,128]{2,1,0:T(8,128)(2,1)S(1)}, u32[]{:S(2)}, u32[]{:S(2)}) collective-permute-start(bf16[4,72,128]{2,1,0:T(8,128)(2,1)} %get-tuple-element.366), channel_id=1, source_target_pairs={{0,7},{1,6},{2,5},{3,4},{4,3},{5,2},{6,1},{7,0},{8,15},{9,14},{10,... | collective-permute-start | bytes 221192 | tf_op jit(solution)/shard_map/while/body/ppermute | solution.py:455
  280.6 21.6 %all-to-all-start.3 = ((bf16[16,72,128]{2,1,0:T(8,128)(2,1)}), bf16[16,72,128]{2,1,0:T(8,128)(2,1)S(1)}, u32[]{:S(2)}, u32[]{:S(2)}) async-start(bf16[16,72,128]{2,1,0:T(8,128)(2,1)} %place.3), calls=%async_computation.3 | async-start | bytes 589824 | tf_op jit(solution)/shard_map/while/body/all_to_all | solution.py:465
  306.4 11.9 %collective-permute-start.45 = (bf16[6,72,128]{2,1,0:T(8,128)(2,1)}, bf16[6,72,128]{2,1,0:T(8,128)(2,1)S(1)}, u32[]{:S(2)}, u32[]{:S(2)}) collective-permute-start(bf16[6,72,128]{2,1,0:T(8,128)(2,1)} %get-tuple-element.392), channel_id=1, source_target_pairs={{0,64},{8,72},{16,80},{24,88},{32,96},{40,104},{48,112},{56,120},{... | collective-permute-start | bytes 331784 | tf_op jit(solution)/shard_map/while/body/ppermute | solution.py:460
  306.5 12.0 %collective-permute-start.46 = (bf16[6,72,128]{2,1,0:T(8,128)(2,1)}, bf16[6,72,128]{2,1,0:T(8,128)(2,1)S(1)}, u32[]{:S(2)}, u32[]{:S(2)}) collective-permute-start(bf16[6,72,128]{2,1,0:T(8,128)(2,1)} %get-tuple-element.393), channel_id=1, source_target_pairs={{0,128},{8,136},{16,144},{24,152},{32,160},{40,168},{48,176},{56,1... | collective-permute-start | bytes 331784 | tf_op jit(solution)/shard_map/while/body/ppermute | solution.py:460
  309.4 9.0 %collective-permute-start.47 = (bf16[6,72,128]{2,1,0:T(8,128)(2,1)}, bf16[6,72,128]{2,1,0:T(8,128)(2,1)S(1)}, u32[]{:S(2)}, u32[]{:S(2)}) collective-permute-start(bf16[6,72,128]{2,1,0:T(8,128)(2,1)} %get-tuple-element.394), channel_id=1, source_target_pairs={{0,192},{8,200},{16,208},{24,216},{32,224},{40,232},{48,240},{56,2... | collective-permute-start | bytes 331784 | tf_op jit(solution)/shard_map/while/body/ppermute | solution.py:460
  (56 other events, 822.2 us)

commit v6 on v5

--- a/solution.py
+++ b/solution.py
@@ -12,7 +12,7 @@
 F32 = jnp.float32
 KX, KZ = 6, 2
 NX, NZ = 3 * KX, 8 * KZ
-SENT, RELAY, POS, HOME, LATE, STEPS, MODE, TABLE = 0, 32, 64, 128, 160, 192, 224, 256
+SENT, RELAY, POS, BACK, HOME, LATE, STEPS, MODE, TABLE = 0, 32, 64, 96, 128, 160, 192, 224, 256
 OUT, BASE, STEP1, RANKED = 0, 32, 64, 96
 
 VMEM = pl.BlockSpec(memory_space=pltpu.VMEM)
@@ -140,7 +140,7 @@
         dens[pl.ds(half + at, 32), 128:256] = parts[n][row, 288:320, :]
 
 
-def one_dimer(steps, me, load, outs, scratch):
+def one_dimer(steps, me, load, out, scratch):
     stacked, weighted, dens, current, squares = scratch
 
     @pl.when(steps > 0)
@@ -198,14 +198,15 @@
             change = current[own, own].astype(F32) - dens[own, :].astype(F32) - eye
             dens[own, :] = change.astype(BF16)
         for n in range(8):
-            at = pl.multiple_of(lax.bitwise_xor(me, n) * 32, 32)
+            to = lax.bitwise_xor(me, n)
+            at = pl.multiple_of(to * 32, 32)
             lanes = slice(n * 128, n * 128 + 128)
             for r in range(2):
                 change = dens[pl.ds(r * 256 + at, 32), :]
-                outs[n][r, 0:32, :] = change[:, 0:128]
-                outs[n][r, 32:64, :] = change[:, 128:256]
+                out[to, r, 0:32, :] = change[:, 0:128]
+                out[to, r, 32:64, :] = change[:, 128:256]
                 partner = jnp.broadcast_to(fits[1 - r][:, lanes], (8, 128))
-                outs[n][r, 64:72, :] = partner.astype(BF16)
+                out[to, r, 64:72, :] = partner.astype(BF16)
 
 
 SCRATCH = [
@@ -218,18 +219,17 @@
 
 
 def run_dimers(kernel, count, tables, blocks, maps, parts):
-    shape = jax.ShapeDtypeStruct((2 * count, 72, 128), BF16)
     specs = []
     for block, index_map in zip(blocks, maps, strict=True):
         specs += [pl.BlockSpec((block, 320, 128), index_map)] * 8
     return pl.pallas_call(
         kernel,
-        out_shape=[shape] * 8,
+        out_shape=jax.ShapeDtypeStruct((8, 2 * count, 72, 128), BF16),
         grid_spec=pltpu.PrefetchScalarGridSpec(
             num_scalar_prefetch=2,
             grid=(count,),
             in_specs=specs,
-            out_specs=[pl.BlockSpec((2, 72, 128), lambda i, *_: (i, 0, 0))] * 8,
+            out_specs=pl.BlockSpec((8, 2, 72, 128), lambda i, *_: (0, i, 0, 0)),
             scratch_shapes=SCRATCH,
         ),
         name="dimers",
@@ -241,7 +241,7 @@
 
 def kernel_1(table_ref, me_ref, *refs):
     me, i = me_ref[0], pl.program_id(0)
-    first, second, outs, scratch = refs[0:8], refs[8:16], refs[16:24], refs[24:]
+    first, second, out, scratch = refs[0:8], refs[8:16], refs[16], refs[17:]
     stacked, dens = scratch[0], scratch[2]
 
     def load():
@@ -249,12 +249,12 @@
         take(256, me, second, 0, stacked, dens)
 
     other = table_ref[RANKED + ranked_at(me, i)]
-    one_dimer(table_ref[STEP1 + other], me, load, outs, scratch)
+    one_dimer(table_ref[STEP1 + other], me, load, out, scratch)
 
 
 def kernel_2(table_ref, me_ref, *refs):
     me, i = me_ref[0], pl.program_id(0)
-    home, late, outs, scratch = refs[0:8], refs[8:16], refs[16:24], refs[24:]
+    home, late, out, scratch = refs[0:8], refs[8:16], refs[16], refs[17:]
     stacked, dens = scratch[0], scratch[2]
     split = table_ref[MODE + me] > 0
 
@@ -278,10 +278,10 @@
         def _():
             take(256, me, late, jnp.where(split, 1, i), stacked, dens)
 
-    one_dimer(table_ref[STEPS + 2 * me + i], me, load, outs, scratch)
-
-
-def plan_kernel(me_ref, inside_ref, count_ref, list_ref, table_ref, left_ref, to_x, to_z, n_direct, n_third, n_self, n_split, room):
+    one_dimer(table_ref[STEPS + 2 * me + i], me, load, out, scratch)
+
+
+def plan_kernel(me_ref, inside_ref, count_ref, list_ref, table_ref, left_ref, to_x, to_z, n_direct, n_third, n_self, n_split, room, taken):
     me = me_ref[0]
     me_x, me_z = me >> 3, me & 7
 
@@ -300,6 +300,7 @@
         n_self[n] = 0
         n_split[n] = inside_ref[n]
         room[n] = 1 + inside_ref[n]
+        taken[n] = 0
 
     loop(TABLE // 8, clear)
     loop(16, clear_x)
@@ -310,11 +311,13 @@
 
     def can(o, c, extra):
         zo, xc, zc = o & 7, c >> 3, c & 7
-        return (to_x[o * 4 + xc] < KX) & ((zo == zc) | (to_z[xc * 64 + zo * 8 + zc] + extra < KZ))
+        free = ((taken[c] >> o) & 1) == 0
+        return free & (to_x[o * 4 + xc] < KX) & ((zo == zc) | (to_z[xc * 64 + zo * 8 + zc] + extra < KZ))
 
     def send(o, slot, c, at_x, at_z, n_x, n_z):
         xo, zo, xc, zc = o >> 3, o & 7, c >> 3, c & 7
         move_x, move_z = xo != xc, zo != zc
+        taken[c] = taken[c] | lax.shift_left(jnp.int32(1), o)
         to_x[at_x] = n_x + jnp.where(move_x, 1, 0)
         to_z[at_z] = n_z + jnp.where(move_z, 1, 0)
         in_x = (lax.bitwise_xor(xo, xc) - 1) * KX + n_x
@@ -322,6 +325,7 @@
         @pl.when(zo == me_z)
         def _():
             put(SENT + in_x, move_x & (o == me), SENT + 31, slot)
+            put(BACK + c, o == me, SENT + 31, slot)
             put(RELAY + zc * KZ + n_z, move_z & (xc == me_x), RELAY + 31, jnp.where(move_x, 32 + in_x, slot))
 
         return jnp.where(move_z, 32 + NX + zo * KZ + n_z, 32 + in_x)
@@ -336,8 +340,9 @@
         x_at_b, z_at_b = oa * 4 + xb, xb * 64 + za * 8 + zb
         x_a, z_a, x_b, z_b = to_x[x_at_a], to_z[z_at_a], to_x[x_at_b], to_z[z_at_b]
         room_a, room_b = room[oa], room[ob]
-        can_a = (x_a < KX) & (z_a < KZ) & (room_a <= 8)
-        can_b = (x_b < KX) & (z_b < KZ) & (room_b <= 8)
+        free_a, free_b = ((taken[oa] >> ob) & 1) == 0, ((taken[ob] >> oa) & 1) == 0
+        can_a = free_a & (x_a < KX) & (z_a < KZ) & (room_a <= 8)
+        can_b = free_b & (x_b < KX) & (z_b < KZ) & (room_b <= 8)
         use_a = can_a & (jnp.logical_not(can_b) | (z_a * 4 + room_a <= z_b * 4 + room_b))
         apart = oa != ob
         direct = apart & (can_a | can_b)
@@ -362,7 +367,7 @@
             @pl.when(c == me)
             def _():
                 table_ref[POS + 2 * at] = stay
-                table_ref[POS + 2 * at + 1] = late
+                table_ref[POS + 2 * at + 1] = 32 + o
                 table_ref[HOME + at] = stay
                 table_ref[LATE + at] = late
                 table_ref[STEPS + at] = cost
@@ -426,8 +431,8 @@
                     @pl.when(c == me)
                     def _():
                         at = 2 * (7 - t)
-                        table_ref[POS + 2 * at] = late_a
-                        table_ref[POS + 2 * at + 1] = late_b
+                        table_ref[POS + 2 * at] = 32 + oa
+                        table_ref[POS + 2 * at + 1] = 32 + ob
                         table_ref[LATE + at] = late_a
                         table_ref[LATE + at + 1] = late_b
                         table_ref[STEPS + at] = cost
@@ -443,7 +448,7 @@
         out_shape=[jax.ShapeDtypeStruct((TABLE,), s32), jax.ShapeDtypeStruct(words.shape, s32)],
         in_specs=[SMEM] * 4,
         out_specs=[SMEM] * 2,
-        scratch_shapes=[pltpu.SMEM((128,), s32), pltpu.SMEM((256,), s32)] + [pltpu.SMEM((32,), s32)] * 5,
+        scratch_shapes=[pltpu.SMEM((128,), s32), pltpu.SMEM((256,), s32)] + [pltpu.SMEM((32,), s32)] * 6,
         name="plan",
         cost_estimate=pl.CostEstimate(flops=1000, bytes_accessed=30_000_000, transcendentals=0),
     )(me, inside_count, count, words)
@@ -454,6 +459,10 @@
     for k in range(1, 8):
         got.append(lax.ppermute(parts[k], "basis", [(i, i ^ k) for i in range(8)]))
     return got
+
+
+def give_back(done):
+    return lax.all_to_all(done, "basis", split_axis=0, concat_axis=0, tiled=True).reshape(-1, 72, 128)
 
 
 def along_x(parts):
@@ -554,6 +563,11 @@
             pack(tables[:1], me_b, lambda t, me, n, row: t[0][BASE + served(t, me, n, row)], 8, 4, home, [])
         )
         in_x = along_x(pack(tables, me_b, lambda t, me, n, row: t[1][SENT + n * KX + row], 3, KX, home, []))
+
+        def home_at(t, me, n, row):
+            return t[1][HOME + 2 * lax.bitwise_xor(me, n) + row]
+
+        home_2 = exchange(pack(tables, me_b, home_at, 8, 2, home, []))
         parts_1 = pack(tables, me_b, served, 8, 4, (), [in_1])
         away_1 = exchange(parts_1)
         (out_2,) = pack(
@@ -561,75 +575,39 @@
         )
         in_z = along_z(out_2)
 
-        def home_at(t, me, n, row):
-            return t[1][HOME + 2 * lax.bitwise_xor(me, n) + row]
-
-        home_parts = pack(tuple(after(tables, away_1)), me_b, home_at, 8, 2, home, [])
-        home_2 = exchange(home_parts)
         one = lambda i, *_: (i, 0, 0)
         ready_1 = run_dimers(kernel_1, 4, (table_1, me_b), (1, 1), (one, one), [*home_1, *away_1])
-        done_1 = exchange(ready_1)
-
-        late_parts = pack(
-            tables,
-            me_b,
-            lambda t, me, n, row: t[1][LATE + 2 * lax.bitwise_xor(me, n) + row] - 32,
-            8,
-            2,
-            (),
-            [*in_x, after(in_z, away_1)],
+        done_1 = give_back(ready_1)
+
+        def late_at(t, me, n, row):
+            return t[1][LATE + 2 * lax.bitwise_xor(me, n) + row] - 32
+
+        late_parts = pack(tables, me_b, late_at, 8, 2, (), [*in_x, after(in_z, away_1)])
+        late_2 = exchange(late_parts)
+        whole = lambda i, *_: (0, 0, 0)
+        ready_2 = run_dimers(kernel_2, 2, (table_2, me_b), (2, 2), (whole, whole), [*home_2, *late_2])
+
+        def place_1(t, row):
+            return t[0][RANKED + ranked_at(row // 8, row % 8 // 2)]
+
+        def place_2(t, row):
+            at = row // 2
+            return jnp.where(t[1][STEPS + at] > 0, t[1][POS + row], -1)
+
+        (ret_1,) = place(
+            tables, me_b, [done_1], [lambda t, me, row: jnp.where(row % 2 == 1, place_1(t, row), -1)], [32]
         )
-        late_2 = exchange(late_parts)
-        done_1 = after(done_1, late_parts)
-        whole = lambda i, *_: (0, 0, 0)
-        done_2 = exchange(
-            run_dimers(kernel_2, 2, (table_2, me_b), (2, 2), (whole, whole), [*home_2, *late_2])
-        )
-
-        def back_to(k):
-            return lambda t, me, row: jnp.where(row % 2 == 1, served(t, me, k, row // 2), -1)
-
-        (ret_1,) = place(tables, me_b, done_1, [back_to(k) for k in range(8)], [32])
         back_1 = across(ret_1)
-
-        def place_2(t, me, k, row):
-            at = 2 * lax.bitwise_xor(me, k) + row // 2
-            return jnp.where(t[1][STEPS + at] > 0, t[1][POS + 2 * at + row % 2], -1)
-
-        def back_z(k):
-            return lambda t, me, row: place_2(t, me, k, row) - 32 - NX
-
-        def back_x(k):
-            return lambda t, me, row: place_2(t, me, k, row) - 32
-
-        (ret_z,) = place(tables, me_b, done_2, [back_z(k) for k in range(8)], [NZ])
-        rest_z = along_z(after(ret_z, back_1))
-        ret_x = place(
-            tables,
-            me_b,
-            [*done_2, rest_z],
-            [back_x(k) for k in range(8)] + [lambda t, me, row: t[1][RELAY + row] - 32],
-            [KX] * 3,
-        )
-        rest_x = along_x(ret_x)
-
-        def stay_1(k):
-            return lambda t, me, row: jnp.where(row % 2 == 0, t[0][BASE + served(t, me, k, row // 2)], -1)
-
-        def stay_2(k):
-            return lambda t, me, row: place_2(t, me, k, row)
-
-        def from_x(k):
-            return lambda t, me, row: t[1][SENT + k * KX + row]
-
-        finds = (
-            [stay_1(k) for k in range(8)]
-            + [stay_2(k) for k in range(8)]
-        )
-        finds += [lambda t, me, row: t[0][OUT + row]]
-        dens, emb = add_up(tables, me_b, [*done_1, *done_2, back_1], finds, dens, emb)
-        finds = [lambda t, me, row: t[1][RELAY + row]] + [from_x(k) for k in range(3)]
-        dens, emb = add_up(tables, me_b, [rest_z, *rest_x], finds, dens, emb)
+        done_2 = give_back(after(ready_2, back_1))
+        (ret_2,) = place(tables, me_b, [done_2], [lambda t, me, row: place_2(t, row) - 32], [32])
+        back_2 = across(ret_2)
+        finds = [
+            lambda t, me, row: jnp.where(row % 2 == 0, t[0][BASE + place_1(t, row)], -1),
+            lambda t, me, row: place_2(t, row),
+            lambda t, me, row: t[0][OUT + row],
+        ]
+        dens, emb = add_up(tables, me_b, [done_1, done_2, back_1], finds, dens, emb)
+        dens, emb = add_up(tables, me_b, [back_2], [lambda t, me, row: t[1][BACK + row]], dens, emb)
         return jnp.sum(left), left, dens, emb
 
     start = (

time: 329 us -> 359 us (1.091)
  waiting for transfers between devices: 105 us -> 143 us
  blocking collectives: 9.55 us -> 28.6 us
  starting transfers between devices: 97.2 us -> 78.2 us
    ppermute x6 -> x3, waiting for transfers between devices: 0.02 us -> 23 us  [along_x(): lax.ppermute(parts[k - 1], 'frag', [(i, i ^ 8 * k) for i in range(32)])]
    all_to_all x0 -> x1, blocking collectives: none -> 19 us  [give_back(): lax.all_to_all(done, 'basis', split_axis=0, concat_axis=0, tiled=True)]
    ppermute x42 -> x28, starting transfers between devices: 43.9 us -> 30.3 us  [exchange(): got.append(lax.ppermute(parts[k], 'basis', [(i, i ^ k) for i in range(8)]))]
    all_to_all x2 -> x1, starting transfers between devices: 17.9 us -> 5.84 us  [along_z(): lax.all_to_all(part, 'frag', 0, 0, tiled=True, axis_index_groups=groups)]
    all_to_all x2 -> x1, waiting for transfers between devices: 10.9 us -> 21 us  [along_z(): lax.all_to_all(part, 'frag', 0, 0, tiled=True, axis_index_groups=groups)]
    all_to_all x3 -> x4, waiting for transfers between devices: 31.1 us -> 40.9 us  [across(): return lax.all_to_all(part, 'frag', split_axis=0, concat_axis=0, tiled=True)]
    all_to_all x3 -> x4, starting transfers between devices: 26 us -> 33.1 us  [across(): return lax.all_to_all(part, 'frag', split_axis=0, concat_axis=0, tiled=True)]
    pallas_call x1, Pallas kernels: 20.1 us -> 25.6 us  [plan_rest(): pl.pallas_call(plan_kernel, out_shape=[jax.ShapeDtypeStruct((TABLE,), s32...]
  transfers between devices with their start and end apart: 53 -> 37, of which waited for: 24 -> 20; matrix products, arithmetic and copies ran while one was open for 2% -> 2% of each run, Pallas kernels for 26% -> 18%
where the time goes in v6:
time: 359 us; the launch traced here: 358 us
  waiting for transfers between devices  143 us (40%)
  Pallas kernels  90.8 us (25%)
  starting transfers between devices  78.2 us (22%)
  blocking collectives  28.6 us (8%)
  other arithmetic  9.57 us (3%)
  local copies, waits for them, and re-layouts  5.45 us (2%)
    ppermute x28, waiting for transfers between devices, exchange(): got.append(lax.ppermute(parts[k], 'basis', [(i, i ^ k) for i in range(8)]))  58.3 us
    all_to_all x4, waiting for transfers between devices, across(): return lax.all_to_all(part, 'frag', split_axis=0, concat_axis=0, tiled=True)  40.9 us
    all_to_all x4, starting transfers between devices, across(): return lax.all_to_all(part, 'frag', split_axis=0, concat_axis=0, tiled=True)  33.1 us
    ppermute x28, starting transfers between devices, exchange(): got.append(lax.ppermute(parts[k], 'basis', [(i, i ^ k) for i in range(8)]))  30.3 us
    pallas_call x2, Pallas kernels, run_dimers(): pl.pallas_call(kernel, out_shape=jax.ShapeDtypeStruct((8, 2 * count, 72,...  29.4 us
    pallas_call x1, Pallas kernels, plan_rest(): pl.pallas_call(plan_kernel, out_shape=[jax.ShapeDtypeStruct((TABLE,), s32...  25.6 us
    ppermute x3, waiting for transfers between devices, along_x(): lax.ppermute(parts[k - 1], 'frag', [(i, i ^ 8 * k) for i in range(32)])  23 us
    pallas_call x7, Pallas kernels, pack(): pl.pallas_call(kernel, out_shape=[jax.ShapeDtypeStruct((rows, 320, 128),...  21.9 us
  transfers between devices with their start and end apart: 37, of which 20 were waited for; matrix products, arithmetic and copies ran while one was open for 2% of the time, Pallas kernels for 18%

profile of v6, /device:TPU:32, one launch (start us, length us, event | category | flops | bytes accessed | tf_op | source)
XLA Modules:
  0.0 357.6 jit_solution(9095987789241530441)
XLA Ops:
  2.3 9.6 %all_to_all.46 = s32[8,1,128]{2,1,0:T(1,128)S(1)} all-to-all(s32[8,1,128]{2,1,0:T(1,128)S(1)} %broadcast_in_dim.142), channel_id=1, replica_groups=mesh['frag'=32,'basis'=8] {'basis'}, dimensions={0} | all-to-all | bytes 8192 | tf_op jit(solution)/shard_map/all_to_all | solution.py:495
  12.8 11.2 %all-to-all-start.7 = ((s32[32,1,128]{2,1,0:T(1,128)}), s32[32,1,128]{2,1,0:T(1,128)S(1)}, u32[]{:S(2)}, u32[]{:S(2)}) async-start(s32[32,1,128]{2,1,0:T(1,128)} %broadcast_in_dim.143), calls=%async_computation.7 | async-start | bytes 32768 | tf_op jit(solution)/shard_map/all_to_all | solution.py:478
  24.0 8.6 %all-to-all-done.7 = s32[32,1,128]{2,1,0:T(1,128)S(1)} async-done(((s32[32,1,128]{2,1,0:T(1,128)}), s32[32,1,128]{2,1,0:T(1,128)S(1)}, u32[]{:S(2)}, u32[]{:S(2)}) %all-to-all-start.7) | async-done | bytes 16416 | tf_op jit(solution)/shard_map/all_to_all | solution.py:478
  34.1 322.9 %while.15 = (s32[]{:T(128)}, s32[1024]{0:T(1024)S(1)}, f32[32,32,256]{2,1,0:T(8,128)}, f32[32,128]{1,0:T(8,128)S(1)}, s32[1024]{0:T(1024)S(1)}, /*index=5*/pred[...) while((s32[]{:T(128)}, s32[1024]{0:T(1024)S(1)}, ...), condition=%region_13.14_spmd.clone.clone, body=%region_1.13_spmd.clone.clone | while | flops 24018298880 | bytes 131915224 | solution.py:619
  35.0 3.8 %pack.9 = bf16[32,320,128]{2,1,0:T(8,128)(2,1)} custom-call(s32[32]{0:T(128)} %get-tuple-element.374.refs_0_, s32[1]{0:T(128)} %get-tuple-element.439.refs_2_.refs_1_.me_ref, bf16[32,256,128]{2,1,0:T(8,128)(2,1)} %get-tuple-element.440.refs_3_.refs_2_, bf16[32,32,256]{2,1,0:T(8,128)(2,1)} %get-tuple-element.441.refs_4_.refs_3_), custom_call_target="tpu_custom_call" | custom-call | tf_op jit(solution)/shard_map/while/body/pack/pallas_call | solution.py:68
  38.8 6.1 %all-to-all-start = ((bf16[32,320,128]{2,1,0:T(8,128)(2,1)}), bf16[32,320,128]{2,1,0:T(8,128)(2,1)}, u32[]{:S(2)}, u32[]{:S(2)}) async-start(bf16[32,320,128]{2,1,0:T(8,128)(2,1)} %pack.9), calls=%async_computation | async-start | bytes 5242880 | tf_op jit(solution)/shard_map/while/body/all_to_all | solution.py:478
  45.8 3.1 pack.13
  57.3 25.6 %plan.1 = (s32[256]{0:T(256)}, s32[1024]{0:T(1024)}) custom-call(s32[1]{0:T(128)} %get-tuple-element.436.me_ref, s32[32]{0:T(128)} %select_reduce_fusion.6.inside_ref, s32[1]{0:T(128)} %bitcast.5.count_ref, s32[1024]{0:T(1024)} %select_reduce_fusion.2.list_ref), custom_call_target="tpu_custom_call" | custom-call | flops 1000 | bytes 30000000 | tf_op jit(solution)/shard_map/while/body/plan/pallas_call | solution.py:446
  83.0 21.6 %all-to-all-done.refs_3_ = bf16[32,320,128]{2,1,0:T(8,128)(2,1)} async-done(((bf16[32,320,128]{2,1,0:T(8,128)(2,1)}), bf16[32,320,128]{2,1,0:T(8,128)(2,1)}, u32[]{:S(2)}, u32[]{:S(2)}) %all-to-all-start) | async-done | bytes 2621472 | tf_op jit(solution)/shard_map/while/body/all_to_all | solution.py:478
  104.5 4.1 %pack.10 = (bf16[4,320,128]{2,1,0:T(8,128)(2,1)}, bf16[4,320,128]{2,1,0:T(8,128)(2,1)}, bf16[4,320,128]{2,1,0:T(8,128)(2,1)}, bf16[4,320,128]{2,1,0:T(8,128)(2,1...) custom-call(s32[128]{0:T(128)} %pad_add_fusion.refs_0_.table_ref, ...), custom_call_target="tpu_custom_call" | custom-call | tf_op jit(solution)/shard_map/while/body/pack/pallas_call | solution.py:68
  109.9 2.2 collective-permute-start.10
  113.6 7.3 %collective-permute-done.29.refs_6_ = bf16[4,320,128]{2,1,0:T(8,128)(2,1)} collective-permute-done((bf16[4,320,128]{2,1,0:T(8,128)(2,1)}, bf16[4,320,128]{2,1,0:T(8,128)(2,1)}, u32[]{:S(2)}, u32[]{:S(2)}) %collective-permute-start.29) | collective-permute-done | bytes 327712 | tf_op jit(solution)/shard_map/while/body/ppermute | solution.py:460
  120.9 2.1 collective-permute-done.30.refs_7_
  123.0 2.1 collective-permute-start.14
  125.1 2.1 collective-permute-start.15
  128.3 9.5 %collective-permute-done.13.refs_12_ = bf16[4,320,128]{2,1,0:T(8,128)(2,1)} collective-permute-done((bf16[4,320,128]{2,1,0:T(8,128)(2,1)}, bf16[4,320,128]{2,1,0:T(8,128)(2,1)}, u32[]{:S(2)}, u32[]{:S(2)}) %collective-permute-start.13) | collective-permute-done | bytes 327712 | tf_op jit(solution)/shard_map/while/body/ppermute | solution.py:460
  137.8 5.3 %collective-permute-done.14.refs_13_ = bf16[4,320,128]{2,1,0:T(8,128)(2,1)} collective-permute-done((bf16[4,320,128]{2,1,0:T(8,128)(2,1)}, bf16[4,320,128]{2,1,0:T(8,128)(2,1)}, u32[]{:S(2)}, u32[]{:S(2)}) %collective-permute-start.14) | collective-permute-done | bytes 327712 | tf_op jit(solution)/shard_map/while/body/ppermute | solution.py:460
  143.0 7.6 %collective-permute-done.15.refs_14_ = bf16[4,320,128]{2,1,0:T(8,128)(2,1)} collective-permute-done((bf16[4,320,128]{2,1,0:T(8,128)(2,1)}, bf16[4,320,128]{2,1,0:T(8,128)(2,1)}, u32[]{:S(2)}, u32[]{:S(2)}) %collective-permute-start.15) | collective-permute-done | bytes 327712 | tf_op jit(solution)/shard_map/while/body/ppermute | solution.py:460
  150.6 6.2 %collective-permute-done.16.refs_15_ = bf16[4,320,128]{2,1,0:T(8,128)(2,1)} collective-permute-done((bf16[4,320,128]{2,1,0:T(8,128)(2,1)}, bf16[4,320,128]{2,1,0:T(8,128)(2,1)}, u32[]{:S(2)}, u32[]{:S(2)}) %collective-permute-start.16) | collective-permute-done | bytes 327712 | tf_op jit(solution)/shard_map/while/body/ppermute | solution.py:460
  156.8 18.5 %dimers.3 = bf16[8,8,72,128]{3,2,1,0:T(8,128)(2,1)} custom-call(s32[128]{0:T(128)} %pad_add_fusion.refs_0_.table_ref, s32[1]{0:T(128)} %get-tuple-element.439.refs_2_.refs_1_.me_ref, bf16[4,320,128]{2,1,0:T(8,128)(2,1)} %get-tuple-element.299.refs_0_, bf16[4,320,128]{2,1,0:T(8,128)(2,1)} %copy-done.10, bf16[4,320,128]{2,1,0:T(8,128)(2,1)} %copy-done.11, ...), custom_call_target="tpu_custom_call" | custom-call | flops 16000000000 | bytes 6000000 | tf_op jit(solution)/shard_map/while/body/dimers/pallas_call | solution.py:225
  175.3 4.3 %all-to-all-start.2 = ((bf16[8,8,72,128]{3,2,1,0:T(8,128)(2,1)}), bf16[8,8,72,128]{3,2,1,0:T(8,128)(2,1)}, u32[]{:S(2)}, u32[]{:S(2)}) async-start(bf16[8,8,72,128]{3,2,1,0:T(8,128)(2,1)} %dimers.3), calls=%async_computation.2 | async-start | bytes 2359296 | tf_op jit(solution)/shard_map/while/body/all_to_all | solution.py:465
  179.5 2.2 pack.8
  184.2 2.2 collective-permute-start.9
  186.4 9.6 %collective-permute-done.7.refs_5_.refs_3_ = bf16[6,320,128]{2,1,0:T(8,128)(2,1)S(1)} collective-permute-done((bf16[6,320,128]{2,1,0:T(8,128)(2,1)}, bf16[6,320,128]{2,1,0:T(8,128)(2,1)S(1)}, u32[]{:S(2)}, u32[]{:S(2)}) %collective-permute-start.7) | collective-permute-done | bytes 491552 | tf_op jit(solution)/shard_map/while/body/ppermute | solution.py:469
  196.0 10.9 %collective-permute-done.8.refs_6_.refs_4_ = bf16[6,320,128]{2,1,0:T(8,128)(2,1)} collective-permute-done((bf16[6,320,128]{2,1,0:T(8,128)(2,1)}, bf16[6,320,128]{2,1,0:T(8,128)(2,1)}, u32[]{:S(2)}, u32[]{:S(2)}) %collective-permute-start.8) | collective-permute-done | bytes 491552 | tf_op jit(solution)/shard_map/while/body/ppermute | solution.py:469
  206.9 2.6 collective-permute-done.9.refs_7_.refs_5_
  209.5 3.0 pack.11
  212.5 5.8 %all-to-all-start.1 = ((bf16[16,320,128]{2,1,0:T(8,128)(2,1)}), bf16[16,320,128]{2,1,0:T(8,128)(2,1)}, u32[]{:S(2)}, u32[]{:S(2)}) async-start(bf16[16,320,128]{2,1,0:T(8,128)(2,1)} %pack.11), calls=%async_computation.1 | async-start | bytes 2621440 | tf_op jit(solution)/shard_map/while/body/all_to_all | solution.py:474
  218.3 2.1 pack.7
  222.3 3.2 collective-permute-start.3
  225.5 4.2 %place.2 = bf16[32,72,128]{2,1,0:T(8,128)(2,1)} custom-call(s32[128]{0:T(128)} %pad_add_fusion.refs_0_.table_ref, s32[256]{0:T(256)} %get-tuple-element.264.refs_1_.table_ref, s32[1]{0:T(128)} %get-tuple-element.439.refs_2_.refs_1_.me_ref, bf16[64,72,128]{2,1,0:T(8,128)(2,1)} %bitcast.6.refs_3_), custom_call_target="tpu_custom_call" | custom-call | tf_op jit(solution)/shard_map/while/body/place/pallas_call | solution.py:95
  229.7 21.0 %all-to-all-done.1.refs_6_ = bf16[16,320,128]{2,1,0:T(8,128)(2,1)} async-done(((bf16[16,320,128]{2,1,0:T(8,128)(2,1)}), bf16[16,320,128]{2,1,0:T(8,128)(2,1)}, u32[]{:S(2)}, u32[]{:S(2)}) %all-to-all-start.1) | async-done | bytes 1310752 | tf_op jit(solution)/shard_map/while/body/all_to_all | solution.py:474
  250.7 5.3 %all-to-all-start.3 = ((bf16[32,72,128]{2,1,0:T(8,128)(2,1)}), bf16[32,72,128]{2,1,0:T(8,128)(2,1)S(1)}, u32[]{:S(2)}, u32[]{:S(2)}) async-start(bf16[32,72,128]{2,1,0:T(8,128)(2,1)} %place.2), calls=%async_computation.3 | async-start | bytes 1179648 | tf_op jit(solution)/shard_map/while/body/all_to_all | solution.py:478
  257.9 3.5 pack.12
  262.6 2.5 collective-permute-start.6
  267.1 2.6 collective-permute-done.5.refs_6_
  269.9 3.3 collective-permute-done.6.refs_7_
  276.2 4.1 %collective-permute-done.20.refs_12_ = bf16[2,320,128]{2,1,0:T(8,128)(2,1)S(1)} collective-permute-done((bf16[2,320,128]{2,1,0:T(8,128)(2,1)}, bf16[2,320,128]{2,1,0:T(8,128)(2,1)S(1)}, u32[]{:S(2)}, u32[]{:S(2)}) %collective-permute-start.20) | collective-permute-done | bytes 163872 | tf_op jit(solution)/shard_map/while/body/ppermute | solution.py:460
  280.3 2.4 collective-permute-done.21.refs_13_
  282.7 4.0 %collective-permute-done.22.refs_14_ = bf16[2,320,128]{2,1,0:T(8,128)(2,1)S(1)} collective-permute-done((bf16[2,320,128]{2,1,0:T(8,128)(2,1)}, bf16[2,320,128]{2,1,0:T(8,128)(2,1)S(1)}, u32[]{:S(2)}, u32[]{:S(2)}) %collective-permute-start.22) | collective-permute-done | bytes 163872 | tf_op jit(solution)/shard_map/while/body/ppermute | solution.py:460
  286.7 3.4 collective-permute-done.23.refs_15_
  290.8 10.9 %dimers.2 = bf16[8,4,72,128]{3,2,1,0:T(8,128)(2,1)} custom-call(s32[256]{0:T(256)} %get-tuple-element.264.refs_1_.table_ref, s32[1]{0:T(128)} %get-tuple-element.439.refs_2_.refs_1_.me_ref, bf16[2,320,128]{2,1,0:T(8,128)(2,1)} %get-tuple-element.268.refs_0_, bf16[2,320,128]{2,1,0:T(8,128)(2,1)} %copy-done.12, bf16[2,320,128]{2,1,0:T(8,128)(2,1)} %copy-done.13, ...), custom_call_target="tpu_custom_call" | custom-call | flops 8000000000 | bytes 3000000 | tf_op jit(solution)/shard_map/while/body/dimers/pallas_call | solution.py:225
  301.7 19.0 %all_to_all.47 = bf16[8,4,72,128]{3,2,1,0:T(8,128)(2,1)} all-to-all(bf16[8,4,72,128]{3,2,1,0:T(8,128)(2,1)} %dimers.2), channel_id=1, replica_groups=mesh['frag'=32,'basis'=8] {'basis'}, dimensions={0} | all-to-all | bytes 1179648 | tf_op jit(solution)/shard_map/while/body/all_to_all | solution.py:465
  320.8 2.6 place.3
  323.4 10.6 %all-to-all-start.5 = ((bf16[32,72,128]{2,1,0:T(8,128)(2,1)}), bf16[32,72,128]{2,1,0:T(8,128)(2,1)S(1)}, u32[]{:S(2)}, u32[]{:S(2)}) async-start(bf16[32,72,128]{2,1,0:T(8,128)(2,1)} %place.3), calls=%async_computation.5 | async-start | bytes 1179648 | tf_op jit(solution)/shard_map/while/body/all_to_all | solution.py:478
  334.6 2.1 select_reduce_fusion
  336.7 5.3 %add_up.2 = (f32[32,32,256]{2,1,0:T(8,128)S(1)}, f32[32,128]{1,0:T(8,128)S(1)}) custom-call(s32[128]{0:T(128)} %pad_add_fusion.refs_0_.table_ref, s32[256]{0:T(256)} %get-tuple-element.264.refs_1_.table_ref, s32[1]{0:T(128)} %get-tuple-element.439.refs_2_.refs_1_.me_ref, ...), custom_call_target="tpu_custom_call", output_to_operand_aliasing={{0}: (6, {}), {1}: (7, {})} | custom-call | tf_op jit(solution)/shard_map/while/body/add_up/pallas_call | solution.py:124
  342.1 10.8 %all-to-all-done.5.refs_3_ = bf16[32,72,128]{2,1,0:T(8,128)(2,1)S(1)} async-done(((bf16[32,72,128]{2,1,0:T(8,128)(2,1)}), bf16[32,72,128]{2,1,0:T(8,128)(2,1)S(1)}, u32[]{:S(2)}, u32[]{:S(2)}) %all-to-all-start.5) | async-done | bytes 589856 | tf_op jit(solution)/shard_map/while/body/all_to_all | solution.py:478
  (136 shorter events, 35.8 us)
Async XLA Ops:
  12.8 19.8 %all-to-all-start.7 = ((s32[32,1,128]{2,1,0:T(1,128)}), s32[32,1,128]{2,1,0:T(1,128)S(1)}, u32[]{:S(2)}, u32[]{:S(2)}) async-start(s32[32,1,128]{2,1,0:T(1,128)} %broadcast_in_dim.143), calls=%async_computation.7 | async-start | bytes 32768 | tf_op jit(solution)/shard_map/all_to_all | solution.py:478
  38.8 65.7 %all-to-all-start = ((bf16[32,320,128]{2,1,0:T(8,128)(2,1)}), bf16[32,320,128]{2,1,0:T(8,128)(2,1)}, u32[]{:S(2)}, u32[]{:S(2)}) async-start(bf16[32,320,128]{2,1,0:T(8,128)(2,1)} %pack.9), calls=%async_computation | async-start | bytes 5242880 | tf_op jit(solution)/shard_map/while/body/all_to_all | solution.py:478
  48.9 59.8 %collective-permute-start.24 = (bf16[4,320,128]{2,1,0:T(8,128)(2,1)}, bf16[4,320,128]{2,1,0:T(8,128)(2,1)S(1)}, u32[]{:S(2)}, u32[]{:S(2)}) collective-permute-start(bf16[4,320,128]{2,1,0:T(8,128)(2,1)} %get-tuple-element.300), channel_id=1, source_target_pairs={{0,1},{1,0},{2,3},{3,2},{4,5},{5,4},{6,7},{7,6},{8,9},{9,8},{10,11... | collective-permute-start | bytes 983048 | tf_op jit(solution)/shard_map/while/body/ppermute | solution.py:460
  48.9 61.0 %collective-permute-start.25 = (bf16[4,320,128]{2,1,0:T(8,128)(2,1)}, bf16[4,320,128]{2,1,0:T(8,128)(2,1)S(1)}, u32[]{:S(2)}, u32[]{:S(2)}) collective-permute-start(bf16[4,320,128]{2,1,0:T(8,128)(2,1)} %get-tuple-element.301), channel_id=1, source_target_pairs={{0,2},{1,3},{2,0},{3,1},{4,6},{5,7},{6,4},{7,5},{8,10},{9,11},{10,... | collective-permute-start | bytes 983048 | tf_op jit(solution)/shard_map/while/body/ppermute | solution.py:460
  49.5 60.5 %collective-permute-start.26 = (bf16[4,320,128]{2,1,0:T(8,128)(2,1)}, bf16[4,320,128]{2,1,0:T(8,128)(2,1)}, u32[]{:S(2)}, u32[]{:S(2)}) collective-permute-start(bf16[4,320,128]{2,1,0:T(8,128)(2,1)} %get-tuple-element.302), channel_id=1, source_target_pairs={{0,3},{1,2},{2,1},{3,0},{4,7},{5,6},{6,5},{7,4},{8,11},{9,10},{10,... | collective-permute-start | bytes 983048 | tf_op jit(solution)/shard_map/while/body/ppermute | solution.py:460
  50.8 61.3 %collective-permute-start.27 = (bf16[4,320,128]{2,1,0:T(8,128)(2,1)}, bf16[4,320,128]{2,1,0:T(8,128)(2,1)}, u32[]{:S(2)}, u32[]{:S(2)}) collective-permute-start(bf16[4,320,128]{2,1,0:T(8,128)(2,1)} %get-tuple-element.303), channel_id=1, source_target_pairs={{0,4},{1,5},{2,6},{3,7},{4,0},{5,1},{6,2},{7,3},{8,12},{9,13},{10,... | collective-permute-start | bytes 983048 | tf_op jit(solution)/shard_map/while/body/ppermute | solution.py:460
  51.9 60.2 %collective-permute-start.28 = (bf16[4,320,128]{2,1,0:T(8,128)(2,1)}, bf16[4,320,128]{2,1,0:T(8,128)(2,1)}, u32[]{:S(2)}, u32[]{:S(2)}) collective-permute-start(bf16[4,320,128]{2,1,0:T(8,128)(2,1)} %get-tuple-element.304), channel_id=1, source_target_pairs={{0,5},{1,4},{2,7},{3,6},{4,1},{5,0},{6,3},{7,2},{8,13},{9,12},{10,... | collective-permute-start | bytes 983048 | tf_op jit(solution)/shard_map/while/body/ppermute | solution.py:460
  108.7 48.2 %copy-start.10 = (bf16[4,320,128]{2,1,0:T(8,128)(2,1)}, bf16[4,320,128]{2,1,0:T(8,128)(2,1)S(1)}, u32[]{:S(2)}) copy-start(bf16[4,320,128]{2,1,0:T(8,128)(2,1)S(1)} %collective-permute-done.24.refs_1_) | copy-start | bytes 983044 | tf_op jit(solution)/shard_map/while
  108.7 12.2 %collective-permute-start.29 = (bf16[4,320,128]{2,1,0:T(8,128)(2,1)}, bf16[4,320,128]{2,1,0:T(8,128)(2,1)}, u32[]{:S(2)}, u32[]{:S(2)}) collective-permute-start(bf16[4,320,128]{2,1,0:T(8,128)(2,1)} %get-tuple-element.305), channel_id=1, source_target_pairs={{0,6},{1,7},{2,4},{3,5},{4,2},{5,3},{6,0},{7,1},{8,14},{9,15},{10,... | collective-permute-start | bytes 983048 | tf_op jit(solution)/shard_map/while/body/ppermute | solution.py:460
  109.9 46.9 %copy-start.11 = (bf16[4,320,128]{2,1,0:T(8,128)(2,1)}, bf16[4,320,128]{2,1,0:T(8,128)(2,1)S(1)}, u32[]{:S(2)}) copy-start(bf16[4,320,128]{2,1,0:T(8,128)(2,1)S(1)} %collective-permute-done.25.refs_2_) | copy-start | bytes 983044 | tf_op jit(solution)/shard_map/while
  109.9 13.1 %collective-permute-start.30 = (bf16[4,320,128]{2,1,0:T(8,128)(2,1)}, bf16[4,320,128]{2,1,0:T(8,128)(2,1)}, u32[]{:S(2)}, u32[]{:S(2)}) collective-permute-start(bf16[4,320,128]{2,1,0:T(8,128)(2,1)} %get-tuple-element.306), channel_id=1, source_target_pairs={{0,7},{1,6},{2,5},{3,4},{4,3},{5,2},{6,1},{7,0},{8,15},{9,14},{10,... | collective-permute-start | bytes 983048 | tf_op jit(solution)/shard_map/while/body/ppermute | solution.py:460
  109.9 15.2 %collective-permute-start.10 = (bf16[4,320,128]{2,1,0:T(8,128)(2,1)}, bf16[4,320,128]{2,1,0:T(8,128)(2,1)}, u32[]{:S(2)}, u32[]{:S(2)}) collective-permute-start(bf16[4,320,128]{2,1,0:T(8,128)(2,1)} %get-tuple-element.280), channel_id=1, source_target_pairs={{0,1},{1,0},{2,3},{3,2},{4,5},{5,4},{6,7},{7,6},{8,9},{9,8},{10,11... | collective-permute-start | bytes 983048 | tf_op jit(solution)/shard_map/while/body/ppermute | solution.py:460
  112.1 15.1 %collective-permute-start.11 = (bf16[4,320,128]{2,1,0:T(8,128)(2,1)}, bf16[4,320,128]{2,1,0:T(8,128)(2,1)}, u32[]{:S(2)}, u32[]{:S(2)}) collective-permute-start(bf16[4,320,128]{2,1,0:T(8,128)(2,1)} %get-tuple-element.281), channel_id=1, source_target_pairs={{0,2},{1,3},{2,0},{3,1},{4,6},{5,7},{6,4},{7,5},{8,10},{9,11},{10,... | collective-permute-start | bytes 983048 | tf_op jit(solution)/shard_map/while/body/ppermute | solution.py:460
  112.1 16.2 %collective-permute-start.12 = (bf16[4,320,128]{2,1,0:T(8,128)(2,1)}, bf16[4,320,128]{2,1,0:T(8,128)(2,1)}, u32[]{:S(2)}, u32[]{:S(2)}) collective-permute-start(bf16[4,320,128]{2,1,0:T(8,128)(2,1)} %get-tuple-element.282), channel_id=1, source_target_pairs={{0,3},{1,2},{2,1},{3,0},{4,7},{5,6},{6,5},{7,4},{8,11},{9,10},{10,... | collective-permute-start | bytes 983048 | tf_op jit(solution)/shard_map/while/body/ppermute | solution.py:460
  120.9 16.9 %collective-permute-start.13 = (bf16[4,320,128]{2,1,0:T(8,128)(2,1)}, bf16[4,320,128]{2,1,0:T(8,128)(2,1)}, u32[]{:S(2)}, u32[]{:S(2)}) collective-permute-start(bf16[4,320,128]{2,1,0:T(8,128)(2,1)} %get-tuple-element.283), channel_id=1, source_target_pairs={{0,4},{1,5},{2,6},{3,7},{4,0},{5,1},{6,2},{7,3},{8,12},{9,13},{10,... | collective-permute-start | bytes 983048 | tf_op jit(solution)/shard_map/while/body/ppermute | solution.py:460
  123.0 20.0 %collective-permute-start.14 = (bf16[4,320,128]{2,1,0:T(8,128)(2,1)}, bf16[4,320,128]{2,1,0:T(8,128)(2,1)}, u32[]{:S(2)}, u32[]{:S(2)}) collective-permute-start(bf16[4,320,128]{2,1,0:T(8,128)(2,1)} %get-tuple-element.284), channel_id=1, source_target_pairs={{0,5},{1,4},{2,7},{3,6},{4,1},{5,0},{6,3},{7,2},{8,13},{9,12},{10,... | collective-permute-start | bytes 983048 | tf_op jit(solution)/shard_map/while/body/ppermute | solution.py:460
  125.1 25.5 %collective-permute-start.15 = (bf16[4,320,128]{2,1,0:T(8,128)(2,1)}, bf16[4,320,128]{2,1,0:T(8,128)(2,1)}, u32[]{:S(2)}, u32[]{:S(2)}) collective-permute-start(bf16[4,320,128]{2,1,0:T(8,128)(2,1)} %get-tuple-element.285), channel_id=1, source_target_pairs={{0,6},{1,7},{2,4},{3,5},{4,2},{5,3},{6,0},{7,1},{8,14},{9,15},{10,... | collective-permute-start | bytes 983048 | tf_op jit(solution)/shard_map/while/body/ppermute | solution.py:460
  127.2 29.6 %collective-permute-start.16 = (bf16[4,320,128]{2,1,0:T(8,128)(2,1)}, bf16[4,320,128]{2,1,0:T(8,128)(2,1)}, u32[]{:S(2)}, u32[]{:S(2)}) collective-permute-start(bf16[4,320,128]{2,1,0:T(8,128)(2,1)} %get-tuple-element.286), channel_id=1, source_target_pairs={{0,7},{1,6},{2,5},{3,4},{4,3},{5,2},{6,1},{7,0},{8,15},{9,14},{10,... | collective-permute-start | bytes 983048 | tf_op jit(solution)/shard_map/while/body/ppermute | solution.py:460
  175.3 37.2 %all-to-all-start.2 = ((bf16[8,8,72,128]{3,2,1,0:T(8,128)(2,1)}), bf16[8,8,72,128]{3,2,1,0:T(8,128)(2,1)}, u32[]{:S(2)}, u32[]{:S(2)}) async-start(bf16[8,8,72,128]{3,2,1,0:T(8,128)(2,1)} %dimers.3), calls=%async_computation.2 | async-start | bytes 2359296 | tf_op jit(solution)/shard_map/while/body/all_to_all | solution.py:465
  181.7 14.3 %collective-permute-start.7 = (bf16[6,320,128]{2,1,0:T(8,128)(2,1)}, bf16[6,320,128]{2,1,0:T(8,128)(2,1)S(1)}, u32[]{:S(2)}, u32[]{:S(2)}) collective-permute-start(bf16[6,320,128]{2,1,0:T(8,128)(2,1)} %get-tuple-element.276), channel_id=1, source_target_pairs={{0,64},{8,72},{16,80},{24,88},{32,96},{40,104},{48,112},{56,120},{... | collective-permute-start | bytes 1474568 | tf_op jit(solution)/shard_map/while/body/ppermute | solution.py:469
  183.0 23.9 %collective-permute-start.8 = (bf16[6,320,128]{2,1,0:T(8,128)(2,1)}, bf16[6,320,128]{2,1,0:T(8,128)(2,1)}, u32[]{:S(2)}, u32[]{:S(2)}) collective-permute-start(bf16[6,320,128]{2,1,0:T(8,128)(2,1)} %get-tuple-element.277), channel_id=1, source_target_pairs={{0,128},{8,136},{16,144},{24,152},{32,160},{40,168},{48,176},{56,1... | collective-permute-start | bytes 1474568 | tf_op jit(solution)/shard_map/while/body/ppermute | solution.py:469
  184.2 25.3 %collective-permute-start.9 = (bf16[6,320,128]{2,1,0:T(8,128)(2,1)}, bf16[6,320,128]{2,1,0:T(8,128)(2,1)}, u32[]{:S(2)}, u32[]{:S(2)}) collective-permute-start(bf16[6,320,128]{2,1,0:T(8,128)(2,1)} %get-tuple-element.278), channel_id=1, source_target_pairs={{0,192},{8,200},{16,208},{24,216},{32,224},{40,232},{48,240},{56,2... | collective-permute-start | bytes 1474568 | tf_op jit(solution)/shard_map/while/body/ppermute | solution.py:469
  212.5 38.2 %all-to-all-start.1 = ((bf16[16,320,128]{2,1,0:T(8,128)(2,1)}), bf16[16,320,128]{2,1,0:T(8,128)(2,1)}, u32[]{:S(2)}, u32[]{:S(2)}) async-start(bf16[16,320,128]{2,1,0:T(8,128)(2,1)} %pack.11), calls=%async_computation.1 | async-start | bytes 2621440 | tf_op jit(solution)/shard_map/while/body/all_to_all | solution.py:474
  220.4 35.5 %copy-start.21 = (bf16[2,320,128]{2,1,0:T(8,128)(2,1)S(1)}, bf16[2,320,128]{2,1,0:T(8,128)(2,1)}, u32[]{:S(2)}) copy-start(bf16[2,320,128]{2,1,0:T(8,128)(2,1)} %get-tuple-element.273) | copy-start | bytes 491524 | tf_op jit(solution)/shard_map/while
  220.4 40.9 %collective-permute-start = (bf16[2,320,128]{2,1,0:T(8,128)(2,1)}, bf16[2,320,128]{2,1,0:T(8,128)(2,1)S(1)}, u32[]{:S(2)}, u32[]{:S(2)}) collective-permute-start(bf16[2,320,128]{2,1,0:T(8,128)(2,1)} %get-tuple-element.269), channel_id=1, source_target_pairs={{0,1},{1,0},{2,3},{3,2},{4,5},{5,4},{6,7},{7,6},{8,9},{9,8},{10,11... | collective-permute-start | bytes 491528 | tf_op jit(solution)/shard_map/while/body/ppermute | solution.py:460
  220.5 42.2 %collective-permute-start.1 = (bf16[2,320,128]{2,1,0:T(8,128)(2,1)}, bf16[2,320,128]{2,1,0:T(8,128)(2,1)S(1)}, u32[]{:S(2)}, u32[]{:S(2)}) collective-permute-start(bf16[2,320,128]{2,1,0:T(8,128)(2,1)} %get-tuple-element.270), channel_id=1, source_target_pairs={{0,2},{1,3},{2,0},{3,1},{4,6},{5,7},{6,4},{7,5},{8,10},{9,11},{10,... | collective-permute-start | bytes 491528 | tf_op jit(solution)/shard_map/while/body/ppermute | solution.py:460
  222.2 43.0 %collective-permute-start.2 = (bf16[2,320,128]{2,1,0:T(8,128)(2,1)}, bf16[2,320,128]{2,1,0:T(8,128)(2,1)S(1)}, u32[]{:S(2)}, u32[]{:S(2)}) collective-permute-start(bf16[2,320,128]{2,1,0:T(8,128)(2,1)} %get-tuple-element.271), channel_id=1, source_target_pairs={{0,3},{1,2},{2,1},{3,0},{4,7},{5,6},{6,5},{7,4},{8,11},{9,10},{10,... | collective-permute-start | bytes 491528 | tf_op jit(solution)/shard_map/while/body/ppermute | solution.py:460
  222.3 42.9 %collective-permute-start.3 = (bf16[2,320,128]{2,1,0:T(8,128)(2,1)}, bf16[2,320,128]{2,1,0:T(8,128)(2,1)S(1)}, u32[]{:S(2)}, u32[]{:S(2)}) collective-permute-start(bf16[2,320,128]{2,1,0:T(8,128)(2,1)} %get-tuple-element.272), channel_id=1, source_target_pairs={{0,4},{1,5},{2,6},{3,7},{4,0},{5,1},{6,2},{7,3},{8,12},{9,13},{10,... | collective-permute-start | bytes 491528 | tf_op jit(solution)/shard_map/while/body/ppermute | solution.py:460
  225.5 35.9 %copy-start.19 = (bf16[2,320,128]{2,1,0:T(8,128)(2,1)S(1)}, bf16[2,320,128]{2,1,0:T(8,128)(2,1)}, u32[]{:S(2)}) copy-start(bf16[2,320,128]{2,1,0:T(8,128)(2,1)} %get-tuple-element.274) | copy-start | bytes 491524 | tf_op jit(solution)/shard_map/while
  225.5 37.2 %copy-start.17 = (bf16[2,320,128]{2,1,0:T(8,128)(2,1)S(1)}, bf16[2,320,128]{2,1,0:T(8,128)(2,1)}, u32[]{:S(2)}) copy-start(bf16[2,320,128]{2,1,0:T(8,128)(2,1)} %get-tuple-element.275) | copy-start | bytes 491524 | tf_op jit(solution)/shard_map/while
  250.7 51.0 %all-to-all-start.3 = ((bf16[32,72,128]{2,1,0:T(8,128)(2,1)}), bf16[32,72,128]{2,1,0:T(8,128)(2,1)S(1)}, u32[]{:S(2)}, u32[]{:S(2)}) async-start(bf16[32,72,128]{2,1,0:T(8,128)(2,1)} %place.2), calls=%async_computation.3 | async-start | bytes 1179648 | tf_op jit(solution)/shard_map/while/body/all_to_all | solution.py:478
  256.0 9.3 %collective-permute-start.4 = (bf16[2,320,128]{2,1,0:T(8,128)(2,1)S(1)}, bf16[2,320,128]{2,1,0:T(8,128)(2,1)S(1)}, u32[]{:S(2)}, u32[]{:S(2)}) collective-permute-start(bf16[2,320,128]{2,1,0:T(8,128)(2,1)S(1)} %copy-done.21), channel_id=1, source_target_pairs={{0,5},{1,4},{2,7},{3,6},{4,1},{5,0},{6,3},{7,2},{8,13},{9,12},{10,... | collective-permute-start | bytes 491528 | tf_op jit(solution)/shard_map/while/body/ppermute | solution.py:460
  261.4 28.7 %copy-start.12 = (bf16[2,320,128]{2,1,0:T(8,128)(2,1)}, bf16[2,320,128]{2,1,0:T(8,128)(2,1)S(1)}, u32[]{:S(2)}) copy-start(bf16[2,320,128]{2,1,0:T(8,128)(2,1)S(1)} %collective-permute-done.refs_1_) | copy-start | bytes 491524 | tf_op jit(solution)/shard_map/while
  261.4 8.3 %collective-permute-start.5 = (bf16[2,320,128]{2,1,0:T(8,128)(2,1)S(1)}, bf16[2,320,128]{2,1,0:T(8,128)(2,1)S(1)}, u32[]{:S(2)}, u32[]{:S(2)}) collective-permute-start(bf16[2,320,128]{2,1,0:T(8,128)(2,1)S(1)} %copy-done.19), channel_id=1, source_target_pairs={{0,6},{1,7},{2,4},{3,5},{4,2},{5,3},{6,0},{7,1},{8,14},{9,15},{10,... | collective-permute-start | bytes 491528 | tf_op jit(solution)/shard_map/while/body/ppermute | solution.py:460
  262.6 27.5 %copy-start.13 = (bf16[2,320,128]{2,1,0:T(8,128)(2,1)}, bf16[2,320,128]{2,1,0:T(8,128)(2,1)S(1)}, u32[]{:S(2)}) copy-start(bf16[2,320,128]{2,1,0:T(8,128)(2,1)S(1)} %collective-permute-done.1.refs_2_) | copy-start | bytes 491524 | tf_op jit(solution)/shard_map/while
  262.6 10.6 %collective-permute-start.6 = (bf16[2,320,128]{2,1,0:T(8,128)(2,1)S(1)}, bf16[2,320,128]{2,1,0:T(8,128)(2,1)S(1)}, u32[]{:S(2)}, u32[]{:S(2)}) collective-permute-start(bf16[2,320,128]{2,1,0:T(8,128)(2,1)S(1)} %copy-done.17), channel_id=1, source_target_pairs={{0,7},{1,6},{2,5},{3,4},{4,3},{5,2},{6,1},{7,0},{8,15},{9,14},{10,... | collective-permute-start | bytes 491528 | tf_op jit(solution)/shard_map/while/body/ppermute | solution.py:460
  265.2 24.9 %copy-start.14 = (bf16[2,320,128]{2,1,0:T(8,128)(2,1)}, bf16[2,320,128]{2,1,0:T(8,128)(2,1)S(1)}, u32[]{:S(2)}) copy-start(bf16[2,320,128]{2,1,0:T(8,128)(2,1)S(1)} %collective-permute-done.2.refs_3_) | copy-start | bytes 491524 | tf_op jit(solution)/shard_map/while
  265.2 8.1 %collective-permute-start.17 = (bf16[2,320,128]{2,1,0:T(8,128)(2,1)}, bf16[2,320,128]{2,1,0:T(8,128)(2,1)S(1)}, u32[]{:S(2)}, u32[]{:S(2)}) collective-permute-start(bf16[2,320,128]{2,1,0:T(8,128)(2,1)} %get-tuple-element.292), channel_id=1, source_target_pairs={{0,1},{1,0},{2,3},{3,2},{4,5},{5,4},{6,7},{7,6},{8,9},{9,8},{10,11... | collective-permute-start | bytes 491528 | tf_op jit(solution)/shard_map/while/body/ppermute | solution.py:460
  265.2 9.7 %collective-permute-start.18 = (bf16[2,320,128]{2,1,0:T(8,128)(2,1)}, bf16[2,320,128]{2,1,0:T(8,128)(2,1)S(1)}, u32[]{:S(2)}, u32[]{:S(2)}) collective-permute-start(bf16[2,320,128]{2,1,0:T(8,128)(2,1)} %get-tuple-element.293), channel_id=1, source_target_pairs={{0,2},{1,3},{2,0},{3,1},{4,6},{5,7},{6,4},{7,5},{8,10},{9,11},{10,... | collective-permute-start | bytes 491528 | tf_op jit(solution)/shard_map/while/body/ppermute | solution.py:460
  265.3 10.8 %collective-permute-start.19 = (bf16[2,320,128]{2,1,0:T(8,128)(2,1)}, bf16[2,320,128]{2,1,0:T(8,128)(2,1)S(1)}, u32[]{:S(2)}, u32[]{:S(2)}) collective-permute-start(bf16[2,320,128]{2,1,0:T(8,128)(2,1)} %get-tuple-element.294), channel_id=1, source_target_pairs={{0,3},{1,2},{2,1},{3,0},{4,7},{5,6},{6,5},{7,4},{8,11},{9,10},{10,... | collective-permute-start | bytes 491528 | tf_op jit(solution)/shard_map/while/body/ppermute | solution.py:460
  269.7 10.6 %collective-permute-start.20 = (bf16[2,320,128]{2,1,0:T(8,128)(2,1)}, bf16[2,320,128]{2,1,0:T(8,128)(2,1)S(1)}, u32[]{:S(2)}, u32[]{:S(2)}) collective-permute-start(bf16[2,320,128]{2,1,0:T(8,128)(2,1)} %get-tuple-element.295), channel_id=1, source_target_pairs={{0,4},{1,5},{2,6},{3,7},{4,0},{5,1},{6,2},{7,3},{8,12},{9,13},{10,... | collective-permute-start | bytes 491528 | tf_op jit(solution)/shard_map/while/body/ppermute | solution.py:460
  273.3 9.4 %collective-permute-start.21 = (bf16[2,320,128]{2,1,0:T(8,128)(2,1)}, bf16[2,320,128]{2,1,0:T(8,128)(2,1)S(1)}, u32[]{:S(2)}, u32[]{:S(2)}) collective-permute-start(bf16[2,320,128]{2,1,0:T(8,128)(2,1)} %get-tuple-element.296), channel_id=1, source_target_pairs={{0,5},{1,4},{2,7},{3,6},{4,1},{5,0},{6,3},{7,2},{8,13},{9,12},{10,... | collective-permute-start | bytes 491528 | tf_op jit(solution)/shard_map/while/body/ppermute | solution.py:460
  273.3 13.4 %collective-permute-start.22 = (bf16[2,320,128]{2,1,0:T(8,128)(2,1)}, bf16[2,320,128]{2,1,0:T(8,128)(2,1)S(1)}, u32[]{:S(2)}, u32[]{:S(2)}) collective-permute-start(bf16[2,320,128]{2,1,0:T(8,128)(2,1)} %get-tuple-element.297), channel_id=1, source_target_pairs={{0,6},{1,7},{2,4},{3,5},{4,2},{5,3},{6,0},{7,1},{8,14},{9,15},{10,... | collective-permute-start | bytes 491528 | tf_op jit(solution)/shard_map/while/body/ppermute | solution.py:460
  275.0 15.1 %collective-permute-start.23 = (bf16[2,320,128]{2,1,0:T(8,128)(2,1)}, bf16[2,320,128]{2,1,0:T(8,128)(2,1)S(1)}, u32[]{:S(2)}, u32[]{:S(2)}) collective-permute-start(bf16[2,320,128]{2,1,0:T(8,128)(2,1)} %get-tuple-element.298), channel_id=1, source_target_pairs={{0,7},{1,6},{2,5},{3,4},{4,3},{5,2},{6,1},{7,0},{8,15},{9,14},{10,... | collective-permute-start | bytes 491528 | tf_op jit(solution)/shard_map/while/body/ppermute | solution.py:460
  301.7 32.3 %copy-start.9 = (s32[1024]{0:T(1024)S(1)}, s32[1024]{0:T(1024)}, u32[]{:S(2)}) copy-start(s32[1024]{0:T(1024)} %get-tuple-element.261) | copy-start | bytes 12292 | tf_op jit(solution)/shard_map/while
  301.7 35.0 %copy-start.2 = (f32[32,32,256]{2,1,0:T(8,128)S(1)}, f32[32,32,256]{2,1,0:T(8,128)}, u32[]{:S(2)}) copy-start(f32[32,32,256]{2,1,0:T(8,128)} %get-tuple-element.415.refs_6_) | copy-start | bytes 3145732 | tf_op jit(solution)/shard_map/while
  301.7 35.0 %copy-start.5 = (bf16[32,72,128]{2,1,0:T(8,128)(2,1)}, bf16[32,72,128]{2,1,0:T(8,128)(2,1)S(1)}, u32[]{:S(2)}) copy-start(bf16[32,72,128]{2,1,0:T(8,128)(2,1)S(1)} %all-to-all-done.3.refs_5_) | copy-start | bytes 1769476 | tf_op jit(solution)/shard_map/while
  323.4 29.4 %all-to-all-start.5 = ((bf16[32,72,128]{2,1,0:T(8,128)(2,1)}), bf16[32,72,128]{2,1,0:T(8,128)(2,1)S(1)}, u32[]{:S(2)}, u32[]{:S(2)}) async-start(bf16[32,72,128]{2,1,0:T(8,128)(2,1)} %place.3), calls=%async_computation.5 | async-start | bytes 1179648 | tf_op jit(solution)/shard_map/while/body/all_to_all | solution.py:478
  (18 other events, 190.8 us)

commit v7 on v6

--- a/solution.py
+++ b/solution.py
@@ -141,7 +141,7 @@
 
 
 def one_dimer(steps, me, load, out, scratch):
-    stacked, weighted, dens, current, squares = scratch
+    stacked, weighted, dens, current = scratch
 
     @pl.when(steps > 0)
     def _():
@@ -163,30 +163,23 @@
             weighted[rows, :] = (stacked[rows, :].astype(F32) * coeff).astype(BF16)
 
         loop(8, weigh)
-        for n in range(4):
-            rows = slice(n * 128, n * 128 + 128)
-            coulomb = lax.dot_general(
-                weighted[rows, :], stacked[...], (((1,), (1,)), ((), ())), preferred_element_type=F32
-            )
-            row_at = lax.broadcasted_iota(jnp.int32, (128, 512), 0) + n * 128
-            col_at = lax.broadcasted_iota(jnp.int32, (128, 512), 1)
-            own = dens[rows, :].astype(F32)
-            blank = jnp.zeros((128, 256), F32)
-            wide = jnp.concatenate([own, blank] if n < 2 else [blank, own], axis=1)
-            eye = jnp.where(row_at == col_at, 0.5, 0.0)
-            current[rows, :] = (eye + wide + COUPLE * coulomb).astype(BF16)
+        coulomb = lax.dot_general(
+            weighted[...], stacked[...], (((1,), (1,)), ((), ())), preferred_element_type=F32
+        )
+        row_at = lax.broadcasted_iota(jnp.int32, (256, 512), 0)
+        col_at = lax.broadcasted_iota(jnp.int32, (256, 512), 1)
+        blank = jnp.zeros((256, 256), F32)
+        for half in (0, 256):
+            own = dens[half : half + 256, :].astype(F32)
+            wide = jnp.concatenate([own, blank] if half == 0 else [blank, own], axis=1)
+            eye = jnp.where(row_at + half == col_at, 0.5, 0.0)
+            current[half : half + 256, :] = (eye + wide + COUPLE * coulomb[half : half + 256, :]).astype(BF16)
 
         def purify(index, unused):
-
-            def block(n):
-                rows = pl.ds(pl.multiple_of(n * 128, 128), 128)
-                square = jnp.dot(current[rows, :], current[...], preferred_element_type=F32)
-                cube = jnp.dot(square.astype(BF16), current[...], preferred_element_type=F32)
-                squares[rows, :] = (3.0 * square - 2.0 * cube).astype(BF16)
-
-            for n in range(4):
-                block(n)
-            current[...] = squares[...]
+            whole = current[...]
+            square = jnp.dot(whole, whole, preferred_element_type=F32)
+            cube = jnp.dot(square.astype(BF16), whole, preferred_element_type=F32)
+            current[...] = (3.0 * square - 2.0 * cube).astype(BF16)
             return unused
 
         lax.fori_loop(0, steps, purify, 0)
@@ -213,7 +206,6 @@
     pltpu.VMEM((512, 1024), BF16),
     pltpu.VMEM((512, 1024), BF16),
     pltpu.VMEM((512, 256), BF16),
-    pltpu.VMEM((512, 512), BF16),
     pltpu.VMEM((512, 512), BF16),
 ]
 
@@ -402,13 +394,14 @@
 
                 def look(carry):
                     n, _ = carry
-                    c = (d + n) & 31
+                    turn = ((d + n) & 3) * 8
+                    c = jnp.where(n < 4, turn + za, jnp.where(n < 8, turn + zb, (d + n) & 31))
                     fit = ((n_direct[c] + 1) >> 1) + jnp.maximum(n_third[c] + 1, inside_ref[c]) <= 8
                     good = fit & can(oa, c, same_z) & can(ob, c, same_z) & (c != oa) & (c != ob)
                     return n + 1, jnp.where(good, c, -1)
 
                 _, c = lax.while_loop(
-                    lambda carry: (carry[0] < 32) & (carry[1] < 0), look, (jnp.int32(0), jnp.int32(-1))
+                    lambda carry: (carry[0] < 40) & (carry[1] < 0), look, (jnp.int32(0), jnp.int32(-1))
                 )
 
                 @pl.when(c < 0)

time: 359 us -> 349 us (0.972)
  Pallas kernels: 90.8 us -> 85.9 us
  blocking collectives: 28.6 us -> 24.9 us
    pallas_call x2, Pallas kernels: 29.4 us -> 21.6 us  [run_dimers(): pl.pallas_call(kernel, out_shape=jax.ShapeDtypeStruct((8, 2 * count, 72,...]
    all_to_all x1, blocking collectives: 19 us -> 15.4 us  [give_back(): lax.all_to_all(done, 'basis', split_axis=0, concat_axis=0, tiled=True)]
  transfers between devices with their start and end apart: 37 -> 37, of which waited for: 20 -> 20; matrix products, arithmetic and copies ran while one was open for 2% -> 2% of each run, Pallas kernels for 18% -> 19%
where the time goes in v7:
time: 349 us; the launch traced here: 348 us
  waiting for transfers between devices  140 us (40%)
  Pallas kernels  85.9 us (25%)
  starting transfers between devices  80.1 us (23%)
  blocking collectives  24.9 us (7%)
  other arithmetic  9.57 us (3%)
  local copies, waits for them, and re-layouts  5.45 us (2%)
    ppermute x28, waiting for transfers between devices, exchange(): got.append(lax.ppermute(parts[k], 'basis', [(i, i ^ k) for i in range(8)]))  58.3 us
    all_to_all x4, waiting for transfers between devices, across(): return lax.all_to_all(part, 'frag', split_axis=0, concat_axis=0, tiled=True)  38 us
    all_to_all x4, starting transfers between devices, across(): return lax.all_to_all(part, 'frag', split_axis=0, concat_axis=0, tiled=True)  35 us
    ppermute x28, starting transfers between devices, exchange(): got.append(lax.ppermute(parts[k], 'basis', [(i, i ^ k) for i in range(8)]))  30.3 us
    pallas_call x1, Pallas kernels, plan_rest(): pl.pallas_call(plan_kernel, out_shape=[jax.ShapeDtypeStruct((TABLE,), s32...  28.5 us
    ppermute x3, waiting for transfers between devices, along_x(): lax.ppermute(parts[k - 1], 'frag', [(i, i ^ 8 * k) for i in range(32)])  23.1 us
    pallas_call x7, Pallas kernels, pack(): pl.pallas_call(kernel, out_shape=[jax.ShapeDtypeStruct((rows, 320, 128),...  21.9 us
    pallas_call x2, Pallas kernels, run_dimers(): pl.pallas_call(kernel, out_shape=jax.ShapeDtypeStruct((8, 2 * count, 72,...  21.6 us
  transfers between devices with their start and end apart: 37, of which 20 were waited for; matrix products, arithmetic and copies ran while one was open for 2% of the time, Pallas kernels for 19%

profile of v7, /device:TPU:32, one launch (start us, length us, event | category | flops | bytes accessed | tf_op | source)
XLA Modules:
  0.0 348.0 jit_solution(17078713453197105012)
XLA Ops:
  2.3 9.6 %all_to_all.46 = s32[8,1,128]{2,1,0:T(1,128)S(1)} all-to-all(s32[8,1,128]{2,1,0:T(1,128)S(1)} %broadcast_in_dim.142), channel_id=1, replica_groups=mesh['frag'=32,'basis'=8] {'basis'}, dimensions={0} | all-to-all | bytes 8192 | tf_op jit(solution)/shard_map/all_to_all | solution.py:488
  12.8 11.2 %all-to-all-start.7 = ((s32[32,1,128]{2,1,0:T(1,128)}), s32[32,1,128]{2,1,0:T(1,128)S(1)}, u32[]{:S(2)}, u32[]{:S(2)}) async-start(s32[32,1,128]{2,1,0:T(1,128)} %broadcast_in_dim.143), calls=%async_computation.7 | async-start | bytes 32768 | tf_op jit(solution)/shard_map/all_to_all | solution.py:471
  24.0 8.6 %all-to-all-done.7 = s32[32,1,128]{2,1,0:T(1,128)S(1)} async-done(((s32[32,1,128]{2,1,0:T(1,128)}), s32[32,1,128]{2,1,0:T(1,128)S(1)}, u32[]{:S(2)}, u32[]{:S(2)}) %all-to-all-start.7) | async-done | bytes 16416 | tf_op jit(solution)/shard_map/all_to_all | solution.py:471
  34.1 313.3 %while.15 = (s32[]{:T(128)}, s32[1024]{0:T(1024)S(1)}, f32[32,32,256]{2,1,0:T(8,128)}, f32[32,128]{1,0:T(8,128)S(1)}, s32[1024]{0:T(1024)S(1)}, /*index=5*/pred[...) while((s32[]{:T(128)}, s32[1024]{0:T(1024)S(1)}, ...), condition=%region_13.14_spmd.clone.clone, body=%region_1.13_spmd.clone.clone | while | flops 24018298880 | bytes 131915224 | solution.py:612
  35.0 3.8 %pack.9 = bf16[32,320,128]{2,1,0:T(8,128)(2,1)} custom-call(s32[32]{0:T(128)} %get-tuple-element.374.refs_0_, s32[1]{0:T(128)} %get-tuple-element.439.refs_2_.refs_1_.me_ref, bf16[32,256,128]{2,1,0:T(8,128)(2,1)} %get-tuple-element.440.refs_3_.refs_2_, bf16[32,32,256]{2,1,0:T(8,128)(2,1)} %get-tuple-element.441.refs_4_.refs_3_), custom_call_target="tpu_custom_call" | custom-call | tf_op jit(solution)/shard_map/while/body/pack/pallas_call | solution.py:68
  38.8 6.1 %all-to-all-start = ((bf16[32,320,128]{2,1,0:T(8,128)(2,1)}), bf16[32,320,128]{2,1,0:T(8,128)(2,1)}, u32[]{:S(2)}, u32[]{:S(2)}) async-start(bf16[32,320,128]{2,1,0:T(8,128)(2,1)} %pack.9), calls=%async_computation | async-start | bytes 5242880 | tf_op jit(solution)/shard_map/while/body/all_to_all | solution.py:471
  45.8 3.1 pack.13
  57.3 28.5 %plan.1 = (s32[256]{0:T(256)}, s32[1024]{0:T(1024)}) custom-call(s32[1]{0:T(128)} %get-tuple-element.436.me_ref, s32[32]{0:T(128)} %select_reduce_fusion.6.inside_ref, s32[1]{0:T(128)} %bitcast.5.count_ref, s32[1024]{0:T(1024)} %select_reduce_fusion.2.list_ref), custom_call_target="tpu_custom_call" | custom-call | flops 1000 | bytes 30000000 | tf_op jit(solution)/shard_map/while/body/plan/pallas_call | solution.py:439
  85.8 18.7 %all-to-all-done.refs_3_ = bf16[32,320,128]{2,1,0:T(8,128)(2,1)} async-done(((bf16[32,320,128]{2,1,0:T(8,128)(2,1)}), bf16[32,320,128]{2,1,0:T(8,128)(2,1)}, u32[]{:S(2)}, u32[]{:S(2)}) %all-to-all-start) | async-done | bytes 2621472 | tf_op jit(solution)/shard_map/while/body/all_to_all | solution.py:471
  104.5 4.1 %pack.10 = (bf16[4,320,128]{2,1,0:T(8,128)(2,1)}, bf16[4,320,128]{2,1,0:T(8,128)(2,1)}, bf16[4,320,128]{2,1,0:T(8,128)(2,1)}, bf16[4,320,128]{2,1,0:T(8,128)(2,1...) custom-call(s32[128]{0:T(128)} %pad_add_fusion.refs_0_.table_ref, ...), custom_call_target="tpu_custom_call" | custom-call | tf_op jit(solution)/shard_map/while/body/pack/pallas_call | solution.py:68
  109.9 2.2 collective-permute-start.10
  113.6 7.3 %collective-permute-done.29.refs_6_ = bf16[4,320,128]{2,1,0:T(8,128)(2,1)} collective-permute-done((bf16[4,320,128]{2,1,0:T(8,128)(2,1)}, bf16[4,320,128]{2,1,0:T(8,128)(2,1)}, u32[]{:S(2)}, u32[]{:S(2)}) %collective-permute-start.29) | collective-permute-done | bytes 327712 | tf_op jit(solution)/shard_map/while/body/ppermute | solution.py:453
  120.9 2.1 collective-permute-done.30.refs_7_
  123.0 2.1 collective-permute-start.14
  125.1 2.1 collective-permute-start.15
  128.3 9.5 %collective-permute-done.13.refs_12_ = bf16[4,320,128]{2,1,0:T(8,128)(2,1)} collective-permute-done((bf16[4,320,128]{2,1,0:T(8,128)(2,1)}, bf16[4,320,128]{2,1,0:T(8,128)(2,1)}, u32[]{:S(2)}, u32[]{:S(2)}) %collective-permute-start.13) | collective-permute-done | bytes 327712 | tf_op jit(solution)/shard_map/while/body/ppermute | solution.py:453
  137.8 5.3 %collective-permute-done.14.refs_13_ = bf16[4,320,128]{2,1,0:T(8,128)(2,1)} collective-permute-done((bf16[4,320,128]{2,1,0:T(8,128)(2,1)}, bf16[4,320,128]{2,1,0:T(8,128)(2,1)}, u32[]{:S(2)}, u32[]{:S(2)}) %collective-permute-start.14) | collective-permute-done | bytes 327712 | tf_op jit(solution)/shard_map/while/body/ppermute | solution.py:453
  143.0 7.6 %collective-permute-done.15.refs_14_ = bf16[4,320,128]{2,1,0:T(8,128)(2,1)} collective-permute-done((bf16[4,320,128]{2,1,0:T(8,128)(2,1)}, bf16[4,320,128]{2,1,0:T(8,128)(2,1)}, u32[]{:S(2)}, u32[]{:S(2)}) %collective-permute-start.15) | collective-permute-done | bytes 327712 | tf_op jit(solution)/shard_map/while/body/ppermute | solution.py:453
  150.6 6.2 %collective-permute-done.16.refs_15_ = bf16[4,320,128]{2,1,0:T(8,128)(2,1)} collective-permute-done((bf16[4,320,128]{2,1,0:T(8,128)(2,1)}, bf16[4,320,128]{2,1,0:T(8,128)(2,1)}, u32[]{:S(2)}, u32[]{:S(2)}) %collective-permute-start.16) | collective-permute-done | bytes 327712 | tf_op jit(solution)/shard_map/while/body/ppermute | solution.py:453
  156.8 13.1 %dimers.3 = bf16[8,8,72,128]{3,2,1,0:T(8,128)(2,1)} custom-call(s32[128]{0:T(128)} %pad_add_fusion.refs_0_.table_ref, s32[1]{0:T(128)} %get-tuple-element.439.refs_2_.refs_1_.me_ref, bf16[4,320,128]{2,1,0:T(8,128)(2,1)} %get-tuple-element.299.refs_0_, bf16[4,320,128]{2,1,0:T(8,128)(2,1)} %copy-done.10, bf16[4,320,128]{2,1,0:T(8,128)(2,1)} %copy-done.11, ...), custom_call_target="tpu_custom_call" | custom-call | flops 16000000000 | bytes 6000000 | tf_op jit(solution)/shard_map/while/body/dimers/pallas_call | solution.py:217
  169.9 4.3 %all-to-all-start.2 = ((bf16[8,8,72,128]{3,2,1,0:T(8,128)(2,1)}), bf16[8,8,72,128]{3,2,1,0:T(8,128)(2,1)}, u32[]{:S(2)}, u32[]{:S(2)}) async-start(bf16[8,8,72,128]{3,2,1,0:T(8,128)(2,1)} %dimers.3), calls=%async_computation.2 | async-start | bytes 2359296 | tf_op jit(solution)/shard_map/while/body/all_to_all | solution.py:458
  174.2 2.2 pack.8
  178.8 2.2 collective-permute-start.9
  181.0 9.6 %collective-permute-done.7.refs_5_.refs_3_ = bf16[6,320,128]{2,1,0:T(8,128)(2,1)S(1)} collective-permute-done((bf16[6,320,128]{2,1,0:T(8,128)(2,1)}, bf16[6,320,128]{2,1,0:T(8,128)(2,1)S(1)}, u32[]{:S(2)}, u32[]{:S(2)}) %collective-permute-start.7) | collective-permute-done | bytes 491552 | tf_op jit(solution)/shard_map/while/body/ppermute | solution.py:462
  190.6 10.9 %collective-permute-done.8.refs_6_.refs_4_ = bf16[6,320,128]{2,1,0:T(8,128)(2,1)} collective-permute-done((bf16[6,320,128]{2,1,0:T(8,128)(2,1)}, bf16[6,320,128]{2,1,0:T(8,128)(2,1)}, u32[]{:S(2)}, u32[]{:S(2)}) %collective-permute-start.8) | collective-permute-done | bytes 491552 | tf_op jit(solution)/shard_map/while/body/ppermute | solution.py:462
  201.5 2.6 collective-permute-done.9.refs_7_.refs_5_
  204.1 3.0 pack.11
  207.1 5.8 %all-to-all-start.1 = ((bf16[16,320,128]{2,1,0:T(8,128)(2,1)}), bf16[16,320,128]{2,1,0:T(8,128)(2,1)}, u32[]{:S(2)}, u32[]{:S(2)}) async-start(bf16[16,320,128]{2,1,0:T(8,128)(2,1)} %pack.11), calls=%async_computation.1 | async-start | bytes 2621440 | tf_op jit(solution)/shard_map/while/body/all_to_all | solution.py:467
  212.9 2.1 pack.7
  216.9 3.2 collective-permute-start.3
  220.1 4.2 %place.2 = bf16[32,72,128]{2,1,0:T(8,128)(2,1)} custom-call(s32[128]{0:T(128)} %pad_add_fusion.refs_0_.table_ref, s32[256]{0:T(256)} %get-tuple-element.264.refs_1_.table_ref, s32[1]{0:T(128)} %get-tuple-element.439.refs_2_.refs_1_.me_ref, bf16[64,72,128]{2,1,0:T(8,128)(2,1)} %bitcast.6.refs_3_), custom_call_target="tpu_custom_call" | custom-call | tf_op jit(solution)/shard_map/while/body/place/pallas_call | solution.py:95
  224.3 21.0 %all-to-all-done.1.refs_6_ = bf16[16,320,128]{2,1,0:T(8,128)(2,1)} async-done(((bf16[16,320,128]{2,1,0:T(8,128)(2,1)}), bf16[16,320,128]{2,1,0:T(8,128)(2,1)}, u32[]{:S(2)}, u32[]{:S(2)}) %all-to-all-start.1) | async-done | bytes 1310752 | tf_op jit(solution)/shard_map/while/body/all_to_all | solution.py:467
  245.3 5.3 %all-to-all-start.3 = ((bf16[32,72,128]{2,1,0:T(8,128)(2,1)}), bf16[32,72,128]{2,1,0:T(8,128)(2,1)S(1)}, u32[]{:S(2)}, u32[]{:S(2)}) async-start(bf16[32,72,128]{2,1,0:T(8,128)(2,1)} %place.2), calls=%async_computation.3 | async-start | bytes 1179648 | tf_op jit(solution)/shard_map/while/body/all_to_all | solution.py:471
  252.5 3.5 %pack.12 = (bf16[2,320,128]{2,1,0:T(8,128)(2,1)}, bf16[2,320,128]{2,1,0:T(8,128)(2,1)}, bf16[2,320,128]{2,1,0:T(8,128)(2,1)}, bf16[2,320,128]{2,1,0:T(8,128)(2,1...) custom-call(s32[128]{0:T(128)} %pad_add_fusion.refs_0_.table_ref, ...), custom_call_target="tpu_custom_call" | custom-call | tf_op jit(solution)/shard_map/while/body/pack/pallas_call | solution.py:68
  257.3 2.5 collective-permute-start.6
  261.7 2.7 collective-permute-done.5.refs_6_
  264.6 3.3 collective-permute-done.6.refs_7_
  270.8 4.1 %collective-permute-done.20.refs_12_ = bf16[2,320,128]{2,1,0:T(8,128)(2,1)S(1)} collective-permute-done((bf16[2,320,128]{2,1,0:T(8,128)(2,1)}, bf16[2,320,128]{2,1,0:T(8,128)(2,1)S(1)}, u32[]{:S(2)}, u32[]{:S(2)}) %collective-permute-start.20) | collective-permute-done | bytes 163872 | tf_op jit(solution)/shard_map/while/body/ppermute | solution.py:453
  274.9 2.4 collective-permute-done.21.refs_13_
  277.3 4.0 %collective-permute-done.22.refs_14_ = bf16[2,320,128]{2,1,0:T(8,128)(2,1)S(1)} collective-permute-done((bf16[2,320,128]{2,1,0:T(8,128)(2,1)}, bf16[2,320,128]{2,1,0:T(8,128)(2,1)S(1)}, u32[]{:S(2)}, u32[]{:S(2)}) %collective-permute-start.22) | collective-permute-done | bytes 163872 | tf_op jit(solution)/shard_map/while/body/ppermute | solution.py:453
  281.3 3.4 collective-permute-done.23.refs_15_
  285.4 8.6 %dimers.2 = bf16[8,4,72,128]{3,2,1,0:T(8,128)(2,1)} custom-call(s32[256]{0:T(256)} %get-tuple-element.264.refs_1_.table_ref, s32[1]{0:T(128)} %get-tuple-element.439.refs_2_.refs_1_.me_ref, bf16[2,320,128]{2,1,0:T(8,128)(2,1)} %get-tuple-element.268.refs_0_, bf16[2,320,128]{2,1,0:T(8,128)(2,1)} %copy-done.12, bf16[2,320,128]{2,1,0:T(8,128)(2,1)} %copy-done.13, ...), custom_call_target="tpu_custom_call" | custom-call | flops 8000000000 | bytes 3000000 | tf_op jit(solution)/shard_map/while/body/dimers/pallas_call | solution.py:217
  294.0 15.4 %all_to_all.47 = bf16[8,4,72,128]{3,2,1,0:T(8,128)(2,1)} all-to-all(bf16[8,4,72,128]{3,2,1,0:T(8,128)(2,1)} %dimers.2), channel_id=1, replica_groups=mesh['frag'=32,'basis'=8] {'basis'}, dimensions={0} | all-to-all | bytes 1179648 | tf_op jit(solution)/shard_map/while/body/all_to_all | solution.py:458
  309.3 2.6 place.3
  312.0 12.4 %all-to-all-start.5 = ((bf16[32,72,128]{2,1,0:T(8,128)(2,1)}), bf16[32,72,128]{2,1,0:T(8,128)(2,1)S(1)}, u32[]{:S(2)}, u32[]{:S(2)}) async-start(bf16[32,72,128]{2,1,0:T(8,128)(2,1)} %place.3), calls=%async_computation.5 | async-start | bytes 1179648 | tf_op jit(solution)/shard_map/while/body/all_to_all | solution.py:471
  325.0 2.1 select_reduce_fusion
  327.1 5.3 %add_up.2 = (f32[32,32,256]{2,1,0:T(8,128)S(1)}, f32[32,128]{1,0:T(8,128)S(1)}) custom-call(s32[128]{0:T(128)} %pad_add_fusion.refs_0_.table_ref, s32[256]{0:T(256)} %get-tuple-element.264.refs_1_.table_ref, s32[1]{0:T(128)} %get-tuple-element.439.refs_2_.refs_1_.me_ref, ...), custom_call_target="tpu_custom_call", output_to_operand_aliasing={{0}: (6, {}), {1}: (7, {})} | custom-call | tf_op jit(solution)/shard_map/while/body/add_up/pallas_call | solution.py:124
  332.5 10.8 %all-to-all-done.5.refs_3_ = bf16[32,72,128]{2,1,0:T(8,128)(2,1)S(1)} async-done(((bf16[32,72,128]{2,1,0:T(8,128)(2,1)}), bf16[32,72,128]{2,1,0:T(8,128)(2,1)S(1)}, u32[]{:S(2)}, u32[]{:S(2)}) %all-to-all-start.5) | async-done | bytes 589856 | tf_op jit(solution)/shard_map/while/body/all_to_all | solution.py:471
  (136 shorter events, 35.8 us)
Async XLA Ops:
  12.8 19.8 %all-to-all-start.7 = ((s32[32,1,128]{2,1,0:T(1,128)}), s32[32,1,128]{2,1,0:T(1,128)S(1)}, u32[]{:S(2)}, u32[]{:S(2)}) async-start(s32[32,1,128]{2,1,0:T(1,128)} %broadcast_in_dim.143), calls=%async_computation.7 | async-start | bytes 32768 | tf_op jit(solution)/shard_map/all_to_all | solution.py:471
  38.8 65.7 %all-to-all-start = ((bf16[32,320,128]{2,1,0:T(8,128)(2,1)}), bf16[32,320,128]{2,1,0:T(8,128)(2,1)}, u32[]{:S(2)}, u32[]{:S(2)}) async-start(bf16[32,320,128]{2,1,0:T(8,128)(2,1)} %pack.9), calls=%async_computation | async-start | bytes 5242880 | tf_op jit(solution)/shard_map/while/body/all_to_all | solution.py:471
  48.9 59.8 %collective-permute-start.24 = (bf16[4,320,128]{2,1,0:T(8,128)(2,1)}, bf16[4,320,128]{2,1,0:T(8,128)(2,1)S(1)}, u32[]{:S(2)}, u32[]{:S(2)}) collective-permute-start(bf16[4,320,128]{2,1,0:T(8,128)(2,1)} %get-tuple-element.300), channel_id=1, source_target_pairs={{0,1},{1,0},{2,3},{3,2},{4,5},{5,4},{6,7},{7,6},{8,9},{9,8},{10,11... | collective-permute-start | bytes 983048 | tf_op jit(solution)/shard_map/while/body/ppermute | solution.py:453
  48.9 61.0 %collective-permute-start.25 = (bf16[4,320,128]{2,1,0:T(8,128)(2,1)}, bf16[4,320,128]{2,1,0:T(8,128)(2,1)S(1)}, u32[]{:S(2)}, u32[]{:S(2)}) collective-permute-start(bf16[4,320,128]{2,1,0:T(8,128)(2,1)} %get-tuple-element.301), channel_id=1, source_target_pairs={{0,2},{1,3},{2,0},{3,1},{4,6},{5,7},{6,4},{7,5},{8,10},{9,11},{10,... | collective-permute-start | bytes 983048 | tf_op jit(solution)/shard_map/while/body/ppermute | solution.py:453
  49.5 60.5 %collective-permute-start.26 = (bf16[4,320,128]{2,1,0:T(8,128)(2,1)}, bf16[4,320,128]{2,1,0:T(8,128)(2,1)}, u32[]{:S(2)}, u32[]{:S(2)}) collective-permute-start(bf16[4,320,128]{2,1,0:T(8,128)(2,1)} %get-tuple-element.302), channel_id=1, source_target_pairs={{0,3},{1,2},{2,1},{3,0},{4,7},{5,6},{6,5},{7,4},{8,11},{9,10},{10,... | collective-permute-start | bytes 983048 | tf_op jit(solution)/shard_map/while/body/ppermute | solution.py:453
  50.8 61.3 %collective-permute-start.27 = (bf16[4,320,128]{2,1,0:T(8,128)(2,1)}, bf16[4,320,128]{2,1,0:T(8,128)(2,1)}, u32[]{:S(2)}, u32[]{:S(2)}) collective-permute-start(bf16[4,320,128]{2,1,0:T(8,128)(2,1)} %get-tuple-element.303), channel_id=1, source_target_pairs={{0,4},{1,5},{2,6},{3,7},{4,0},{5,1},{6,2},{7,3},{8,12},{9,13},{10,... | collective-permute-start | bytes 983048 | tf_op jit(solution)/shard_map/while/body/ppermute | solution.py:453
  51.9 60.2 %collective-permute-start.28 = (bf16[4,320,128]{2,1,0:T(8,128)(2,1)}, bf16[4,320,128]{2,1,0:T(8,128)(2,1)}, u32[]{:S(2)}, u32[]{:S(2)}) collective-permute-start(bf16[4,320,128]{2,1,0:T(8,128)(2,1)} %get-tuple-element.304), channel_id=1, source_target_pairs={{0,5},{1,4},{2,7},{3,6},{4,1},{5,0},{6,3},{7,2},{8,13},{9,12},{10,... | collective-permute-start | bytes 983048 | tf_op jit(solution)/shard_map/while/body/ppermute | solution.py:453
  108.7 48.2 %copy-start.10 = (bf16[4,320,128]{2,1,0:T(8,128)(2,1)}, bf16[4,320,128]{2,1,0:T(8,128)(2,1)S(1)}, u32[]{:S(2)}) copy-start(bf16[4,320,128]{2,1,0:T(8,128)(2,1)S(1)} %collective-permute-done.24.refs_1_) | copy-start | bytes 983044 | tf_op jit(solution)/shard_map/while
  108.7 12.2 %collective-permute-start.29 = (bf16[4,320,128]{2,1,0:T(8,128)(2,1)}, bf16[4,320,128]{2,1,0:T(8,128)(2,1)}, u32[]{:S(2)}, u32[]{:S(2)}) collective-permute-start(bf16[4,320,128]{2,1,0:T(8,128)(2,1)} %get-tuple-element.305), channel_id=1, source_target_pairs={{0,6},{1,7},{2,4},{3,5},{4,2},{5,3},{6,0},{7,1},{8,14},{9,15},{10,... | collective-permute-start | bytes 983048 | tf_op jit(solution)/shard_map/while/body/ppermute | solution.py:453
  109.9 46.9 %copy-start.11 = (bf16[4,320,128]{2,1,0:T(8,128)(2,1)}, bf16[4,320,128]{2,1,0:T(8,128)(2,1)S(1)}, u32[]{:S(2)}) copy-start(bf16[4,320,128]{2,1,0:T(8,128)(2,1)S(1)} %collective-permute-done.25.refs_2_) | copy-start | bytes 983044 | tf_op jit(solution)/shard_map/while
  109.9 13.1 %collective-permute-start.30 = (bf16[4,320,128]{2,1,0:T(8,128)(2,1)}, bf16[4,320,128]{2,1,0:T(8,128)(2,1)}, u32[]{:S(2)}, u32[]{:S(2)}) collective-permute-start(bf16[4,320,128]{2,1,0:T(8,128)(2,1)} %get-tuple-element.306), channel_id=1, source_target_pairs={{0,7},{1,6},{2,5},{3,4},{4,3},{5,2},{6,1},{7,0},{8,15},{9,14},{10,... | collective-permute-start | bytes 983048 | tf_op jit(solution)/shard_map/while/body/ppermute | solution.py:453
  109.9 15.2 %collective-permute-start.10 = (bf16[4,320,128]{2,1,0:T(8,128)(2,1)}, bf16[4,320,128]{2,1,0:T(8,128)(2,1)}, u32[]{:S(2)}, u32[]{:S(2)}) collective-permute-start(bf16[4,320,128]{2,1,0:T(8,128)(2,1)} %get-tuple-element.280), channel_id=1, source_target_pairs={{0,1},{1,0},{2,3},{3,2},{4,5},{5,4},{6,7},{7,6},{8,9},{9,8},{10,11... | collective-permute-start | bytes 983048 | tf_op jit(solution)/shard_map/while/body/ppermute | solution.py:453
  112.1 15.1 %collective-permute-start.11 = (bf16[4,320,128]{2,1,0:T(8,128)(2,1)}, bf16[4,320,128]{2,1,0:T(8,128)(2,1)}, u32[]{:S(2)}, u32[]{:S(2)}) collective-permute-start(bf16[4,320,128]{2,1,0:T(8,128)(2,1)} %get-tuple-element.281), channel_id=1, source_target_pairs={{0,2},{1,3},{2,0},{3,1},{4,6},{5,7},{6,4},{7,5},{8,10},{9,11},{10,... | collective-permute-start | bytes 983048 | tf_op jit(solution)/shard_map/while/body/ppermute | solution.py:453
  112.1 16.2 %collective-permute-start.12 = (bf16[4,320,128]{2,1,0:T(8,128)(2,1)}, bf16[4,320,128]{2,1,0:T(8,128)(2,1)}, u32[]{:S(2)}, u32[]{:S(2)}) collective-permute-start(bf16[4,320,128]{2,1,0:T(8,128)(2,1)} %get-tuple-element.282), channel_id=1, source_target_pairs={{0,3},{1,2},{2,1},{3,0},{4,7},{5,6},{6,5},{7,4},{8,11},{9,10},{10,... | collective-permute-start | bytes 983048 | tf_op jit(solution)/shard_map/while/body/ppermute | solution.py:453
  120.9 16.9 %collective-permute-start.13 = (bf16[4,320,128]{2,1,0:T(8,128)(2,1)}, bf16[4,320,128]{2,1,0:T(8,128)(2,1)}, u32[]{:S(2)}, u32[]{:S(2)}) collective-permute-start(bf16[4,320,128]{2,1,0:T(8,128)(2,1)} %get-tuple-element.283), channel_id=1, source_target_pairs={{0,4},{1,5},{2,6},{3,7},{4,0},{5,1},{6,2},{7,3},{8,12},{9,13},{10,... | collective-permute-start | bytes 983048 | tf_op jit(solution)/shard_map/while/body/ppermute | solution.py:453
  123.0 20.0 %collective-permute-start.14 = (bf16[4,320,128]{2,1,0:T(8,128)(2,1)}, bf16[4,320,128]{2,1,0:T(8,128)(2,1)}, u32[]{:S(2)}, u32[]{:S(2)}) collective-permute-start(bf16[4,320,128]{2,1,0:T(8,128)(2,1)} %get-tuple-element.284), channel_id=1, source_target_pairs={{0,5},{1,4},{2,7},{3,6},{4,1},{5,0},{6,3},{7,2},{8,13},{9,12},{10,... | collective-permute-start | bytes 983048 | tf_op jit(solution)/shard_map/while/body/ppermute | solution.py:453
  125.1 25.5 %collective-permute-start.15 = (bf16[4,320,128]{2,1,0:T(8,128)(2,1)}, bf16[4,320,128]{2,1,0:T(8,128)(2,1)}, u32[]{:S(2)}, u32[]{:S(2)}) collective-permute-start(bf16[4,320,128]{2,1,0:T(8,128)(2,1)} %get-tuple-element.285), channel_id=1, source_target_pairs={{0,6},{1,7},{2,4},{3,5},{4,2},{5,3},{6,0},{7,1},{8,14},{9,15},{10,... | collective-permute-start | bytes 983048 | tf_op jit(solution)/shard_map/while/body/ppermute | solution.py:453
  127.2 29.6 %collective-permute-start.16 = (bf16[4,320,128]{2,1,0:T(8,128)(2,1)}, bf16[4,320,128]{2,1,0:T(8,128)(2,1)}, u32[]{:S(2)}, u32[]{:S(2)}) collective-permute-start(bf16[4,320,128]{2,1,0:T(8,128)(2,1)} %get-tuple-element.286), channel_id=1, source_target_pairs={{0,7},{1,6},{2,5},{3,4},{4,3},{5,2},{6,1},{7,0},{8,15},{9,14},{10,... | collective-permute-start | bytes 983048 | tf_op jit(solution)/shard_map/while/body/ppermute | solution.py:453
  169.9 37.2 %all-to-all-start.2 = ((bf16[8,8,72,128]{3,2,1,0:T(8,128)(2,1)}), bf16[8,8,72,128]{3,2,1,0:T(8,128)(2,1)}, u32[]{:S(2)}, u32[]{:S(2)}) async-start(bf16[8,8,72,128]{3,2,1,0:T(8,128)(2,1)} %dimers.3), calls=%async_computation.2 | async-start | bytes 2359296 | tf_op jit(solution)/shard_map/while/body/all_to_all | solution.py:458
  176.3 14.3 %collective-permute-start.7 = (bf16[6,320,128]{2,1,0:T(8,128)(2,1)}, bf16[6,320,128]{2,1,0:T(8,128)(2,1)S(1)}, u32[]{:S(2)}, u32[]{:S(2)}) collective-permute-start(bf16[6,320,128]{2,1,0:T(8,128)(2,1)} %get-tuple-element.276), channel_id=1, source_target_pairs={{0,64},{8,72},{16,80},{24,88},{32,96},{40,104},{48,112},{56,120},{... | collective-permute-start | bytes 1474568 | tf_op jit(solution)/shard_map/while/body/ppermute | solution.py:462
  177.6 23.9 %collective-permute-start.8 = (bf16[6,320,128]{2,1,0:T(8,128)(2,1)}, bf16[6,320,128]{2,1,0:T(8,128)(2,1)}, u32[]{:S(2)}, u32[]{:S(2)}) collective-permute-start(bf16[6,320,128]{2,1,0:T(8,128)(2,1)} %get-tuple-element.277), channel_id=1, source_target_pairs={{0,128},{8,136},{16,144},{24,152},{32,160},{40,168},{48,176},{56,1... | collective-permute-start | bytes 1474568 | tf_op jit(solution)/shard_map/while/body/ppermute | solution.py:462
  178.8 25.3 %collective-permute-start.9 = (bf16[6,320,128]{2,1,0:T(8,128)(2,1)}, bf16[6,320,128]{2,1,0:T(8,128)(2,1)}, u32[]{:S(2)}, u32[]{:S(2)}) collective-permute-start(bf16[6,320,128]{2,1,0:T(8,128)(2,1)} %get-tuple-element.278), channel_id=1, source_target_pairs={{0,192},{8,200},{16,208},{24,216},{32,224},{40,232},{48,240},{56,2... | collective-permute-start | bytes 1474568 | tf_op jit(solution)/shard_map/while/body/ppermute | solution.py:462
  207.1 38.2 %all-to-all-start.1 = ((bf16[16,320,128]{2,1,0:T(8,128)(2,1)}), bf16[16,320,128]{2,1,0:T(8,128)(2,1)}, u32[]{:S(2)}, u32[]{:S(2)}) async-start(bf16[16,320,128]{2,1,0:T(8,128)(2,1)} %pack.11), calls=%async_computation.1 | async-start | bytes 2621440 | tf_op jit(solution)/shard_map/while/body/all_to_all | solution.py:467
  215.1 35.6 %copy-start.21 = (bf16[2,320,128]{2,1,0:T(8,128)(2,1)S(1)}, bf16[2,320,128]{2,1,0:T(8,128)(2,1)}, u32[]{:S(2)}) copy-start(bf16[2,320,128]{2,1,0:T(8,128)(2,1)} %get-tuple-element.273) | copy-start | bytes 491524 | tf_op jit(solution)/shard_map/while
  215.1 40.9 %collective-permute-start = (bf16[2,320,128]{2,1,0:T(8,128)(2,1)}, bf16[2,320,128]{2,1,0:T(8,128)(2,1)S(1)}, u32[]{:S(2)}, u32[]{:S(2)}) collective-permute-start(bf16[2,320,128]{2,1,0:T(8,128)(2,1)} %get-tuple-element.269), channel_id=1, source_target_pairs={{0,1},{1,0},{2,3},{3,2},{4,5},{5,4},{6,7},{7,6},{8,9},{9,8},{10,11... | collective-permute-start | bytes 491528 | tf_op jit(solution)/shard_map/while/body/ppermute | solution.py:453
  215.1 42.2 %collective-permute-start.1 = (bf16[2,320,128]{2,1,0:T(8,128)(2,1)}, bf16[2,320,128]{2,1,0:T(8,128)(2,1)S(1)}, u32[]{:S(2)}, u32[]{:S(2)}) collective-permute-start(bf16[2,320,128]{2,1,0:T(8,128)(2,1)} %get-tuple-element.270), channel_id=1, source_target_pairs={{0,2},{1,3},{2,0},{3,1},{4,6},{5,7},{6,4},{7,5},{8,10},{9,11},{10,... | collective-permute-start | bytes 491528 | tf_op jit(solution)/shard_map/while/body/ppermute | solution.py:453
  216.8 43.0 %collective-permute-start.2 = (bf16[2,320,128]{2,1,0:T(8,128)(2,1)}, bf16[2,320,128]{2,1,0:T(8,128)(2,1)S(1)}, u32[]{:S(2)}, u32[]{:S(2)}) collective-permute-start(bf16[2,320,128]{2,1,0:T(8,128)(2,1)} %get-tuple-element.271), channel_id=1, source_target_pairs={{0,3},{1,2},{2,1},{3,0},{4,7},{5,6},{6,5},{7,4},{8,11},{9,10},{10,... | collective-permute-start | bytes 491528 | tf_op jit(solution)/shard_map/while/body/ppermute | solution.py:453
  216.9 42.9 %collective-permute-start.3 = (bf16[2,320,128]{2,1,0:T(8,128)(2,1)}, bf16[2,320,128]{2,1,0:T(8,128)(2,1)S(1)}, u32[]{:S(2)}, u32[]{:S(2)}) collective-permute-start(bf16[2,320,128]{2,1,0:T(8,128)(2,1)} %get-tuple-element.272), channel_id=1, source_target_pairs={{0,4},{1,5},{2,6},{3,7},{4,0},{5,1},{6,2},{7,3},{8,12},{9,13},{10,... | collective-permute-start | bytes 491528 | tf_op jit(solution)/shard_map/while/body/ppermute | solution.py:453
  220.1 35.9 %copy-start.19 = (bf16[2,320,128]{2,1,0:T(8,128)(2,1)S(1)}, bf16[2,320,128]{2,1,0:T(8,128)(2,1)}, u32[]{:S(2)}) copy-start(bf16[2,320,128]{2,1,0:T(8,128)(2,1)} %get-tuple-element.274) | copy-start | bytes 491524 | tf_op jit(solution)/shard_map/while
  220.1 37.2 %copy-start.17 = (bf16[2,320,128]{2,1,0:T(8,128)(2,1)S(1)}, bf16[2,320,128]{2,1,0:T(8,128)(2,1)}, u32[]{:S(2)}) copy-start(bf16[2,320,128]{2,1,0:T(8,128)(2,1)} %get-tuple-element.275) | copy-start | bytes 491524 | tf_op jit(solution)/shard_map/while
  245.3 48.7 %all-to-all-start.3 = ((bf16[32,72,128]{2,1,0:T(8,128)(2,1)}), bf16[32,72,128]{2,1,0:T(8,128)(2,1)S(1)}, u32[]{:S(2)}, u32[]{:S(2)}) async-start(bf16[32,72,128]{2,1,0:T(8,128)(2,1)} %place.2), calls=%async_computation.3 | async-start | bytes 1179648 | tf_op jit(solution)/shard_map/while/body/all_to_all | solution.py:471
  250.6 9.3 %collective-permute-start.4 = (bf16[2,320,128]{2,1,0:T(8,128)(2,1)S(1)}, bf16[2,320,128]{2,1,0:T(8,128)(2,1)S(1)}, u32[]{:S(2)}, u32[]{:S(2)}) collective-permute-start(bf16[2,320,128]{2,1,0:T(8,128)(2,1)S(1)} %copy-done.21), channel_id=1, source_target_pairs={{0,5},{1,4},{2,7},{3,6},{4,1},{5,0},{6,3},{7,2},{8,13},{9,12},{10,... | collective-permute-start | bytes 491528 | tf_op jit(solution)/shard_map/while/body/ppermute | solution.py:453
  256.0 28.7 %copy-start.12 = (bf16[2,320,128]{2,1,0:T(8,128)(2,1)}, bf16[2,320,128]{2,1,0:T(8,128)(2,1)S(1)}, u32[]{:S(2)}) copy-start(bf16[2,320,128]{2,1,0:T(8,128)(2,1)S(1)} %collective-permute-done.refs_1_) | copy-start | bytes 491524 | tf_op jit(solution)/shard_map/while
  256.0 8.3 %collective-permute-start.5 = (bf16[2,320,128]{2,1,0:T(8,128)(2,1)S(1)}, bf16[2,320,128]{2,1,0:T(8,128)(2,1)S(1)}, u32[]{:S(2)}, u32[]{:S(2)}) collective-permute-start(bf16[2,320,128]{2,1,0:T(8,128)(2,1)S(1)} %copy-done.19), channel_id=1, source_target_pairs={{0,6},{1,7},{2,4},{3,5},{4,2},{5,3},{6,0},{7,1},{8,14},{9,15},{10,... | collective-permute-start | bytes 491528 | tf_op jit(solution)/shard_map/while/body/ppermute | solution.py:453
  257.3 27.4 %copy-start.13 = (bf16[2,320,128]{2,1,0:T(8,128)(2,1)}, bf16[2,320,128]{2,1,0:T(8,128)(2,1)S(1)}, u32[]{:S(2)}) copy-start(bf16[2,320,128]{2,1,0:T(8,128)(2,1)S(1)} %collective-permute-done.1.refs_2_) | copy-start | bytes 491524 | tf_op jit(solution)/shard_map/while
  257.3 10.6 %collective-permute-start.6 = (bf16[2,320,128]{2,1,0:T(8,128)(2,1)S(1)}, bf16[2,320,128]{2,1,0:T(8,128)(2,1)S(1)}, u32[]{:S(2)}, u32[]{:S(2)}) collective-permute-start(bf16[2,320,128]{2,1,0:T(8,128)(2,1)S(1)} %copy-done.17), channel_id=1, source_target_pairs={{0,7},{1,6},{2,5},{3,4},{4,3},{5,2},{6,1},{7,0},{8,15},{9,14},{10,... | collective-permute-start | bytes 491528 | tf_op jit(solution)/shard_map/while/body/ppermute | solution.py:453
  259.8 24.9 %copy-start.14 = (bf16[2,320,128]{2,1,0:T(8,128)(2,1)}, bf16[2,320,128]{2,1,0:T(8,128)(2,1)S(1)}, u32[]{:S(2)}) copy-start(bf16[2,320,128]{2,1,0:T(8,128)(2,1)S(1)} %collective-permute-done.2.refs_3_) | copy-start | bytes 491524 | tf_op jit(solution)/shard_map/while
  259.8 8.1 %collective-permute-start.17 = (bf16[2,320,128]{2,1,0:T(8,128)(2,1)}, bf16[2,320,128]{2,1,0:T(8,128)(2,1)S(1)}, u32[]{:S(2)}, u32[]{:S(2)}) collective-permute-start(bf16[2,320,128]{2,1,0:T(8,128)(2,1)} %get-tuple-element.292), channel_id=1, source_target_pairs={{0,1},{1,0},{2,3},{3,2},{4,5},{5,4},{6,7},{7,6},{8,9},{9,8},{10,11... | collective-permute-start | bytes 491528 | tf_op jit(solution)/shard_map/while/body/ppermute | solution.py:453
  259.8 9.8 %collective-permute-start.18 = (bf16[2,320,128]{2,1,0:T(8,128)(2,1)}, bf16[2,320,128]{2,1,0:T(8,128)(2,1)S(1)}, u32[]{:S(2)}, u32[]{:S(2)}) collective-permute-start(bf16[2,320,128]{2,1,0:T(8,128)(2,1)} %get-tuple-element.293), channel_id=1, source_target_pairs={{0,2},{1,3},{2,0},{3,1},{4,6},{5,7},{6,4},{7,5},{8,10},{9,11},{10,... | collective-permute-start | bytes 491528 | tf_op jit(solution)/shard_map/while/body/ppermute | solution.py:453
  259.9 10.8 %collective-permute-start.19 = (bf16[2,320,128]{2,1,0:T(8,128)(2,1)}, bf16[2,320,128]{2,1,0:T(8,128)(2,1)S(1)}, u32[]{:S(2)}, u32[]{:S(2)}) collective-permute-start(bf16[2,320,128]{2,1,0:T(8,128)(2,1)} %get-tuple-element.294), channel_id=1, source_target_pairs={{0,3},{1,2},{2,1},{3,0},{4,7},{5,6},{6,5},{7,4},{8,11},{9,10},{10,... | collective-permute-start | bytes 491528 | tf_op jit(solution)/shard_map/while/body/ppermute | solution.py:453
  264.3 10.6 %collective-permute-start.20 = (bf16[2,320,128]{2,1,0:T(8,128)(2,1)}, bf16[2,320,128]{2,1,0:T(8,128)(2,1)S(1)}, u32[]{:S(2)}, u32[]{:S(2)}) collective-permute-start(bf16[2,320,128]{2,1,0:T(8,128)(2,1)} %get-tuple-element.295), channel_id=1, source_target_pairs={{0,4},{1,5},{2,6},{3,7},{4,0},{5,1},{6,2},{7,3},{8,12},{9,13},{10,... | collective-permute-start | bytes 491528 | tf_op jit(solution)/shard_map/while/body/ppermute | solution.py:453
  267.9 9.4 %collective-permute-start.21 = (bf16[2,320,128]{2,1,0:T(8,128)(2,1)}, bf16[2,320,128]{2,1,0:T(8,128)(2,1)S(1)}, u32[]{:S(2)}, u32[]{:S(2)}) collective-permute-start(bf16[2,320,128]{2,1,0:T(8,128)(2,1)} %get-tuple-element.296), channel_id=1, source_target_pairs={{0,5},{1,4},{2,7},{3,6},{4,1},{5,0},{6,3},{7,2},{8,13},{9,12},{10,... | collective-permute-start | bytes 491528 | tf_op jit(solution)/shard_map/while/body/ppermute | solution.py:453
  267.9 13.4 %collective-permute-start.22 = (bf16[2,320,128]{2,1,0:T(8,128)(2,1)}, bf16[2,320,128]{2,1,0:T(8,128)(2,1)S(1)}, u32[]{:S(2)}, u32[]{:S(2)}) collective-permute-start(bf16[2,320,128]{2,1,0:T(8,128)(2,1)} %get-tuple-element.297), channel_id=1, source_target_pairs={{0,6},{1,7},{2,4},{3,5},{4,2},{5,3},{6,0},{7,1},{8,14},{9,15},{10,... | collective-permute-start | bytes 491528 | tf_op jit(solution)/shard_map/while/body/ppermute | solution.py:453
  269.6 15.1 %collective-permute-start.23 = (bf16[2,320,128]{2,1,0:T(8,128)(2,1)}, bf16[2,320,128]{2,1,0:T(8,128)(2,1)S(1)}, u32[]{:S(2)}, u32[]{:S(2)}) collective-permute-start(bf16[2,320,128]{2,1,0:T(8,128)(2,1)} %get-tuple-element.298), channel_id=1, source_target_pairs={{0,7},{1,6},{2,5},{3,4},{4,3},{5,2},{6,1},{7,0},{8,15},{9,14},{10,... | collective-permute-start | bytes 491528 | tf_op jit(solution)/shard_map/while/body/ppermute | solution.py:453
  293.9 30.5 %copy-start.9 = (s32[1024]{0:T(1024)S(1)}, s32[1024]{0:T(1024)}, u32[]{:S(2)}) copy-start(s32[1024]{0:T(1024)} %get-tuple-element.261) | copy-start | bytes 12292 | tf_op jit(solution)/shard_map/while
  293.9 33.2 %copy-start.2 = (f32[32,32,256]{2,1,0:T(8,128)S(1)}, f32[32,32,256]{2,1,0:T(8,128)}, u32[]{:S(2)}) copy-start(f32[32,32,256]{2,1,0:T(8,128)} %get-tuple-element.415.refs_6_) | copy-start | bytes 3145732 | tf_op jit(solution)/shard_map/while
  294.0 33.2 %copy-start.5 = (bf16[32,72,128]{2,1,0:T(8,128)(2,1)}, bf16[32,72,128]{2,1,0:T(8,128)(2,1)S(1)}, u32[]{:S(2)}) copy-start(bf16[32,72,128]{2,1,0:T(8,128)(2,1)S(1)} %all-to-all-done.3.refs_5_) | copy-start | bytes 1769476 | tf_op jit(solution)/shard_map/while
  312.0 31.3 %all-to-all-start.5 = ((bf16[32,72,128]{2,1,0:T(8,128)(2,1)}), bf16[32,72,128]{2,1,0:T(8,128)(2,1)S(1)}, u32[]{:S(2)}, u32[]{:S(2)}) async-start(bf16[32,72,128]{2,1,0:T(8,128)(2,1)} %place.3), calls=%async_computation.5 | async-start | bytes 1179648 | tf_op jit(solution)/shard_map/while/body/all_to_all | solution.py:471
  (18 other events, 190.6 us)

commit v8 on v7

--- a/solution.py
+++ b/solution.py
@@ -273,7 +273,7 @@
     one_dimer(table_ref[STEPS + 2 * me + i], me, load, out, scratch)
 
 
-def plan_kernel(me_ref, inside_ref, count_ref, list_ref, table_ref, left_ref, to_x, to_z, n_direct, n_third, n_self, n_split, room, taken):
+def plan_kernel(me_ref, inside_ref, count_ref, list_ref, table_ref, left_ref, to_x, to_z, n_direct, n_third, n_self, n_split, room, taken, mine):
     me = me_ref[0]
     me_x, me_z = me >> 3, me & 7
 
@@ -358,11 +358,10 @@
 
             @pl.when(c == me)
             def _():
-                table_ref[POS + 2 * at] = stay
-                table_ref[POS + 2 * at + 1] = 32 + o
-                table_ref[HOME + at] = stay
-                table_ref[LATE + at] = late
-                table_ref[STEPS + at] = cost
+                mine[at * 4] = stay
+                mine[at * 4 + 1] = 32 + o
+                mine[at * 4 + 2] = late
+                mine[at * 4 + 3] = cost
 
         @pl.when(jnp.logical_not(direct))
         def _():
@@ -432,6 +431,18 @@
                         table_ref[MODE + 7 - t] = 1
 
     loop(count_ref[0], visit)
+    devices = 8 - jnp.maximum(n_third[me], n_self[me])
+
+    def settle(n):
+        second = n >= devices
+        at = 2 * jnp.where(second, n - devices, n) + jnp.where(second, 1, 0)
+        table_ref[POS + 2 * at] = mine[n * 4]
+        table_ref[POS + 2 * at + 1] = mine[n * 4 + 1]
+        table_ref[HOME + at] = mine[n * 4]
+        table_ref[LATE + at] = mine[n * 4 + 2]
+        table_ref[STEPS + at] = mine[n * 4 + 3]
+
+    loop(n_direct[me], settle)
 
 
 def plan_rest(me, inside_count, count, words):
@@ -441,7 +452,7 @@
         out_shape=[jax.ShapeDtypeStruct((TABLE,), s32), jax.ShapeDtypeStruct(words.shape, s32)],
         in_specs=[SMEM] * 4,
         out_specs=[SMEM] * 2,
-        scratch_shapes=[pltpu.SMEM((128,), s32), pltpu.SMEM((256,), s32)] + [pltpu.SMEM((32,), s32)] * 6,
+        scratch_shapes=[pltpu.SMEM((128,), s32), pltpu.SMEM((256,), s32)] + [pltpu.SMEM((32,), s32)] * 6 + [pltpu.SMEM((64,), s32)],
         name="plan",
         cost_estimate=pl.CostEstimate(flops=1000, bytes_accessed=30_000_000, transcendentals=0),
     )(me, inside_count, count, words)
@@ -538,7 +549,8 @@
         earlier = (pair_id[:, None] == pair_id[None, :]) & (order[None, :] < order[:, None])
         earlier = jnp.sum(jnp.where(earlier & open_dimer[None, :], 1, 0), axis=1)
         flagged = open_dimer & ((earlier >= 2) | inside)
-        ahead = jnp.sum(jnp.where((order[None, :] < order[:, None]) & flagged[None, :], 1, 0), axis=1)
+        turn = order + jnp.where(inside, 2 * dimers, dimers * (2 - jnp.clip(earlier - 2, 0, 2)))
+        ahead = jnp.sum(jnp.where((turn[None, :] < turn[:, None]) & flagged[None, :], 1, 0), axis=1)
         ahead = jnp.where(flagged, ahead, -1)
         words = jnp.sum(jnp.where(ahead[None, :] == order[:, None], word[None, :], 0), axis=1)
         count = jnp.sum(jnp.where(flagged, 1, 0)).reshape(1)
@@ -570,15 +582,7 @@
 
         one = lambda i, *_: (i, 0, 0)
         ready_1 = run_dimers(kernel_1, 4, (table_1, me_b), (1, 1), (one, one), [*home_1, *away_1])
-        done_1 = give_back(ready_1)
-
-        def late_at(t, me, n, row):
-            return t[1][LATE + 2 * lax.bitwise_xor(me, n) + row] - 32
-
-        late_parts = pack(tables, me_b, late_at, 8, 2, (), [*in_x, after(in_z, away_1)])
-        late_2 = exchange(late_parts)
-        whole = lambda i, *_: (0, 0, 0)
-        ready_2 = run_dimers(kernel_2, 2, (table_2, me_b), (2, 2), (whole, whole), [*home_2, *late_2])
+        done_1 = give_back(after(ready_1, in_z))
 
         def place_1(t, row):
             return t[0][RANKED + ranked_at(row // 8, row % 8 // 2)]
@@ -591,6 +595,14 @@
             tables, me_b, [done_1], [lambda t, me, row: jnp.where(row % 2 == 1, place_1(t, row), -1)], [32]
         )
         back_1 = across(ret_1)
+
+        def late_at(t, me, n, row):
+            return t[1][LATE + 2 * lax.bitwise_xor(me, n) + row] - 32
+
+        late_parts = pack(tables, me_b, late_at, 8, 2, (), [*in_x, after(in_z, ret_1)])
+        late_2 = exchange(late_parts)
+        whole = lambda i, *_: (0, 0, 0)
+        ready_2 = run_dimers(kernel_2, 2, (table_2, me_b), (2, 2), (whole, whole), [*home_2, *late_2])
         done_2 = give_back(after(ready_2, back_1))
         (ret_2,) = place(tables, me_b, [done_2], [lambda t, me, row: place_2(t, row) - 32], [32])
         back_2 = across(ret_2)

time: 349 us -> 329 us (0.943)
  waiting for transfers between devices: 140 us -> 116 us
  starting transfers between devices: 80.1 us -> 88.1 us
  Pallas kernels: 85.9 us -> 80.8 us
    all_to_all x1, waiting for transfers between devices: 21 us -> 0.01 us  [along_z(): lax.all_to_all(part, 'frag', 0, 0, tiled=True, axis_index_groups=groups)]
    all_to_all x4, waiting for transfers between devices: 38 us -> 19.5 us  [across(): return lax.all_to_all(part, 'frag', split_axis=0, concat_axis=0, tiled=True)]
    all_to_all x1, waiting for transfers between devices: 0.01 us -> 10.4 us  [give_back(): lax.all_to_all(done, 'basis', split_axis=0, concat_axis=0, tiled=True)]
    all_to_all x4, starting transfers between devices: 35 us -> 43.8 us  [across(): return lax.all_to_all(part, 'frag', split_axis=0, concat_axis=0, tiled=True)]
    ppermute x28, waiting for transfers between devices: 58.3 us -> 62.1 us  [exchange(): got.append(lax.ppermute(parts[k], 'basis', [(i, i ^ k) for i in range(8)]))]
  transfers between devices with their start and end apart: 37 -> 37, of which waited for: 20 -> 18; matrix products, arithmetic and copies ran while one was open for 2% -> 2% of each run, Pallas kernels for 19% -> 22%
where the time goes in v8:
time: 329 us; the launch traced here: 328 us
  waiting for transfers between devices  116 us (35%)
  starting transfers between devices  88.1 us (27%)
  Pallas kernels  80.8 us (25%)
  blocking collectives  25 us (8%)
  other arithmetic  10.2 us (3%)
  local copies, waits for them, and re-layouts  6.23 us (2%)
    ppermute x28, waiting for transfers between devices, exchange(): got.append(lax.ppermute(parts[k], 'basis', [(i, i ^ k) for i in range(8)]))  62.1 us
    all_to_all x4, starting transfers between devices, across(): return lax.all_to_all(part, 'frag', split_axis=0, concat_axis=0, tiled=True)  43.8 us
    ppermute x28, starting transfers between devices, exchange(): got.append(lax.ppermute(parts[k], 'basis', [(i, i ^ k) for i in range(8)]))  27.9 us
    pallas_call x1, Pallas kernels, plan_rest(): pl.pallas_call(plan_kernel, out_shape=[jax.ShapeDtypeStruct((TABLE,), s32...  26 us
    ppermute x3, waiting for transfers between devices, along_x(): lax.ppermute(parts[k - 1], 'frag', [(i, i ^ 8 * k) for i in range(32)])  23.9 us
    pallas_call x7, Pallas kernels, pack(): pl.pallas_call(kernel, out_shape=[jax.ShapeDtypeStruct((rows, 320, 128),...  21.9 us
    all_to_all x4, waiting for transfers between devices, across(): return lax.all_to_all(part, 'frag', split_axis=0, concat_axis=0, tiled=True)  19.5 us
    pallas_call x2, Pallas kernels, run_dimers(): pl.pallas_call(kernel, out_shape=jax.ShapeDtypeStruct((8, 2 * count, 72,...  19.1 us
  transfers between devices with their start and end apart: 37, of which 18 were waited for; matrix products, arithmetic and copies ran while one was open for 2% of the time, Pallas kernels for 22%

profile of v8, /device:TPU:32, one launch (start us, length us, event | category | flops | bytes accessed | tf_op | source)
XLA Modules:
  0.0 327.8 jit_solution(8076476978640131235)
XLA Ops:
  2.3 9.6 %all_to_all.55 = s32[8,1,128]{2,1,0:T(1,128)S(1)} all-to-all(s32[8,1,128]{2,1,0:T(1,128)S(1)} %broadcast_in_dim.188), channel_id=1, replica_groups=mesh['frag'=32,'basis'=8] {'basis'}, dimensions={0} | all-to-all | bytes 8192 | tf_op jit(solution)/shard_map/all_to_all | solution.py:499
  12.8 11.2 %all-to-all-start.7 = ((s32[32,1,128]{2,1,0:T(1,128)}), s32[32,1,128]{2,1,0:T(1,128)S(1)}, u32[]{:S(2)}, u32[]{:S(2)}) async-start(s32[32,1,128]{2,1,0:T(1,128)} %broadcast_in_dim.189), calls=%async_computation.7 | async-start | bytes 32768 | tf_op jit(solution)/shard_map/all_to_all | solution.py:482
  24.0 8.6 %all-to-all-done.7 = s32[32,1,128]{2,1,0:T(1,128)S(1)} async-done(((s32[32,1,128]{2,1,0:T(1,128)}), s32[32,1,128]{2,1,0:T(1,128)S(1)}, u32[]{:S(2)}, u32[]{:S(2)}) %all-to-all-start.7) | async-done | bytes 16416 | tf_op jit(solution)/shard_map/all_to_all | solution.py:482
  34.1 293.1 %while.17 = (s32[]{:T(128)}, s32[1024]{0:T(1024)S(1)}, f32[32,32,256]{2,1,0:T(8,128)}, f32[32,128]{1,0:T(8,128)S(1)}, s32[1024]{0:T(1024)S(1)}, /*index=5*/pred[...) while((s32[]{:T(128)}, s32[1024]{0:T(1024)S(1)}, ...), condition=%region_13.14_spmd.clone.clone, body=%region_1.13_spmd.clone.clone | while | flops 24018305024 | bytes 145030896 | solution.py:624
  35.0 3.8 %pack.30 = bf16[32,320,128]{2,1,0:T(8,128)(2,1)} custom-call(s32[32]{0:T(128)} %get-tuple-element.493.refs_0_, s32[1]{0:T(128)} %get-tuple-element.558.refs_2_.refs_1_.me_ref, bf16[32,256,128]{2,1,0:T(8,128)(2,1)} %get-tuple-element.559.refs_3_.refs_2_, bf16[32,32,256]{2,1,0:T(8,128)(2,1)} %get-tuple-element.560.refs_4_.refs_3_), custom_call_target="tpu_custom_call" | custom-call | tf_op jit(solution)/shard_map/while/body/pack/pallas_call | solution.py:68
  38.8 6.1 %all-to-all-start = ((bf16[32,320,128]{2,1,0:T(8,128)(2,1)}), bf16[32,320,128]{2,1,0:T(8,128)(2,1)}, u32[]{:S(2)}, u32[]{:S(2)}) async-start(bf16[32,320,128]{2,1,0:T(8,128)(2,1)} %pack.30), calls=%async_computation | async-start | bytes 5242880 | tf_op jit(solution)/shard_map/while/body/all_to_all | solution.py:482
  49.0 26.0 %plan.4 = (s32[256]{0:T(256)}, s32[1024]{0:T(1024)}) custom-call(s32[1]{0:T(128)} %get-tuple-element.555.me_ref, s32[32]{0:T(128)} %select_reduce_fusion.6.inside_ref, s32[1]{0:T(128)} %bitcast.5.count_ref, s32[1024]{0:T(1024)} %select_reduce_fusion.2.list_ref), custom_call_target="tpu_custom_call" | custom-call | flops 1000 | bytes 30000000 | tf_op jit(solution)/shard_map/while/body/plan/pallas_call | solution.py:450
  75.9 2.2 pack.29
  79.6 2.8 collective-permute-start.8
  82.8 3.1 pack.33
  86.5 10.1 %collective-permute-done.7.refs_5_.refs_3_ = bf16[6,320,128]{2,1,0:T(8,128)(2,1)S(1)} collective-permute-done((bf16[6,320,128]{2,1,0:T(8,128)(2,1)}, bf16[6,320,128]{2,1,0:T(8,128)(2,1)S(1)}, u32[]{:S(2)}, u32[]{:S(2)}) %collective-permute-start.7) | collective-permute-done | bytes 491552 | tf_op jit(solution)/shard_map/while/body/ppermute | solution.py:473
  96.7 13.8 %collective-permute-done.8.refs_6_.refs_4_ = bf16[6,320,128]{2,1,0:T(8,128)(2,1)} collective-permute-done((bf16[6,320,128]{2,1,0:T(8,128)(2,1)}, bf16[6,320,128]{2,1,0:T(8,128)(2,1)}, u32[]{:S(2)}, u32[]{:S(2)}) %collective-permute-start.8) | collective-permute-done | bytes 491552 | tf_op jit(solution)/shard_map/while/body/ppermute | solution.py:473
  111.6 4.1 %pack.31 = (bf16[4,320,128]{2,1,0:T(8,128)(2,1)}, bf16[4,320,128]{2,1,0:T(8,128)(2,1)}, bf16[4,320,128]{2,1,0:T(8,128)(2,1)}, bf16[4,320,128]{2,1,0:T(8,128)(2,1...) custom-call(s32[128]{0:T(128)} %pad_add_fusion.refs_0_.table_ref, ...), custom_call_target="tpu_custom_call" | custom-call | tf_op jit(solution)/shard_map/while/body/pack/pallas_call | solution.py:68
  115.7 3.0 pack.32
  118.7 7.5 %all-to-all-start.1 = ((bf16[16,320,128]{2,1,0:T(8,128)(2,1)}), bf16[16,320,128]{2,1,0:T(8,128)(2,1)}, u32[]{:S(2)}, u32[]{:S(2)}) async-start(bf16[16,320,128]{2,1,0:T(8,128)(2,1)} %pack.32), calls=%async_computation.1 | async-start | bytes 2621440 | tf_op jit(solution)/shard_map/while/body/all_to_all | solution.py:478
  126.2 2.2 collective-permute-start.15
  128.4 2.9 collective-permute-start.16
  131.4 6.6 %collective-permute-done.14.refs_5_ = bf16[4,320,128]{2,1,0:T(8,128)(2,1)S(1)} collective-permute-done((bf16[4,320,128]{2,1,0:T(8,128)(2,1)}, bf16[4,320,128]{2,1,0:T(8,128)(2,1)S(1)}, u32[]{:S(2)}, u32[]{:S(2)}) %collective-permute-start.14) | collective-permute-done | bytes 327712 | tf_op jit(solution)/shard_map/while/body/ppermute | solution.py:464
  138.0 6.3 %collective-permute-done.15.refs_6_ = bf16[4,320,128]{2,1,0:T(8,128)(2,1)S(1)} collective-permute-done((bf16[4,320,128]{2,1,0:T(8,128)(2,1)}, bf16[4,320,128]{2,1,0:T(8,128)(2,1)S(1)}, u32[]{:S(2)}, u32[]{:S(2)}) %collective-permute-start.15) | collective-permute-done | bytes 327712 | tf_op jit(solution)/shard_map/while/body/ppermute | solution.py:464
  145.5 6.4 %collective-permute-done.16.refs_7_ = bf16[4,320,128]{2,1,0:T(8,128)(2,1)S(1)} collective-permute-done((bf16[4,320,128]{2,1,0:T(8,128)(2,1)}, bf16[4,320,128]{2,1,0:T(8,128)(2,1)S(1)}, u32[]{:S(2)}, u32[]{:S(2)}) %collective-permute-start.16) | collective-permute-done | bytes 327712 | tf_op jit(solution)/shard_map/while/body/ppermute | solution.py:464
  151.9 2.2 collective-permute-start.21
  155.1 2.0 collective-permute-start.23
  157.9 7.7 %collective-permute-done.21.refs_13_ = bf16[4,320,128]{2,1,0:T(8,128)(2,1)S(1)} collective-permute-done((bf16[4,320,128]{2,1,0:T(8,128)(2,1)}, bf16[4,320,128]{2,1,0:T(8,128)(2,1)S(1)}, u32[]{:S(2)}, u32[]{:S(2)}) %collective-permute-start.21) | collective-permute-done | bytes 327712 | tf_op jit(solution)/shard_map/while/body/ppermute | solution.py:464
  165.6 7.0 %collective-permute-done.22.refs_14_ = bf16[4,320,128]{2,1,0:T(8,128)(2,1)S(1)} collective-permute-done((bf16[4,320,128]{2,1,0:T(8,128)(2,1)}, bf16[4,320,128]{2,1,0:T(8,128)(2,1)S(1)}, u32[]{:S(2)}, u32[]{:S(2)}) %collective-permute-start.22) | collective-permute-done | bytes 327712 | tf_op jit(solution)/shard_map/while/body/ppermute | solution.py:464
  172.5 6.9 %collective-permute-done.23.refs_15_ = bf16[4,320,128]{2,1,0:T(8,128)(2,1)S(1)} collective-permute-done((bf16[4,320,128]{2,1,0:T(8,128)(2,1)S(1)}, bf16[4,320,128]{2,1,0:T(8,128)(2,1)S(1)}, u32[]{:S(2)}, u32[]{:S(2)}) %collective-permute-start.23) | collective-permute-done | bytes 327712 | tf_op jit(solution)/shard_map/while/body/ppermute | solution.py:464
  180.3 13.1 %dimers.8 = bf16[8,8,72,128]{3,2,1,0:T(8,128)(2,1)} custom-call(s32[128]{0:T(128)} %pad_add_fusion.refs_0_.table_ref, s32[1]{0:T(128)} %get-tuple-element.558.refs_2_.refs_1_.me_ref, bf16[4,320,128]{2,1,0:T(8,128)(2,1)} %get-tuple-element.407.refs_0_, bf16[4,320,128]{2,1,0:T(8,128)(2,1)} %copy-done.10, bf16[4,320,128]{2,1,0:T(8,128)(2,1)} %collective-permute-done.11.refs_2_, ...), custom_call_target="tpu_custom_call" | custom-call | flops 16000000000 | bytes 6000000 | tf_op jit(solution)/shard_map/while/body/dimers/pallas_call | solution.py:217
  193.4 4.3 %all-to-all-start.2 = ((bf16[8,8,72,128]{3,2,1,0:T(8,128)(2,1)}), bf16[8,8,72,128]{3,2,1,0:T(8,128)(2,1)}, u32[]{:S(2)}, u32[]{:S(2)}) async-start(bf16[8,8,72,128]{3,2,1,0:T(8,128)(2,1)} %dimers.8), calls=%async_computation.2 | async-start | bytes 2359296 | tf_op jit(solution)/shard_map/while/body/all_to_all | solution.py:469
  197.7 2.2 pack.28
  201.9 3.3 collective-permute-start.3
  205.1 10.4 %all-to-all-done.2 = bf16[8,8,72,128]{3,2,1,0:T(8,128)(2,1)} async-done(((bf16[8,8,72,128]{3,2,1,0:T(8,128)(2,1)}), bf16[8,8,72,128]{3,2,1,0:T(8,128)(2,1)}, u32[]{:S(2)}, u32[]{:S(2)}) %all-to-all-start.2) | async-done | bytes 1179680 | tf_op jit(solution)/shard_map/while/body/all_to_all | solution.py:469
  215.6 4.2 %place.8 = bf16[32,72,128]{2,1,0:T(8,128)(2,1)} custom-call(s32[128]{0:T(128)} %pad_add_fusion.refs_0_.table_ref, s32[256]{0:T(256)} %get-tuple-element.381.refs_1_.table_ref, s32[1]{0:T(128)} %get-tuple-element.558.refs_2_.refs_1_.me_ref, bf16[64,72,128]{2,1,0:T(8,128)(2,1)} %bitcast.6.refs_3_), custom_call_target="tpu_custom_call" | custom-call | tf_op jit(solution)/shard_map/while/body/place/pallas_call | solution.py:95
  219.8 11.2 %all-to-all-start.3 = ((bf16[32,72,128]{2,1,0:T(8,128)(2,1)}), bf16[32,72,128]{2,1,0:T(8,128)(2,1)S(1)}, u32[]{:S(2)}, u32[]{:S(2)}) async-start(bf16[32,72,128]{2,1,0:T(8,128)(2,1)} %place.8), calls=%async_computation.3 | async-start | bytes 1179648 | tf_op jit(solution)/shard_map/while/body/all_to_all | solution.py:482
  231.1 3.5 %pack.34 = (bf16[2,320,128]{2,1,0:T(8,128)(2,1)}, bf16[2,320,128]{2,1,0:T(8,128)(2,1)}, bf16[2,320,128]{2,1,0:T(8,128)(2,1)}, bf16[2,320,128]{2,1,0:T(8,128)(2,1...) custom-call(s32[128]{0:T(128)} %pad_add_fusion.refs_0_.table_ref, ...), custom_call_target="tpu_custom_call" | custom-call | tf_op jit(solution)/shard_map/while/body/pack/pallas_call | solution.py:68
  235.9 1.8 collective-permute-start.6
  239.6 3.3 %collective-permute-done.5.refs_6_ = bf16[2,320,128]{2,1,0:T(8,128)(2,1)S(1)} collective-permute-done((bf16[2,320,128]{2,1,0:T(8,128)(2,1)S(1)}, bf16[2,320,128]{2,1,0:T(8,128)(2,1)S(1)}, u32[]{:S(2)}, u32[]{:S(2)}) %collective-permute-start.5) | collective-permute-done | bytes 163872 | tf_op jit(solution)/shard_map/while/body/ppermute | solution.py:464
  243.0 2.3 collective-permute-done.6.refs_7_
  245.4 2.9 collective-permute-start.29
  249.5 5.1 %collective-permute-done.27.refs_12_ = bf16[2,320,128]{2,1,0:T(8,128)(2,1)S(1)} collective-permute-done((bf16[2,320,128]{2,1,0:T(8,128)(2,1)}, bf16[2,320,128]{2,1,0:T(8,128)(2,1)S(1)}, u32[]{:S(2)}, u32[]{:S(2)}) %collective-permute-start.27) | collective-permute-done | bytes 163872 | tf_op jit(solution)/shard_map/while/body/ppermute | solution.py:464
  254.6 2.4 collective-permute-done.28.refs_13_
  257.0 3.4 %collective-permute-done.29.refs_14_ = bf16[2,320,128]{2,1,0:T(8,128)(2,1)S(1)} collective-permute-done((bf16[2,320,128]{2,1,0:T(8,128)(2,1)}, bf16[2,320,128]{2,1,0:T(8,128)(2,1)S(1)}, u32[]{:S(2)}, u32[]{:S(2)}) %collective-permute-start.29) | collective-permute-done | bytes 163872 | tf_op jit(solution)/shard_map/while/body/ppermute | solution.py:464
  260.4 3.8 %collective-permute-done.30.refs_15_ = bf16[2,320,128]{2,1,0:T(8,128)(2,1)S(1)} collective-permute-done((bf16[2,320,128]{2,1,0:T(8,128)(2,1)}, bf16[2,320,128]{2,1,0:T(8,128)(2,1)S(1)}, u32[]{:S(2)}, u32[]{:S(2)}) %collective-permute-start.30) | collective-permute-done | bytes 163872 | tf_op jit(solution)/shard_map/while/body/ppermute | solution.py:464
  264.9 6.0 %dimers.9 = bf16[8,4,72,128]{3,2,1,0:T(8,128)(2,1)} custom-call(s32[256]{0:T(256)} %get-tuple-element.381.refs_1_.table_ref, s32[1]{0:T(128)} %get-tuple-element.558.refs_2_.refs_1_.me_ref, bf16[2,320,128]{2,1,0:T(8,128)(2,1)} %get-tuple-element.385.refs_0_, bf16[2,320,128]{2,1,0:T(8,128)(2,1)} %copy-done.22, bf16[2,320,128]{2,1,0:T(8,128)(2,1)} %copy-done.23, ...), custom_call_target="tpu_custom_call" | custom-call | flops 8000000000 | bytes 3000000 | tf_op jit(solution)/shard_map/while/body/dimers/pallas_call | solution.py:217
  270.9 15.4 %all_to_all.56 = bf16[8,4,72,128]{3,2,1,0:T(8,128)(2,1)} all-to-all(bf16[8,4,72,128]{3,2,1,0:T(8,128)(2,1)} %dimers.9), channel_id=1, replica_groups=mesh['frag'=32,'basis'=8] {'basis'}, dimensions={0} | all-to-all | bytes 1179648 | tf_op jit(solution)/shard_map/while/body/all_to_all | solution.py:469
  286.3 2.6 place.9
  288.9 15.3 %all-to-all-start.5 = ((bf16[32,72,128]{2,1,0:T(8,128)(2,1)}), bf16[32,72,128]{2,1,0:T(8,128)(2,1)S(1)}, u32[]{:S(2)}, u32[]{:S(2)}) async-start(bf16[32,72,128]{2,1,0:T(8,128)(2,1)} %place.9), calls=%async_computation.5 | async-start | bytes 1179648 | tf_op jit(solution)/shard_map/while/body/all_to_all | solution.py:482
  304.8 2.0 select_reduce_fusion
  306.9 5.3 %add_up.8 = (f32[32,32,256]{2,1,0:T(8,128)S(1)}, f32[32,128]{1,0:T(8,128)S(1)}) custom-call(s32[128]{0:T(128)} %pad_add_fusion.refs_0_.table_ref, s32[256]{0:T(256)} %get-tuple-element.381.refs_1_.table_ref, s32[1]{0:T(128)} %get-tuple-element.558.refs_2_.refs_1_.me_ref, ...), custom_call_target="tpu_custom_call", output_to_operand_aliasing={{0}: (6, {}), {1}: (7, {})} | custom-call | tf_op jit(solution)/shard_map/while/body/add_up/pallas_call | solution.py:124
  312.2 10.9 %all-to-all-done.5.refs_3_ = bf16[32,72,128]{2,1,0:T(8,128)(2,1)S(1)} async-done(((bf16[32,72,128]{2,1,0:T(8,128)(2,1)}), bf16[32,72,128]{2,1,0:T(8,128)(2,1)S(1)}, u32[]{:S(2)}, u32[]{:S(2)}) %all-to-all-start.5) | async-done | bytes 589856 | tf_op jit(solution)/shard_map/while/body/all_to_all | solution.py:482
  (156 shorter events, 29.6 us)
Async XLA Ops:
  12.8 19.8 %all-to-all-start.7 = ((s32[32,1,128]{2,1,0:T(1,128)}), s32[32,1,128]{2,1,0:T(1,128)S(1)}, u32[]{:S(2)}, u32[]{:S(2)}) async-start(s32[32,1,128]{2,1,0:T(1,128)} %broadcast_in_dim.189), calls=%async_computation.7 | async-start | bytes 32768 | tf_op jit(solution)/shard_map/all_to_all | solution.py:482
  38.8 36.5 %copy-start.8 = (s32[32]{0:T(128)S(1)}, s32[32]{0:T(128)}, u32[]{:S(2)}) copy-start(s32[32]{0:T(128)} %get-tuple-element.493.refs_0_) | copy-start | bytes 388 | tf_op jit(solution)/shard_map/while
  38.8 37.1 %copy-start = (bf16[32,256,128]{2,1,0:T(8,128)(2,1)S(1)}, bf16[32,256,128]{2,1,0:T(8,128)(2,1)}, u32[]{:S(2)}) copy-start(bf16[32,256,128]{2,1,0:T(8,128)(2,1)} %get-tuple-element.559.refs_3_.refs_2_) | copy-start | bytes 6291460 | tf_op jit(solution)/shard_map/while
  38.8 37.1 %copy-start.1 = (bf16[32,32,256]{2,1,0:T(8,128)(2,1)S(1)}, bf16[32,32,256]{2,1,0:T(8,128)(2,1)}, u32[]{:S(2)}) copy-start(bf16[32,32,256]{2,1,0:T(8,128)(2,1)} %get-tuple-element.560.refs_4_.refs_3_) | copy-start | bytes 1572868 | tf_op jit(solution)/shard_map/while
  38.8 72.8 %all-to-all-start = ((bf16[32,320,128]{2,1,0:T(8,128)(2,1)}), bf16[32,320,128]{2,1,0:T(8,128)(2,1)}, u32[]{:S(2)}, u32[]{:S(2)}) async-start(bf16[32,320,128]{2,1,0:T(8,128)(2,1)} %pack.30), calls=%async_computation | async-start | bytes 5242880 | tf_op jit(solution)/shard_map/while/body/all_to_all | solution.py:482
  78.1 18.5 %collective-permute-start.7 = (bf16[6,320,128]{2,1,0:T(8,128)(2,1)}, bf16[6,320,128]{2,1,0:T(8,128)(2,1)S(1)}, u32[]{:S(2)}, u32[]{:S(2)}) collective-permute-start(bf16[6,320,128]{2,1,0:T(8,128)(2,1)} %get-tuple-element.393), channel_id=1, source_target_pairs={{0,64},{8,72},{16,80},{24,88},{32,96},{40,104},{48,112},{56,120},{... | collective-permute-start | bytes 1474568 | tf_op jit(solution)/shard_map/while/body/ppermute | solution.py:473
  79.6 30.8 %collective-permute-start.8 = (bf16[6,320,128]{2,1,0:T(8,128)(2,1)}, bf16[6,320,128]{2,1,0:T(8,128)(2,1)}, u32[]{:S(2)}, u32[]{:S(2)}) collective-permute-start(bf16[6,320,128]{2,1,0:T(8,128)(2,1)} %get-tuple-element.394), channel_id=1, source_target_pairs={{0,128},{8,136},{16,144},{24,152},{32,160},{40,168},{48,176},{56,1... | collective-permute-start | bytes 1474568 | tf_op jit(solution)/shard_map/while/body/ppermute | solution.py:473
  82.4 33.3 %collective-permute-start.9 = (bf16[6,320,128]{2,1,0:T(8,128)(2,1)}, bf16[6,320,128]{2,1,0:T(8,128)(2,1)}, u32[]{:S(2)}, u32[]{:S(2)}) collective-permute-start(bf16[6,320,128]{2,1,0:T(8,128)(2,1)} %get-tuple-element.395), channel_id=1, source_target_pairs={{0,192},{8,200},{16,208},{24,216},{32,224},{40,232},{48,240},{56,2... | collective-permute-start | bytes 1474568 | tf_op jit(solution)/shard_map/while/body/ppermute | solution.py:473
  85.9 40.3 %collective-permute-start.10 = (bf16[4,320,128]{2,1,0:T(8,128)(2,1)}, bf16[4,320,128]{2,1,0:T(8,128)(2,1)S(1)}, u32[]{:S(2)}, u32[]{:S(2)}) collective-permute-start(bf16[4,320,128]{2,1,0:T(8,128)(2,1)} %get-tuple-element.408), channel_id=1, source_target_pairs={{0,1},{1,0},{2,3},{3,2},{4,5},{5,4},{6,7},{7,6},{8,9},{9,8},{10,11... | collective-permute-start | bytes 983048 | tf_op jit(solution)/shard_map/while/body/ppermute | solution.py:464
  85.9 42.5 %collective-permute-start.11 = (bf16[4,320,128]{2,1,0:T(8,128)(2,1)}, bf16[4,320,128]{2,1,0:T(8,128)(2,1)}, u32[]{:S(2)}, u32[]{:S(2)}) collective-permute-start(bf16[4,320,128]{2,1,0:T(8,128)(2,1)} %get-tuple-element.409), channel_id=1, source_target_pairs={{0,2},{1,3},{2,0},{3,1},{4,6},{5,7},{6,4},{7,5},{8,10},{9,11},{10,... | collective-permute-start | bytes 983048 | tf_op jit(solution)/shard_map/while/body/ppermute | solution.py:464
  96.6 34.7 %collective-permute-start.12 = (bf16[4,320,128]{2,1,0:T(8,128)(2,1)}, bf16[4,320,128]{2,1,0:T(8,128)(2,1)}, u32[]{:S(2)}, u32[]{:S(2)}) collective-permute-start(bf16[4,320,128]{2,1,0:T(8,128)(2,1)} %get-tuple-element.410), channel_id=1, source_target_pairs={{0,3},{1,2},{2,1},{3,0},{4,7},{5,6},{6,5},{7,4},{8,11},{9,10},{10,... | collective-permute-start | bytes 983048 | tf_op jit(solution)/shard_map/while/body/ppermute | solution.py:464
  110.5 20.8 %collective-permute-start.13 = (bf16[4,320,128]{2,1,0:T(8,128)(2,1)}, bf16[4,320,128]{2,1,0:T(8,128)(2,1)}, u32[]{:S(2)}, u32[]{:S(2)}) collective-permute-start(bf16[4,320,128]{2,1,0:T(8,128)(2,1)} %get-tuple-element.411), channel_id=1, source_target_pairs={{0,4},{1,5},{2,6},{3,7},{4,0},{5,1},{6,2},{7,3},{8,12},{9,13},{10,... | collective-permute-start | bytes 983048 | tf_op jit(solution)/shard_map/while/body/ppermute | solution.py:464
  118.7 36.4 %copy-start.11 = (bf16[4,320,128]{2,1,0:T(8,128)(2,1)S(1)}, bf16[4,320,128]{2,1,0:T(8,128)(2,1)}, u32[]{:S(2)}) copy-start(bf16[4,320,128]{2,1,0:T(8,128)(2,1)} %get-tuple-element.403) | copy-start | bytes 983044 | tf_op jit(solution)/shard_map/while
  118.7 74.7 %all-to-all-start.1 = ((bf16[16,320,128]{2,1,0:T(8,128)(2,1)}), bf16[16,320,128]{2,1,0:T(8,128)(2,1)}, u32[]{:S(2)}, u32[]{:S(2)}) async-start(bf16[16,320,128]{2,1,0:T(8,128)(2,1)} %pack.32), calls=%async_computation.1 | async-start | bytes 2621440 | tf_op jit(solution)/shard_map/while/body/all_to_all | solution.py:478
  126.2 11.8 %collective-permute-start.14 = (bf16[4,320,128]{2,1,0:T(8,128)(2,1)}, bf16[4,320,128]{2,1,0:T(8,128)(2,1)S(1)}, u32[]{:S(2)}, u32[]{:S(2)}) collective-permute-start(bf16[4,320,128]{2,1,0:T(8,128)(2,1)} %get-tuple-element.412), channel_id=1, source_target_pairs={{0,5},{1,4},{2,7},{3,6},{4,1},{5,0},{6,3},{7,2},{8,13},{9,12},{10,... | collective-permute-start | bytes 983048 | tf_op jit(solution)/shard_map/while/body/ppermute | solution.py:464
  126.2 54.1 %copy-start.10 = (bf16[4,320,128]{2,1,0:T(8,128)(2,1)}, bf16[4,320,128]{2,1,0:T(8,128)(2,1)S(1)}, u32[]{:S(2)}) copy-start(bf16[4,320,128]{2,1,0:T(8,128)(2,1)S(1)} %collective-permute-done.10.refs_1_) | copy-start | bytes 983044 | tf_op jit(solution)/shard_map/while
  126.2 18.0 %collective-permute-start.15 = (bf16[4,320,128]{2,1,0:T(8,128)(2,1)}, bf16[4,320,128]{2,1,0:T(8,128)(2,1)S(1)}, u32[]{:S(2)}, u32[]{:S(2)}) collective-permute-start(bf16[4,320,128]{2,1,0:T(8,128)(2,1)} %get-tuple-element.413), channel_id=1, source_target_pairs={{0,6},{1,7},{2,4},{3,5},{4,2},{5,3},{6,0},{7,1},{8,14},{9,15},{10,... | collective-permute-start | bytes 983048 | tf_op jit(solution)/shard_map/while/body/ppermute | solution.py:464
  128.4 23.5 %collective-permute-start.16 = (bf16[4,320,128]{2,1,0:T(8,128)(2,1)}, bf16[4,320,128]{2,1,0:T(8,128)(2,1)S(1)}, u32[]{:S(2)}, u32[]{:S(2)}) collective-permute-start(bf16[4,320,128]{2,1,0:T(8,128)(2,1)} %get-tuple-element.414), channel_id=1, source_target_pairs={{0,7},{1,6},{2,5},{3,4},{4,3},{5,2},{6,1},{7,0},{8,15},{9,14},{10,... | collective-permute-start | bytes 983048 | tf_op jit(solution)/shard_map/while/body/ppermute | solution.py:464
  131.2 22.8 %collective-permute-start.17 = (bf16[4,320,128]{2,1,0:T(8,128)(2,1)}, bf16[4,320,128]{2,1,0:T(8,128)(2,1)S(1)}, u32[]{:S(2)}, u32[]{:S(2)}) collective-permute-start(bf16[4,320,128]{2,1,0:T(8,128)(2,1)} %get-tuple-element.397), channel_id=1, source_target_pairs={{0,1},{1,0},{2,3},{3,2},{4,5},{5,4},{6,7},{7,6},{8,9},{9,8},{10,11... | collective-permute-start | bytes 983048 | tf_op jit(solution)/shard_map/while/body/ppermute | solution.py:464
  131.3 23.8 %collective-permute-start.18 = (bf16[4,320,128]{2,1,0:T(8,128)(2,1)}, bf16[4,320,128]{2,1,0:T(8,128)(2,1)S(1)}, u32[]{:S(2)}, u32[]{:S(2)}) collective-permute-start(bf16[4,320,128]{2,1,0:T(8,128)(2,1)} %get-tuple-element.398), channel_id=1, source_target_pairs={{0,2},{1,3},{2,0},{3,1},{4,6},{5,7},{6,4},{7,5},{8,10},{9,11},{10,... | collective-permute-start | bytes 983048 | tf_op jit(solution)/shard_map/while/body/ppermute | solution.py:464
  137.9 41.5 %copy-start.12 = (bf16[4,320,128]{2,1,0:T(8,128)(2,1)}, bf16[4,320,128]{2,1,0:T(8,128)(2,1)S(1)}, u32[]{:S(2)}) copy-start(bf16[4,320,128]{2,1,0:T(8,128)(2,1)S(1)} %collective-permute-done.14.refs_5_) | copy-start | bytes 983044 | tf_op jit(solution)/shard_map/while
  137.9 19.1 %collective-permute-start.19 = (bf16[4,320,128]{2,1,0:T(8,128)(2,1)}, bf16[4,320,128]{2,1,0:T(8,128)(2,1)S(1)}, u32[]{:S(2)}, u32[]{:S(2)}) collective-permute-start(bf16[4,320,128]{2,1,0:T(8,128)(2,1)} %get-tuple-element.399), channel_id=1, source_target_pairs={{0,3},{1,2},{2,1},{3,0},{4,7},{5,6},{6,5},{7,4},{8,11},{9,10},{10,... | collective-permute-start | bytes 983048 | tf_op jit(solution)/shard_map/while/body/ppermute | solution.py:464
  144.3 35.2 %copy-start.13 = (bf16[4,320,128]{2,1,0:T(8,128)(2,1)}, bf16[4,320,128]{2,1,0:T(8,128)(2,1)S(1)}, u32[]{:S(2)}) copy-start(bf16[4,320,128]{2,1,0:T(8,128)(2,1)S(1)} %collective-permute-done.15.refs_6_) | copy-start | bytes 983044 | tf_op jit(solution)/shard_map/while
  144.3 13.6 %collective-permute-start.20 = (bf16[4,320,128]{2,1,0:T(8,128)(2,1)}, bf16[4,320,128]{2,1,0:T(8,128)(2,1)S(1)}, u32[]{:S(2)}, u32[]{:S(2)}) collective-permute-start(bf16[4,320,128]{2,1,0:T(8,128)(2,1)} %get-tuple-element.400), channel_id=1, source_target_pairs={{0,4},{1,5},{2,6},{3,7},{4,0},{5,1},{6,2},{7,3},{8,12},{9,13},{10,... | collective-permute-start | bytes 983048 | tf_op jit(solution)/shard_map/while/body/ppermute | solution.py:464
  151.9 13.7 %collective-permute-start.21 = (bf16[4,320,128]{2,1,0:T(8,128)(2,1)}, bf16[4,320,128]{2,1,0:T(8,128)(2,1)S(1)}, u32[]{:S(2)}, u32[]{:S(2)}) collective-permute-start(bf16[4,320,128]{2,1,0:T(8,128)(2,1)} %get-tuple-element.401), channel_id=1, source_target_pairs={{0,5},{1,4},{2,7},{3,6},{4,1},{5,0},{6,3},{7,2},{8,13},{9,12},{10,... | collective-permute-start | bytes 983048 | tf_op jit(solution)/shard_map/while/body/ppermute | solution.py:464
  154.1 18.5 %collective-permute-start.22 = (bf16[4,320,128]{2,1,0:T(8,128)(2,1)}, bf16[4,320,128]{2,1,0:T(8,128)(2,1)S(1)}, u32[]{:S(2)}, u32[]{:S(2)}) collective-permute-start(bf16[4,320,128]{2,1,0:T(8,128)(2,1)} %get-tuple-element.402), channel_id=1, source_target_pairs={{0,6},{1,7},{2,4},{3,5},{4,2},{5,3},{6,0},{7,1},{8,14},{9,15},{10,... | collective-permute-start | bytes 983048 | tf_op jit(solution)/shard_map/while/body/ppermute | solution.py:464
  155.1 24.4 %collective-permute-start.23 = (bf16[4,320,128]{2,1,0:T(8,128)(2,1)S(1)}, bf16[4,320,128]{2,1,0:T(8,128)(2,1)S(1)}, u32[]{:S(2)}, u32[]{:S(2)}) collective-permute-start(bf16[4,320,128]{2,1,0:T(8,128)(2,1)S(1)} %copy-done.11), channel_id=1, source_target_pairs={{0,7},{1,6},{2,5},{3,4},{4,3},{5,2},{6,1},{7,0},{8,15},{9,14},{10,... | collective-permute-start | bytes 983048 | tf_op jit(solution)/shard_map/while/body/ppermute | solution.py:464
  193.4 22.2 %all-to-all-start.2 = ((bf16[8,8,72,128]{3,2,1,0:T(8,128)(2,1)}), bf16[8,8,72,128]{3,2,1,0:T(8,128)(2,1)}, u32[]{:S(2)}, u32[]{:S(2)}) async-start(bf16[8,8,72,128]{3,2,1,0:T(8,128)(2,1)} %dimers.8), calls=%async_computation.2 | async-start | bytes 2359296 | tf_op jit(solution)/shard_map/while/body/all_to_all | solution.py:469
  199.9 31.1 %copy-start.31 = (bf16[2,320,128]{2,1,0:T(8,128)(2,1)S(1)}, bf16[2,320,128]{2,1,0:T(8,128)(2,1)}, u32[]{:S(2)}) copy-start(bf16[2,320,128]{2,1,0:T(8,128)(2,1)} %get-tuple-element.390) | copy-start | bytes 491524 | tf_op jit(solution)/shard_map/while
  199.9 34.7 %collective-permute-start = (bf16[2,320,128]{2,1,0:T(8,128)(2,1)}, bf16[2,320,128]{2,1,0:T(8,128)(2,1)S(1)}, u32[]{:S(2)}, u32[]{:S(2)}) collective-permute-start(bf16[2,320,128]{2,1,0:T(8,128)(2,1)} %get-tuple-element.386), channel_id=1, source_target_pairs={{0,1},{1,0},{2,3},{3,2},{4,5},{5,4},{6,7},{7,6},{8,9},{9,8},{10,11... | collective-permute-start | bytes 491528 | tf_op jit(solution)/shard_map/while/body/ppermute | solution.py:464
  200.2 35.7 %collective-permute-start.1 = (bf16[2,320,128]{2,1,0:T(8,128)(2,1)}, bf16[2,320,128]{2,1,0:T(8,128)(2,1)S(1)}, u32[]{:S(2)}, u32[]{:S(2)}) collective-permute-start(bf16[2,320,128]{2,1,0:T(8,128)(2,1)} %get-tuple-element.387), channel_id=1, source_target_pairs={{0,2},{1,3},{2,0},{3,1},{4,6},{5,7},{6,4},{7,5},{8,10},{9,11},{10,... | collective-permute-start | bytes 491528 | tf_op jit(solution)/shard_map/while/body/ppermute | solution.py:464
  201.9 35.9 %collective-permute-start.2 = (bf16[2,320,128]{2,1,0:T(8,128)(2,1)}, bf16[2,320,128]{2,1,0:T(8,128)(2,1)S(1)}, u32[]{:S(2)}, u32[]{:S(2)}) collective-permute-start(bf16[2,320,128]{2,1,0:T(8,128)(2,1)} %get-tuple-element.388), channel_id=1, source_target_pairs={{0,3},{1,2},{2,1},{3,0},{4,7},{5,6},{6,5},{7,4},{8,11},{9,10},{10,... | collective-permute-start | bytes 491528 | tf_op jit(solution)/shard_map/while/body/ppermute | solution.py:464
  201.9 36.3 %collective-permute-start.3 = (bf16[2,320,128]{2,1,0:T(8,128)(2,1)}, bf16[2,320,128]{2,1,0:T(8,128)(2,1)S(1)}, u32[]{:S(2)}, u32[]{:S(2)}) collective-permute-start(bf16[2,320,128]{2,1,0:T(8,128)(2,1)} %get-tuple-element.389), channel_id=1, source_target_pairs={{0,4},{1,5},{2,6},{3,7},{4,0},{5,1},{6,2},{7,3},{8,12},{9,13},{10,... | collective-permute-start | bytes 491528 | tf_op jit(solution)/shard_map/while/body/ppermute | solution.py:464
  219.8 51.1 %all-to-all-start.3 = ((bf16[32,72,128]{2,1,0:T(8,128)(2,1)}), bf16[32,72,128]{2,1,0:T(8,128)(2,1)S(1)}, u32[]{:S(2)}, u32[]{:S(2)}) async-start(bf16[32,72,128]{2,1,0:T(8,128)(2,1)} %place.8), calls=%async_computation.3 | async-start | bytes 1179648 | tf_op jit(solution)/shard_map/while/body/all_to_all | solution.py:482
  231.0 7.4 %collective-permute-start.4 = (bf16[2,320,128]{2,1,0:T(8,128)(2,1)S(1)}, bf16[2,320,128]{2,1,0:T(8,128)(2,1)S(1)}, u32[]{:S(2)}, u32[]{:S(2)}) collective-permute-start(bf16[2,320,128]{2,1,0:T(8,128)(2,1)S(1)} %copy-done.31), channel_id=1, source_target_pairs={{0,5},{1,4},{2,7},{3,6},{4,1},{5,0},{6,3},{7,2},{8,13},{9,12},{10,... | collective-permute-start | bytes 491528 | tf_op jit(solution)/shard_map/while/body/ppermute | solution.py:464
  234.6 8.4 %collective-permute-start.5 = (bf16[2,320,128]{2,1,0:T(8,128)(2,1)S(1)}, bf16[2,320,128]{2,1,0:T(8,128)(2,1)S(1)}, u32[]{:S(2)}, u32[]{:S(2)}) collective-permute-start(bf16[2,320,128]{2,1,0:T(8,128)(2,1)S(1)} %copy-done.29), channel_id=1, source_target_pairs={{0,6},{1,7},{2,4},{3,5},{4,2},{5,3},{6,0},{7,1},{8,14},{9,15},{10,... | collective-permute-start | bytes 491528 | tf_op jit(solution)/shard_map/while/body/ppermute | solution.py:464
  235.9 9.4 %collective-permute-start.6 = (bf16[2,320,128]{2,1,0:T(8,128)(2,1)S(1)}, bf16[2,320,128]{2,1,0:T(8,128)(2,1)S(1)}, u32[]{:S(2)}, u32[]{:S(2)}) collective-permute-start(bf16[2,320,128]{2,1,0:T(8,128)(2,1)S(1)} %copy-done.27), channel_id=1, source_target_pairs={{0,7},{1,6},{2,5},{3,4},{4,3},{5,2},{6,1},{7,0},{8,15},{9,14},{10,... | collective-permute-start | bytes 491528 | tf_op jit(solution)/shard_map/while/body/ppermute | solution.py:464
  237.8 7.6 %collective-permute-start.24 = (bf16[2,320,128]{2,1,0:T(8,128)(2,1)}, bf16[2,320,128]{2,1,0:T(8,128)(2,1)S(1)}, u32[]{:S(2)}, u32[]{:S(2)}) collective-permute-start(bf16[2,320,128]{2,1,0:T(8,128)(2,1)} %get-tuple-element.418), channel_id=1, source_target_pairs={{0,1},{1,0},{2,3},{3,2},{4,5},{5,4},{6,7},{7,6},{8,9},{9,8},{10,11... | collective-permute-start | bytes 491528 | tf_op jit(solution)/shard_map/while/body/ppermute | solution.py:464
  238.1 10.2 %collective-permute-start.25 = (bf16[2,320,128]{2,1,0:T(8,128)(2,1)}, bf16[2,320,128]{2,1,0:T(8,128)(2,1)S(1)}, u32[]{:S(2)}, u32[]{:S(2)}) collective-permute-start(bf16[2,320,128]{2,1,0:T(8,128)(2,1)} %get-tuple-element.419), channel_id=1, source_target_pairs={{0,2},{1,3},{2,0},{3,1},{4,6},{5,7},{6,4},{7,5},{8,10},{9,11},{10,... | collective-permute-start | bytes 491528 | tf_op jit(solution)/shard_map/while/body/ppermute | solution.py:464
  238.4 11.1 %collective-permute-start.26 = (bf16[2,320,128]{2,1,0:T(8,128)(2,1)}, bf16[2,320,128]{2,1,0:T(8,128)(2,1)S(1)}, u32[]{:S(2)}, u32[]{:S(2)}) collective-permute-start(bf16[2,320,128]{2,1,0:T(8,128)(2,1)} %get-tuple-element.420), channel_id=1, source_target_pairs={{0,3},{1,2},{2,1},{3,0},{4,7},{5,6},{6,5},{7,4},{8,11},{9,10},{10,... | collective-permute-start | bytes 491528 | tf_op jit(solution)/shard_map/while/body/ppermute | solution.py:464
  243.0 11.7 %collective-permute-start.27 = (bf16[2,320,128]{2,1,0:T(8,128)(2,1)}, bf16[2,320,128]{2,1,0:T(8,128)(2,1)S(1)}, u32[]{:S(2)}, u32[]{:S(2)}) collective-permute-start(bf16[2,320,128]{2,1,0:T(8,128)(2,1)} %get-tuple-element.421), channel_id=1, source_target_pairs={{0,4},{1,5},{2,6},{3,7},{4,0},{5,1},{6,2},{7,3},{8,12},{9,13},{10,... | collective-permute-start | bytes 491528 | tf_op jit(solution)/shard_map/while/body/ppermute | solution.py:464
  245.3 11.7 %collective-permute-start.28 = (bf16[2,320,128]{2,1,0:T(8,128)(2,1)}, bf16[2,320,128]{2,1,0:T(8,128)(2,1)S(1)}, u32[]{:S(2)}, u32[]{:S(2)}) collective-permute-start(bf16[2,320,128]{2,1,0:T(8,128)(2,1)} %get-tuple-element.422), channel_id=1, source_target_pairs={{0,5},{1,4},{2,7},{3,6},{4,1},{5,0},{6,3},{7,2},{8,13},{9,12},{10,... | collective-permute-start | bytes 491528 | tf_op jit(solution)/shard_map/while/body/ppermute | solution.py:464
  245.4 15.0 %collective-permute-start.29 = (bf16[2,320,128]{2,1,0:T(8,128)(2,1)}, bf16[2,320,128]{2,1,0:T(8,128)(2,1)S(1)}, u32[]{:S(2)}, u32[]{:S(2)}) collective-permute-start(bf16[2,320,128]{2,1,0:T(8,128)(2,1)} %get-tuple-element.423), channel_id=1, source_target_pairs={{0,6},{1,7},{2,4},{3,5},{4,2},{5,3},{6,0},{7,1},{8,14},{9,15},{10,... | collective-permute-start | bytes 491528 | tf_op jit(solution)/shard_map/while/body/ppermute | solution.py:464
  248.3 15.9 %collective-permute-start.30 = (bf16[2,320,128]{2,1,0:T(8,128)(2,1)}, bf16[2,320,128]{2,1,0:T(8,128)(2,1)S(1)}, u32[]{:S(2)}, u32[]{:S(2)}) collective-permute-start(bf16[2,320,128]{2,1,0:T(8,128)(2,1)} %get-tuple-element.424), channel_id=1, source_target_pairs={{0,7},{1,6},{2,5},{3,4},{4,3},{5,2},{6,1},{7,0},{8,15},{9,14},{10,... | collective-permute-start | bytes 491528 | tf_op jit(solution)/shard_map/while/body/ppermute | solution.py:464
  270.8 33.4 %copy-start.9 = (s32[1024]{0:T(1024)S(1)}, s32[1024]{0:T(1024)}, u32[]{:S(2)}) copy-start(s32[1024]{0:T(1024)} %get-tuple-element.378) | copy-start | bytes 12292 | tf_op jit(solution)/shard_map/while
  270.8 36.1 %copy-start.2 = (f32[32,32,256]{2,1,0:T(8,128)S(1)}, f32[32,32,256]{2,1,0:T(8,128)}, u32[]{:S(2)}) copy-start(f32[32,32,256]{2,1,0:T(8,128)} %get-tuple-element.534.refs_6_) | copy-start | bytes 3145732 | tf_op jit(solution)/shard_map/while
  270.8 36.0 %copy-start.5 = (bf16[32,72,128]{2,1,0:T(8,128)(2,1)}, bf16[32,72,128]{2,1,0:T(8,128)(2,1)S(1)}, u32[]{:S(2)}) copy-start(bf16[32,72,128]{2,1,0:T(8,128)(2,1)S(1)} %all-to-all-done.3.refs_5_) | copy-start | bytes 1769476 | tf_op jit(solution)/shard_map/while
  288.9 34.2 %all-to-all-start.5 = ((bf16[32,72,128]{2,1,0:T(8,128)(2,1)}), bf16[32,72,128]{2,1,0:T(8,128)(2,1)S(1)}, u32[]{:S(2)}, u32[]{:S(2)}) async-start(bf16[32,72,128]{2,1,0:T(8,128)(2,1)} %place.9), calls=%async_computation.5 | async-start | bytes 1179648 | tf_op jit(solution)/shard_map/while/body/all_to_all | solution.py:482
  (28 other events, 451.5 us)

commit v9 on v8

--- a/solution.py
+++ b/solution.py
@@ -196,10 +196,11 @@
             lanes = slice(n * 128, n * 128 + 128)
             for r in range(2):
                 change = dens[pl.ds(r * 256 + at, 32), :]
-                out[to, r, 0:32, :] = change[:, 0:128]
-                out[to, r, 32:64, :] = change[:, 128:256]
+                target = out[0].at[to, r] if len(out) == 1 else out[n].at[r]
+                target[0:32, :] = change[:, 0:128]
+                target[32:64, :] = change[:, 128:256]
                 partner = jnp.broadcast_to(fits[1 - r][:, lanes], (8, 128))
-                out[to, r, 64:72, :] = partner.astype(BF16)
+                target[64:72, :] = partner.astype(BF16)
 
 
 SCRATCH = [
@@ -210,18 +211,23 @@
 ]
 
 
-def run_dimers(kernel, count, tables, blocks, maps, parts):
+def run_dimers(kernel, count, tables, blocks, maps, parts, apart=False):
+    rows = 2 * count
+    shapes = [(rows, 72, 128)] * 8 if apart else [(8, rows, 72, 128)]
+    out_block = pl.BlockSpec((2, 72, 128), lambda i, *_: (i, 0, 0))
+    if not apart:
+        out_block = pl.BlockSpec((8, 2, 72, 128), lambda i, *_: (0, i, 0, 0))
     specs = []
     for block, index_map in zip(blocks, maps, strict=True):
         specs += [pl.BlockSpec((block, 320, 128), index_map)] * 8
     return pl.pallas_call(
         kernel,
-        out_shape=jax.ShapeDtypeStruct((8, 2 * count, 72, 128), BF16),
+        out_shape=[jax.ShapeDtypeStruct(shape, BF16) for shape in shapes],
         grid_spec=pltpu.PrefetchScalarGridSpec(
             num_scalar_prefetch=2,
             grid=(count,),
             in_specs=specs,
-            out_specs=pl.BlockSpec((8, 2, 72, 128), lambda i, *_: (0, i, 0, 0)),
+            out_specs=[out_block] * len(shapes),
             scratch_shapes=SCRATCH,
         ),
         name="dimers",
@@ -233,7 +239,7 @@
 
 def kernel_1(table_ref, me_ref, *refs):
     me, i = me_ref[0], pl.program_id(0)
-    first, second, out, scratch = refs[0:8], refs[8:16], refs[16], refs[17:]
+    first, second, out, scratch = refs[0:8], refs[8:16], refs[16:17], refs[17:]
     stacked, dens = scratch[0], scratch[2]
 
     def load():
@@ -246,7 +252,7 @@
 
 def kernel_2(table_ref, me_ref, *refs):
     me, i = me_ref[0], pl.program_id(0)
-    home, late, out, scratch = refs[0:8], refs[8:16], refs[16], refs[17:]
+    home, late, out, scratch = refs[0:8], refs[8:16], refs[16:24], refs[24:]
     stacked, dens = scratch[0], scratch[2]
     split = table_ref[MODE + me] > 0
 
@@ -549,8 +555,7 @@
         earlier = (pair_id[:, None] == pair_id[None, :]) & (order[None, :] < order[:, None])
         earlier = jnp.sum(jnp.where(earlier & open_dimer[None, :], 1, 0), axis=1)
         flagged = open_dimer & ((earlier >= 2) | inside)
-        turn = order + jnp.where(inside, 2 * dimers, dimers * (2 - jnp.clip(earlier - 2, 0, 2)))
-        ahead = jnp.sum(jnp.where((turn[None, :] < turn[:, None]) & flagged[None, :], 1, 0), axis=1)
+        ahead = jnp.sum(jnp.where((order[None, :] < order[:, None]) & flagged[None, :], 1, 0), axis=1)
         ahead = jnp.where(flagged, ahead, -1)
         words = jnp.sum(jnp.where(ahead[None, :] == order[:, None], word[None, :], 0), axis=1)
         count = jnp.sum(jnp.where(flagged, 1, 0)).reshape(1)
@@ -581,37 +586,43 @@
         in_z = along_z(out_2)
 
         one = lambda i, *_: (i, 0, 0)
-        ready_1 = run_dimers(kernel_1, 4, (table_1, me_b), (1, 1), (one, one), [*home_1, *away_1])
+        (ready_1,) = run_dimers(kernel_1, 4, (table_1, me_b), (1, 1), (one, one), [*home_1, *away_1])
         done_1 = give_back(after(ready_1, in_z))
+
+        def late_at(t, me, n, row):
+            return t[1][LATE + 2 * lax.bitwise_xor(me, n) + row] - 32
+
+        late_parts = pack(tables, me_b, late_at, 8, 2, (), [*in_x, after(in_z, away_1)])
+        late_2 = exchange(late_parts)
+        whole = lambda i, *_: (0, 0, 0)
+        ready_2 = run_dimers(kernel_2, 2, (table_2, me_b), (2, 2), (whole, whole), [*home_2, *late_2], True)
 
         def place_1(t, row):
             return t[0][RANKED + ranked_at(row // 8, row % 8 // 2)]
 
-        def place_2(t, row):
-            at = row // 2
-            return jnp.where(t[1][STEPS + at] > 0, t[1][POS + row], -1)
+        def place_2(k):
+            def find(t, me, row):
+                at = 2 * lax.bitwise_xor(me, k) + row // 2
+                return jnp.where(t[1][STEPS + at] > 0, t[1][POS + 2 * at + row % 2], -1)
+
+            return find
+
+        def owner_2(k):
+            return lambda t, me, row: place_2(k)(t, me, row) - 32
 
         (ret_1,) = place(
             tables, me_b, [done_1], [lambda t, me, row: jnp.where(row % 2 == 1, place_1(t, row), -1)], [32]
         )
         back_1 = across(ret_1)
-
-        def late_at(t, me, n, row):
-            return t[1][LATE + 2 * lax.bitwise_xor(me, n) + row] - 32
-
-        late_parts = pack(tables, me_b, late_at, 8, 2, (), [*in_x, after(in_z, ret_1)])
-        late_2 = exchange(late_parts)
-        whole = lambda i, *_: (0, 0, 0)
-        ready_2 = run_dimers(kernel_2, 2, (table_2, me_b), (2, 2), (whole, whole), [*home_2, *late_2])
-        done_2 = give_back(after(ready_2, back_1))
-        (ret_2,) = place(tables, me_b, [done_2], [lambda t, me, row: place_2(t, row) - 32], [32])
-        back_2 = across(ret_2)
+        done_2 = exchange(ready_2)
+        (ret_2,) = place(tables, me_b, done_2, [owner_2(k) for k in range(8)], [32])
+        back_2 = across(after(ret_2, back_1))
         finds = [
             lambda t, me, row: jnp.where(row % 2 == 0, t[0][BASE + place_1(t, row)], -1),
-            lambda t, me, row: place_2(t, row),
+            *[place_2(k) for k in range(8)],
             lambda t, me, row: t[0][OUT + row],
         ]
-        dens, emb = add_up(tables, me_b, [done_1, done_2, back_1], finds, dens, emb)
+        dens, emb = add_up(tables, me_b, [done_1, *done_2, back_1], finds, dens, emb)
         dens, emb = add_up(tables, me_b, [back_2], [lambda t, me, row: t[1][BACK + row]], dens, emb)
         return jnp.sum(left), left, dens, emb
 

time: 329 us -> 328 us (level)
  blocking collectives: 25 us -> 9.55 us
  starting transfers between devices: 88.1 us -> 98.5 us
    all_to_all x1 -> x0, blocking collectives: 15.4 us -> none  [give_back(): lax.all_to_all(done, 'basis', split_axis=0, concat_axis=0, tiled=True)]
    ppermute x28 -> x35, waiting for transfers between devices: 62.1 us -> 74.7 us  [exchange(): got.append(lax.ppermute(parts[k], 'basis', [(i, i ^ k) for i in range(8)]))]
    ppermute x28 -> x35, starting transfers between devices: 27.9 us -> 40.1 us  [exchange(): got.append(lax.ppermute(parts[k], 'basis', [(i, i ^ k) for i in range(8)]))]
    all_to_all x1, waiting for transfers between devices: 10.4 us -> 0.01 us  [give_back(): lax.all_to_all(done, 'basis', split_axis=0, concat_axis=0, tiled=True)]
  transfers between devices with their start and end apart: 37 -> 44, of which waited for: 18 -> 21; matrix products, arithmetic and copies ran while one was open for 2% -> 2% of each run, Pallas kernels for 22% -> 24%
where the time goes in v9:
time: 328 us; the launch traced here: 327 us
  waiting for transfers between devices  117 us (36%)
  starting transfers between devices  98.5 us (30%)
  Pallas kernels  83 us (25%)
  other arithmetic  9.59 us (3%)
  blocking collectives  9.55 us (3%)
  local copies, waits for them, and re-layouts  6.96 us (2%)
    ppermute x35, waiting for transfers between devices, exchange(): got.append(lax.ppermute(parts[k], 'basis', [(i, i ^ k) for i in range(8)]))  74.7 us
    all_to_all x4, starting transfers between devices, across(): return lax.all_to_all(part, 'frag', split_axis=0, concat_axis=0, tiled=True)  41.3 us
    ppermute x35, starting transfers between devices, exchange(): got.append(lax.ppermute(parts[k], 'basis', [(i, i ^ k) for i in range(8)]))  40.1 us
    pallas_call x1, Pallas kernels, plan_rest(): pl.pallas_call(plan_kernel, out_shape=[jax.ShapeDtypeStruct((TABLE,), s32...  28 us
    ppermute x3, waiting for transfers between devices, along_x(): lax.ppermute(parts[k - 1], 'frag', [(i, i ^ 8 * k) for i in range(32)])  22.8 us
    pallas_call x7, Pallas kernels, pack(): pl.pallas_call(kernel, out_shape=[jax.ShapeDtypeStruct((rows, 320, 128),...  21.9 us
    all_to_all x4, waiting for transfers between devices, across(): return lax.all_to_all(part, 'frag', split_axis=0, concat_axis=0, tiled=True)  19.7 us
    pallas_call x2, Pallas kernels, run_dimers(): pl.pallas_call(kernel, out_shape=[jax.ShapeDtypeStruct(shape, BF16) for s...  19.1 us
  transfers between devices with their start and end apart: 44, of which 21 were waited for; matrix products, arithmetic and copies ran while one was open for 2% of the time, Pallas kernels for 24%

profile of v9, /device:TPU:32, one launch (start us, length us, event | category | flops | bytes accessed | tf_op | source)
XLA Modules:
  0.0 326.7 jit_solution(9293111879956400447)
XLA Ops:
  2.3 9.6 %all_to_all.40 = s32[8,1,128]{2,1,0:T(1,128)S(1)} all-to-all(s32[8,1,128]{2,1,0:T(1,128)S(1)} %broadcast_in_dim.142), channel_id=1, replica_groups=mesh['frag'=32,'basis'=8] {'basis'}, dimensions={0} | all-to-all | bytes 8192 | tf_op jit(solution)/shard_map/all_to_all | solution.py:505
  12.8 11.2 %all-to-all-start.6 = ((s32[32,1,128]{2,1,0:T(1,128)}), s32[32,1,128]{2,1,0:T(1,128)S(1)}, u32[]{:S(2)}, u32[]{:S(2)}) async-start(s32[32,1,128]{2,1,0:T(1,128)} %broadcast_in_dim.143), calls=%async_computation.6 | async-start | bytes 32768 | tf_op jit(solution)/shard_map/all_to_all | solution.py:488
  24.0 8.6 %all-to-all-done.6 = s32[32,1,128]{2,1,0:T(1,128)S(1)} async-done(((s32[32,1,128]{2,1,0:T(1,128)}), s32[32,1,128]{2,1,0:T(1,128)S(1)}, u32[]{:S(2)}, u32[]{:S(2)}) %all-to-all-start.6) | async-done | bytes 16416 | tf_op jit(solution)/shard_map/all_to_all | solution.py:488
  34.1 292.0 %while.15 = (s32[]{:T(128)}, s32[1024]{0:T(1024)S(1)}, f32[32,32,256]{2,1,0:T(8,128)}, f32[32,128]{1,0:T(8,128)S(1)}, s32[1024]{0:T(1024)S(1)}, /*index=5*/pred[...) while((s32[]{:T(128)}, s32[1024]{0:T(1024)S(1)}, ...), condition=%region_13.14_spmd.clone.clone, body=%region_1.13_spmd.clone.clone | while | flops 24018298880 | bytes 150593808 | solution.py:635
  35.0 3.8 %pack.9 = bf16[32,320,128]{2,1,0:T(8,128)(2,1)} custom-call(s32[32]{0:T(128)} %get-tuple-element.401.refs_0_, s32[1]{0:T(128)} %get-tuple-element.466.refs_2_.refs_1_.me_ref, bf16[32,256,128]{2,1,0:T(8,128)(2,1)} %get-tuple-element.467.refs_3_.refs_2_, bf16[32,32,256]{2,1,0:T(8,128)(2,1)} %get-tuple-element.468.refs_4_.refs_3_), custom_call_target="tpu_custom_call" | custom-call | tf_op jit(solution)/shard_map/while/body/pack/pallas_call | solution.py:68
  38.8 6.1 %all-to-all-start = ((bf16[32,320,128]{2,1,0:T(8,128)(2,1)}), bf16[32,320,128]{2,1,0:T(8,128)(2,1)}, u32[]{:S(2)}, u32[]{:S(2)}) async-start(bf16[32,320,128]{2,1,0:T(8,128)(2,1)} %pack.9), calls=%async_computation | async-start | bytes 5242880 | tf_op jit(solution)/shard_map/while/body/all_to_all | solution.py:488
  48.3 28.0 %plan.1 = (s32[256]{0:T(256)}, s32[1024]{0:T(1024)}) custom-call(s32[1]{0:T(128)} %get-tuple-element.463.me_ref, s32[32]{0:T(128)} %select_reduce_fusion.6.inside_ref, s32[1]{0:T(128)} %bitcast.5.count_ref, s32[1024]{0:T(1024)} %select_reduce_fusion.2.list_ref), custom_call_target="tpu_custom_call" | custom-call | flops 1000 | bytes 30000000 | tf_op jit(solution)/shard_map/while/body/plan/pallas_call | solution.py:456
  77.2 2.2 pack.8
  80.9 2.8 collective-permute-start.8
  84.1 3.1 pack.13
  87.8 9.5 %collective-permute-done.7.refs_5_.refs_3_ = bf16[6,320,128]{2,1,0:T(8,128)(2,1)S(1)} collective-permute-done((bf16[6,320,128]{2,1,0:T(8,128)(2,1)}, bf16[6,320,128]{2,1,0:T(8,128)(2,1)S(1)}, u32[]{:S(2)}, u32[]{:S(2)}) %collective-permute-start.7) | collective-permute-done | bytes 491552 | tf_op jit(solution)/shard_map/while/body/ppermute | solution.py:479
  97.3 13.3 %collective-permute-done.8.refs_6_.refs_4_ = bf16[6,320,128]{2,1,0:T(8,128)(2,1)} collective-permute-done((bf16[6,320,128]{2,1,0:T(8,128)(2,1)}, bf16[6,320,128]{2,1,0:T(8,128)(2,1)}, u32[]{:S(2)}, u32[]{:S(2)}) %collective-permute-start.8) | collective-permute-done | bytes 491552 | tf_op jit(solution)/shard_map/while/body/ppermute | solution.py:479
  111.7 4.0 %pack.10 = (bf16[4,320,128]{2,1,0:T(8,128)(2,1)}, bf16[4,320,128]{2,1,0:T(8,128)(2,1)}, bf16[4,320,128]{2,1,0:T(8,128)(2,1)}, bf16[4,320,128]{2,1,0:T(8,128)(2,1...) custom-call(s32[128]{0:T(128)} %pad_add_fusion.refs_0_.table_ref, ...), custom_call_target="tpu_custom_call" | custom-call | tf_op jit(solution)/shard_map/while/body/pack/pallas_call | solution.py:68
  115.8 3.0 pack.11
  118.8 8.2 %all-to-all-start.1 = ((bf16[16,320,128]{2,1,0:T(8,128)(2,1)}), bf16[16,320,128]{2,1,0:T(8,128)(2,1)}, u32[]{:S(2)}, u32[]{:S(2)}) async-start(bf16[16,320,128]{2,1,0:T(8,128)(2,1)} %pack.11), calls=%async_computation.1 | async-start | bytes 2621440 | tf_op jit(solution)/shard_map/while/body/all_to_all | solution.py:484
  127.0 2.2 collective-permute-start.36
  129.1 2.9 collective-permute-start.37
  132.1 6.6 %collective-permute-done.35.refs_5_ = bf16[4,320,128]{2,1,0:T(8,128)(2,1)S(1)} collective-permute-done((bf16[4,320,128]{2,1,0:T(8,128)(2,1)}, bf16[4,320,128]{2,1,0:T(8,128)(2,1)S(1)}, u32[]{:S(2)}, u32[]{:S(2)}) %collective-permute-start.35) | collective-permute-done | bytes 327712 | tf_op jit(solution)/shard_map/while/body/ppermute | solution.py:470
  138.7 6.3 %collective-permute-done.36.refs_6_ = bf16[4,320,128]{2,1,0:T(8,128)(2,1)S(1)} collective-permute-done((bf16[4,320,128]{2,1,0:T(8,128)(2,1)}, bf16[4,320,128]{2,1,0:T(8,128)(2,1)S(1)}, u32[]{:S(2)}, u32[]{:S(2)}) %collective-permute-start.36) | collective-permute-done | bytes 327712 | tf_op jit(solution)/shard_map/while/body/ppermute | solution.py:470
  146.3 6.4 %collective-permute-done.37.refs_7_ = bf16[4,320,128]{2,1,0:T(8,128)(2,1)S(1)} collective-permute-done((bf16[4,320,128]{2,1,0:T(8,128)(2,1)}, bf16[4,320,128]{2,1,0:T(8,128)(2,1)S(1)}, u32[]{:S(2)}, u32[]{:S(2)}) %collective-permute-start.37) | collective-permute-done | bytes 327712 | tf_op jit(solution)/shard_map/while/body/ppermute | solution.py:470
  152.7 2.2 collective-permute-start.14
  158.6 7.7 %collective-permute-done.14.refs_13_ = bf16[4,320,128]{2,1,0:T(8,128)(2,1)S(1)} collective-permute-done((bf16[4,320,128]{2,1,0:T(8,128)(2,1)}, bf16[4,320,128]{2,1,0:T(8,128)(2,1)S(1)}, u32[]{:S(2)}, u32[]{:S(2)}) %collective-permute-start.14) | collective-permute-done | bytes 327712 | tf_op jit(solution)/shard_map/while/body/ppermute | solution.py:470
  166.3 7.0 %collective-permute-done.15.refs_14_ = bf16[4,320,128]{2,1,0:T(8,128)(2,1)S(1)} collective-permute-done((bf16[4,320,128]{2,1,0:T(8,128)(2,1)}, bf16[4,320,128]{2,1,0:T(8,128)(2,1)S(1)}, u32[]{:S(2)}, u32[]{:S(2)}) %collective-permute-start.15) | collective-permute-done | bytes 327712 | tf_op jit(solution)/shard_map/while/body/ppermute | solution.py:470
  173.3 6.9 %collective-permute-done.16.refs_15_ = bf16[4,320,128]{2,1,0:T(8,128)(2,1)S(1)} collective-permute-done((bf16[4,320,128]{2,1,0:T(8,128)(2,1)S(1)}, bf16[4,320,128]{2,1,0:T(8,128)(2,1)S(1)}, u32[]{:S(2)}, u32[]{:S(2)}) %collective-permute-start.16) | collective-permute-done | bytes 327712 | tf_op jit(solution)/shard_map/while/body/ppermute | solution.py:470
  181.0 13.1 %dimers.3 = bf16[8,8,72,128]{3,2,1,0:T(8,128)(2,1)} custom-call(s32[128]{0:T(128)} %pad_add_fusion.refs_0_.table_ref, s32[1]{0:T(128)} %get-tuple-element.466.refs_2_.refs_1_.me_ref, bf16[4,320,128]{2,1,0:T(8,128)(2,1)} %get-tuple-element.325.refs_0_, bf16[4,320,128]{2,1,0:T(8,128)(2,1)} %copy-done.17, bf16[4,320,128]{2,1,0:T(8,128)(2,1)} %collective-permute-done.32.refs_2_, ...), custom_call_target="tpu_custom_call" | custom-call | flops 16000000000 | bytes 6000000 | tf_op jit(solution)/shard_map/while/body/dimers/pallas_call | solution.py:223
  194.1 4.3 %all-to-all-start.2 = ((bf16[8,8,72,128]{3,2,1,0:T(8,128)(2,1)}), bf16[8,8,72,128]{3,2,1,0:T(8,128)(2,1)}, u32[]{:S(2)}, u32[]{:S(2)}) async-start(bf16[8,8,72,128]{3,2,1,0:T(8,128)(2,1)} %dimers.3), calls=%async_computation.2 | async-start | bytes 2359296 | tf_op jit(solution)/shard_map/while/body/all_to_all | solution.py:475
  198.4 2.2 pack.7
  202.7 3.3 collective-permute-start.3
  206.0 3.5 %pack.12 = (bf16[2,320,128]{2,1,0:T(8,128)(2,1)}, bf16[2,320,128]{2,1,0:T(8,128)(2,1)}, bf16[2,320,128]{2,1,0:T(8,128)(2,1)}, bf16[2,320,128]{2,1,0:T(8,128)(2,1...) custom-call(s32[128]{0:T(128)} %pad_add_fusion.refs_0_.table_ref, ...), custom_call_target="tpu_custom_call" | custom-call | tf_op jit(solution)/shard_map/while/body/pack/pallas_call | solution.py:68
  209.6 3.0 collective-permute-start.5
  212.6 5.6 %collective-permute-done.1.refs_2_ = bf16[2,320,128]{2,1,0:T(8,128)(2,1)S(1)} collective-permute-done((bf16[2,320,128]{2,1,0:T(8,128)(2,1)}, bf16[2,320,128]{2,1,0:T(8,128)(2,1)S(1)}, u32[]{:S(2)}, u32[]{:S(2)}) %collective-permute-start.1) | collective-permute-done | bytes 163872 | tf_op jit(solution)/shard_map/while/body/ppermute | solution.py:470
  221.5 5.3 %collective-permute-done.3.refs_4_ = bf16[2,320,128]{2,1,0:T(8,128)(2,1)S(1)} collective-permute-done((bf16[2,320,128]{2,1,0:T(8,128)(2,1)}, bf16[2,320,128]{2,1,0:T(8,128)(2,1)S(1)}, u32[]{:S(2)}, u32[]{:S(2)}) %collective-permute-start.3) | collective-permute-done | bytes 163872 | tf_op jit(solution)/shard_map/while/body/ppermute | solution.py:470
  227.4 4.2 %place.3 = bf16[32,72,128]{2,1,0:T(8,128)(2,1)} custom-call(s32[128]{0:T(128)} %pad_add_fusion.refs_0_.table_ref, s32[256]{0:T(256)} %get-tuple-element.282.refs_1_.table_ref, s32[1]{0:T(128)} %get-tuple-element.466.refs_2_.refs_1_.me_ref, bf16[64,72,128]{2,1,0:T(8,128)(2,1)} %bitcast.6.refs_3_), custom_call_target="tpu_custom_call" | custom-call | tf_op jit(solution)/shard_map/while/body/place/pallas_call | solution.py:95
  231.6 10.5 %all-to-all-start.3 = ((bf16[32,72,128]{2,1,0:T(8,128)(2,1)}), bf16[32,72,128]{2,1,0:T(8,128)(2,1)S(1)}, u32[]{:S(2)}, u32[]{:S(2)}) async-start(bf16[32,72,128]{2,1,0:T(8,128)(2,1)} %place.3), calls=%async_computation.3 | async-start | bytes 1179648 | tf_op jit(solution)/shard_map/while/body/all_to_all | solution.py:488
  244.3 2.4 collective-permute-start.21
  248.8 4.1 %collective-permute-done.20.refs_12_ = bf16[2,320,128]{2,1,0:T(8,128)(2,1)S(1)} collective-permute-done((bf16[2,320,128]{2,1,0:T(8,128)(2,1)S(1)}, bf16[2,320,128]{2,1,0:T(8,128)(2,1)S(1)}, u32[]{:S(2)}, u32[]{:S(2)}) %collective-permute-start.20) | collective-permute-done | bytes 163872 | tf_op jit(solution)/shard_map/while/body/ppermute | solution.py:470
  252.9 2.5 collective-permute-done.21.refs_13_
  255.3 4.0 %collective-permute-done.22.refs_14_ = bf16[2,320,128]{2,1,0:T(8,128)(2,1)S(1)} collective-permute-done((bf16[2,320,128]{2,1,0:T(8,128)(2,1)S(1)}, bf16[2,320,128]{2,1,0:T(8,128)(2,1)S(1)}, u32[]{:S(2)}, u32[]{:S(2)}) %collective-permute-start.22) | collective-permute-done | bytes 163872 | tf_op jit(solution)/shard_map/while/body/ppermute | solution.py:470
  259.4 3.3 %collective-permute-done.23.refs_15_ = bf16[2,320,128]{2,1,0:T(8,128)(2,1)S(1)} collective-permute-done((bf16[2,320,128]{2,1,0:T(8,128)(2,1)S(1)}, bf16[2,320,128]{2,1,0:T(8,128)(2,1)S(1)}, u32[]{:S(2)}, u32[]{:S(2)}) %collective-permute-start.23) | collective-permute-done | bytes 163872 | tf_op jit(solution)/shard_map/while/body/ppermute | solution.py:470
  263.5 6.0 %dimers.2 = (bf16[4,72,128]{2,1,0:T(8,128)(2,1)}, bf16[4,72,128]{2,1,0:T(8,128)(2,1)}, bf16[4,72,128]{2,1,0:T(8,128)(2,1)}, bf16[4,72,128]{2,1,0:T(8,128)(2,1)},...) custom-call(s32[256]{0:T(256)} %get-tuple-element.282.refs_1_.table_, ...), custom_call_target="tpu_custom_call" | custom-call | flops 8000000000 | bytes 3000000 | tf_op jit(solution)/shard_map/while/body/dimers/pallas_call | solution.py:223
  271.5 4.2 %collective-permute-start.27 = (bf16[4,72,128]{2,1,0:T(8,128)(2,1)}, bf16[4,72,128]{2,1,0:T(8,128)(2,1)S(1)}, u32[]{:S(2)}, u32[]{:S(2)}) collective-permute-start(bf16[4,72,128]{2,1,0:T(8,128)(2,1)} %get-tuple-element.321), channel_id=1, source_target_pairs={{0,4},{1,5},{2,6},{3,7},{4,0},{5,1},{6,2},{7,3},{8,12},{9,13},{10,... | collective-permute-start | bytes 221192 | tf_op jit(solution)/shard_map/while/body/ppermute | solution.py:470
  275.6 3.5 %collective-permute-start.29 = (bf16[4,72,128]{2,1,0:T(8,128)(2,1)}, bf16[4,72,128]{2,1,0:T(8,128)(2,1)S(1)}, u32[]{:S(2)}, u32[]{:S(2)}) collective-permute-start(bf16[4,72,128]{2,1,0:T(8,128)(2,1)} %get-tuple-element.323), channel_id=1, source_target_pairs={{0,6},{1,7},{2,4},{3,5},{4,2},{5,3},{6,0},{7,1},{8,14},{9,15},{10,... | collective-permute-start | bytes 221192 | tf_op jit(solution)/shard_map/while/body/ppermute | solution.py:470
  279.2 2.9 collective-permute-done.27.refs_7_.refs_8_
  282.1 2.4 collective-permute-done.29.refs_9_.refs_10_
  286.3 2.7 place.2
  289.1 13.5 %all-to-all-start.4 = ((bf16[32,72,128]{2,1,0:T(8,128)(2,1)}), bf16[32,72,128]{2,1,0:T(8,128)(2,1)S(1)}, u32[]{:S(2)}, u32[]{:S(2)}) async-start(bf16[32,72,128]{2,1,0:T(8,128)(2,1)} %place.2), calls=%async_computation.4 | async-start | bytes 1179648 | tf_op jit(solution)/shard_map/while/body/all_to_all | solution.py:488
  305.4 5.4 %add_up.2 = (f32[32,32,256]{2,1,0:T(8,128)S(1)}, f32[32,128]{1,0:T(8,128)S(1)}) custom-call(s32[128]{0:T(128)} %pad_add_fusion.refs_0_.table_ref, s32[256]{0:T(256)} %get-tuple-element.282.refs_1_.table_ref, s32[1]{0:T(128)} %get-tuple-element.466.refs_2_.refs_1_.me_ref, ...), custom_call_target="tpu_custom_call", output_to_operand_aliasing={{0}: (13, {}), {1}: (14, {})} | custom-call | tf_op jit(solution)/shard_map/while/body/add_up/pallas_call | solution.py:124
  310.8 11.2 %all-to-all-done.4.refs_3_ = bf16[32,72,128]{2,1,0:T(8,128)(2,1)S(1)} async-done(((bf16[32,72,128]{2,1,0:T(8,128)(2,1)}), bf16[32,72,128]{2,1,0:T(8,128)(2,1)S(1)}, u32[]{:S(2)}, u32[]{:S(2)}) %all-to-all-start.4) | async-done | bytes 589856 | tf_op jit(solution)/shard_map/while/body/all_to_all | solution.py:488
  (191 shorter events, 40.5 us)
Async XLA Ops:
  12.8 19.8 %all-to-all-start.6 = ((s32[32,1,128]{2,1,0:T(1,128)}), s32[32,1,128]{2,1,0:T(1,128)S(1)}, u32[]{:S(2)}, u32[]{:S(2)}) async-start(s32[32,1,128]{2,1,0:T(1,128)} %broadcast_in_dim.143), calls=%async_computation.6 | async-start | bytes 32768 | tf_op jit(solution)/shard_map/all_to_all | solution.py:488
  38.8 73.0 %all-to-all-start = ((bf16[32,320,128]{2,1,0:T(8,128)(2,1)}), bf16[32,320,128]{2,1,0:T(8,128)(2,1)}, u32[]{:S(2)}, u32[]{:S(2)}) async-start(bf16[32,320,128]{2,1,0:T(8,128)(2,1)} %pack.9), calls=%async_computation | async-start | bytes 5242880 | tf_op jit(solution)/shard_map/while/body/all_to_all | solution.py:488
  79.4 17.9 %collective-permute-start.7 = (bf16[6,320,128]{2,1,0:T(8,128)(2,1)}, bf16[6,320,128]{2,1,0:T(8,128)(2,1)S(1)}, u32[]{:S(2)}, u32[]{:S(2)}) collective-permute-start(bf16[6,320,128]{2,1,0:T(8,128)(2,1)} %get-tuple-element.294), channel_id=1, source_target_pairs={{0,64},{8,72},{16,80},{24,88},{32,96},{40,104},{48,112},{56,120},{... | collective-permute-start | bytes 1474568 | tf_op jit(solution)/shard_map/while/body/ppermute | solution.py:479
  80.9 29.6 %collective-permute-start.8 = (bf16[6,320,128]{2,1,0:T(8,128)(2,1)}, bf16[6,320,128]{2,1,0:T(8,128)(2,1)}, u32[]{:S(2)}, u32[]{:S(2)}) collective-permute-start(bf16[6,320,128]{2,1,0:T(8,128)(2,1)} %get-tuple-element.295), channel_id=1, source_target_pairs={{0,128},{8,136},{16,144},{24,152},{32,160},{40,168},{48,176},{56,1... | collective-permute-start | bytes 1474568 | tf_op jit(solution)/shard_map/while/body/ppermute | solution.py:479
  83.7 32.0 %collective-permute-start.9 = (bf16[6,320,128]{2,1,0:T(8,128)(2,1)}, bf16[6,320,128]{2,1,0:T(8,128)(2,1)}, u32[]{:S(2)}, u32[]{:S(2)}) collective-permute-start(bf16[6,320,128]{2,1,0:T(8,128)(2,1)} %get-tuple-element.296), channel_id=1, source_target_pairs={{0,192},{8,200},{16,208},{24,216},{32,224},{40,232},{48,240},{56,2... | collective-permute-start | bytes 1474568 | tf_op jit(solution)/shard_map/while/body/ppermute | solution.py:479
  87.2 39.7 %collective-permute-start.31 = (bf16[4,320,128]{2,1,0:T(8,128)(2,1)}, bf16[4,320,128]{2,1,0:T(8,128)(2,1)S(1)}, u32[]{:S(2)}, u32[]{:S(2)}) collective-permute-start(bf16[4,320,128]{2,1,0:T(8,128)(2,1)} %get-tuple-element.326), channel_id=1, source_target_pairs={{0,1},{1,0},{2,3},{3,2},{4,5},{5,4},{6,7},{7,6},{8,9},{9,8},{10,11... | collective-permute-start | bytes 983048 | tf_op jit(solution)/shard_map/while/body/ppermute | solution.py:470
  87.2 41.9 %collective-permute-start.32 = (bf16[4,320,128]{2,1,0:T(8,128)(2,1)}, bf16[4,320,128]{2,1,0:T(8,128)(2,1)}, u32[]{:S(2)}, u32[]{:S(2)}) collective-permute-start(bf16[4,320,128]{2,1,0:T(8,128)(2,1)} %get-tuple-element.327), channel_id=1, source_target_pairs={{0,2},{1,3},{2,0},{3,1},{4,6},{5,7},{6,4},{7,5},{8,10},{9,11},{10,... | collective-permute-start | bytes 983048 | tf_op jit(solution)/shard_map/while/body/ppermute | solution.py:470
  97.3 34.7 %collective-permute-start.33 = (bf16[4,320,128]{2,1,0:T(8,128)(2,1)}, bf16[4,320,128]{2,1,0:T(8,128)(2,1)}, u32[]{:S(2)}, u32[]{:S(2)}) collective-permute-start(bf16[4,320,128]{2,1,0:T(8,128)(2,1)} %get-tuple-element.328), channel_id=1, source_target_pairs={{0,3},{1,2},{2,1},{3,0},{4,7},{5,6},{6,5},{7,4},{8,11},{9,10},{10,... | collective-permute-start | bytes 983048 | tf_op jit(solution)/shard_map/while/body/ppermute | solution.py:470
  110.6 21.4 %collective-permute-start.34 = (bf16[4,320,128]{2,1,0:T(8,128)(2,1)}, bf16[4,320,128]{2,1,0:T(8,128)(2,1)}, u32[]{:S(2)}, u32[]{:S(2)}) collective-permute-start(bf16[4,320,128]{2,1,0:T(8,128)(2,1)} %get-tuple-element.329), channel_id=1, source_target_pairs={{0,4},{1,5},{2,6},{3,7},{4,0},{5,1},{6,2},{7,3},{8,12},{9,13},{10,... | collective-permute-start | bytes 983048 | tf_op jit(solution)/shard_map/while/body/ppermute | solution.py:470
  118.8 75.3 %all-to-all-start.1 = ((bf16[16,320,128]{2,1,0:T(8,128)(2,1)}), bf16[16,320,128]{2,1,0:T(8,128)(2,1)}, u32[]{:S(2)}, u32[]{:S(2)}) async-start(bf16[16,320,128]{2,1,0:T(8,128)(2,1)} %pack.11), calls=%async_computation.1 | async-start | bytes 2621440 | tf_op jit(solution)/shard_map/while/body/all_to_all | solution.py:484
  127.0 11.8 %collective-permute-start.35 = (bf16[4,320,128]{2,1,0:T(8,128)(2,1)}, bf16[4,320,128]{2,1,0:T(8,128)(2,1)S(1)}, u32[]{:S(2)}, u32[]{:S(2)}) collective-permute-start(bf16[4,320,128]{2,1,0:T(8,128)(2,1)} %get-tuple-element.330), channel_id=1, source_target_pairs={{0,5},{1,4},{2,7},{3,6},{4,1},{5,0},{6,3},{7,2},{8,13},{9,12},{10,... | collective-permute-start | bytes 983048 | tf_op jit(solution)/shard_map/while/body/ppermute | solution.py:470
  127.0 54.0 %copy-start.17 = (bf16[4,320,128]{2,1,0:T(8,128)(2,1)}, bf16[4,320,128]{2,1,0:T(8,128)(2,1)S(1)}, u32[]{:S(2)}) copy-start(bf16[4,320,128]{2,1,0:T(8,128)(2,1)S(1)} %collective-permute-done.31.refs_1_) | copy-start | bytes 983044 | tf_op jit(solution)/shard_map/while
  127.0 18.0 %collective-permute-start.36 = (bf16[4,320,128]{2,1,0:T(8,128)(2,1)}, bf16[4,320,128]{2,1,0:T(8,128)(2,1)S(1)}, u32[]{:S(2)}, u32[]{:S(2)}) collective-permute-start(bf16[4,320,128]{2,1,0:T(8,128)(2,1)} %get-tuple-element.331), channel_id=1, source_target_pairs={{0,6},{1,7},{2,4},{3,5},{4,2},{5,3},{6,0},{7,1},{8,14},{9,15},{10,... | collective-permute-start | bytes 983048 | tf_op jit(solution)/shard_map/while/body/ppermute | solution.py:470
  129.1 23.5 %collective-permute-start.37 = (bf16[4,320,128]{2,1,0:T(8,128)(2,1)}, bf16[4,320,128]{2,1,0:T(8,128)(2,1)S(1)}, u32[]{:S(2)}, u32[]{:S(2)}) collective-permute-start(bf16[4,320,128]{2,1,0:T(8,128)(2,1)} %get-tuple-element.332), channel_id=1, source_target_pairs={{0,7},{1,6},{2,5},{3,4},{4,3},{5,2},{6,1},{7,0},{8,15},{9,14},{10,... | collective-permute-start | bytes 983048 | tf_op jit(solution)/shard_map/while/body/ppermute | solution.py:470
  132.0 22.8 %collective-permute-start.10 = (bf16[4,320,128]{2,1,0:T(8,128)(2,1)}, bf16[4,320,128]{2,1,0:T(8,128)(2,1)S(1)}, u32[]{:S(2)}, u32[]{:S(2)}) collective-permute-start(bf16[4,320,128]{2,1,0:T(8,128)(2,1)} %get-tuple-element.298), channel_id=1, source_target_pairs={{0,1},{1,0},{2,3},{3,2},{4,5},{5,4},{6,7},{7,6},{8,9},{9,8},{10,11... | collective-permute-start | bytes 983048 | tf_op jit(solution)/shard_map/while/body/ppermute | solution.py:470
  132.0 23.8 %collective-permute-start.11 = (bf16[4,320,128]{2,1,0:T(8,128)(2,1)}, bf16[4,320,128]{2,1,0:T(8,128)(2,1)S(1)}, u32[]{:S(2)}, u32[]{:S(2)}) collective-permute-start(bf16[4,320,128]{2,1,0:T(8,128)(2,1)} %get-tuple-element.299), channel_id=1, source_target_pairs={{0,2},{1,3},{2,0},{3,1},{4,6},{5,7},{6,4},{7,5},{8,10},{9,11},{10,... | collective-permute-start | bytes 983048 | tf_op jit(solution)/shard_map/while/body/ppermute | solution.py:470
  138.7 19.1 %collective-permute-start.12 = (bf16[4,320,128]{2,1,0:T(8,128)(2,1)}, bf16[4,320,128]{2,1,0:T(8,128)(2,1)S(1)}, u32[]{:S(2)}, u32[]{:S(2)}) collective-permute-start(bf16[4,320,128]{2,1,0:T(8,128)(2,1)} %get-tuple-element.300), channel_id=1, source_target_pairs={{0,3},{1,2},{2,1},{3,0},{4,7},{5,6},{6,5},{7,4},{8,11},{9,10},{10,... | collective-permute-start | bytes 983048 | tf_op jit(solution)/shard_map/while/body/ppermute | solution.py:470
  145.0 13.6 %collective-permute-start.13 = (bf16[4,320,128]{2,1,0:T(8,128)(2,1)}, bf16[4,320,128]{2,1,0:T(8,128)(2,1)S(1)}, u32[]{:S(2)}, u32[]{:S(2)}) collective-permute-start(bf16[4,320,128]{2,1,0:T(8,128)(2,1)} %get-tuple-element.301), channel_id=1, source_target_pairs={{0,4},{1,5},{2,6},{3,7},{4,0},{5,1},{6,2},{7,3},{8,12},{9,13},{10,... | collective-permute-start | bytes 983048 | tf_op jit(solution)/shard_map/while/body/ppermute | solution.py:470
  152.7 13.7 %collective-permute-start.14 = (bf16[4,320,128]{2,1,0:T(8,128)(2,1)}, bf16[4,320,128]{2,1,0:T(8,128)(2,1)S(1)}, u32[]{:S(2)}, u32[]{:S(2)}) collective-permute-start(bf16[4,320,128]{2,1,0:T(8,128)(2,1)} %get-tuple-element.302), channel_id=1, source_target_pairs={{0,5},{1,4},{2,7},{3,6},{4,1},{5,0},{6,3},{7,2},{8,13},{9,12},{10,... | collective-permute-start | bytes 983048 | tf_op jit(solution)/shard_map/while/body/ppermute | solution.py:470
  154.8 18.5 %collective-permute-start.15 = (bf16[4,320,128]{2,1,0:T(8,128)(2,1)}, bf16[4,320,128]{2,1,0:T(8,128)(2,1)S(1)}, u32[]{:S(2)}, u32[]{:S(2)}) collective-permute-start(bf16[4,320,128]{2,1,0:T(8,128)(2,1)} %get-tuple-element.303), channel_id=1, source_target_pairs={{0,6},{1,7},{2,4},{3,5},{4,2},{5,3},{6,0},{7,1},{8,14},{9,15},{10,... | collective-permute-start | bytes 983048 | tf_op jit(solution)/shard_map/while/body/ppermute | solution.py:470
  155.9 24.4 %collective-permute-start.16 = (bf16[4,320,128]{2,1,0:T(8,128)(2,1)S(1)}, bf16[4,320,128]{2,1,0:T(8,128)(2,1)S(1)}, u32[]{:S(2)}, u32[]{:S(2)}) collective-permute-start(bf16[4,320,128]{2,1,0:T(8,128)(2,1)S(1)} %copy-done.18), channel_id=1, source_target_pairs={{0,7},{1,6},{2,5},{3,4},{4,3},{5,2},{6,1},{7,0},{8,15},{9,14},{10,... | collective-permute-start | bytes 983048 | tf_op jit(solution)/shard_map/while/body/ppermute | solution.py:470
  194.1 33.3 %all-to-all-start.2 = ((bf16[8,8,72,128]{3,2,1,0:T(8,128)(2,1)}), bf16[8,8,72,128]{3,2,1,0:T(8,128)(2,1)}, u32[]{:S(2)}, u32[]{:S(2)}) async-start(bf16[8,8,72,128]{3,2,1,0:T(8,128)(2,1)} %dimers.3), calls=%async_computation.2 | async-start | bytes 2359296 | tf_op jit(solution)/shard_map/while/body/all_to_all | solution.py:475
  200.6 9.0 %collective-permute-start = (bf16[2,320,128]{2,1,0:T(8,128)(2,1)}, bf16[2,320,128]{2,1,0:T(8,128)(2,1)S(1)}, u32[]{:S(2)}, u32[]{:S(2)}) collective-permute-start(bf16[2,320,128]{2,1,0:T(8,128)(2,1)} %get-tuple-element.287), channel_id=1, source_target_pairs={{0,1},{1,0},{2,3},{3,2},{4,5},{5,4},{6,7},{7,6},{8,9},{9,8},{10,11... | collective-permute-start | bytes 491528 | tf_op jit(solution)/shard_map/while/body/ppermute | solution.py:470
  201.0 17.2 %collective-permute-start.1 = (bf16[2,320,128]{2,1,0:T(8,128)(2,1)}, bf16[2,320,128]{2,1,0:T(8,128)(2,1)S(1)}, u32[]{:S(2)}, u32[]{:S(2)}) collective-permute-start(bf16[2,320,128]{2,1,0:T(8,128)(2,1)} %get-tuple-element.288), channel_id=1, source_target_pairs={{0,2},{1,3},{2,0},{3,1},{4,6},{5,7},{6,4},{7,5},{8,10},{9,11},{10,... | collective-permute-start | bytes 491528 | tf_op jit(solution)/shard_map/while/body/ppermute | solution.py:470
  202.7 17.9 %collective-permute-start.2 = (bf16[2,320,128]{2,1,0:T(8,128)(2,1)}, bf16[2,320,128]{2,1,0:T(8,128)(2,1)S(1)}, u32[]{:S(2)}, u32[]{:S(2)}) collective-permute-start(bf16[2,320,128]{2,1,0:T(8,128)(2,1)} %get-tuple-element.289), channel_id=1, source_target_pairs={{0,3},{1,2},{2,1},{3,0},{4,7},{5,6},{6,5},{7,4},{8,11},{9,10},{10,... | collective-permute-start | bytes 491528 | tf_op jit(solution)/shard_map/while/body/ppermute | solution.py:470
  202.7 24.1 %collective-permute-start.3 = (bf16[2,320,128]{2,1,0:T(8,128)(2,1)}, bf16[2,320,128]{2,1,0:T(8,128)(2,1)S(1)}, u32[]{:S(2)}, u32[]{:S(2)}) collective-permute-start(bf16[2,320,128]{2,1,0:T(8,128)(2,1)} %get-tuple-element.290), channel_id=1, source_target_pairs={{0,4},{1,5},{2,6},{3,7},{4,0},{5,1},{6,2},{7,3},{8,12},{9,13},{10,... | collective-permute-start | bytes 491528 | tf_op jit(solution)/shard_map/while/body/ppermute | solution.py:470
  205.9 36.1 %collective-permute-start.4 = (bf16[2,320,128]{2,1,0:T(8,128)(2,1)}, bf16[2,320,128]{2,1,0:T(8,128)(2,1)S(1)}, u32[]{:S(2)}, u32[]{:S(2)}) collective-permute-start(bf16[2,320,128]{2,1,0:T(8,128)(2,1)} %get-tuple-element.291), channel_id=1, source_target_pairs={{0,5},{1,4},{2,7},{3,6},{4,1},{5,0},{6,3},{7,2},{8,13},{9,12},{10,... | collective-permute-start | bytes 491528 | tf_op jit(solution)/shard_map/while/body/ppermute | solution.py:470
  209.6 53.8 %copy-start.29 = (bf16[2,320,128]{2,1,0:T(8,128)(2,1)}, bf16[2,320,128]{2,1,0:T(8,128)(2,1)S(1)}, u32[]{:S(2)}) copy-start(bf16[2,320,128]{2,1,0:T(8,128)(2,1)S(1)} %collective-permute-done.refs_1_) | copy-start | bytes 491524 | tf_op jit(solution)/shard_map/while
  209.6 32.6 %collective-permute-start.5 = (bf16[2,320,128]{2,1,0:T(8,128)(2,1)S(1)}, bf16[2,320,128]{2,1,0:T(8,128)(2,1)S(1)}, u32[]{:S(2)}, u32[]{:S(2)}) collective-permute-start(bf16[2,320,128]{2,1,0:T(8,128)(2,1)S(1)} %copy-done.44), channel_id=1, source_target_pairs={{0,6},{1,7},{2,4},{3,5},{4,2},{5,3},{6,0},{7,1},{8,14},{9,15},{10,... | collective-permute-start | bytes 491528 | tf_op jit(solution)/shard_map/while/body/ppermute | solution.py:470
  218.2 45.2 %copy-start.30 = (bf16[2,320,128]{2,1,0:T(8,128)(2,1)}, bf16[2,320,128]{2,1,0:T(8,128)(2,1)S(1)}, u32[]{:S(2)}) copy-start(bf16[2,320,128]{2,1,0:T(8,128)(2,1)S(1)} %collective-permute-done.1.refs_2_) | copy-start | bytes 491524 | tf_op jit(solution)/shard_map/while
  218.2 26.2 %collective-permute-start.6 = (bf16[2,320,128]{2,1,0:T(8,128)(2,1)S(1)}, bf16[2,320,128]{2,1,0:T(8,128)(2,1)S(1)}, u32[]{:S(2)}, u32[]{:S(2)}) collective-permute-start(bf16[2,320,128]{2,1,0:T(8,128)(2,1)S(1)} %copy-done.41), channel_id=1, source_target_pairs={{0,7},{1,6},{2,5},{3,4},{4,3},{5,2},{6,1},{7,0},{8,15},{9,14},{10,... | collective-permute-start | bytes 491528 | tf_op jit(solution)/shard_map/while/body/ppermute | solution.py:470
  220.5 42.8 %copy-start.31 = (bf16[2,320,128]{2,1,0:T(8,128)(2,1)}, bf16[2,320,128]{2,1,0:T(8,128)(2,1)S(1)}, u32[]{:S(2)}) copy-start(bf16[2,320,128]{2,1,0:T(8,128)(2,1)S(1)} %collective-permute-done.2.refs_3_) | copy-start | bytes 491524 | tf_op jit(solution)/shard_map/while
  220.5 26.2 %collective-permute-start.17 = (bf16[2,320,128]{2,1,0:T(8,128)(2,1)}, bf16[2,320,128]{2,1,0:T(8,128)(2,1)S(1)}, u32[]{:S(2)}, u32[]{:S(2)}) collective-permute-start(bf16[2,320,128]{2,1,0:T(8,128)(2,1)} %get-tuple-element.310), channel_id=1, source_target_pairs={{0,1},{1,0},{2,3},{3,2},{4,5},{5,4},{6,7},{7,6},{8,9},{9,8},{10,11... | collective-permute-start | bytes 491528 | tf_op jit(solution)/shard_map/while/body/ppermute | solution.py:470
  226.8 21.2 %collective-permute-start.18 = (bf16[2,320,128]{2,1,0:T(8,128)(2,1)}, bf16[2,320,128]{2,1,0:T(8,128)(2,1)S(1)}, u32[]{:S(2)}, u32[]{:S(2)}) collective-permute-start(bf16[2,320,128]{2,1,0:T(8,128)(2,1)} %get-tuple-element.311), channel_id=1, source_target_pairs={{0,2},{1,3},{2,0},{3,1},{4,6},{5,7},{6,4},{7,5},{8,10},{9,11},{10,... | collective-permute-start | bytes 491528 | tf_op jit(solution)/shard_map/while/body/ppermute | solution.py:470
  231.6 57.5 %all-to-all-start.3 = ((bf16[32,72,128]{2,1,0:T(8,128)(2,1)}), bf16[32,72,128]{2,1,0:T(8,128)(2,1)S(1)}, u32[]{:S(2)}, u32[]{:S(2)}) async-start(bf16[32,72,128]{2,1,0:T(8,128)(2,1)} %place.3), calls=%async_computation.3 | async-start | bytes 1179648 | tf_op jit(solution)/shard_map/while/body/all_to_all | solution.py:488
  242.1 6.7 %collective-permute-start.19 = (bf16[2,320,128]{2,1,0:T(8,128)(2,1)S(1)}, bf16[2,320,128]{2,1,0:T(8,128)(2,1)S(1)}, u32[]{:S(2)}, u32[]{:S(2)}) collective-permute-start(bf16[2,320,128]{2,1,0:T(8,128)(2,1)S(1)} %copy-done.42), channel_id=1, source_target_pairs={{0,3},{1,2},{2,1},{3,0},{4,7},{5,6},{6,5},{7,4},{8,11},{9,10},{10,... | collective-permute-start | bytes 491528 | tf_op jit(solution)/shard_map/while/body/ppermute | solution.py:470
  242.2 10.7 %collective-permute-start.20 = (bf16[2,320,128]{2,1,0:T(8,128)(2,1)S(1)}, bf16[2,320,128]{2,1,0:T(8,128)(2,1)S(1)}, u32[]{:S(2)}, u32[]{:S(2)}) collective-permute-start(bf16[2,320,128]{2,1,0:T(8,128)(2,1)S(1)} %copy-done.40), channel_id=1, source_target_pairs={{0,4},{1,5},{2,6},{3,7},{4,0},{5,1},{6,2},{7,3},{8,12},{9,13},{10,... | collective-permute-start | bytes 491528 | tf_op jit(solution)/shard_map/while/body/ppermute | solution.py:470
  244.3 11.0 %collective-permute-start.21 = (bf16[2,320,128]{2,1,0:T(8,128)(2,1)S(1)}, bf16[2,320,128]{2,1,0:T(8,128)(2,1)S(1)}, u32[]{:S(2)}, u32[]{:S(2)}) collective-permute-start(bf16[2,320,128]{2,1,0:T(8,128)(2,1)S(1)} %copy-done.38), channel_id=1, source_target_pairs={{0,5},{1,4},{2,7},{3,6},{4,1},{5,0},{6,3},{7,2},{8,13},{9,12},{10,... | collective-permute-start | bytes 491528 | tf_op jit(solution)/shard_map/while/body/ppermute | solution.py:470
  246.8 12.6 %collective-permute-start.22 = (bf16[2,320,128]{2,1,0:T(8,128)(2,1)S(1)}, bf16[2,320,128]{2,1,0:T(8,128)(2,1)S(1)}, u32[]{:S(2)}, u32[]{:S(2)}) collective-permute-start(bf16[2,320,128]{2,1,0:T(8,128)(2,1)S(1)} %copy-done.37), channel_id=1, source_target_pairs={{0,6},{1,7},{2,4},{3,5},{4,2},{5,3},{6,0},{7,1},{8,14},{9,15},{10,... | collective-permute-start | bytes 491528 | tf_op jit(solution)/shard_map/while/body/ppermute | solution.py:470
  248.0 14.7 %collective-permute-start.23 = (bf16[2,320,128]{2,1,0:T(8,128)(2,1)S(1)}, bf16[2,320,128]{2,1,0:T(8,128)(2,1)S(1)}, u32[]{:S(2)}, u32[]{:S(2)}) collective-permute-start(bf16[2,320,128]{2,1,0:T(8,128)(2,1)S(1)} %copy-done.36), channel_id=1, source_target_pairs={{0,7},{1,6},{2,5},{3,4},{4,3},{5,2},{6,1},{7,0},{8,15},{9,14},{10,... | collective-permute-start | bytes 491528 | tf_op jit(solution)/shard_map/while/body/ppermute | solution.py:470
  269.5 6.1 %collective-permute-start.24 = (bf16[4,72,128]{2,1,0:T(8,128)(2,1)}, bf16[4,72,128]{2,1,0:T(8,128)(2,1)S(1)}, u32[]{:S(2)}, u32[]{:S(2)}) collective-permute-start(bf16[4,72,128]{2,1,0:T(8,128)(2,1)} %get-tuple-element.318), channel_id=1, source_target_pairs={{0,1},{1,0},{2,3},{3,2},{4,5},{5,4},{6,7},{7,6},{8,9},{9,8},{10,11... | collective-permute-start | bytes 221192 | tf_op jit(solution)/shard_map/while/body/ppermute | solution.py:470
  269.7 9.5 %collective-permute-start.25 = (bf16[4,72,128]{2,1,0:T(8,128)(2,1)}, bf16[4,72,128]{2,1,0:T(8,128)(2,1)S(1)}, u32[]{:S(2)}, u32[]{:S(2)}) collective-permute-start(bf16[4,72,128]{2,1,0:T(8,128)(2,1)} %get-tuple-element.319), channel_id=1, source_target_pairs={{0,2},{1,3},{2,0},{3,1},{4,6},{5,7},{6,4},{7,5},{8,10},{9,11},{10,... | collective-permute-start | bytes 221192 | tf_op jit(solution)/shard_map/while/body/ppermute | solution.py:470
  269.7 9.5 %collective-permute-start.26 = (bf16[4,72,128]{2,1,0:T(8,128)(2,1)}, bf16[4,72,128]{2,1,0:T(8,128)(2,1)S(1)}, u32[]{:S(2)}, u32[]{:S(2)}) collective-permute-start(bf16[4,72,128]{2,1,0:T(8,128)(2,1)} %get-tuple-element.320), channel_id=1, source_target_pairs={{0,3},{1,2},{2,1},{3,0},{4,7},{5,6},{6,5},{7,4},{8,11},{9,10},{10,... | collective-permute-start | bytes 221192 | tf_op jit(solution)/shard_map/while/body/ppermute | solution.py:470
  271.5 10.7 %collective-permute-start.27 = (bf16[4,72,128]{2,1,0:T(8,128)(2,1)}, bf16[4,72,128]{2,1,0:T(8,128)(2,1)S(1)}, u32[]{:S(2)}, u32[]{:S(2)}) collective-permute-start(bf16[4,72,128]{2,1,0:T(8,128)(2,1)} %get-tuple-element.321), channel_id=1, source_target_pairs={{0,4},{1,5},{2,6},{3,7},{4,0},{5,1},{6,2},{7,3},{8,12},{9,13},{10,... | collective-permute-start | bytes 221192 | tf_op jit(solution)/shard_map/while/body/ppermute | solution.py:470
  275.6 6.5 %collective-permute-start.28 = (bf16[4,72,128]{2,1,0:T(8,128)(2,1)}, bf16[4,72,128]{2,1,0:T(8,128)(2,1)S(1)}, u32[]{:S(2)}, u32[]{:S(2)}) collective-permute-start(bf16[4,72,128]{2,1,0:T(8,128)(2,1)} %get-tuple-element.322), channel_id=1, source_target_pairs={{0,5},{1,4},{2,7},{3,6},{4,1},{5,0},{6,3},{7,2},{8,13},{9,12},{10,... | collective-permute-start | bytes 221192 | tf_op jit(solution)/shard_map/while/body/ppermute | solution.py:470
  275.6 8.9 %collective-permute-start.29 = (bf16[4,72,128]{2,1,0:T(8,128)(2,1)}, bf16[4,72,128]{2,1,0:T(8,128)(2,1)S(1)}, u32[]{:S(2)}, u32[]{:S(2)}) collective-permute-start(bf16[4,72,128]{2,1,0:T(8,128)(2,1)} %get-tuple-element.323), channel_id=1, source_target_pairs={{0,6},{1,7},{2,4},{3,5},{4,2},{5,3},{6,0},{7,1},{8,14},{9,15},{10,... | collective-permute-start | bytes 221192 | tf_op jit(solution)/shard_map/while/body/ppermute | solution.py:470
  279.2 6.5 %collective-permute-start.30 = (bf16[4,72,128]{2,1,0:T(8,128)(2,1)}, bf16[4,72,128]{2,1,0:T(8,128)(2,1)S(1)}, u32[]{:S(2)}, u32[]{:S(2)}) collective-permute-start(bf16[4,72,128]{2,1,0:T(8,128)(2,1)} %get-tuple-element.324), channel_id=1, source_target_pairs={{0,7},{1,6},{2,5},{3,4},{4,3},{5,2},{6,1},{7,0},{8,15},{9,14},{10,... | collective-permute-start | bytes 221192 | tf_op jit(solution)/shard_map/while/body/ppermute | solution.py:470
  289.1 32.9 %all-to-all-start.4 = ((bf16[32,72,128]{2,1,0:T(8,128)(2,1)}), bf16[32,72,128]{2,1,0:T(8,128)(2,1)S(1)}, u32[]{:S(2)}, u32[]{:S(2)}) async-start(bf16[32,72,128]{2,1,0:T(8,128)(2,1)} %place.2), calls=%async_computation.4 | async-start | bytes 1179648 | tf_op jit(solution)/shard_map/while/body/all_to_all | solution.py:488
  (46 other events, 885.5 us)

commit v10 on v9

--- a/solution.py
+++ b/solution.py
@@ -279,7 +279,7 @@
     one_dimer(table_ref[STEPS + 2 * me + i], me, load, out, scratch)
 
 
-def plan_kernel(me_ref, inside_ref, count_ref, list_ref, table_ref, left_ref, to_x, to_z, n_direct, n_third, n_self, n_split, room, taken, mine):
+def plan_kernel(me_ref, inside_ref, count_ref, list_ref, table_ref, left_ref, to_x, to_z, n_direct, n_third, n_self, n_split, n_next, room, taken, mine):
     me = me_ref[0]
     me_x, me_z = me >> 3, me & 7
 
@@ -297,6 +297,7 @@
         n_third[n] = 0
         n_self[n] = 0
         n_split[n] = inside_ref[n]
+        n_next[n] = jnp.maximum(1, inside_ref[n])
         room[n] = 1 + inside_ref[n]
         taken[n] = 0
 
@@ -398,15 +399,17 @@
                 same_z = jnp.where(za == zb, 1, 0)
 
                 def look(carry):
-                    n, _ = carry
-                    turn = ((d + n) & 3) * 8
-                    c = jnp.where(n < 4, turn + za, jnp.where(n < 8, turn + zb, (d + n) & 31))
-                    fit = ((n_direct[c] + 1) >> 1) + jnp.maximum(n_third[c] + 1, inside_ref[c]) <= 8
-                    good = fit & can(oa, c, same_z) & can(ob, c, same_z) & (c != oa) & (c != ob)
-                    return n + 1, jnp.where(good, c, -1)
+                    n, found = carry
+                    for i in (3, 2, 1, 0):
+                        turn = ((d + i) & 3) * 8
+                        c = jnp.where(n == 0, turn + za, jnp.where(n == 1, turn + zb, (d + 4 * n + i) & 31))
+                        fit = ((n_direct[c] + 1) >> 1) + n_next[c] <= 8
+                        good = fit & can(oa, c, same_z) & can(ob, c, same_z) & (c != oa) & (c != ob)
+                        found = jnp.where(good, c, found)
+                    return n + 1, found
 
                 _, c = lax.while_loop(
-                    lambda carry: (carry[0] < 40) & (carry[1] < 0), look, (jnp.int32(0), jnp.int32(-1))
+                    lambda carry: (carry[0] < 10) & (carry[1] < 0), look, (jnp.int32(0), jnp.int32(-1))
                 )
 
                 @pl.when(c < 0)
@@ -419,6 +422,7 @@
                     n_third[c] = t + 1
                     split = jnp.maximum(t + 1, inside_ref[c])
                     n_split[c] = split
+                    n_next[c] = jnp.maximum(t + 2, inside_ref[c])
                     room[c] = ((n_direct[c] + 2) >> 1) + split
                     xc, zc = c >> 3, c & 7
                     x_at, z_at = oa * 4 + xc, xc * 64 + za * 8 + zc
@@ -458,7 +462,7 @@
         out_shape=[jax.ShapeDtypeStruct((TABLE,), s32), jax.ShapeDtypeStruct(words.shape, s32)],
         in_specs=[SMEM] * 4,
         out_specs=[SMEM] * 2,
-        scratch_shapes=[pltpu.SMEM((128,), s32), pltpu.SMEM((256,), s32)] + [pltpu.SMEM((32,), s32)] * 6 + [pltpu.SMEM((64,), s32)],
+        scratch_shapes=[pltpu.SMEM((128,), s32), pltpu.SMEM((256,), s32)] + [pltpu.SMEM((32,), s32)] * 7 + [pltpu.SMEM((64,), s32)],
         name="plan",
         cost_estimate=pl.CostEstimate(flops=1000, bytes_accessed=30_000_000, transcendentals=0),
     )(me, inside_count, count, words)
@@ -555,7 +559,9 @@
         earlier = (pair_id[:, None] == pair_id[None, :]) & (order[None, :] < order[:, None])
         earlier = jnp.sum(jnp.where(earlier & open_dimer[None, :], 1, 0), axis=1)
         flagged = open_dimer & ((earlier >= 2) | inside)
-        ahead = jnp.sum(jnp.where((order[None, :] < order[:, None]) & flagged[None, :], 1, 0), axis=1)
+        late_turn = jnp.where(inside | (earlier == 2), 2, jnp.where(earlier == 3, 0, 1))
+        turn = order + dimers * late_turn
+        ahead = jnp.sum(jnp.where((turn[None, :] < turn[:, None]) & flagged[None, :], 1, 0), axis=1)
         ahead = jnp.where(flagged, ahead, -1)
         words = jnp.sum(jnp.where(ahead[None, :] == order[:, None], word[None, :], 0), axis=1)
         count = jnp.sum(jnp.where(flagged, 1, 0)).reshape(1)

time: 328 us -> 327 us (level)
  transfers between devices with their start and end apart: 44 -> 44, of which waited for: 21 -> 21; matrix products, arithmetic and copies ran while one was open for 2% -> 2% of each run, Pallas kernels for 24% -> 23%
where the time goes in v10:
time: 327 us; the launch traced here: 326 us
  waiting for transfers between devices  117 us (36%)
  starting transfers between devices  98.5 us (30%)
  Pallas kernels  81.5 us (25%)
  other arithmetic  10.3 us (3%)
  blocking collectives  9.55 us (3%)
  local copies, waits for them, and re-layouts  6.96 us (2%)
    ppermute x35, waiting for transfers between devices, exchange(): got.append(lax.ppermute(parts[k], 'basis', [(i, i ^ k) for i in range(8)]))  73.8 us
    all_to_all x4, starting transfers between devices, across(): return lax.all_to_all(part, 'frag', split_axis=0, concat_axis=0, tiled=True)  43.2 us
    ppermute x35, starting transfers between devices, exchange(): got.append(lax.ppermute(parts[k], 'basis', [(i, i ^ k) for i in range(8)]))  38.6 us
    pallas_call x1, Pallas kernels, plan_rest(): pl.pallas_call(plan_kernel, out_shape=[jax.ShapeDtypeStruct((TABLE,), s32...  26.5 us
    ppermute x3, waiting for transfers between devices, along_x(): lax.ppermute(parts[k - 1], 'frag', [(i, i ^ 8 * k) for i in range(32)])  23.5 us
    pallas_call x7, Pallas kernels, pack(): pl.pallas_call(kernel, out_shape=[jax.ShapeDtypeStruct((rows, 320, 128),...  21.9 us
    all_to_all x4, waiting for transfers between devices, across(): return lax.all_to_all(part, 'frag', split_axis=0, concat_axis=0, tiled=True)  19.6 us
    pallas_call x2, Pallas kernels, run_dimers(): pl.pallas_call(kernel, out_shape=[jax.ShapeDtypeStruct(shape, BF16) for s...  19.1 us
  transfers between devices with their start and end apart: 44, of which 21 were waited for; matrix products, arithmetic and copies ran while one was open for 2% of the time, Pallas kernels for 23%

profile of v10, /device:TPU:32, one launch (start us, length us, event | category | flops | bytes accessed | tf_op | source)
XLA Modules:
  0.0 325.6 jit_solution(4254697780961645063)
XLA Ops:
  2.3 9.6 %all_to_all.40 = s32[8,1,128]{2,1,0:T(1,128)S(1)} all-to-all(s32[8,1,128]{2,1,0:T(1,128)S(1)} %broadcast_in_dim.146), channel_id=1, replica_groups=mesh['frag'=32,'basis'=8] {'basis'}, dimensions={0} | all-to-all | bytes 8192 | tf_op jit(solution)/shard_map/all_to_all | solution.py:509
  12.8 11.2 %all-to-all-start.6 = ((s32[32,1,128]{2,1,0:T(1,128)}), s32[32,1,128]{2,1,0:T(1,128)S(1)}, u32[]{:S(2)}, u32[]{:S(2)}) async-start(s32[32,1,128]{2,1,0:T(1,128)} %broadcast_in_dim.147), calls=%async_computation.6 | async-start | bytes 32768 | tf_op jit(solution)/shard_map/all_to_all | solution.py:492
  24.0 8.6 %all-to-all-done.6 = s32[32,1,128]{2,1,0:T(1,128)S(1)} async-done(((s32[32,1,128]{2,1,0:T(1,128)}), s32[32,1,128]{2,1,0:T(1,128)S(1)}, u32[]{:S(2)}, u32[]{:S(2)}) %all-to-all-start.6) | async-done | bytes 16416 | tf_op jit(solution)/shard_map/all_to_all | solution.py:492
  34.1 290.9 %while.15 = (s32[]{:T(128)}, s32[1024]{0:T(1024)S(1)}, f32[32,32,256]{2,1,0:T(8,128)}, f32[32,128]{1,0:T(8,128)S(1)}, s32[1024]{0:T(1024)S(1)}, /*index=5*/pred[...) while((s32[]{:T(128)}, s32[1024]{0:T(1024)S(1)}, ...), condition=%region_13.14_spmd.clone.clone, body=%region_1.13_spmd.clone.clone | while | flops 24018305024 | bytes 150602000 | solution.py:641
  35.0 3.8 %pack.9 = bf16[32,320,128]{2,1,0:T(8,128)(2,1)} custom-call(s32[32]{0:T(128)} %get-tuple-element.402.refs_0_, s32[1]{0:T(128)} %get-tuple-element.467.refs_2_.refs_1_.me_ref, bf16[32,256,128]{2,1,0:T(8,128)(2,1)} %get-tuple-element.468.refs_3_.refs_2_, bf16[32,32,256]{2,1,0:T(8,128)(2,1)} %get-tuple-element.469.refs_4_.refs_3_), custom_call_target="tpu_custom_call" | custom-call | tf_op jit(solution)/shard_map/while/body/pack/pallas_call | solution.py:68
  38.8 6.1 %all-to-all-start = ((bf16[32,320,128]{2,1,0:T(8,128)(2,1)}), bf16[32,320,128]{2,1,0:T(8,128)(2,1)}, u32[]{:S(2)}, u32[]{:S(2)}) async-start(bf16[32,320,128]{2,1,0:T(8,128)(2,1)} %pack.9), calls=%async_computation | async-start | bytes 5242880 | tf_op jit(solution)/shard_map/while/body/all_to_all | solution.py:492
  49.0 26.5 %plan.1 = (s32[256]{0:T(256)}, s32[1024]{0:T(1024)}) custom-call(s32[1]{0:T(128)} %get-tuple-element.464.me_ref, s32[32]{0:T(128)} %select_reduce_fusion.6.inside_ref, s32[1]{0:T(128)} %bitcast.5.count_ref, s32[1024]{0:T(1024)} %select_reduce_fusion.2.list_ref), custom_call_target="tpu_custom_call" | custom-call | flops 1000 | bytes 30000000 | tf_op jit(solution)/shard_map/while/body/plan/pallas_call | solution.py:460
  76.4 2.2 pack.8
  80.2 2.8 collective-permute-start.8
  83.3 3.1 pack.13
  87.0 9.7 %collective-permute-done.7.refs_5_.refs_3_ = bf16[6,320,128]{2,1,0:T(8,128)(2,1)S(1)} collective-permute-done((bf16[6,320,128]{2,1,0:T(8,128)(2,1)}, bf16[6,320,128]{2,1,0:T(8,128)(2,1)S(1)}, u32[]{:S(2)}, u32[]{:S(2)}) %collective-permute-start.7) | collective-permute-done | bytes 491552 | tf_op jit(solution)/shard_map/while/body/ppermute | solution.py:483
  96.8 13.7 %collective-permute-done.8.refs_6_.refs_4_ = bf16[6,320,128]{2,1,0:T(8,128)(2,1)} collective-permute-done((bf16[6,320,128]{2,1,0:T(8,128)(2,1)}, bf16[6,320,128]{2,1,0:T(8,128)(2,1)}, u32[]{:S(2)}, u32[]{:S(2)}) %collective-permute-start.8) | collective-permute-done | bytes 491552 | tf_op jit(solution)/shard_map/while/body/ppermute | solution.py:483
  111.7 4.0 %pack.10 = (bf16[4,320,128]{2,1,0:T(8,128)(2,1)}, bf16[4,320,128]{2,1,0:T(8,128)(2,1)}, bf16[4,320,128]{2,1,0:T(8,128)(2,1)}, bf16[4,320,128]{2,1,0:T(8,128)(2,1...) custom-call(s32[128]{0:T(128)} %pad_add_fusion.refs_0_.table_ref, ...), custom_call_target="tpu_custom_call" | custom-call | tf_op jit(solution)/shard_map/while/body/pack/pallas_call | solution.py:68
  115.7 3.0 pack.11
  118.7 7.7 %all-to-all-start.1 = ((bf16[16,320,128]{2,1,0:T(8,128)(2,1)}), bf16[16,320,128]{2,1,0:T(8,128)(2,1)}, u32[]{:S(2)}, u32[]{:S(2)}) async-start(bf16[16,320,128]{2,1,0:T(8,128)(2,1)} %pack.11), calls=%async_computation.1 | async-start | bytes 2621440 | tf_op jit(solution)/shard_map/while/body/all_to_all | solution.py:488
  126.4 2.2 collective-permute-start.36
  128.6 2.9 collective-permute-start.37
  131.6 6.6 %collective-permute-done.35.refs_5_ = bf16[4,320,128]{2,1,0:T(8,128)(2,1)S(1)} collective-permute-done((bf16[4,320,128]{2,1,0:T(8,128)(2,1)}, bf16[4,320,128]{2,1,0:T(8,128)(2,1)S(1)}, u32[]{:S(2)}, u32[]{:S(2)}) %collective-permute-start.35) | collective-permute-done | bytes 327712 | tf_op jit(solution)/shard_map/while/body/ppermute | solution.py:474
  138.2 6.3 %collective-permute-done.36.refs_6_ = bf16[4,320,128]{2,1,0:T(8,128)(2,1)S(1)} collective-permute-done((bf16[4,320,128]{2,1,0:T(8,128)(2,1)}, bf16[4,320,128]{2,1,0:T(8,128)(2,1)S(1)}, u32[]{:S(2)}, u32[]{:S(2)}) %collective-permute-start.36) | collective-permute-done | bytes 327712 | tf_op jit(solution)/shard_map/while/body/ppermute | solution.py:474
  145.7 6.4 %collective-permute-done.37.refs_7_ = bf16[4,320,128]{2,1,0:T(8,128)(2,1)S(1)} collective-permute-done((bf16[4,320,128]{2,1,0:T(8,128)(2,1)}, bf16[4,320,128]{2,1,0:T(8,128)(2,1)S(1)}, u32[]{:S(2)}, u32[]{:S(2)}) %collective-permute-start.37) | collective-permute-done | bytes 327712 | tf_op jit(solution)/shard_map/while/body/ppermute | solution.py:474
  152.1 2.2 collective-permute-start.14
  155.3 2.0 collective-permute-start.16
  158.1 7.7 %collective-permute-done.14.refs_13_ = bf16[4,320,128]{2,1,0:T(8,128)(2,1)S(1)} collective-permute-done((bf16[4,320,128]{2,1,0:T(8,128)(2,1)}, bf16[4,320,128]{2,1,0:T(8,128)(2,1)S(1)}, u32[]{:S(2)}, u32[]{:S(2)}) %collective-permute-start.14) | collective-permute-done | bytes 327712 | tf_op jit(solution)/shard_map/while/body/ppermute | solution.py:474
  165.8 7.0 %collective-permute-done.15.refs_14_ = bf16[4,320,128]{2,1,0:T(8,128)(2,1)S(1)} collective-permute-done((bf16[4,320,128]{2,1,0:T(8,128)(2,1)}, bf16[4,320,128]{2,1,0:T(8,128)(2,1)S(1)}, u32[]{:S(2)}, u32[]{:S(2)}) %collective-permute-start.15) | collective-permute-done | bytes 327712 | tf_op jit(solution)/shard_map/while/body/ppermute | solution.py:474
  172.8 6.9 %collective-permute-done.16.refs_15_ = bf16[4,320,128]{2,1,0:T(8,128)(2,1)S(1)} collective-permute-done((bf16[4,320,128]{2,1,0:T(8,128)(2,1)S(1)}, bf16[4,320,128]{2,1,0:T(8,128)(2,1)S(1)}, u32[]{:S(2)}, u32[]{:S(2)}) %collective-permute-start.16) | collective-permute-done | bytes 327712 | tf_op jit(solution)/shard_map/while/body/ppermute | solution.py:474
  180.5 13.1 %dimers.3 = bf16[8,8,72,128]{3,2,1,0:T(8,128)(2,1)} custom-call(s32[128]{0:T(128)} %pad_add_fusion.refs_0_.table_ref, s32[1]{0:T(128)} %get-tuple-element.467.refs_2_.refs_1_.me_ref, bf16[4,320,128]{2,1,0:T(8,128)(2,1)} %get-tuple-element.325.refs_0_, bf16[4,320,128]{2,1,0:T(8,128)(2,1)} %copy-done.17, bf16[4,320,128]{2,1,0:T(8,128)(2,1)} %collective-permute-done.32.refs_2_, ...), custom_call_target="tpu_custom_call" | custom-call | flops 16000000000 | bytes 6000000 | tf_op jit(solution)/shard_map/while/body/dimers/pallas_call | solution.py:223
  193.6 4.3 %all-to-all-start.2 = ((bf16[8,8,72,128]{3,2,1,0:T(8,128)(2,1)}), bf16[8,8,72,128]{3,2,1,0:T(8,128)(2,1)}, u32[]{:S(2)}, u32[]{:S(2)}) async-start(bf16[8,8,72,128]{3,2,1,0:T(8,128)(2,1)} %dimers.3), calls=%async_computation.2 | async-start | bytes 2359296 | tf_op jit(solution)/shard_map/while/body/all_to_all | solution.py:479
  197.9 2.2 pack.7
  202.1 3.3 collective-permute-start.3
  205.5 3.5 %pack.12 = (bf16[2,320,128]{2,1,0:T(8,128)(2,1)}, bf16[2,320,128]{2,1,0:T(8,128)(2,1)}, bf16[2,320,128]{2,1,0:T(8,128)(2,1)}, bf16[2,320,128]{2,1,0:T(8,128)(2,1...) custom-call(s32[128]{0:T(128)} %pad_add_fusion.refs_0_.table_ref, ...), custom_call_target="tpu_custom_call" | custom-call | tf_op jit(solution)/shard_map/while/body/pack/pallas_call | solution.py:68
  209.1 3.0 collective-permute-start.5
  212.1 5.6 %collective-permute-done.1.refs_2_ = bf16[2,320,128]{2,1,0:T(8,128)(2,1)S(1)} collective-permute-done((bf16[2,320,128]{2,1,0:T(8,128)(2,1)}, bf16[2,320,128]{2,1,0:T(8,128)(2,1)S(1)}, u32[]{:S(2)}, u32[]{:S(2)}) %collective-permute-start.1) | collective-permute-done | bytes 163872 | tf_op jit(solution)/shard_map/while/body/ppermute | solution.py:474
  221.0 5.3 %collective-permute-done.3.refs_4_ = bf16[2,320,128]{2,1,0:T(8,128)(2,1)S(1)} collective-permute-done((bf16[2,320,128]{2,1,0:T(8,128)(2,1)}, bf16[2,320,128]{2,1,0:T(8,128)(2,1)S(1)}, u32[]{:S(2)}, u32[]{:S(2)}) %collective-permute-start.3) | collective-permute-done | bytes 163872 | tf_op jit(solution)/shard_map/while/body/ppermute | solution.py:474
  226.9 4.2 %place.3 = bf16[32,72,128]{2,1,0:T(8,128)(2,1)} custom-call(s32[128]{0:T(128)} %pad_add_fusion.refs_0_.table_ref, s32[256]{0:T(256)} %get-tuple-element.282.refs_1_.table_ref, s32[1]{0:T(128)} %get-tuple-element.467.refs_2_.refs_1_.me_ref, bf16[64,72,128]{2,1,0:T(8,128)(2,1)} %bitcast.6.refs_3_), custom_call_target="tpu_custom_call" | custom-call | tf_op jit(solution)/shard_map/while/body/place/pallas_call | solution.py:95
  231.1 10.9 %all-to-all-start.3 = ((bf16[32,72,128]{2,1,0:T(8,128)(2,1)}), bf16[32,72,128]{2,1,0:T(8,128)(2,1)S(1)}, u32[]{:S(2)}, u32[]{:S(2)}) async-start(bf16[32,72,128]{2,1,0:T(8,128)(2,1)} %place.3), calls=%async_computation.3 | async-start | bytes 1179648 | tf_op jit(solution)/shard_map/while/body/all_to_all | solution.py:492
  242.1 2.1 collective-permute-start.20
  244.2 2.4 collective-permute-start.21
  248.7 4.1 %collective-permute-done.20.refs_12_ = bf16[2,320,128]{2,1,0:T(8,128)(2,1)S(1)} collective-permute-done((bf16[2,320,128]{2,1,0:T(8,128)(2,1)S(1)}, bf16[2,320,128]{2,1,0:T(8,128)(2,1)S(1)}, u32[]{:S(2)}, u32[]{:S(2)}) %collective-permute-start.20) | collective-permute-done | bytes 163872 | tf_op jit(solution)/shard_map/while/body/ppermute | solution.py:474
  252.8 2.5 collective-permute-done.21.refs_13_
  255.2 4.0 %collective-permute-done.22.refs_14_ = bf16[2,320,128]{2,1,0:T(8,128)(2,1)S(1)} collective-permute-done((bf16[2,320,128]{2,1,0:T(8,128)(2,1)S(1)}, bf16[2,320,128]{2,1,0:T(8,128)(2,1)S(1)}, u32[]{:S(2)}, u32[]{:S(2)}) %collective-permute-start.22) | collective-permute-done | bytes 163872 | tf_op jit(solution)/shard_map/while/body/ppermute | solution.py:474
  259.3 3.3 %collective-permute-done.23.refs_15_ = bf16[2,320,128]{2,1,0:T(8,128)(2,1)S(1)} collective-permute-done((bf16[2,320,128]{2,1,0:T(8,128)(2,1)S(1)}, bf16[2,320,128]{2,1,0:T(8,128)(2,1)S(1)}, u32[]{:S(2)}, u32[]{:S(2)}) %collective-permute-start.23) | collective-permute-done | bytes 163872 | tf_op jit(solution)/shard_map/while/body/ppermute | solution.py:474
  263.4 6.0 %dimers.2 = (bf16[4,72,128]{2,1,0:T(8,128)(2,1)}, bf16[4,72,128]{2,1,0:T(8,128)(2,1)}, bf16[4,72,128]{2,1,0:T(8,128)(2,1)}, bf16[4,72,128]{2,1,0:T(8,128)(2,1)},...) custom-call(s32[256]{0:T(256)} %get-tuple-element.282.refs_1_.table_, ...), custom_call_target="tpu_custom_call" | custom-call | flops 8000000000 | bytes 3000000 | tf_op jit(solution)/shard_map/while/body/dimers/pallas_call | solution.py:223
  279.3 2.4 collective-permute-done.29.refs_9_.refs_10_
  283.8 2.7 place.2
  286.5 15.1 %all-to-all-start.4 = ((bf16[32,72,128]{2,1,0:T(8,128)(2,1)}), bf16[32,72,128]{2,1,0:T(8,128)(2,1)S(1)}, u32[]{:S(2)}, u32[]{:S(2)}) async-start(bf16[32,72,128]{2,1,0:T(8,128)(2,1)} %place.2), calls=%async_computation.4 | async-start | bytes 1179648 | tf_op jit(solution)/shard_map/while/body/all_to_all | solution.py:492
  302.3 2.1 select_reduce_fusion
  304.4 5.4 %add_up.2 = (f32[32,32,256]{2,1,0:T(8,128)S(1)}, f32[32,128]{1,0:T(8,128)S(1)}) custom-call(s32[128]{0:T(128)} %pad_add_fusion.refs_0_.table_ref, s32[256]{0:T(256)} %get-tuple-element.282.refs_1_.table_ref, s32[1]{0:T(128)} %get-tuple-element.467.refs_2_.refs_1_.me_ref, ...), custom_call_target="tpu_custom_call", output_to_operand_aliasing={{0}: (13, {}), {1}: (14, {})} | custom-call | tf_op jit(solution)/shard_map/while/body/add_up/pallas_call | solution.py:124
  309.8 11.0 %all-to-all-done.4.refs_3_ = bf16[32,72,128]{2,1,0:T(8,128)(2,1)S(1)} async-done(((bf16[32,72,128]{2,1,0:T(8,128)(2,1)}), bf16[32,72,128]{2,1,0:T(8,128)(2,1)S(1)}, u32[]{:S(2)}, u32[]{:S(2)}) %all-to-all-start.4) | async-done | bytes 589856 | tf_op jit(solution)/shard_map/while/body/all_to_all | solution.py:492
  (191 shorter events, 43.2 us)
Async XLA Ops:
  12.8 19.8 %all-to-all-start.6 = ((s32[32,1,128]{2,1,0:T(1,128)}), s32[32,1,128]{2,1,0:T(1,128)S(1)}, u32[]{:S(2)}, u32[]{:S(2)}) async-start(s32[32,1,128]{2,1,0:T(1,128)} %broadcast_in_dim.147), calls=%async_computation.6 | async-start | bytes 32768 | tf_op jit(solution)/shard_map/all_to_all | solution.py:492
  38.8 72.9 %all-to-all-start = ((bf16[32,320,128]{2,1,0:T(8,128)(2,1)}), bf16[32,320,128]{2,1,0:T(8,128)(2,1)}, u32[]{:S(2)}, u32[]{:S(2)}) async-start(bf16[32,320,128]{2,1,0:T(8,128)(2,1)} %pack.9), calls=%async_computation | async-start | bytes 5242880 | tf_op jit(solution)/shard_map/while/body/all_to_all | solution.py:492
  78.6 18.1 %collective-permute-start.7 = (bf16[6,320,128]{2,1,0:T(8,128)(2,1)}, bf16[6,320,128]{2,1,0:T(8,128)(2,1)S(1)}, u32[]{:S(2)}, u32[]{:S(2)}) collective-permute-start(bf16[6,320,128]{2,1,0:T(8,128)(2,1)} %get-tuple-element.294), channel_id=1, source_target_pairs={{0,64},{8,72},{16,80},{24,88},{32,96},{40,104},{48,112},{56,120},{... | collective-permute-start | bytes 1474568 | tf_op jit(solution)/shard_map/while/body/ppermute | solution.py:483
  80.2 30.3 %collective-permute-start.8 = (bf16[6,320,128]{2,1,0:T(8,128)(2,1)}, bf16[6,320,128]{2,1,0:T(8,128)(2,1)}, u32[]{:S(2)}, u32[]{:S(2)}) collective-permute-start(bf16[6,320,128]{2,1,0:T(8,128)(2,1)} %get-tuple-element.295), channel_id=1, source_target_pairs={{0,128},{8,136},{16,144},{24,152},{32,160},{40,168},{48,176},{56,1... | collective-permute-start | bytes 1474568 | tf_op jit(solution)/shard_map/while/body/ppermute | solution.py:483
  83.0 32.8 %collective-permute-start.9 = (bf16[6,320,128]{2,1,0:T(8,128)(2,1)}, bf16[6,320,128]{2,1,0:T(8,128)(2,1)}, u32[]{:S(2)}, u32[]{:S(2)}) collective-permute-start(bf16[6,320,128]{2,1,0:T(8,128)(2,1)} %get-tuple-element.296), channel_id=1, source_target_pairs={{0,192},{8,200},{16,208},{24,216},{32,224},{40,232},{48,240},{56,2... | collective-permute-start | bytes 1474568 | tf_op jit(solution)/shard_map/while/body/ppermute | solution.py:483
  86.5 39.9 %collective-permute-start.31 = (bf16[4,320,128]{2,1,0:T(8,128)(2,1)}, bf16[4,320,128]{2,1,0:T(8,128)(2,1)S(1)}, u32[]{:S(2)}, u32[]{:S(2)}) collective-permute-start(bf16[4,320,128]{2,1,0:T(8,128)(2,1)} %get-tuple-element.326), channel_id=1, source_target_pairs={{0,1},{1,0},{2,3},{3,2},{4,5},{5,4},{6,7},{7,6},{8,9},{9,8},{10,11... | collective-permute-start | bytes 983048 | tf_op jit(solution)/shard_map/while/body/ppermute | solution.py:474
  86.5 42.1 %collective-permute-start.32 = (bf16[4,320,128]{2,1,0:T(8,128)(2,1)}, bf16[4,320,128]{2,1,0:T(8,128)(2,1)}, u32[]{:S(2)}, u32[]{:S(2)}) collective-permute-start(bf16[4,320,128]{2,1,0:T(8,128)(2,1)} %get-tuple-element.327), channel_id=1, source_target_pairs={{0,2},{1,3},{2,0},{3,1},{4,6},{5,7},{6,4},{7,5},{8,10},{9,11},{10,... | collective-permute-start | bytes 983048 | tf_op jit(solution)/shard_map/while/body/ppermute | solution.py:474
  96.8 34.7 %collective-permute-start.33 = (bf16[4,320,128]{2,1,0:T(8,128)(2,1)}, bf16[4,320,128]{2,1,0:T(8,128)(2,1)}, u32[]{:S(2)}, u32[]{:S(2)}) collective-permute-start(bf16[4,320,128]{2,1,0:T(8,128)(2,1)} %get-tuple-element.328), channel_id=1, source_target_pairs={{0,3},{1,2},{2,1},{3,0},{4,7},{5,6},{6,5},{7,4},{8,11},{9,10},{10,... | collective-permute-start | bytes 983048 | tf_op jit(solution)/shard_map/while/body/ppermute | solution.py:474
  110.5 21.0 %collective-permute-start.34 = (bf16[4,320,128]{2,1,0:T(8,128)(2,1)}, bf16[4,320,128]{2,1,0:T(8,128)(2,1)}, u32[]{:S(2)}, u32[]{:S(2)}) collective-permute-start(bf16[4,320,128]{2,1,0:T(8,128)(2,1)} %get-tuple-element.329), channel_id=1, source_target_pairs={{0,4},{1,5},{2,6},{3,7},{4,0},{5,1},{6,2},{7,3},{8,12},{9,13},{10,... | collective-permute-start | bytes 983048 | tf_op jit(solution)/shard_map/while/body/ppermute | solution.py:474
  118.7 74.9 %all-to-all-start.1 = ((bf16[16,320,128]{2,1,0:T(8,128)(2,1)}), bf16[16,320,128]{2,1,0:T(8,128)(2,1)}, u32[]{:S(2)}, u32[]{:S(2)}) async-start(bf16[16,320,128]{2,1,0:T(8,128)(2,1)} %pack.11), calls=%async_computation.1 | async-start | bytes 2621440 | tf_op jit(solution)/shard_map/while/body/all_to_all | solution.py:488
  126.4 11.8 %collective-permute-start.35 = (bf16[4,320,128]{2,1,0:T(8,128)(2,1)}, bf16[4,320,128]{2,1,0:T(8,128)(2,1)S(1)}, u32[]{:S(2)}, u32[]{:S(2)}) collective-permute-start(bf16[4,320,128]{2,1,0:T(8,128)(2,1)} %get-tuple-element.330), channel_id=1, source_target_pairs={{0,5},{1,4},{2,7},{3,6},{4,1},{5,0},{6,3},{7,2},{8,13},{9,12},{10,... | collective-permute-start | bytes 983048 | tf_op jit(solution)/shard_map/while/body/ppermute | solution.py:474
  126.4 54.0 %copy-start.17 = (bf16[4,320,128]{2,1,0:T(8,128)(2,1)}, bf16[4,320,128]{2,1,0:T(8,128)(2,1)S(1)}, u32[]{:S(2)}) copy-start(bf16[4,320,128]{2,1,0:T(8,128)(2,1)S(1)} %collective-permute-done.31.refs_1_) | copy-start | bytes 983044 | tf_op jit(solution)/shard_map/while
  126.4 18.0 %collective-permute-start.36 = (bf16[4,320,128]{2,1,0:T(8,128)(2,1)}, bf16[4,320,128]{2,1,0:T(8,128)(2,1)S(1)}, u32[]{:S(2)}, u32[]{:S(2)}) collective-permute-start(bf16[4,320,128]{2,1,0:T(8,128)(2,1)} %get-tuple-element.331), channel_id=1, source_target_pairs={{0,6},{1,7},{2,4},{3,5},{4,2},{5,3},{6,0},{7,1},{8,14},{9,15},{10,... | collective-permute-start | bytes 983048 | tf_op jit(solution)/shard_map/while/body/ppermute | solution.py:474
  128.6 23.5 %collective-permute-start.37 = (bf16[4,320,128]{2,1,0:T(8,128)(2,1)}, bf16[4,320,128]{2,1,0:T(8,128)(2,1)S(1)}, u32[]{:S(2)}, u32[]{:S(2)}) collective-permute-start(bf16[4,320,128]{2,1,0:T(8,128)(2,1)} %get-tuple-element.332), channel_id=1, source_target_pairs={{0,7},{1,6},{2,5},{3,4},{4,3},{5,2},{6,1},{7,0},{8,15},{9,14},{10,... | collective-permute-start | bytes 983048 | tf_op jit(solution)/shard_map/while/body/ppermute | solution.py:474
  131.5 22.8 %collective-permute-start.10 = (bf16[4,320,128]{2,1,0:T(8,128)(2,1)}, bf16[4,320,128]{2,1,0:T(8,128)(2,1)S(1)}, u32[]{:S(2)}, u32[]{:S(2)}) collective-permute-start(bf16[4,320,128]{2,1,0:T(8,128)(2,1)} %get-tuple-element.298), channel_id=1, source_target_pairs={{0,1},{1,0},{2,3},{3,2},{4,5},{5,4},{6,7},{7,6},{8,9},{9,8},{10,11... | collective-permute-start | bytes 983048 | tf_op jit(solution)/shard_map/while/body/ppermute | solution.py:474
  131.5 23.8 %collective-permute-start.11 = (bf16[4,320,128]{2,1,0:T(8,128)(2,1)}, bf16[4,320,128]{2,1,0:T(8,128)(2,1)S(1)}, u32[]{:S(2)}, u32[]{:S(2)}) collective-permute-start(bf16[4,320,128]{2,1,0:T(8,128)(2,1)} %get-tuple-element.299), channel_id=1, source_target_pairs={{0,2},{1,3},{2,0},{3,1},{4,6},{5,7},{6,4},{7,5},{8,10},{9,11},{10,... | collective-permute-start | bytes 983048 | tf_op jit(solution)/shard_map/while/body/ppermute | solution.py:474
  138.2 19.1 %collective-permute-start.12 = (bf16[4,320,128]{2,1,0:T(8,128)(2,1)}, bf16[4,320,128]{2,1,0:T(8,128)(2,1)S(1)}, u32[]{:S(2)}, u32[]{:S(2)}) collective-permute-start(bf16[4,320,128]{2,1,0:T(8,128)(2,1)} %get-tuple-element.300), channel_id=1, source_target_pairs={{0,3},{1,2},{2,1},{3,0},{4,7},{5,6},{6,5},{7,4},{8,11},{9,10},{10,... | collective-permute-start | bytes 983048 | tf_op jit(solution)/shard_map/while/body/ppermute | solution.py:474
  144.5 13.6 %collective-permute-start.13 = (bf16[4,320,128]{2,1,0:T(8,128)(2,1)}, bf16[4,320,128]{2,1,0:T(8,128)(2,1)S(1)}, u32[]{:S(2)}, u32[]{:S(2)}) collective-permute-start(bf16[4,320,128]{2,1,0:T(8,128)(2,1)} %get-tuple-element.301), channel_id=1, source_target_pairs={{0,4},{1,5},{2,6},{3,7},{4,0},{5,1},{6,2},{7,3},{8,12},{9,13},{10,... | collective-permute-start | bytes 983048 | tf_op jit(solution)/shard_map/while/body/ppermute | solution.py:474
  152.1 13.7 %collective-permute-start.14 = (bf16[4,320,128]{2,1,0:T(8,128)(2,1)}, bf16[4,320,128]{2,1,0:T(8,128)(2,1)S(1)}, u32[]{:S(2)}, u32[]{:S(2)}) collective-permute-start(bf16[4,320,128]{2,1,0:T(8,128)(2,1)} %get-tuple-element.302), channel_id=1, source_target_pairs={{0,5},{1,4},{2,7},{3,6},{4,1},{5,0},{6,3},{7,2},{8,13},{9,12},{10,... | collective-permute-start | bytes 983048 | tf_op jit(solution)/shard_map/while/body/ppermute | solution.py:474
  154.3 18.5 %collective-permute-start.15 = (bf16[4,320,128]{2,1,0:T(8,128)(2,1)}, bf16[4,320,128]{2,1,0:T(8,128)(2,1)S(1)}, u32[]{:S(2)}, u32[]{:S(2)}) collective-permute-start(bf16[4,320,128]{2,1,0:T(8,128)(2,1)} %get-tuple-element.303), channel_id=1, source_target_pairs={{0,6},{1,7},{2,4},{3,5},{4,2},{5,3},{6,0},{7,1},{8,14},{9,15},{10,... | collective-permute-start | bytes 983048 | tf_op jit(solution)/shard_map/while/body/ppermute | solution.py:474
  155.3 24.4 %collective-permute-start.16 = (bf16[4,320,128]{2,1,0:T(8,128)(2,1)S(1)}, bf16[4,320,128]{2,1,0:T(8,128)(2,1)S(1)}, u32[]{:S(2)}, u32[]{:S(2)}) collective-permute-start(bf16[4,320,128]{2,1,0:T(8,128)(2,1)S(1)} %copy-done.18), channel_id=1, source_target_pairs={{0,7},{1,6},{2,5},{3,4},{4,3},{5,2},{6,1},{7,0},{8,15},{9,14},{10,... | collective-permute-start | bytes 983048 | tf_op jit(solution)/shard_map/while/body/ppermute | solution.py:474
  193.6 33.3 %all-to-all-start.2 = ((bf16[8,8,72,128]{3,2,1,0:T(8,128)(2,1)}), bf16[8,8,72,128]{3,2,1,0:T(8,128)(2,1)}, u32[]{:S(2)}, u32[]{:S(2)}) async-start(bf16[8,8,72,128]{3,2,1,0:T(8,128)(2,1)} %dimers.3), calls=%async_computation.2 | async-start | bytes 2359296 | tf_op jit(solution)/shard_map/while/body/all_to_all | solution.py:479
  200.1 9.0 %collective-permute-start = (bf16[2,320,128]{2,1,0:T(8,128)(2,1)}, bf16[2,320,128]{2,1,0:T(8,128)(2,1)S(1)}, u32[]{:S(2)}, u32[]{:S(2)}) collective-permute-start(bf16[2,320,128]{2,1,0:T(8,128)(2,1)} %get-tuple-element.287), channel_id=1, source_target_pairs={{0,1},{1,0},{2,3},{3,2},{4,5},{5,4},{6,7},{7,6},{8,9},{9,8},{10,11... | collective-permute-start | bytes 491528 | tf_op jit(solution)/shard_map/while/body/ppermute | solution.py:474
  200.5 17.2 %collective-permute-start.1 = (bf16[2,320,128]{2,1,0:T(8,128)(2,1)}, bf16[2,320,128]{2,1,0:T(8,128)(2,1)S(1)}, u32[]{:S(2)}, u32[]{:S(2)}) collective-permute-start(bf16[2,320,128]{2,1,0:T(8,128)(2,1)} %get-tuple-element.288), channel_id=1, source_target_pairs={{0,2},{1,3},{2,0},{3,1},{4,6},{5,7},{6,4},{7,5},{8,10},{9,11},{10,... | collective-permute-start | bytes 491528 | tf_op jit(solution)/shard_map/while/body/ppermute | solution.py:474
  202.1 17.9 %collective-permute-start.2 = (bf16[2,320,128]{2,1,0:T(8,128)(2,1)}, bf16[2,320,128]{2,1,0:T(8,128)(2,1)S(1)}, u32[]{:S(2)}, u32[]{:S(2)}) collective-permute-start(bf16[2,320,128]{2,1,0:T(8,128)(2,1)} %get-tuple-element.289), channel_id=1, source_target_pairs={{0,3},{1,2},{2,1},{3,0},{4,7},{5,6},{6,5},{7,4},{8,11},{9,10},{10,... | collective-permute-start | bytes 491528 | tf_op jit(solution)/shard_map/while/body/ppermute | solution.py:474
  202.1 24.1 %collective-permute-start.3 = (bf16[2,320,128]{2,1,0:T(8,128)(2,1)}, bf16[2,320,128]{2,1,0:T(8,128)(2,1)S(1)}, u32[]{:S(2)}, u32[]{:S(2)}) collective-permute-start(bf16[2,320,128]{2,1,0:T(8,128)(2,1)} %get-tuple-element.290), channel_id=1, source_target_pairs={{0,4},{1,5},{2,6},{3,7},{4,0},{5,1},{6,2},{7,3},{8,12},{9,13},{10,... | collective-permute-start | bytes 491528 | tf_op jit(solution)/shard_map/while/body/ppermute | solution.py:474
  205.4 36.5 %collective-permute-start.4 = (bf16[2,320,128]{2,1,0:T(8,128)(2,1)}, bf16[2,320,128]{2,1,0:T(8,128)(2,1)S(1)}, u32[]{:S(2)}, u32[]{:S(2)}) collective-permute-start(bf16[2,320,128]{2,1,0:T(8,128)(2,1)} %get-tuple-element.291), channel_id=1, source_target_pairs={{0,5},{1,4},{2,7},{3,6},{4,1},{5,0},{6,3},{7,2},{8,13},{9,12},{10,... | collective-permute-start | bytes 491528 | tf_op jit(solution)/shard_map/while/body/ppermute | solution.py:474
  209.1 54.2 %copy-start.29 = (bf16[2,320,128]{2,1,0:T(8,128)(2,1)}, bf16[2,320,128]{2,1,0:T(8,128)(2,1)S(1)}, u32[]{:S(2)}) copy-start(bf16[2,320,128]{2,1,0:T(8,128)(2,1)S(1)} %collective-permute-done.refs_1_) | copy-start | bytes 491524 | tf_op jit(solution)/shard_map/while
  209.1 33.0 %collective-permute-start.5 = (bf16[2,320,128]{2,1,0:T(8,128)(2,1)S(1)}, bf16[2,320,128]{2,1,0:T(8,128)(2,1)S(1)}, u32[]{:S(2)}, u32[]{:S(2)}) collective-permute-start(bf16[2,320,128]{2,1,0:T(8,128)(2,1)S(1)} %copy-done.44), channel_id=1, source_target_pairs={{0,6},{1,7},{2,4},{3,5},{4,2},{5,3},{6,0},{7,1},{8,14},{9,15},{10,... | collective-permute-start | bytes 491528 | tf_op jit(solution)/shard_map/while/body/ppermute | solution.py:474
  217.6 45.6 %copy-start.30 = (bf16[2,320,128]{2,1,0:T(8,128)(2,1)}, bf16[2,320,128]{2,1,0:T(8,128)(2,1)S(1)}, u32[]{:S(2)}) copy-start(bf16[2,320,128]{2,1,0:T(8,128)(2,1)S(1)} %collective-permute-done.1.refs_2_) | copy-start | bytes 491524 | tf_op jit(solution)/shard_map/while
  217.7 26.6 %collective-permute-start.6 = (bf16[2,320,128]{2,1,0:T(8,128)(2,1)S(1)}, bf16[2,320,128]{2,1,0:T(8,128)(2,1)S(1)}, u32[]{:S(2)}, u32[]{:S(2)}) collective-permute-start(bf16[2,320,128]{2,1,0:T(8,128)(2,1)S(1)} %copy-done.41), channel_id=1, source_target_pairs={{0,7},{1,6},{2,5},{3,4},{4,3},{5,2},{6,1},{7,0},{8,15},{9,14},{10,... | collective-permute-start | bytes 491528 | tf_op jit(solution)/shard_map/while/body/ppermute | solution.py:474
  220.0 43.3 %copy-start.31 = (bf16[2,320,128]{2,1,0:T(8,128)(2,1)}, bf16[2,320,128]{2,1,0:T(8,128)(2,1)S(1)}, u32[]{:S(2)}) copy-start(bf16[2,320,128]{2,1,0:T(8,128)(2,1)S(1)} %collective-permute-done.2.refs_3_) | copy-start | bytes 491524 | tf_op jit(solution)/shard_map/while
  220.0 26.6 %collective-permute-start.17 = (bf16[2,320,128]{2,1,0:T(8,128)(2,1)}, bf16[2,320,128]{2,1,0:T(8,128)(2,1)S(1)}, u32[]{:S(2)}, u32[]{:S(2)}) collective-permute-start(bf16[2,320,128]{2,1,0:T(8,128)(2,1)} %get-tuple-element.310), channel_id=1, source_target_pairs={{0,1},{1,0},{2,3},{3,2},{4,5},{5,4},{6,7},{7,6},{8,9},{9,8},{10,11... | collective-permute-start | bytes 491528 | tf_op jit(solution)/shard_map/while/body/ppermute | solution.py:474
  226.3 21.6 %collective-permute-start.18 = (bf16[2,320,128]{2,1,0:T(8,128)(2,1)}, bf16[2,320,128]{2,1,0:T(8,128)(2,1)S(1)}, u32[]{:S(2)}, u32[]{:S(2)}) collective-permute-start(bf16[2,320,128]{2,1,0:T(8,128)(2,1)} %get-tuple-element.311), channel_id=1, source_target_pairs={{0,2},{1,3},{2,0},{3,1},{4,6},{5,7},{6,4},{7,5},{8,10},{9,11},{10,... | collective-permute-start | bytes 491528 | tf_op jit(solution)/shard_map/while/body/ppermute | solution.py:474
  231.1 55.5 %all-to-all-start.3 = ((bf16[32,72,128]{2,1,0:T(8,128)(2,1)}), bf16[32,72,128]{2,1,0:T(8,128)(2,1)S(1)}, u32[]{:S(2)}, u32[]{:S(2)}) async-start(bf16[32,72,128]{2,1,0:T(8,128)(2,1)} %place.3), calls=%async_computation.3 | async-start | bytes 1179648 | tf_op jit(solution)/shard_map/while/body/all_to_all | solution.py:492
  242.0 6.7 %collective-permute-start.19 = (bf16[2,320,128]{2,1,0:T(8,128)(2,1)S(1)}, bf16[2,320,128]{2,1,0:T(8,128)(2,1)S(1)}, u32[]{:S(2)}, u32[]{:S(2)}) collective-permute-start(bf16[2,320,128]{2,1,0:T(8,128)(2,1)S(1)} %copy-done.42), channel_id=1, source_target_pairs={{0,3},{1,2},{2,1},{3,0},{4,7},{5,6},{6,5},{7,4},{8,11},{9,10},{10,... | collective-permute-start | bytes 491528 | tf_op jit(solution)/shard_map/while/body/ppermute | solution.py:474
  242.1 10.7 %collective-permute-start.20 = (bf16[2,320,128]{2,1,0:T(8,128)(2,1)S(1)}, bf16[2,320,128]{2,1,0:T(8,128)(2,1)S(1)}, u32[]{:S(2)}, u32[]{:S(2)}) collective-permute-start(bf16[2,320,128]{2,1,0:T(8,128)(2,1)S(1)} %copy-done.40), channel_id=1, source_target_pairs={{0,4},{1,5},{2,6},{3,7},{4,0},{5,1},{6,2},{7,3},{8,12},{9,13},{10,... | collective-permute-start | bytes 491528 | tf_op jit(solution)/shard_map/while/body/ppermute | solution.py:474
  244.2 11.0 %collective-permute-start.21 = (bf16[2,320,128]{2,1,0:T(8,128)(2,1)S(1)}, bf16[2,320,128]{2,1,0:T(8,128)(2,1)S(1)}, u32[]{:S(2)}, u32[]{:S(2)}) collective-permute-start(bf16[2,320,128]{2,1,0:T(8,128)(2,1)S(1)} %copy-done.38), channel_id=1, source_target_pairs={{0,5},{1,4},{2,7},{3,6},{4,1},{5,0},{6,3},{7,2},{8,13},{9,12},{10,... | collective-permute-start | bytes 491528 | tf_op jit(solution)/shard_map/while/body/ppermute | solution.py:474
  246.7 12.6 %collective-permute-start.22 = (bf16[2,320,128]{2,1,0:T(8,128)(2,1)S(1)}, bf16[2,320,128]{2,1,0:T(8,128)(2,1)S(1)}, u32[]{:S(2)}, u32[]{:S(2)}) collective-permute-start(bf16[2,320,128]{2,1,0:T(8,128)(2,1)S(1)} %copy-done.37), channel_id=1, source_target_pairs={{0,6},{1,7},{2,4},{3,5},{4,2},{5,3},{6,0},{7,1},{8,14},{9,15},{10,... | collective-permute-start | bytes 491528 | tf_op jit(solution)/shard_map/while/body/ppermute | solution.py:474
  247.9 14.7 %collective-permute-start.23 = (bf16[2,320,128]{2,1,0:T(8,128)(2,1)S(1)}, bf16[2,320,128]{2,1,0:T(8,128)(2,1)S(1)}, u32[]{:S(2)}, u32[]{:S(2)}) collective-permute-start(bf16[2,320,128]{2,1,0:T(8,128)(2,1)S(1)} %copy-done.36), channel_id=1, source_target_pairs={{0,7},{1,6},{2,5},{3,4},{4,3},{5,2},{6,1},{7,0},{8,15},{9,14},{10,... | collective-permute-start | bytes 491528 | tf_op jit(solution)/shard_map/while/body/ppermute | solution.py:474
  269.4 5.2 %collective-permute-start.24 = (bf16[4,72,128]{2,1,0:T(8,128)(2,1)}, bf16[4,72,128]{2,1,0:T(8,128)(2,1)S(1)}, u32[]{:S(2)}, u32[]{:S(2)}) collective-permute-start(bf16[4,72,128]{2,1,0:T(8,128)(2,1)} %get-tuple-element.318), channel_id=1, source_target_pairs={{0,1},{1,0},{2,3},{3,2},{4,5},{5,4},{6,7},{7,6},{8,9},{9,8},{10,11... | collective-permute-start | bytes 221192 | tf_op jit(solution)/shard_map/while/body/ppermute | solution.py:474
  269.6 6.8 %collective-permute-start.25 = (bf16[4,72,128]{2,1,0:T(8,128)(2,1)}, bf16[4,72,128]{2,1,0:T(8,128)(2,1)S(1)}, u32[]{:S(2)}, u32[]{:S(2)}) collective-permute-start(bf16[4,72,128]{2,1,0:T(8,128)(2,1)} %get-tuple-element.319), channel_id=1, source_target_pairs={{0,2},{1,3},{2,0},{3,1},{4,6},{5,7},{6,4},{7,5},{8,10},{9,11},{10,... | collective-permute-start | bytes 221192 | tf_op jit(solution)/shard_map/while/body/ppermute | solution.py:474
  269.6 8.0 %collective-permute-start.26 = (bf16[4,72,128]{2,1,0:T(8,128)(2,1)}, bf16[4,72,128]{2,1,0:T(8,128)(2,1)S(1)}, u32[]{:S(2)}, u32[]{:S(2)}) collective-permute-start(bf16[4,72,128]{2,1,0:T(8,128)(2,1)} %get-tuple-element.320), channel_id=1, source_target_pairs={{0,3},{1,2},{2,1},{3,0},{4,7},{5,6},{6,5},{7,4},{8,11},{9,10},{10,... | collective-permute-start | bytes 221192 | tf_op jit(solution)/shard_map/while/body/ppermute | solution.py:474
  271.4 7.9 %collective-permute-start.27 = (bf16[4,72,128]{2,1,0:T(8,128)(2,1)}, bf16[4,72,128]{2,1,0:T(8,128)(2,1)S(1)}, u32[]{:S(2)}, u32[]{:S(2)}) collective-permute-start(bf16[4,72,128]{2,1,0:T(8,128)(2,1)} %get-tuple-element.321), channel_id=1, source_target_pairs={{0,4},{1,5},{2,6},{3,7},{4,0},{5,1},{6,2},{7,3},{8,12},{9,13},{10,... | collective-permute-start | bytes 221192 | tf_op jit(solution)/shard_map/while/body/ppermute | solution.py:474
  272.9 6.4 %collective-permute-start.28 = (bf16[4,72,128]{2,1,0:T(8,128)(2,1)}, bf16[4,72,128]{2,1,0:T(8,128)(2,1)S(1)}, u32[]{:S(2)}, u32[]{:S(2)}) collective-permute-start(bf16[4,72,128]{2,1,0:T(8,128)(2,1)} %get-tuple-element.322), channel_id=1, source_target_pairs={{0,5},{1,4},{2,7},{3,6},{4,1},{5,0},{6,3},{7,2},{8,13},{9,12},{10,... | collective-permute-start | bytes 221192 | tf_op jit(solution)/shard_map/while/body/ppermute | solution.py:474
  274.6 7.1 %collective-permute-start.29 = (bf16[4,72,128]{2,1,0:T(8,128)(2,1)}, bf16[4,72,128]{2,1,0:T(8,128)(2,1)S(1)}, u32[]{:S(2)}, u32[]{:S(2)}) collective-permute-start(bf16[4,72,128]{2,1,0:T(8,128)(2,1)} %get-tuple-element.323), channel_id=1, source_target_pairs={{0,6},{1,7},{2,4},{3,5},{4,2},{5,3},{6,0},{7,1},{8,14},{9,15},{10,... | collective-permute-start | bytes 221192 | tf_op jit(solution)/shard_map/while/body/ppermute | solution.py:474
  276.4 6.8 %collective-permute-start.30 = (bf16[4,72,128]{2,1,0:T(8,128)(2,1)}, bf16[4,72,128]{2,1,0:T(8,128)(2,1)S(1)}, u32[]{:S(2)}, u32[]{:S(2)}) collective-permute-start(bf16[4,72,128]{2,1,0:T(8,128)(2,1)} %get-tuple-element.324), channel_id=1, source_target_pairs={{0,7},{1,6},{2,5},{3,4},{4,3},{5,2},{6,1},{7,0},{8,15},{9,14},{10,... | collective-permute-start | bytes 221192 | tf_op jit(solution)/shard_map/while/body/ppermute | solution.py:474
  286.5 34.3 %all-to-all-start.4 = ((bf16[32,72,128]{2,1,0:T(8,128)(2,1)}), bf16[32,72,128]{2,1,0:T(8,128)(2,1)S(1)}, u32[]{:S(2)}, u32[]{:S(2)}) async-start(bf16[32,72,128]{2,1,0:T(8,128)(2,1)} %place.2), calls=%async_computation.4 | async-start | bytes 1179648 | tf_op jit(solution)/shard_map/while/body/all_to_all | solution.py:492
  (46 other events, 884.3 us)
